TPU v7x, 512 devices: a whole 4x8x8 slice. The times are simulated.
512 devices in a mesh: item: 2 (over core), row: 16 (over y, z_lo), col: 16 (over z_hi, x).
Axes of the slice: x: 4, y: 8, z: 8 (z_hi: 4, z_lo: 2; z = z_hi * 2 + z_lo), core: 2. Of those that a mesh axis runs over, the one named last changes fastest.
Arguments:
- latents: bfloat16 [2, 2, 64, 64, 3072], P('item', None, 'row', 'col'), may hold values from -640 to 640
- prompt_rows: bfloat16 [2, 226, 3072], P('item'), may hold values from -640 to 640
- peg_weight: bfloat16 [3, 3, 3072], replicated, may hold values from -1 to 1
- modulation_weight: bfloat16 [512, 6144], P(None, 'col'), may hold values from -0.5 to 0.5
- qkv_weight: bfloat16 [3072, 3, 2048], P(('item', 'row'), None, 'col'), may hold values from -3 to 3
- text_len: int32 [2], P('item'), may hold values from 56 to 226, as said below
- timestep: int32 [2], P('item'), may hold values from 0 to 999
Outputs:
- attended: bfloat16 [2, 2, 64, 64, 2048], P('item', None, 'row', None, 'col')
Inputs may be any that keep to these rules, and one draw needn't show every extreme that they name: `text_len`: one item has all 226 text tokens valid; the others have fewer.
All inputs are finite; a program needn't handle non-finite values.
Results may differ from a plain program's by a relative error of at most 0.02.
Values may be sent and summed in bfloat16 or wider, within the bound.
No kernel may reach another device: no remote copies, remote signals or barrier semaphores. Data moves between devices by JAX's collectives and lax.ppermute only.
A program may use at most 64 MiB of HBM per device.

v0:
```python
import math

import jax
import jax.numpy as jnp
from jax import lax
from jax.sharding import PartitionSpec as P

HD = 64


def with_halo(block, sides, width):
    for axis, dim in sides:
        count = lax.axis_size(axis)
        forward = [(i, i + 1) for i in range(count - 1)]
        backward = [(target, source) for source, target in forward]
        low = lax.ppermute(
            lax.slice_in_dim(block, block.shape[dim] - width, None, axis=dim), axis, forward
        )
        high = lax.ppermute(lax.slice_in_dim(block, 0, width, axis=dim), axis, backward)
        block = jnp.concatenate([low, block, high], axis=dim)
    return block


def time_angles(step, count):
    half = count // 2
    freqs = jnp.exp(-math.log(10000.0) * jnp.arange(half, dtype=jnp.float32) / half)
    angle = step.astype(jnp.float32) * freqs
    return jnp.concatenate([jnp.cos(angle), jnp.sin(angle)])


def modulate(rows, shift, scale):
    values = rows.astype(jnp.float32)
    center = jnp.mean(values, axis=-1, keepdims=True)
    centered = values - center
    spread = jnp.mean(centered * centered, axis=-1, keepdims=True)
    return (centered * lax.rsqrt(spread + 1e-06) * (1.0 + scale) + shift).astype(jnp.bfloat16)


def absorb(carry, queries, key_rows, value_rows, valid):
    running_max, running_sum, weighted = carry
    count = key_rows.shape[0]
    heads = queries.shape[1]
    key_heads = key_rows.reshape(count, heads, HD)
    value_heads = value_rows.reshape(count, heads, HD)
    scores = (
        jnp.einsum("rhd,bhd->rhb", queries, key_heads, preferred_element_type=jnp.float32) * 0.125
    )
    if valid is not None:
        scores = jnp.where(valid[None, None, :], scores, -jnp.inf)
    newest = jnp.maximum(running_max, jnp.max(scores, axis=-1))
    weights = jnp.exp(scores - newest[..., None])
    shrink_by = jnp.exp(running_max - newest)
    running_sum = running_sum * shrink_by + jnp.sum(weights, axis=-1)
    weighted = weighted * shrink_by[..., None] + jnp.einsum(
        "rhb,bhd->rhd",
        weights.astype(jnp.bfloat16),
        value_heads,
        preferred_element_type=jnp.float32,
    )
    return (newest, running_sum, weighted)


def on_device(latents, prompt_rows, peg_weight, modulation_weight, qkv_weight, text_len, timestep):
    tile_h = latents.shape[2]
    tile_w = latents.shape[3]
    width = latents.shape[4]
    padded = with_halo(latents, (("row", 2), ("col", 3)), 1)
    summed = latents.astype(jnp.float32)
    for row_tap in range(3):
        for col_tap in range(3):
            summed = summed + padded[
                :, :, row_tap : row_tap + tile_h, col_tap : col_tap + tile_w, :
            ].astype(jnp.float32) * peg_weight[row_tap, col_tap].astype(jnp.float32)
    convolved = summed.astype(jnp.bfloat16)
    activation = jax.nn.silu(time_angles(timestep[0], modulation_weight.shape[0])).astype(
        jnp.bfloat16
    )
    own_columns = jnp.dot(
        activation[None, :], modulation_weight, preferred_element_type=jnp.float32
    )
    modulation = lax.all_gather(own_columns, "col", axis=1, tiled=True)[0]
    shift = modulation[:width]
    scale = modulation[width:]
    group_rows = lax.all_gather(modulate(convolved, shift, scale), "col", axis=3, tiled=True)
    frames = group_rows.shape[1]
    grid_w = group_rows.shape[3]
    flat_rows = group_rows.reshape(-1, width)
    row_count = flat_rows.shape[0]
    text_normed = modulate(prompt_rows[0], shift, scale)
    text_count = text_normed.shape[0]
    head_width = qkv_weight.shape[2]
    full_weight = lax.all_gather(qkv_weight, ("item", "row"), axis=0, tiled=True)
    latent_proj = jnp.einsum(
        "rd,dkc->rkc", flat_rows, full_weight, preferred_element_type=jnp.float32
    )
    text_proj = jnp.einsum(
        "rd,dkc->rkc", text_normed, full_weight, preferred_element_type=jnp.float32
    )
    latent_qkv = latent_proj.astype(jnp.bfloat16)
    text_qkv = text_proj.astype(jnp.bfloat16)
    heads = head_width // HD
    queries = latent_qkv[:, 0, :].reshape(row_count, heads, HD)
    local_keys = latent_qkv[:, 1, :]
    local_values = latent_qkv[:, 2, :]
    text_valid = jnp.arange(text_count, dtype=jnp.int32) < text_len[0]
    start_carry = (
        jnp.full((row_count, heads), -jnp.inf, jnp.float32),
        jnp.zeros((row_count, heads), jnp.float32),
        jnp.zeros((row_count, heads, HD), jnp.float32),
    )
    text_carry = absorb(start_carry, queries, text_qkv[:, 1, :], text_qkv[:, 2, :], text_valid)
    key_rows = lax.all_gather(local_keys, "row", axis=0, tiled=True)
    value_rows = lax.all_gather(local_values, "row", axis=0, tiled=True)
    total_rows = key_rows.shape[0]
    block_count = total_rows // row_count

    def one_block(state, pair):
        return (absorb(state, queries, pair[0], pair[1], None), None)

    state, unused = lax.scan(
        one_block,
        text_carry,
        (
            key_rows.reshape(block_count, row_count, head_width),
            value_rows.reshape(block_count, row_count, head_width),
        ),
    )
    running_max, running_sum, weighted = state
    attended = (weighted / running_sum[..., None]).astype(jnp.bfloat16)
    return attended.reshape(1, frames, tile_h, grid_w, head_width)


def solution(mesh):
    in_specs = (
        P("item", None, "row", "col", None),
        P("item", None, None),
        P(),
        P(None, "col"),
        P(("item", "row"), None, "col"),
        P("item"),
        P("item"),
    )
    out_specs = P("item", None, "row", None, "col")
    return jax.shard_map(
        on_device, mesh=mesh, in_specs=in_specs, out_specs=out_specs, check_vma=False
    )
```

profile of v0, /device:TPU:6, one launch (start us, length us, event | category | flops | bytes accessed | tf_op | source)
XLA Modules:
  0.0 427.7 jit_solution(11197046939042537317)
XLA Ops:
  6.5 1.1 copy.22
  7.8 1.3 collective-permute-start.1
  9.1 4.9 %collective-permute-start = (bf16[1,2,1,4,3072]{4,2,1,0,3:T(2,128)(2,1)S(1)}, bf16[1,2,1,4,3072]{4,2,1,0,3:T(2,128)(2,1)S(1)}, u32[]{:S(2)}, u32[]{:S(2)}) collective-permute-start(bf16[1,2,1,4,3072]{4,2,1,0,3:T(2,128)(2,1)S(1)} %get-tuple-element.95), channel_id=1, source_target_pairs={{0,16},{16,32},{32,48},{48,64},{64,80},{80,96},{96,112},{112,128},... | collective-permute-start | bytes 147464 | tf_op jit(solution)/shard_map/ppermute | solution.py:16
  14.7 1.0 slice_convert_fusion.8
  15.9 39.2 %all-gather.3 = f32[16,1,384]{2,1,0:T(1,128)S(1)} all-gather(f32[1,1,384]{2,1,0:T(1,128)S(1)} %convolution_bitcast_fusion.2), channel_id=2, replica_groups=mesh['item'=2,'row'=16,'col'=16] {'col'}, dimensions={0}, use_global_device_ids=true | all-gather | bytes 26112 | tf_op jit(solution)/shard_map/all_gather | solution.py:81
  55.2 6.1 %collective-permute-start.2 = (bf16[1,2,6,1,3072]{4,2,1,0,3:T(8,128)(2,1)S(1)}, bf16[1,2,6,1,3072]{4,2,1,0,3:T(8,128)(2,1)S(1)}, u32[]{:S(2)}, u32[]{:S(2)}) collective-permute-start(bf16[1,2,6,1,3072]{4,2,1,0,3:T(8,128)(2,1)S(1)} %get-tuple-element.93), channel_id=1, source_target_pairs={{0,1},{1,2},{2,3},{3,4},{4,5},{5,6},{6,7},{7,8},{8,9},{9,10},{10,1... | collective-permute-start | bytes 221192 | tf_op jit(solution)/shard_map/ppermute | solution.py:16
  61.4 3.1 collective-permute-start.3
  65.1 5.7 %collective-permute-done.3 = bf16[1,2,6,1,3072]{4,2,1,0,3:T(8,128)(2,1)S(1)} collective-permute-done((bf16[1,2,6,1,3072]{4,2,1,0,3:T(8,128)(2,1)S(1)}, bf16[1,2,6,1,3072]{4,2,1,0,3:T(8,128)(2,1)S(1)}, u32[]{:S(2)}, u32[]{:S(2)}) %collective-permute-start.3) | collective-permute-done | bytes 73760 | tf_op jit(solution)/shard_map/ppermute | solution.py:19
  71.5 1.4 convert_reduce_fusion.1
  74.8 77.8 %all-gather.11.cloned.1.call-done = bf16[1,2,4,64,3072]{4,2,1,0,3:T(4,128)(2,1)} async-done(((bf16[1,2,4,4,3072]{4,2,1,0,3:T(4,128)(2,1)}), bf16[1,2,4,64,3072]{4,2,1,0,3:T(4,128)(2,1)}) %all-gather.11.cloned.1.call-update) | async-done | bytes 3145744 | tf_op jit(solution)/shard_map/all_gather | solution.py:84
  152.7 5.3 %copy.28 = bf16[1,2,4,64,3072]{4,3,2,1,0:T(8,128)(2,1)} copy(bf16[1,2,4,64,3072]{4,2,1,0,3:T(4,128)(2,1)} %all-gather.11.cloned.1.call-done) | data formatting | bytes 6291456 | tf_op jit(solution)/shard_map/all_gather | solution.py:84
  158.0 62.5 %all-gather.9.cloned.1.call-done = bf16[3072,3,128]{2,0,1:T(8,128)(2,1)} async-done(((bf16[96,3,128]{2,0,1:T(8,128)(2,1)}), bf16[3072,3,128]{2,0,1:T(8,128)(2,1)}) %all-gather.9.cloned.1.call-update) | async-done | bytes 2359312 | tf_op jit(solution)/shard_map/all_gather | solution.py:92
  220.5 4.1 convolution_convert_fusion
  227.6 1.1 fusion.24
  229.7 71.5 %all-gather.13.cloned.1.call-done = bf16[8192,1,128]{0,2,1:T(8,128)(2,1)} async-done(((bf16[512,1,128]{0,2,1:T(8,128)(2,1)}), bf16[8192,1,128]{0,2,1:T(8,128)(2,1)}) %all-gather.13.cloned.1.call-update) | async-done | bytes 2097168 | tf_op jit(solution)/shard_map/all_gather | solution.py:112
  301.2 2.4 copy.35
  303.6 1.2 copy.30
  304.8 72.2 %all-gather.15.cloned.1.call-done = bf16[8192,1,128]{0,2,1:T(8,128)(2,1)} async-done(((bf16[512,1,128]{0,2,1:T(8,128)(2,1)}), bf16[8192,1,128]{0,2,1:T(8,128)(2,1)}) %all-gather.15.cloned.1.call-update) | async-done | bytes 2097168 | tf_op jit(solution)/shard_map/all_gather | solution.py:113
  377.0 2.4 copy.36
  379.5 2.5 copy.31
  382.0 38.1 %while.14 = (s32[]{:T(128)}, f32[512,2]{0,1:T(2,128)S(1)}, f32[512,2]{0,1:T(2,128)S(1)}, f32[512,2,64]{0,2,1:T(8,128)S(1)}, bf16[16,512,128]{1,2,0:T(8,128)(2,1)...) while((s32[]{:T(128)}, f32[512,2]{0,1:T(2,128)S(1)}, ...), condition=%wide.region_9.10_spmd, body=%wide.region_6.9_spmd.sunk | while | flops 138545152 | bytes 7798881 | solution.py:120
  384.3 0.9 constant_dynamic-slice_fusion.3
  386.7 0.9 constant_dynamic-slice_fusion.3
  389.1 0.9 constant_dynamic-slice_fusion.3
  (154 shorter events, 42.5 us)
Async XLA Ops:
  6.5 9.2 %copy-start = (bf16[512,384]{1,0:T(8,128)(2,1)S(1)}, bf16[512,384]{1,0:T(8,128)(2,1)}, u32[]{:S(2)}) copy-start(bf16[512,384]{1,0:T(8,128)(2,1)} %param.12) | copy-start | bytes 1179652
  6.5 146.1 %all-gather.11.cloned.1.call-start = ((), (), s32[]{:S(2)}) async-start(), calls=%async_computation.1 | async-start | bytes 3342336 | tf_op jit(solution)/shard_map/all_gather | solution.py:84
  7.8 47.3 %collective-permute-start.1 = (bf16[1,2,1,4,3072]{4,2,1,0,3:T(2,128)(2,1)S(1)}, bf16[1,2,1,4,3072]{4,2,1,0,3:T(2,128)(2,1)S(1)}, u32[]{:S(2)}, u32[]{:S(2)}) collective-permute-start(bf16[1,2,1,4,3072]{4,2,1,0,3:T(2,128)(2,1)S(1)} %get-tuple-element.96), channel_id=1, source_target_pairs={{16,0},{32,16},{48,32},{64,48},{80,64},{96,80},{112,96},{128,112},... | collective-permute-start | bytes 147464 | tf_op jit(solution)/shard_map/ppermute | solution.py:19
  9.1 46.0 %collective-permute-start = (bf16[1,2,1,4,3072]{4,2,1,0,3:T(2,128)(2,1)S(1)}, bf16[1,2,1,4,3072]{4,2,1,0,3:T(2,128)(2,1)S(1)}, u32[]{:S(2)}, u32[]{:S(2)}) collective-permute-start(bf16[1,2,1,4,3072]{4,2,1,0,3:T(2,128)(2,1)S(1)} %get-tuple-element.95), channel_id=1, source_target_pairs={{0,16},{16,32},{32,48},{48,64},{64,80},{80,96},{96,112},{112,128},... | collective-permute-start | bytes 147464 | tf_op jit(solution)/shard_map/ppermute | solution.py:16
  55.2 9.9 %collective-permute-start.2 = (bf16[1,2,6,1,3072]{4,2,1,0,3:T(8,128)(2,1)S(1)}, bf16[1,2,6,1,3072]{4,2,1,0,3:T(8,128)(2,1)S(1)}, u32[]{:S(2)}, u32[]{:S(2)}) collective-permute-start(bf16[1,2,6,1,3072]{4,2,1,0,3:T(8,128)(2,1)S(1)} %get-tuple-element.93), channel_id=1, source_target_pairs={{0,1},{1,2},{2,3},{3,4},{4,5},{5,6},{6,7},{7,8},{8,9},{9,10},{10,1... | collective-permute-start | bytes 221192 | tf_op jit(solution)/shard_map/ppermute | solution.py:16
  61.4 9.5 %collective-permute-start.3 = (bf16[1,2,6,1,3072]{4,2,1,0,3:T(8,128)(2,1)S(1)}, bf16[1,2,6,1,3072]{4,2,1,0,3:T(8,128)(2,1)S(1)}, u32[]{:S(2)}, u32[]{:S(2)}) collective-permute-start(bf16[1,2,6,1,3072]{4,2,1,0,3:T(8,128)(2,1)S(1)} %get-tuple-element.94), channel_id=1, source_target_pairs={{1,0},{2,1},{3,2},{4,3},{5,4},{6,5},{7,6},{8,7},{9,8},{10,9},{11,1... | collective-permute-start | bytes 221192 | tf_op jit(solution)/shard_map/ppermute | solution.py:19
  74.0 146.4 %all-gather.9.cloned.1.call-start = ((), (), s32[]{:S(2)}) async-start(), calls=%async_computation | async-start | bytes 2433024 | tf_op jit(solution)/shard_map/all_gather | solution.py:92
  74.8 226.4 %all-gather.13.cloned.1.call-start = ((), (), s32[]{:S(2)}) async-start(), calls=%async_computation.2 | async-start | bytes 2228224 | tf_op jit(solution)/shard_map/all_gather | solution.py:112
  220.5 6.3 %copy-start.1 = (bf16[1,226,3072]{2,1,0:T(8,128)(2,1)S(1)}, bf16[1,226,3072]{2,1,0:T(8,128)(2,1)}, u32[]{:S(2)}) copy-start(bf16[1,226,3072]{2,1,0:T(8,128)(2,1)} %param.10) | copy-start | bytes 4165636
  225.4 151.7 %all-gather.15.cloned.1.call-start = ((), (), s32[]{:S(2)}) async-start(), calls=%async_computation.3 | async-start | bytes 2228224 | tf_op jit(solution)/shard_map/all_gather | solution.py:113
  225.9 1.7 copy-start.2
Sparse Core Ops, SparseCore 0:
  74.2 78.4 all-gather.10
  154.8 65.5 all-gather.8
  225.5 75.6 all-gather.12
  303.2 73.8 all-gather.14
where the time goes:
time: 428 us
  waiting for transfers between devices  291 us (68%)
  blocking collectives  39.2 us (9%)
  local copies, waits for them, and re-layouts  31.9 us (7%)
  matrix products  22.3 us (5%)
  starting transfers between devices  15.8 us (4%)
  between operations  14.8 us (3%)
  other arithmetic  11.6 us (3%)
    all_gather x1, waiting for transfers between devices, on_device(): lax.all_gather(modulate(convolved, shift, scale), 'col', axis=3, tiled=True)  77.8 us
    all_gather x1, waiting for transfers between devices, on_device(): value_rows = lax.all_gather(local_values, 'row', axis=0, tiled=True)  72.2 us
    all_gather x1, waiting for transfers between devices, on_device(): key_rows = lax.all_gather(local_keys, 'row', axis=0, tiled=True)  71.5 us
    all_gather x1, waiting for transfers between devices, on_device(): lax.all_gather(qkv_weight, ('item', 'row'), axis=0, tiled=True)  62.5 us
    all_gather x1, blocking collectives, on_device(): modulation = lax.all_gather(own_columns, 'col', axis=1, tiled=True)[0]  39.2 us
    dynamic_slice x16, local copies, waits for them, and re-layouts, on_device(): lax.scan(one_block, text_carry, (key_rows.reshape(block_count, row_count,...  14.8 us
    ppermute x2, starting transfers between devices, with_halo(): lax.ppermute(lax.slice_in_dim(block, block.shape[dim] - width, None, axis...  11 us
  transfers between devices with their start and end apart: 8, of which 6 were waited for; matrix products, arithmetic and copies ran while one was open for 3% of the time, Pallas kernels for 0%

commit v1 on v0

v1 whole, which is shorter than its diff:
```python
import functools
import math

import jax
import jax.numpy as jnp
from jax import lax
from jax.experimental import pallas as pl
from jax.experimental.pallas import tpu as pltpu
from jax.sharding import Mesh, PartitionSpec as P

HD = 64
LOG2E = 1.4426950408889634
SCALE2 = 0.125 * LOG2E
BF = jnp.bfloat16
F32 = jnp.float32
TEXT_PART = 64


def vmem(*shape):
    return pl.BlockSpec(memory_space=pltpu.VMEM)


def params(mib):
    return pltpu.CompilerParams(vmem_limit_bytes=mib << 20)


def with_halo(block, sides, width):
    for axis, dim in sides:
        count = lax.axis_size(axis)
        forward = [(i, i + 1) for i in range(count - 1)]
        backward = [(target, source) for source, target in forward]
        low = lax.ppermute(
            lax.slice_in_dim(block, block.shape[dim] - width, None, axis=dim), axis, forward
        )
        high = lax.ppermute(lax.slice_in_dim(block, 0, width, axis=dim), axis, backward)
        block = jnp.concatenate([low, block, high], axis=dim)
    return block


def time_angles(step, count):
    half = count // 2
    freqs = jnp.exp(-math.log(10000.0) * jnp.arange(half, dtype=F32) / half)
    angle = step.astype(F32) * freqs
    return jnp.concatenate([jnp.cos(angle), jnp.sin(angle)])


def project_kernel(x_ref, mod_ref, w_ref, *outs):
    values = x_ref[...].astype(F32)
    width = values.shape[1]
    center = jnp.sum(values, axis=1, keepdims=True) * (1.0 / width)
    centered = values - center
    spread = jnp.sum(centered * centered, axis=1, keepdims=True) * (1.0 / width)
    normed = centered * lax.rsqrt(spread + 1e-06) * (1.0 + mod_ref[1:2, :]) + mod_ref[0:1, :]
    rows = jnp.dot(normed.astype(BF), w_ref[...], preferred_element_type=F32).astype(BF)
    at = 0
    for out in outs:
        size = out.shape[1]
        first = rows.shape[1] - sum(o.shape[1] for o in outs) + at
        out[...] = rows[:, first : first + size]
        at += size


def project(x, mod, weight, sizes):
    rows = x.shape[0]
    return pl.pallas_call(
        project_kernel,
        out_shape=[jax.ShapeDtypeStruct((rows, size), BF) for size in sizes],
        in_specs=[vmem()] * 3,
        out_specs=[vmem()] * len(sizes),
        compiler_params=params(24),
        cost_estimate=pl.CostEstimate(
            flops=2 * rows * x.shape[1] * weight.shape[1],
            bytes_accessed=2 * (x.size + weight.size),
            transcendentals=rows,
        ),
        name="project",
    )(x, mod, weight)


def attend_kernel(info, q0, q1, q2, q3, kv, text_kv, o0, o1, o2, o3, values, text_values, *, tile):
    count = kv.shape[0]
    values[:, :128] = kv[:, 128:]
    values[:, 128:] = jnp.ones((count, 128), BF)
    text_values[:, :128] = text_kv[:, 128:]
    text_values[:, 128:] = jnp.ones((TEXT_PART, 128), BF)
    contract = (((1,), (1,)), ((), ()))
    lane = lax.broadcasted_iota(jnp.int32, (tile, 128), 1)
    position = info[0] + lax.broadcasted_iota(jnp.int32, (tile, TEXT_PART), 1)
    valid = (position >= info[1]) & (position < info[2])
    for q_ref, o_ref in ((q0, o0), (q1, o1), (q2, o2), (q3, o3)):

        @pl.loop(0, q_ref.shape[0] // tile)
        def _(step):
            rows = pl.ds(pl.multiple_of(step * tile, tile), tile)
            q = q_ref[rows, :].astype(F32)
            outs, sums = [], []
            for head in range(2):
                own = jnp.where(lane // HD == head, q, 0.0).astype(BF)
                s = lax.dot_general(own, kv[:, :128], contract, preferred_element_type=F32)
                t = lax.dot_general(own, text_kv[:, :128], contract, preferred_element_type=F32)
                t = jnp.where(valid, t, -1e30)
                top = jnp.maximum(
                    jnp.max(s, axis=1, keepdims=True), jnp.max(t, axis=1, keepdims=True)
                )
                top = top * SCALE2
                p = jnp.exp2(s * SCALE2 - top).astype(BF)
                pt = jnp.where(valid, jnp.exp2(t * SCALE2 - top), 0.0).astype(BF)
                acc = jnp.dot(p, values[...], preferred_element_type=F32)
                acc = acc + jnp.dot(pt, text_values[...], preferred_element_type=F32)
                total = acc[:, 128:]
                outs.append(acc[:, :128] / total)
                sums.append(top + jnp.log(total) * LOG2E)
            o_ref[rows, :128] = jnp.where(lane < HD, outs[0], outs[1]).astype(BF)
            stats = jnp.zeros((tile, 128), F32)
            for head in range(2):
                rest = sums[head]
                for part in range(3):
                    piece = rest.astype(BF).astype(F32)
                    stats = jnp.where(lane == 3 * head + part, piece, stats)
                    rest = rest - piece
            o_ref[rows, 128:] = stats.astype(BF)


def attend(info, qs, kv, text_kv):
    count = qs[0].shape[0]
    keys = kv.shape[0]
    return pl.pallas_call(
        functools.partial(attend_kernel, tile=128),
        out_shape=[jax.ShapeDtypeStruct((count, 256), BF)] * 4,
        in_specs=[pl.BlockSpec(memory_space=pltpu.SMEM)] + [vmem()] * 6,
        out_specs=[vmem()] * 4,
        scratch_shapes=[pltpu.VMEM((keys, 256), BF), pltpu.VMEM((TEXT_PART, 256), BF)],
        compiler_params=params(40),
        cost_estimate=pl.CostEstimate(
            flops=4 * 4 * count * (keys + TEXT_PART) * 256,
            bytes_accessed=2 * 256 * (6 * count + keys),
            transcendentals=8 * count * (keys + TEXT_PART),
        ),
        name="attend",
    )(info, *qs, kv, text_kv)


def combine_kernel(slots, p0, p1, p2, p3, out):
    parts = [p[...].astype(F32) for p in (p0, p1, p2, p3)]
    lane = lax.broadcasted_iota(jnp.int32, (parts[0].shape[0], 128), 1)
    lses = []
    for part in parts:
        heads = [
            part[:, 128 + 3 * h : 129 + 3 * h]
            + part[:, 129 + 3 * h : 130 + 3 * h]
            + part[:, 130 + 3 * h : 131 + 3 * h]
            for h in range(2)
        ]
        lses.append(jnp.where(lane < HD, heads[0], heads[1]))
    top = functools.reduce(jnp.maximum, lses)
    shares = [jnp.exp2(lse - top) for lse in lses]
    total = sum(shares)
    weighted = sum(share * part[:, :128] for share, part in zip(shares, parts))
    out[...] = (weighted / total).astype(BF)


def combine(slots, parts):
    count = parts[0].shape[0]
    block = count // 4
    return pl.pallas_call(
        combine_kernel,
        out_shape=jax.ShapeDtypeStruct((count, 128), BF),
        grid_spec=pltpu.PrefetchScalarGridSpec(
            num_scalar_prefetch=1,
            grid=(4,),
            in_specs=[pl.BlockSpec((block, 256), lambda i, slots: (slots[i], 0))] * 4,
            out_specs=pl.BlockSpec((block, 128), lambda i, slots: (i, 0)),
        ),
        compiler_params=params(8),
        name="combine",
    )(slots, *parts)


def on_device(latents, prompt_rows, peg_weight, modulation_weight, qkv_weight, text_len, timestep):
    frames, tile_h, tile_w, width = latents.shape[1:]
    rows_axes = ("u", "v", "zl")
    head_width = qkv_weight.shape[2]
    weight = lax.all_gather(
        qkv_weight.reshape(qkv_weight.shape[0], 3 * head_width),
        ("item",) + rows_axes,
        axis=0,
        tiled=True,
    )
    padded = with_halo(latents, ((rows_axes, 2), (("zh", "x"), 3)), 1)
    summed = latents.astype(F32)
    for row_tap in range(3):
        for col_tap in range(3):
            summed = summed + padded[
                :, :, row_tap : row_tap + tile_h, col_tap : col_tap + tile_w, :
            ].astype(F32) * peg_weight[row_tap, col_tap].astype(F32)
    peg = summed.astype(BF).reshape(frames * tile_h * tile_w, width)
    tokens = lax.all_gather(peg, "zh", axis=0, tiled=True)
    blocks = [tokens] + [
        lax.ppermute(tokens, "x", [(i, (i + k) % 4) for i in range(4)]) for k in (1, 3, 2)
    ]
    activation = jax.nn.silu(time_angles(timestep[0], modulation_weight.shape[0])).astype(BF)
    own_columns = jnp.dot(activation[None, :], modulation_weight, preferred_element_type=F32)
    modulation = lax.all_gather(own_columns, "x", axis=1, tiled=True)
    modulation = lax.all_gather(modulation, "zh", axis=1, tiled=True)
    modulation = modulation.reshape(2, width)

    member = lax.axis_index("v") * 2 + lax.axis_index("zl")
    lower = member * TEXT_PART
    start = jnp.minimum(lower, prompt_rows.shape[1] - TEXT_PART)
    text_rows = lax.dynamic_slice_in_dim(prompt_rows[0], start, TEXT_PART, axis=0)
    (text_kv,) = project(text_rows, modulation, weight, (2 * head_width,))
    projected = [project(block, modulation, weight, (head_width, 2 * head_width)) for block in blocks]
    queries = jnp.concatenate([q for q, _ in projected], axis=0)
    kv = jnp.concatenate([pair for _, pair in projected], axis=0)

    swaps = (
        ("zl", [(0, 1), (1, 0)]),
        ("v", [(0, 1), (1, 0)]),
        (("v", "zl"), [(0, 3), (3, 0), (1, 2), (2, 1)]),
    )
    qs = [queries] + [lax.ppermute(queries, axis, swap) for axis, swap in swaps]
    all_kv = lax.all_gather(kv, "u", axis=0, tiled=True)
    info = jnp.stack([start, lower, text_len[0]])
    parts = attend(info, qs, all_kv, text_kv)
    parts = [parts[0]] + [
        lax.ppermute(part, axis, swap) for part, (axis, swap) in zip(parts[1:], swaps)
    ]
    x_at = lax.axis_index("x")
    slots = jnp.array([0, 2, 3, 1], jnp.int32)[(jnp.arange(4, dtype=jnp.int32) - x_at) % 4]
    attended = combine(slots, parts)
    attended = attended.reshape(4, 4, frames, tile_h, tile_w, head_width)
    attended = attended.transpose(2, 3, 1, 0, 4, 5)
    return attended.reshape(1, frames, tile_h, 16 * tile_w, head_width)


def solution(mesh):
    fine = Mesh(mesh.devices.reshape(2, 4, 2, 2, 4, 4), ("item", "u", "v", "zl", "zh", "x"))
    row = ("u", "v", "zl")
    col = ("zh", "x")
    in_specs = (
        P("item", None, row, col, None),
        P("item", None, None),
        P(),
        P(None, col),
        P(("item",) + row, None, col),
        P("item"),
        P("item"),
    )
    out_specs = P("item", None, row, None, col)
    return jax.shard_map(
        on_device, mesh=fine, in_specs=in_specs, out_specs=out_specs, check_vma=False
    )
```

time: 428 us -> 218 us (0.51)
  waiting for transfers between devices: 291 us -> 34.2 us
  blocking collectives: 39.2 us -> 78.9 us
  Pallas kernels: 0 us -> 31.2 us
  starting transfers between devices: 15.8 us -> 44.4 us
  matrix products: 22.3 us -> 0.17 us
  local copies, waits for them, and re-layouts: 31.9 us -> 10.6 us
  other arithmetic: 11.6 us -> 2.48 us
    all_gather x4 -> x2, waiting for transfers between devices: 284 us -> 15.2 us  [the longest x1 15.2 us: on_device(): all_kv = lax.all_gather(kv, 'u', axis=0, tiled=True)]
    all_gather x1 -> x3, blocking collectives: 39.2 us -> 78.9 us  [the longest x1 36.3 us: on_device(): modulation = lax.all_gather(own_columns, 'x', axis=1, tiled=True)]
    pallas_call x0 -> x7, Pallas kernels: none -> 31.2 us  [the longest x1 21.5 us: attend(): pl.pallas_call(functools.partial(attend_kernel, tile=128), out_shape=[jax...]
    ppermute x0 -> x9, starting transfers between devices: none -> 29.8 us  [the longest x3 11.2 us: on_device(): lax.ppermute(tokens, 'x', [(i, (i + k) % 4) for i in range(4)])]
    dot_general x37 -> x1, matrix products: 22.3 us -> 0.17 us  [on_device(): jnp.dot(activation[None, :], modulation_weight, preferred_element_type=F32)]
    dynamic_slice x16 -> x1, local copies, waits for them, and re-layouts: 14.8 us -> 0.11 us  [on_device(): lax.dynamic_slice_in_dim(prompt_rows[0], start, TEXT_PART, axis=0)]
    ppermute x0 -> x9, waiting for transfers between devices: none -> 12.2 us  [the longest x3 8.79 us: on_device(): lax.ppermute(part, axis, swap)]
    reduce_sum x21 -> x0, other arithmetic: 8.4 us -> none  [the longest x17 5.96 us: absorb(): running_sum = running_sum * shrink_by + jnp.sum(weights, axis=-1)]
  transfers between devices with their start and end apart: 8 -> 15, of which waited for: 6 -> 8; matrix products, arithmetic and copies ran while one was open for 3% -> 2% of each run, Pallas kernels for 0% -> 3%
where the time goes in v1:
time: 218 us; the launch traced here: 217 us
  blocking collectives  78.9 us (36%)
  starting transfers between devices  44.4 us (20%)
  waiting for transfers between devices  34.2 us (16%)
  Pallas kernels  31.2 us (14%)
  between operations  15.1 us (7%)
  local copies, waits for them, and re-layouts  10.6 us (5%)
  other arithmetic  2.48 us (1%)
    all_gather x1, blocking collectives, on_device(): modulation = lax.all_gather(own_columns, 'x', axis=1, tiled=True)  36.3 us
    all_gather x1, blocking collectives, on_device(): tokens = lax.all_gather(peg, 'zh', axis=0, tiled=True)  28.8 us
    pallas_call x1, Pallas kernels, attend(): pl.pallas_call(functools.partial(attend_kernel, tile=128), out_shape=[jax...  21.5 us
    all_gather x1, waiting for transfers between devices, on_device(): all_kv = lax.all_gather(kv, 'u', axis=0, tiled=True)  15.2 us
    all_gather x1, blocking collectives, on_device(): modulation = lax.all_gather(modulation, 'zh', axis=1, tiled=True)  13.8 us
    ppermute x3, starting transfers between devices, on_device(): lax.ppermute(tokens, 'x', [(i, (i + k) % 4) for i in range(4)])  11.2 us
    ppermute x2, starting transfers between devices, with_halo(): lax.ppermute(lax.slice_in_dim(block, block.shape[dim] - width, None, axis...  10.4 us
    ppermute x3, starting transfers between devices, on_device(): qs = [queries] + [lax.ppermute(queries, axis, swap) for axis, swap in swaps]  9.39 us
  transfers between devices with their start and end apart: 15, of which 8 were waited for; matrix products, arithmetic and copies ran while one was open for 2% of the time, Pallas kernels for 3%

profile of v1, /device:TPU:6, one launch (start us, length us, event | category | flops | bytes accessed | tf_op | source)
XLA Modules:
  0.0 217.0 jit_solution(11165728748663626152)
XLA Ops:
  9.1 4.3 %collective-permute-start = (bf16[1,2,1,4,3072]{4,3,2,1,0:T(4,128)(2,1)S(1)}, bf16[1,2,1,4,3072]{4,3,2,1,0:T(4,128)(2,1)S(1)}, u32[]{:S(2)}, u32[]{:S(2)}) collective-permute-start(bf16[1,2,1,4,3072]{4,3,2,1,0:T(4,128)(2,1)S(1)} %get-tuple-element.32), channel_id=1, source_target_pairs={{0,16},{16,32},{32,48},{48,64},{64,80},{80,96},{96,112},{112,128},... | collective-permute-start | bytes 147464 | tf_op jit(solution)/shard_map/ppermute | solution.py:32
  16.2 3.2 %collective-permute-done.1 = bf16[1,2,1,4,3072]{4,3,2,1,0:T(4,128)(2,1)S(1)} collective-permute-done((bf16[1,2,1,4,3072]{4,3,2,1,0:T(4,128)(2,1)S(1)}, bf16[1,2,1,4,3072]{4,3,2,1,0:T(4,128)(2,1)S(1)}, u32[]{:S(2)}, u32[]{:S(2)}) %collective-permute-start.1) | collective-permute-done | bytes 49184 | tf_op jit(solution)/shard_map/ppermute | solution.py:35
  19.7 2.9 %collective-permute-start.3 = (bf16[1,2,6,1,3072]{4,3,2,1,0:T(2,128)(2,1)S(1)}, bf16[1,2,6,1,3072]{4,3,2,1,0:T(2,128)(2,1)S(1)}, u32[]{:S(2)}, u32[]{:S(2)}) collective-permute-start(bf16[1,2,6,1,3072]{4,3,2,1,0:T(2,128)(2,1)S(1)} %get-tuple-element.30), channel_id=1, source_target_pairs={{1,0},{2,1},{3,2},{4,3},{5,4},{6,5},{7,6},{8,7},{9,8},{10,9},{11,1... | collective-permute-start | bytes 221192 | tf_op jit(solution)/shard_map/ppermute | solution.py:35
  22.6 6.1 %collective-permute-start.2 = (bf16[1,2,6,1,3072]{4,3,2,1,0:T(2,128)(2,1)S(1)}, bf16[1,2,6,1,3072]{4,3,2,1,0:T(2,128)(2,1)S(1)}, u32[]{:S(2)}, u32[]{:S(2)}) collective-permute-start(bf16[1,2,6,1,3072]{4,3,2,1,0:T(2,128)(2,1)S(1)} %get-tuple-element.29), channel_id=1, source_target_pairs={{0,1},{1,2},{2,3},{3,4},{4,5},{5,6},{6,7},{7,8},{8,9},{9,10},{10,1... | collective-permute-start | bytes 221192 | tf_op jit(solution)/shard_map/ppermute | solution.py:32
  28.8 3.1 %collective-permute-done.3 = bf16[1,2,6,1,3072]{4,3,2,1,0:T(2,128)(2,1)S(1)} collective-permute-done((bf16[1,2,6,1,3072]{4,3,2,1,0:T(2,128)(2,1)S(1)}, bf16[1,2,6,1,3072]{4,3,2,1,0:T(2,128)(2,1)S(1)}, u32[]{:S(2)}, u32[]{:S(2)}) %collective-permute-start.3) | collective-permute-done | bytes 73760 | tf_op jit(solution)/shard_map/ppermute | solution.py:35
  33.4 28.8 %all_gather.15.x_ref = bf16[128,3072]{1,0:T(8,128)(2,1)S(1)} all-gather(bf16[32,3072]{1,0:T(8,128)(2,1)S(1)} %reshape.155), channel_id=1, replica_groups=mesh['item'=2,'u'=4,'v'=2,'zl'=2,'zh'=4,'x'=4] {'zh'}, dimensions={0}, use_global_device_ids=true | all-gather | bytes 983040 | tf_op jit(solution)/shard_map/all_gather | solution.py:197
  62.2 5.9 %collective-permute-start.4 = (bf16[128,3072]{1,0:T(8,128)(2,1)S(1)}, bf16[128,3072]{1,0:T(8,128)(2,1)}, u32[]{:S(2)}, u32[]{:S(2)}) collective-permute-start(bf16[128,3072]{1,0:T(8,128)(2,1)S(1)} %all_gather.15.x_ref), channel_id=1, source_target_pairs={{0,1},{1,2},{2,3},{3,0},{4,5},{5,6},{6,7},{7,4},{8,9},{9,10},{10,1... | collective-permute-start | bytes 2359304 | tf_op jit(solution)/shard_map/ppermute | solution.py:199
  68.1 1.9 collective-permute-start.5
  70.0 3.4 %collective-permute-start.6 = (bf16[128,3072]{1,0:T(8,128)(2,1)S(1)}, bf16[128,3072]{1,0:T(8,128)(2,1)S(1)}, u32[]{:S(2)}, u32[]{:S(2)}) collective-permute-start(bf16[128,3072]{1,0:T(8,128)(2,1)S(1)} %all_gather.15.x_ref), channel_id=1, source_target_pairs={{0,2},{1,3},{2,0},{3,1},{4,6},{5,7},{6,4},{7,5},{8,10},{9,11},{10,... | collective-permute-start | bytes 2359304 | tf_op jit(solution)/shard_map/ppermute | solution.py:199
  74.3 36.3 %all-gather.2 = f32[4,1,384]{2,1,0:T(1,128)S(1)} all-gather(f32[1,1,384]{2,1,0:T(1,128)S(1)} %convolution_bitcast_fusion), channel_id=2, replica_groups=mesh['item'=2,'u'=4,'v'=2,'zl'=2,'zh'=4,'x'=4] {'x'}, dimensions={0}, use_global_device_ids=true | all-gather | bytes 7680 | tf_op jit(solution)/shard_map/all_gather | solution.py:203
  110.6 13.8 %all-gather.3 = f32[4,1,1536]{2,1,0:T(1,128)S(1)} all-gather(f32[1,1,1536]{2,1,0:T(1,128)S(1)} %bitcast.40), channel_id=3, replica_groups=mesh['item'=2,'u'=4,'v'=2,'zl'=2,'zh'=4,'x'=4] {'zh'}, dimensions={0}, use_global_device_ids=true | all-gather | bytes 30720 | tf_op jit(solution)/shard_map/all_gather | solution.py:204
  127.9 2.1 project.6
  130.1 2.1 project.7
  134.1 1.9 collective-permute-start.7
  137.9 5.6 %collective-permute-start.9 = (bf16[512,128]{1,0:T(8,128)(2,1)S(1)}, bf16[512,128]{1,0:T(8,128)(2,1)S(1)}, u32[]{:S(2)}, u32[]{:S(2)}) collective-permute-start(bf16[512,128]{1,0:T(8,128)(2,1)S(1)} %constant_dynamic-update-slice_fusion.3.q0), channel_id=1, source_target_pairs={{0,48},{48,0},{16,32},{32,16},{1,49},{49,1},{17,33},{33,17},{2,50}... | collective-permute-start | bytes 393224 | tf_op jit(solution)/shard_map/ppermute | solution.py:221
  146.8 3.4 %collective-permute-done.9.q3 = bf16[512,128]{1,0:T(8,128)(2,1)S(1)} collective-permute-done((bf16[512,128]{1,0:T(8,128)(2,1)S(1)}, bf16[512,128]{1,0:T(8,128)(2,1)S(1)}, u32[]{:S(2)}, u32[]{:S(2)}) %collective-permute-start.9) | collective-permute-done | bytes 131104 | tf_op jit(solution)/shard_map/ppermute | solution.py:221
  150.2 15.2 %all-gather.9.cloned.1.call-done.kv = bf16[2048,256]{1,0:T(8,128)(2,1)} async-done(((bf16[512,256]{1,0:T(8,128)(2,1)}), bf16[2048,256]{1,0:T(8,128)(2,1)}) %all-gather.9.cloned.1.call-update) | async-done | bytes 1048592 | tf_op jit(solution)/shard_map/all_gather | solution.py:222
  166.6 21.5 %attend.1 = (bf16[512,256]{1,0:T(8,128)(2,1)S(1)}, bf16[512,256]{1,0:T(8,128)(2,1)S(1)}, bf16[512,256]{1,0:T(8,128)(2,1)S(1)}, bf16[512,256]{1,0:T(8,128)(2,1)S(1)}) custom-call(s32[3]{0:T(128)S(1)} %pad_add_fusion.info, bf16[512,128]{1,0:T(8,128)(2,1)S(1)} %constant_dynamic-update-slice_fusion.3.q0, bf16[512,128]{1,0:T(8,128)(2,1)S(1)} %collective-permute-done.7.q1, ...), custom_call_target="tpu_custom_call" | custom-call | flops 4429185024 | bytes 2621440 | tf_op jit(solution)/shard_map/attend/pallas_call | solution.py:127
  188.1 3.7 %collective-permute-start.10 = (bf16[512,256]{1,0:T(8,128)(2,1)S(1)}, bf16[512,256]{1,0:T(8,128)(2,1)S(1)}, u32[]{:S(2)}, u32[]{:S(2)}) collective-permute-start(bf16[512,256]{1,0:T(8,128)(2,1)S(1)} %get-tuple-element.26), channel_id=1, source_target_pairs={{0,16},{16,0},{1,17},{17,1},{2,18},{18,2},{3,19},{19,3},{4,20},{20... | collective-permute-start | bytes 786440 | tf_op jit(solution)/shard_map/ppermute | solution.py:226
  191.8 2.2 %collective-permute-start.11 = (bf16[512,256]{1,0:T(8,128)(2,1)S(1)}, bf16[512,256]{1,0:T(8,128)(2,1)S(1)}, u32[]{:S(2)}, u32[]{:S(2)}) collective-permute-start(bf16[512,256]{1,0:T(8,128)(2,1)S(1)} %get-tuple-element.27), channel_id=1, source_target_pairs={{0,32},{32,0},{1,33},{33,1},{2,34},{34,2},{3,35},{35,3},{4,36},{36... | collective-permute-start | bytes 786440 | tf_op jit(solution)/shard_map/ppermute | solution.py:226
  194.0 3.3 %collective-permute-start.12 = (bf16[512,256]{1,0:T(8,128)(2,1)S(1)}, bf16[512,256]{1,0:T(8,128)(2,1)S(1)}, u32[]{:S(2)}, u32[]{:S(2)}) collective-permute-start(bf16[512,256]{1,0:T(8,128)(2,1)S(1)} %get-tuple-element.28), channel_id=1, source_target_pairs={{0,48},{48,0},{16,32},{32,16},{1,49},{49,1},{17,33},{33,17},{2,50}... | collective-permute-start | bytes 786440 | tf_op jit(solution)/shard_map/ppermute | solution.py:226
  198.1 4.8 %collective-permute-done.11.p2 = bf16[512,256]{1,0:T(8,128)(2,1)S(1)} collective-permute-done((bf16[512,256]{1,0:T(8,128)(2,1)S(1)}, bf16[512,256]{1,0:T(8,128)(2,1)S(1)}, u32[]{:S(2)}, u32[]{:S(2)}) %collective-permute-start.11) | collective-permute-done | bytes 262176 | tf_op jit(solution)/shard_map/ppermute | solution.py:226
  202.9 3.9 %collective-permute-done.12.p3 = bf16[512,256]{1,0:T(8,128)(2,1)S(1)} collective-permute-done((bf16[512,256]{1,0:T(8,128)(2,1)S(1)}, bf16[512,256]{1,0:T(8,128)(2,1)S(1)}, u32[]{:S(2)}, u32[]{:S(2)}) %collective-permute-start.12) | collective-permute-done | bytes 262176 | tf_op jit(solution)/shard_map/ppermute | solution.py:226
  206.8 2.6 %combine.1 = bf16[512,128]{1,0:T(8,128)(2,1)S(1)} custom-call(s32[4]{0:T(128)S(1)} %gather_fusion, bf16[512,256]{1,0:T(8,128)(2,1)S(1)} %get-tuple-element.25.p0, bf16[512,256]{1,0:T(8,128)(2,1)S(1)} %collective-permute-done.10.p1, bf16[512,256]{1,0:T(8,128)(2,1)S(1)} %collective-permute-done.11.p2, bf16[512,256]{1,0:T(8,128)(2,1)S(1)} %collective-permute-done.12.p3), custom_call_target="tpu_custom_call" | custom-call | tf_op jit(solution)/shard_map/combine/pallas_call | solution.py:165
  (62 shorter events, 19.8 us)
Async XLA Ops:
  6.5 137.0 %copy-start = (bf16[1,226,3072]{2,1,0:T(8,128)(2,1)S(1)}, bf16[1,226,3072]{2,1,0:T(8,128)(2,1)}, u32[]{:S(2)}) copy-start(bf16[1,226,3072]{2,1,0:T(8,128)(2,1)} %param.9) | copy-start | bytes 4165636
  6.5 25.3 %copy-start.6 = (bf16[1,2,4,4,3072]{4,3,2,1,0:T(4,128)(2,1)S(1)}, bf16[1,2,4,4,3072]{4,3,2,1,0:T(4,128)(2,1)}, u32[]{:S(2)}) copy-start(bf16[1,2,4,4,3072]{4,3,2,1,0:T(4,128)(2,1)} %param.8) | copy-start | bytes 589828
  6.5 22.1 %copy-start.8 = (bf16[3,3,3072]{2,1,0:T(4,128)(2,1)S(1)}, bf16[3,3,3072]{2,1,0:T(4,128)(2,1)}, u32[]{:S(2)}) copy-start(bf16[3,3,3072]{2,1,0:T(4,128)(2,1)} %param.10) | copy-start | bytes 165892
  6.5 118.0 %all-gather.7.cloned.1.call-start = ((), (), s32[]{:S(2)}) async-start(), calls=%async_computation | async-start | bytes 2433024 | tf_op jit(solution)/shard_map/all_gather | solution.py:183
  8.2 157.1 %all-gather.9.cloned.1.call-start = ((), (), s32[]{:S(2)}) async-start(), calls=%async_computation.1 | async-start | bytes 1310720 | tf_op jit(solution)/shard_map/all_gather | solution.py:222
  9.1 6.0 %collective-permute-start = (bf16[1,2,1,4,3072]{4,3,2,1,0:T(4,128)(2,1)S(1)}, bf16[1,2,1,4,3072]{4,3,2,1,0:T(4,128)(2,1)S(1)}, u32[]{:S(2)}, u32[]{:S(2)}) collective-permute-start(bf16[1,2,1,4,3072]{4,3,2,1,0:T(4,128)(2,1)S(1)} %get-tuple-element.32), channel_id=1, source_target_pairs={{0,16},{16,32},{32,48},{48,64},{64,80},{80,96},{96,112},{112,128},... | collective-permute-start | bytes 147464 | tf_op jit(solution)/shard_map/ppermute | solution.py:32
  13.4 6.0 %collective-permute-start.1 = (bf16[1,2,1,4,3072]{4,3,2,1,0:T(4,128)(2,1)S(1)}, bf16[1,2,1,4,3072]{4,3,2,1,0:T(4,128)(2,1)S(1)}, u32[]{:S(2)}, u32[]{:S(2)}) collective-permute-start(bf16[1,2,1,4,3072]{4,3,2,1,0:T(4,128)(2,1)S(1)} %get-tuple-element.31), channel_id=1, source_target_pairs={{16,0},{32,16},{48,32},{64,48},{80,64},{96,80},{112,96},{128,112},... | collective-permute-start | bytes 147464 | tf_op jit(solution)/shard_map/ppermute | solution.py:35
  19.7 54.5 %copy-start.7 = (bf16[512,384]{1,0:T(8,128)(2,1)S(1)}, bf16[512,384]{1,0:T(8,128)(2,1)}, u32[]{:S(2)}) copy-start(bf16[512,384]{1,0:T(8,128)(2,1)} %param.11) | copy-start | bytes 1179652
  19.7 12.2 %collective-permute-start.3 = (bf16[1,2,6,1,3072]{4,3,2,1,0:T(2,128)(2,1)S(1)}, bf16[1,2,6,1,3072]{4,3,2,1,0:T(2,128)(2,1)S(1)}, u32[]{:S(2)}, u32[]{:S(2)}) collective-permute-start(bf16[1,2,6,1,3072]{4,3,2,1,0:T(2,128)(2,1)S(1)} %get-tuple-element.30), channel_id=1, source_target_pairs={{1,0},{2,1},{3,2},{4,3},{5,4},{6,5},{7,6},{8,7},{9,8},{10,9},{11,1... | collective-permute-start | bytes 221192 | tf_op jit(solution)/shard_map/ppermute | solution.py:35
  22.6 9.3 %collective-permute-start.2 = (bf16[1,2,6,1,3072]{4,3,2,1,0:T(2,128)(2,1)S(1)}, bf16[1,2,6,1,3072]{4,3,2,1,0:T(2,128)(2,1)S(1)}, u32[]{:S(2)}, u32[]{:S(2)}) collective-permute-start(bf16[1,2,6,1,3072]{4,3,2,1,0:T(2,128)(2,1)S(1)} %get-tuple-element.29), channel_id=1, source_target_pairs={{0,1},{1,2},{2,3},{3,4},{4,5},{5,6},{6,7},{7,8},{8,9},{9,10},{10,1... | collective-permute-start | bytes 221192 | tf_op jit(solution)/shard_map/ppermute | solution.py:32
  62.2 65.1 %collective-permute-start.4 = (bf16[128,3072]{1,0:T(8,128)(2,1)S(1)}, bf16[128,3072]{1,0:T(8,128)(2,1)}, u32[]{:S(2)}, u32[]{:S(2)}) collective-permute-start(bf16[128,3072]{1,0:T(8,128)(2,1)S(1)} %all_gather.15.x_ref), channel_id=1, source_target_pairs={{0,1},{1,2},{2,3},{3,0},{4,5},{5,6},{6,7},{7,4},{8,9},{9,10},{10,1... | collective-permute-start | bytes 2359304 | tf_op jit(solution)/shard_map/ppermute | solution.py:199
  68.1 62.0 %collective-permute-start.5 = (bf16[128,3072]{1,0:T(8,128)(2,1)S(1)}, bf16[128,3072]{1,0:T(8,128)(2,1)}, u32[]{:S(2)}, u32[]{:S(2)}) collective-permute-start(bf16[128,3072]{1,0:T(8,128)(2,1)S(1)} %all_gather.15.x_ref), channel_id=1, source_target_pairs={{0,3},{1,0},{2,1},{3,2},{4,7},{5,4},{6,5},{7,6},{8,11},{9,8},{10,9... | collective-permute-start | bytes 2359304 | tf_op jit(solution)/shard_map/ppermute | solution.py:199
  70.0 62.2 %collective-permute-start.6 = (bf16[128,3072]{1,0:T(8,128)(2,1)S(1)}, bf16[128,3072]{1,0:T(8,128)(2,1)S(1)}, u32[]{:S(2)}, u32[]{:S(2)}) collective-permute-start(bf16[128,3072]{1,0:T(8,128)(2,1)S(1)} %all_gather.15.x_ref), channel_id=1, source_target_pairs={{0,2},{1,3},{2,0},{3,1},{4,6},{5,7},{6,4},{7,5},{8,10},{9,11},{10,... | collective-permute-start | bytes 2359304 | tf_op jit(solution)/shard_map/ppermute | solution.py:199
  124.6 1.7 copy-start.1
  126.2 1.7 copy-start.2
  134.1 12.7 %collective-permute-start.7 = (bf16[512,128]{1,0:T(8,128)(2,1)S(1)}, bf16[512,128]{1,0:T(8,128)(2,1)S(1)}, u32[]{:S(2)}, u32[]{:S(2)}) collective-permute-start(bf16[512,128]{1,0:T(8,128)(2,1)S(1)} %constant_dynamic-update-slice_fusion.3.q0), channel_id=1, source_target_pairs={{0,16},{16,0},{1,17},{17,1},{2,18},{18,2},{3,19},{19,3},{4,20},{20... | collective-permute-start | bytes 393224 | tf_op jit(solution)/shard_map/ppermute | solution.py:221
  136.0 10.8 %collective-permute-start.8 = (bf16[512,128]{1,0:T(8,128)(2,1)S(1)}, bf16[512,128]{1,0:T(8,128)(2,1)S(1)}, u32[]{:S(2)}, u32[]{:S(2)}) collective-permute-start(bf16[512,128]{1,0:T(8,128)(2,1)S(1)} %constant_dynamic-update-slice_fusion.3.q0), channel_id=1, source_target_pairs={{0,32},{32,0},{1,33},{33,1},{2,34},{34,2},{3,35},{35,3},{4,36},{36... | collective-permute-start | bytes 393224 | tf_op jit(solution)/shard_map/ppermute | solution.py:221
  137.9 12.3 %collective-permute-start.9 = (bf16[512,128]{1,0:T(8,128)(2,1)S(1)}, bf16[512,128]{1,0:T(8,128)(2,1)S(1)}, u32[]{:S(2)}, u32[]{:S(2)}) collective-permute-start(bf16[512,128]{1,0:T(8,128)(2,1)S(1)} %constant_dynamic-update-slice_fusion.3.q0), channel_id=1, source_target_pairs={{0,48},{48,0},{16,32},{32,16},{1,49},{49,1},{17,33},{33,17},{2,50}... | collective-permute-start | bytes 393224 | tf_op jit(solution)/shard_map/ppermute | solution.py:221
  144.4 1.7 copy-start.3
  146.0 51.4 %copy-start.5 = (s32[4]{0:T(128)S(1)}, s32[4]{0:T(128)}, u32[]{:S(2)}) copy-start(s32[4]{0:T(128)} %constant.51.clone) | copy-start | bytes 52
  165.4 1.2 copy-start.4
  188.1 10.0 %collective-permute-start.10 = (bf16[512,256]{1,0:T(8,128)(2,1)S(1)}, bf16[512,256]{1,0:T(8,128)(2,1)S(1)}, u32[]{:S(2)}, u32[]{:S(2)}) collective-permute-start(bf16[512,256]{1,0:T(8,128)(2,1)S(1)} %get-tuple-element.26), channel_id=1, source_target_pairs={{0,16},{16,0},{1,17},{17,1},{2,18},{18,2},{3,19},{19,3},{4,20},{20... | collective-permute-start | bytes 786440 | tf_op jit(solution)/shard_map/ppermute | solution.py:226
  191.8 11.1 %collective-permute-start.11 = (bf16[512,256]{1,0:T(8,128)(2,1)S(1)}, bf16[512,256]{1,0:T(8,128)(2,1)S(1)}, u32[]{:S(2)}, u32[]{:S(2)}) collective-permute-start(bf16[512,256]{1,0:T(8,128)(2,1)S(1)} %get-tuple-element.27), channel_id=1, source_target_pairs={{0,32},{32,0},{1,33},{33,1},{2,34},{34,2},{3,35},{35,3},{4,36},{36... | collective-permute-start | bytes 786440 | tf_op jit(solution)/shard_map/ppermute | solution.py:226
  194.0 12.8 %collective-permute-start.12 = (bf16[512,256]{1,0:T(8,128)(2,1)S(1)}, bf16[512,256]{1,0:T(8,128)(2,1)S(1)}, u32[]{:S(2)}, u32[]{:S(2)}) collective-permute-start(bf16[512,256]{1,0:T(8,128)(2,1)S(1)} %get-tuple-element.28), channel_id=1, source_target_pairs={{0,48},{48,0},{16,32},{32,16},{1,49},{49,1},{17,33},{33,17},{2,50}... | collective-permute-start | bytes 786440 | tf_op jit(solution)/shard_map/ppermute | solution.py:226
Sparse Core Ops, SparseCore 0:
  9.5 74.3 all-gather.6
  134.1 31.1 all-gather.8

commit v2 on v1

v2 whole, which is shorter than its diff:
```python
import functools
import math

import jax
import jax.numpy as jnp
from jax import lax
from jax.experimental import pallas as pl
from jax.experimental.pallas import tpu as pltpu
from jax.sharding import Mesh, PartitionSpec as P

HD = 64
LOG2E = 1.4426950408889634
SCALE2 = 0.125 * LOG2E
BF = jnp.bfloat16
F32 = jnp.float32
TEXT_PART = 64
STAT_ROWS = 16


def vmem(*shape):
    return pl.BlockSpec(memory_space=pltpu.VMEM)


def params(mib):
    return pltpu.CompilerParams(vmem_limit_bytes=mib << 20)


def with_halo(block, sides, width):
    for axis, dim in sides:
        count = lax.axis_size(axis)
        forward = [(i, i + 1) for i in range(count - 1)]
        backward = [(target, source) for source, target in forward]
        low = lax.ppermute(
            lax.slice_in_dim(block, block.shape[dim] - width, None, axis=dim), axis, forward
        )
        high = lax.ppermute(lax.slice_in_dim(block, 0, width, axis=dim), axis, backward)
        block = jnp.concatenate([low, block, high], axis=dim)
    return block


def time_angles(step, count):
    half = count // 2
    freqs = jnp.exp(-math.log(10000.0) * jnp.arange(half, dtype=F32) / half)
    angle = step.astype(F32) * freqs
    return jnp.concatenate([jnp.cos(angle), jnp.sin(angle)])


def project_kernel(x_ref, mod_ref, w_ref, *outs):
    values = x_ref[...].astype(F32)
    width = values.shape[1]
    center = jnp.sum(values, axis=1, keepdims=True) * (1.0 / width)
    centered = values - center
    spread = jnp.sum(centered * centered, axis=1, keepdims=True) * (1.0 / width)
    normed = centered * lax.rsqrt(spread + 1e-06) * (1.0 + mod_ref[1:2, :]) + mod_ref[0:1, :]
    rows = jnp.dot(normed.astype(BF), w_ref[...], preferred_element_type=F32).astype(BF)
    at = 0
    for out in outs:
        size = out.shape[1]
        first = rows.shape[1] - sum(o.shape[1] for o in outs) + at
        out[...] = rows[:, first : first + size]
        at += size


def project(x, mod, weight, sizes):
    rows = x.shape[0]
    return pl.pallas_call(
        project_kernel,
        out_shape=[jax.ShapeDtypeStruct((rows, size), BF) for size in sizes],
        in_specs=[vmem()] * 3,
        out_specs=[vmem()] * len(sizes),
        compiler_params=params(16),
        cost_estimate=pl.CostEstimate(
            flops=2 * rows * x.shape[1] * weight.shape[1],
            bytes_accessed=2 * (x.size + weight.size),
            transcendentals=rows,
        ),
        name="project",
    )(x, mod, weight)


def softmax_tile(q, keys, values, text, valid):
    contract = (((1,), (1,)), ((), ()))
    lane = lax.broadcasted_iota(jnp.int32, (q.shape[0], 128), 1)
    outs, sums = [], []
    for head in range(2):
        own = jnp.where(lane // HD == head, q, 0.0).astype(BF)
        s = lax.dot_general(own, keys, contract, preferred_element_type=F32)
        top = jnp.max(s, axis=1, keepdims=True)
        if text is not None:
            t = lax.dot_general(own, text[0], contract, preferred_element_type=F32)
            t = jnp.where(valid, t, -1e30)
            top = jnp.maximum(top, jnp.max(t, axis=1, keepdims=True))
        top = top * SCALE2
        p = jnp.exp2(s * SCALE2 - top).astype(BF)
        acc = jnp.dot(p, values, preferred_element_type=F32)
        if text is not None:
            pt = jnp.where(valid, jnp.exp2(t * SCALE2 - top), 0.0).astype(BF)
            acc = acc + jnp.dot(pt, text[1], preferred_element_type=F32)
        total = acc[:, 128:]
        outs.append(acc[:, :128] / total)
        sums.append(top + jnp.log(total) * LOG2E)
    return jnp.where(lane < HD, outs[0], outs[1]), jnp.where(lane < HD, sums[0], sums[1])


def first_kernel(info, q0, q1, q2, q3, kv, text_kv, o_ref, l_ref, values, text_values, *, tile):
    count = q0.shape[0]
    values[:, :128] = kv[:, 128:]
    values[:, 128:] = jnp.ones((kv.shape[0], 128), BF)
    text_values[:, :128] = text_kv[:, 128:]
    text_values[:, 128:] = jnp.ones((TEXT_PART, 128), BF)
    position = info[0] + lax.broadcasted_iota(jnp.int32, (tile, TEXT_PART), 1)
    valid = (position >= info[1]) & (position < info[2])
    for member, q_ref in enumerate((q0, q1, q2, q3)):

        @pl.loop(0, count // tile)
        def _(step):
            rows = pl.ds(pl.multiple_of(step * tile, tile), tile)
            out, lse = softmax_tile(
                q_ref[rows, :].astype(F32),
                kv[:, :128],
                values[...],
                (text_kv[:, :128], text_values[...]),
                valid,
            )
            o_ref[member, rows, :] = out
            l_ref[member, rows, :] = lse


def attend_first(info, qs, kv, text_kv):
    count = qs[0].shape[0]
    keys = kv.shape[0]
    return pl.pallas_call(
        functools.partial(first_kernel, tile=128),
        out_shape=[jax.ShapeDtypeStruct((4, count, 128), F32)] * 2,
        in_specs=[pl.BlockSpec(memory_space=pltpu.SMEM)] + [vmem()] * 6,
        out_specs=[vmem()] * 2,
        scratch_shapes=[pltpu.VMEM((keys, 256), BF), pltpu.VMEM((TEXT_PART, 256), BF)],
        compiler_params=params(16),
        cost_estimate=pl.CostEstimate(
            flops=4 * 4 * count * (keys + TEXT_PART) * 256,
            bytes_accessed=2 * 256 * (6 * count + keys),
            transcendentals=8 * count * (keys + TEXT_PART),
        ),
        name="attend_first",
    )(info, *qs, kv, text_kv)


def rest_kernel(info, q0, q1, q2, q3, kv, o_first, l_first, o_ref, keys, values, *, tile):
    count = q0.shape[0]
    blocks, size = kv.shape[:2]
    for step in range(blocks - 1):
        block = lax.rem(info[3] + step + 1, blocks)
        rows = pl.ds(step * size, size)
        keys[rows, :] = kv[block, :, :128]
        values[rows, :128] = kv[block, :, 128:]
    values[:, 128:] = jnp.ones((values.shape[0], 128), BF)
    lane = lax.broadcasted_iota(jnp.int32, (tile, 128), 1)
    for member, q_ref in enumerate((q0, q1, q2, q3)):
        target = info[4 + member]

        @pl.loop(0, count // tile)
        def _(step):
            rows = pl.ds(pl.multiple_of(step * tile, tile), tile)
            out, lse = softmax_tile(
                q_ref[rows, :].astype(F32), keys[...], values[...], None, None
            )
            before = l_first[member, rows, :]
            top = jnp.maximum(lse, before)
            new = jnp.exp2(lse - top)
            old = jnp.exp2(before - top)
            total = new + old
            o_ref[target, rows, :] = ((new * out + old * o_first[member, rows, :]) / total).astype(BF)
            rest = top + jnp.log(total) * LOG2E
            stats = jnp.zeros((tile, 128), F32)
            for part in range(3):
                piece = rest.astype(BF).astype(F32)
                stats = jnp.where(lane % HD == part, piece, stats)
                rest = rest - piece
            across = jnp.transpose(stats)
            across = jnp.concatenate([across[:8], across[HD : HD + 8]], axis=0)
            at = pl.multiple_of(count + step * STAT_ROWS, STAT_ROWS)
            o_ref[target, pl.ds(at, STAT_ROWS), :] = across.astype(BF)


def attend_rest(info, qs, kv, first):
    count = qs[0].shape[0]
    keys = (kv.shape[0] - 1) * kv.shape[1]
    tile = 128
    rows = count + count // tile * STAT_ROWS
    return pl.pallas_call(
        functools.partial(rest_kernel, tile=tile),
        out_shape=jax.ShapeDtypeStruct((4, rows, 128), BF),
        in_specs=[pl.BlockSpec(memory_space=pltpu.SMEM)] + [vmem()] * 7,
        out_specs=vmem(),
        scratch_shapes=[pltpu.VMEM((keys, 128), BF), pltpu.VMEM((keys, 256), BF)],
        compiler_params=params(20),
        cost_estimate=pl.CostEstimate(
            flops=4 * 4 * count * keys * 256,
            bytes_accessed=2 * 256 * (6 * count + keys),
            transcendentals=8 * count * keys,
        ),
        name="attend_rest",
    )(info, *qs, kv, *first)


def combine_kernel(slots, parts_ref, out):
    members = parts_ref.shape[0]
    block = 128
    count = out.shape[0] * block
    lane = lax.broadcasted_iota(jnp.int32, (block, 128), 1)
    for place in range(out.shape[0]):
        slot = slots[place]
        rows = pl.ds(pl.multiple_of(slot * block, block), block)
        at = pl.ds(pl.multiple_of(count + slot * STAT_ROWS, STAT_ROWS), STAT_ROWS)
        lses = []
        for member in range(members):
            across = parts_ref[member, at, :].astype(F32)
            across = jnp.concatenate([across, jnp.zeros((128 - STAT_ROWS, 128), F32)], axis=0)
            stats = jnp.transpose(across)
            heads = [
                stats[:, 8 * h : 8 * h + 1]
                + stats[:, 8 * h + 1 : 8 * h + 2]
                + stats[:, 8 * h + 2 : 8 * h + 3]
                for h in range(2)
            ]
            lses.append(jnp.where(lane < HD, heads[0], heads[1]))
        top = functools.reduce(jnp.maximum, lses)
        shares = [jnp.exp2(lse - top) for lse in lses]
        weighted = sum(
            share * parts_ref[member, rows, :].astype(F32) for member, share in enumerate(shares)
        )
        out[place] = (weighted / sum(shares)).astype(BF)


def combine(slots, parts):
    return pl.pallas_call(
        combine_kernel,
        out_shape=jax.ShapeDtypeStruct((4, 128, 128), BF),
        in_specs=[pl.BlockSpec(memory_space=pltpu.SMEM), vmem()],
        out_specs=vmem(),
        compiler_params=params(8),
        name="combine",
    )(slots, parts)


def share(block, axis, count):
    copies = jnp.broadcast_to(block[None], (count,) + block.shape)
    return lax.all_to_all(copies, axis, split_axis=0, concat_axis=0, tiled=True)


def on_device(latents, prompt_rows, peg_weight, modulation_weight, qkv_weight, text_len, timestep):
    frames, tile_h, tile_w, width = latents.shape[1:]
    rows_axes = ("u", "v", "zl")
    head_width = qkv_weight.shape[2]
    zl_at = lax.axis_index("zl")
    shard = qkv_weight.reshape(qkv_weight.shape[0], 3 * head_width)
    other = lax.ppermute(shard, "zl", [(0, 1), (1, 0)])
    shards = jnp.where(
        zl_at == 0, jnp.stack([shard, other]), jnp.stack([other, shard])
    ).reshape(2 * shard.shape[0], shard.shape[1])
    weight = lax.all_gather(shards, ("item", "u", "v"), axis=0, tiled=True)
    activation = jax.nn.silu(time_angles(timestep[0], modulation_weight.shape[0])).astype(BF)
    own_columns = jnp.dot(activation[None, :], modulation_weight, preferred_element_type=F32)
    modulation = share(own_columns[0], ("zh", "x"), 16).reshape(2, width)
    padded = with_halo(latents, ((rows_axes, 2), (("zh", "x"), 3)), 1)
    summed = latents.astype(F32)
    for row_tap in range(3):
        for col_tap in range(3):
            summed = summed + padded[
                :, :, row_tap : row_tap + tile_h, col_tap : col_tap + tile_w, :
            ].astype(F32) * peg_weight[row_tap, col_tap].astype(F32)
    peg = summed.astype(BF).reshape(frames * tile_h * tile_w, width)
    peg, modulation = lax.optimization_barrier((peg, modulation))
    tokens = lax.all_gather(peg, "zh", axis=0, tiled=True)
    blocks = [tokens] + [
        lax.ppermute(tokens, "x", [(i, (i + k) % 4) for i in range(4)]) for k in (1, 3, 2)
    ]
    member = lax.axis_index("v") * 2 + zl_at
    lower = member * TEXT_PART
    start = jnp.minimum(lower, prompt_rows.shape[1] - TEXT_PART)
    text_rows = lax.dynamic_slice_in_dim(prompt_rows[0], start, TEXT_PART, axis=0)
    (text_kv,) = project(text_rows, modulation, weight, (2 * head_width,))
    projected = [project(block, modulation, weight, (head_width, 2 * head_width)) for block in blocks]
    queries = jnp.concatenate([q for q, _ in projected], axis=0)
    kv = jnp.concatenate([pair for _, pair in projected], axis=0)

    swaps = (
        ("zl", [(0, 1), (1, 0)]),
        ("v", [(0, 1), (1, 0)]),
        (("v", "zl"), [(0, 3), (3, 0), (1, 2), (2, 1)]),
    )
    qs = [queries] + [lax.ppermute(queries, axis, swap) for axis, swap in swaps]
    all_kv = share(kv, "u", 4)
    info = jnp.stack(
        [start, lower, text_len[0], lax.axis_index("u")] + [member ^ k for k in range(4)]
    )
    first = attend_first(info, qs, kv, text_kv)
    parts = attend_rest(info, qs, all_kv, first)
    parts = lax.all_to_all(parts, ("v", "zl"), split_axis=0, concat_axis=0, tiled=True)
    x_at = lax.axis_index("x")
    slots = jnp.array([0, 2, 3, 1], jnp.int32)[(jnp.arange(4, dtype=jnp.int32) - x_at) % 4]
    attended = combine(slots, parts)
    attended = attended.reshape(4, 4, frames, tile_h, tile_w, head_width)
    attended = attended.transpose(2, 3, 1, 0, 4, 5)
    return attended.reshape(1, frames, tile_h, 16 * tile_w, head_width)


def solution(mesh):
    fine = Mesh(mesh.devices.reshape(2, 4, 2, 2, 4, 4), ("item", "u", "v", "zl", "zh", "x"))
    row = ("u", "v", "zl")
    col = ("zh", "x")
    in_specs = (
        P("item", None, row, col, None),
        P("item", None, None),
        P(),
        P(None, col),
        P(("item",) + row, None, col),
        P("item"),
        P("item"),
    )
    out_specs = P("item", None, row, None, col)
    return jax.shard_map(
        on_device, mesh=fine, in_specs=in_specs, out_specs=out_specs, check_vma=False
    )
```

time: 218 us -> 212 us (0.972)
  blocking collectives: 78.9 us -> 21.6 us
  waiting for transfers between devices: 34.2 us -> 54.7 us
  starting transfers between devices: 44.4 us -> 60 us
  Pallas kernels: 31.2 us -> 41.7 us
  local copies, waits for them, and re-layouts: 10.6 us -> 14.3 us
    all_gather x2 -> x0, blocking collectives: 50.1 us -> none  [the longest x1 36.3 us: on_device(): modulation = lax.all_gather(own_columns, 'x', axis=1, tiled=True)]
    all_to_all x0 -> x3, starting transfers between devices: none -> 27.9 us  [the longest x2 24.3 us: share(): return lax.all_to_all(copies, axis, split_axis=0, concat_axis=0, tiled=True)]
    ppermute x3, waiting for transfers between devices: 0.01 us -> 18.7 us  [on_device(): lax.ppermute(tokens, 'x', [(i, (i + k) % 4) for i in range(4)])]
    all_gather x2 -> x1, waiting for transfers between devices: 15.2 us -> 0.02 us  [on_device(): weight = lax.all_gather(shards, ('item', 'u', 'v'), axis=0, tiled=True)]
    ppermute x3, waiting for transfers between devices: 3.42 us -> 15.2 us  [on_device(): qs = [queries] + [lax.ppermute(queries, axis, swap) for axis, swap in swaps]]
    pallas_call x2 -> x3, Pallas kernels: 24.1 us -> 33.6 us  [the longest x1 19.5 us: attend_rest(): pl.pallas_call(functools.partial(rest_kernel, tile=tile), out_shape=jax.S...]
    ppermute x3 -> x1, waiting for transfers between devices: 8.79 us -> 0.01 us  [on_device(): other = lax.ppermute(shard, 'zl', [(0, 1), (1, 0)])]
    all_to_all x0 -> x3, waiting for transfers between devices: none -> 7.23 us  [the longest x1 7.22 us: on_device(): lax.all_to_all(parts, ('v', 'zl'), split_axis=0, concat_axis=0, tiled=True)]
  transfers between devices with their start and end apart: 15 -> 15, of which waited for: 8 -> 7; matrix products, arithmetic and copies ran while one was open for 2% -> 3% of each run, Pallas kernels for 3% -> 8%
where the time goes in v2:
time: 212 us; the launch traced here: 211 us
  starting transfers between devices  60 us (28%)
  waiting for transfers between devices  54.7 us (26%)
  Pallas kernels  41.7 us (20%)
  blocking collectives  21.6 us (10%)
  between operations  15.1 us (7%)
  local copies, waits for them, and re-layouts  14.3 us (7%)
  other arithmetic  2.35 us (1%)
    all_to_all x2, starting transfers between devices, share(): return lax.all_to_all(copies, axis, split_axis=0, concat_axis=0, tiled=True)  24.3 us
    all_gather x1, blocking collectives, on_device(): tokens = lax.all_gather(peg, 'zh', axis=0, tiled=True)  21.6 us
    pallas_call x1, Pallas kernels, attend_rest(): pl.pallas_call(functools.partial(rest_kernel, tile=tile), out_shape=jax.S...  19.5 us
    ppermute x3, waiting for transfers between devices, on_device(): lax.ppermute(tokens, 'x', [(i, (i + k) % 4) for i in range(4)])  18.7 us
    ppermute x3, waiting for transfers between devices, on_device(): qs = [queries] + [lax.ppermute(queries, axis, swap) for axis, swap in swaps]  15.2 us
    ppermute x2, waiting for transfers between devices, with_halo(): lax.ppermute(lax.slice_in_dim(block, 0, width, axis=dim), axis, backward)  12.8 us
    pallas_call x1, Pallas kernels, attend_first(): pl.pallas_call(functools.partial(first_kernel, tile=128), out_shape=[jax....  11.3 us
    ppermute x3, starting transfers between devices, on_device(): qs = [queries] + [lax.ppermute(queries, axis, swap) for axis, swap in swaps]  9.58 us
  transfers between devices with their start and end apart: 15, of which 7 were waited for; matrix products, arithmetic and copies ran while one was open for 3% of the time, Pallas kernels for 8%

profile of v2, /device:TPU:6, one launch (start us, length us, event | category | flops | bytes accessed | tf_op | source)
XLA Modules:
  0.0 211.0 jit_solution(1338475606990047254)
XLA Ops:
  7.6 4.3 %collective-permute-start.4 = (bf16[96,384]{1,0:T(8,128)(2,1)S(1)}, bf16[96,384]{1,0:T(8,128)(2,1)S(1)}, u32[]{:S(2)}, u32[]{:S(2)}) collective-permute-start(bf16[96,384]{1,0:T(8,128)(2,1)S(1)} %copy_bitcast_fusion), channel_id=1, source_target_pairs={{0,16},{16,0},{1,17},{17,1},{2,18},{18,2},{3,19},{19,3},{4,20},{20... | collective-permute-start | bytes 221192 | tf_op jit(solution)/shard_map/ppermute | solution.py:257
  18.9 12.9 %all-to-all-start = ((f32[16,1,384]{2,1,0:T(1,128)}), f32[16,1,384]{2,1,0:T(1,128)S(1)}, u32[]{:S(2)}, u32[]{:S(2)}) async-start(f32[16,1,384]{2,1,0:T(1,128)} %broadcast_in_dim.4), calls=%async_computation | async-start | bytes 49152 | tf_op jit(solution)/shard_map/all_to_all | solution.py:248
  33.3 5.1 %collective-permute-done.1 = bf16[1,2,1,4,3072]{4,3,2,1,0:T(4,128)(2,1)S(1)} collective-permute-done((bf16[1,2,1,4,3072]{4,3,2,1,0:T(4,128)(2,1)S(1)}, bf16[1,2,1,4,3072]{4,3,2,1,0:T(4,128)(2,1)S(1)}, u32[]{:S(2)}, u32[]{:S(2)}) %collective-permute-start.1) | collective-permute-done | bytes 49184 | tf_op jit(solution)/shard_map/ppermute | solution.py:36
  38.6 4.2 %collective-permute-start.2 = (bf16[1,2,6,1,3072]{4,3,2,1,0:T(2,128)(2,1)S(1)}, bf16[1,2,6,1,3072]{4,3,2,1,0:T(2,128)(2,1)S(1)}, u32[]{:S(2)}, u32[]{:S(2)}) collective-permute-start(bf16[1,2,6,1,3072]{4,3,2,1,0:T(2,128)(2,1)S(1)} %get-tuple-element.29), channel_id=1, source_target_pairs={{0,1},{1,2},{2,3},{3,4},{4,5},{5,6},{6,7},{7,8},{8,9},{9,10},{10,1... | collective-permute-start | bytes 221192 | tf_op jit(solution)/shard_map/ppermute | solution.py:33
  42.8 1.9 collective-permute-start.3
  45.6 7.8 %collective-permute-done.3 = bf16[1,2,6,1,3072]{4,3,2,1,0:T(2,128)(2,1)S(1)} collective-permute-done((bf16[1,2,6,1,3072]{4,3,2,1,0:T(2,128)(2,1)S(1)}, bf16[1,2,6,1,3072]{4,3,2,1,0:T(2,128)(2,1)S(1)}, u32[]{:S(2)}, u32[]{:S(2)}) %collective-permute-start.3) | collective-permute-done | bytes 73760 | tf_op jit(solution)/shard_map/ppermute | solution.py:36
  54.9 21.6 %all_gather.6.x_ref = bf16[128,3072]{1,0:T(8,128)(2,1)S(1)} all-gather(bf16[32,3072]{1,0:T(8,128)(2,1)S(1)} %reshape.168), channel_id=1, replica_groups=mesh['item'=2,'u'=4,'v'=2,'zl'=2,'zh'=4,'x'=4] {'zh'}, dimensions={0}, use_global_device_ids=true | all-gather | bytes 983040 | tf_op jit(solution)/shard_map/all_gather | solution.py:274
  78.4 5.1 %collective-permute-start.5 = (bf16[128,3072]{1,0:T(8,128)(2,1)S(1)}, bf16[128,3072]{1,0:T(8,128)(2,1)}, u32[]{:S(2)}, u32[]{:S(2)}) collective-permute-start(bf16[128,3072]{1,0:T(8,128)(2,1)S(1)} %all_gather.6.x_ref), channel_id=1, source_target_pairs={{0,1},{1,2},{2,3},{3,0},{4,5},{5,6},{6,7},{7,4},{8,9},{9,10},{10,1... | collective-permute-start | bytes 2359304 | tf_op jit(solution)/shard_map/ppermute | solution.py:276
  83.6 1.9 collective-permute-start.7
  88.2 7.8 %collective-permute-done.6.x_ref = bf16[128,3072]{1,0:T(8,128)(2,1)} collective-permute-done((bf16[128,3072]{1,0:T(8,128)(2,1)S(1)}, bf16[128,3072]{1,0:T(8,128)(2,1)}, u32[]{:S(2)}, u32[]{:S(2)}) %collective-permute-start.6) | collective-permute-done | bytes 786464 | tf_op jit(solution)/shard_map/ppermute | solution.py:276
  96.0 2.1 %project.7 = (bf16[128,128]{1,0:T(8,128)(2,1)S(1)}, bf16[128,256]{1,0:T(8,128)(2,1)S(1)}) custom-call(bf16[128,3072]{1,0:T(8,128)(2,1)} %collective-permute-done.6.x_ref, f32[2,3072]{1,0:T(2,128)S(1)} %reshape.169.mod_ref, bf16[3072,384]{1,0:T(8,128)(2,1)S(1)} %copy-done.2), custom_call_target="tpu_custom_call" | custom-call | flops 301989888 | bytes 3145728 | tf_op jit(solution)/shard_map/project/pallas_call | solution.py:66
  98.1 10.9 %collective-permute-done.5.x_ref = bf16[128,3072]{1,0:T(8,128)(2,1)} collective-permute-done((bf16[128,3072]{1,0:T(8,128)(2,1)S(1)}, bf16[128,3072]{1,0:T(8,128)(2,1)}, u32[]{:S(2)}, u32[]{:S(2)}) %collective-permute-start.5) | collective-permute-done | bytes 786464 | tf_op jit(solution)/shard_map/ppermute | solution.py:276
  109.0 2.1 %project.6 = (bf16[128,128]{1,0:T(8,128)(2,1)S(1)}, bf16[128,256]{1,0:T(8,128)(2,1)S(1)}) custom-call(bf16[128,3072]{1,0:T(8,128)(2,1)} %collective-permute-done.5.x_ref, f32[2,3072]{1,0:T(2,128)S(1)} %reshape.169.mod_ref, bf16[3072,384]{1,0:T(8,128)(2,1)S(1)} %copy-done.2), custom_call_target="tpu_custom_call" | custom-call | flops 301989888 | bytes 3145728 | tf_op jit(solution)/shard_map/project/pallas_call | solution.py:66
  111.2 2.1 %project.8 = (bf16[128,128]{1,0:T(8,128)(2,1)S(1)}, bf16[128,256]{1,0:T(8,128)(2,1)S(1)}) custom-call(bf16[128,3072]{1,0:T(8,128)(2,1)} %collective-permute-done.7.x_ref, f32[2,3072]{1,0:T(2,128)S(1)} %reshape.169.mod_ref, bf16[3072,384]{1,0:T(8,128)(2,1)S(1)} %copy-done.2), custom_call_target="tpu_custom_call" | custom-call | flops 301989888 | bytes 3145728 | tf_op jit(solution)/shard_map/project/pallas_call | solution.py:66
  114.4 11.4 %all-to-all-start.1 = ((bf16[4,512,256]{2,1,0:T(8,128)(2,1)}), bf16[4,512,256]{2,1,0:T(8,128)(2,1)S(1)}, u32[]{:S(2)}, u32[]{:S(2)}) async-start(bf16[4,512,256]{2,1,0:T(8,128)(2,1)} %broadcast_in_dim.5), calls=%async_computation.1 | async-start | bytes 2097152 | tf_op jit(solution)/shard_map/all_to_all | solution.py:248
  125.8 5.0 %collective-permute-start.10 = (bf16[512,128]{1,0:T(8,128)(2,1)S(1)}, bf16[512,128]{1,0:T(8,128)(2,1)S(1)}, u32[]{:S(2)}, u32[]{:S(2)}) collective-permute-start(bf16[512,128]{1,0:T(8,128)(2,1)S(1)} %constant_dynamic-update-slice_fusion.3.q0), channel_id=1, source_target_pairs={{0,48},{48,0},{16,32},{32,16},{1,49},{49,1},{17,33},{33,17},{2,50}... | collective-permute-start | bytes 393224 | tf_op jit(solution)/shard_map/ppermute | solution.py:292
  130.8 1.9 collective-permute-start.9
  132.7 2.7 %collective-permute-start.8 = (bf16[512,128]{1,0:T(8,128)(2,1)S(1)}, bf16[512,128]{1,0:T(8,128)(2,1)}, u32[]{:S(2)}, u32[]{:S(2)}) collective-permute-start(bf16[512,128]{1,0:T(8,128)(2,1)S(1)} %constant_dynamic-update-slice_fusion.3.q0), channel_id=1, source_target_pairs={{0,16},{16,0},{1,17},{17,1},{2,18},{18,2},{3,19},{19,3},{4,20},{20... | collective-permute-start | bytes 393224 | tf_op jit(solution)/shard_map/ppermute | solution.py:292
  138.7 15.2 %collective-permute-done.10.q3 = bf16[512,128]{1,0:T(8,128)(2,1)S(1)} collective-permute-done((bf16[512,128]{1,0:T(8,128)(2,1)S(1)}, bf16[512,128]{1,0:T(8,128)(2,1)S(1)}, u32[]{:S(2)}, u32[]{:S(2)}) %collective-permute-start.10) | collective-permute-done | bytes 131104 | tf_op jit(solution)/shard_map/ppermute | solution.py:292
  153.9 11.3 %attend_first.1 = (f32[4,512,128]{2,1,0:T(8,128)S(1)}, f32[4,512,128]{2,1,0:T(8,128)S(1)}) custom-call(s32[8]{0:T(128)S(1)} %stack.41.info, bf16[512,128]{1,0:T(8,128)(2,1)S(1)} %constant_dynamic-update-slice_fusion.3.q0, bf16[512,128]{1,0:T(8,128)(2,1)} %collective-permute-done.8.q1, bf16[512,128]{1,0:T(8,128)(2,1)} %collective-permute-done.9.q2, ...), custom_call_target="tpu_custom_call" | custom-call | flops 1207959552 | bytes 1835008 | tf_op jit(solution)/shard_map/attend_first/pallas_call | solution.py:132
  169.6 19.5 %attend_rest.1 = bf16[4,576,128]{2,1,0:T(8,128)(2,1)} custom-call(s32[8]{0:T(128)S(1)} %stack.41.info, bf16[512,128]{1,0:T(8,128)(2,1)S(1)} %constant_dynamic-update-slice_fusion.3.q0, bf16[512,128]{1,0:T(8,128)(2,1)} %collective-permute-done.8.q1, bf16[512,128]{1,0:T(8,128)(2,1)} %collective-permute-done.9.q2, ...), custom_call_target="tpu_custom_call" | custom-call | flops 3221225472 | bytes 2359296 | tf_op jit(solution)/shard_map/attend_rest/pallas_call | solution.py:190
  189.0 3.6 %all-to-all-start.2 = ((bf16[4,576,128]{2,1,0:T(8,128)(2,1)}), bf16[4,576,128]{2,1,0:T(8,128)(2,1)S(1)}, u32[]{:S(2)}, u32[]{:S(2)}) async-start(bf16[4,576,128]{2,1,0:T(8,128)(2,1)} %attend_rest.1), calls=%async_computation.2 | async-start | bytes 1179648 | tf_op jit(solution)/shard_map/all_to_all | solution.py:299
  193.3 7.2 %all-to-all-done.2.parts_ref = bf16[4,576,128]{2,1,0:T(8,128)(2,1)S(1)} async-done(((bf16[4,576,128]{2,1,0:T(8,128)(2,1)}), bf16[4,576,128]{2,1,0:T(8,128)(2,1)S(1)}, u32[]{:S(2)}, u32[]{:S(2)}) %all-to-all-start.2) | async-done | bytes 589856 | tf_op jit(solution)/shard_map/all_to_all | solution.py:299
  200.6 2.9 %combine.1 = bf16[4,128,128]{2,1,0:T(8,128)(2,1)S(1)} custom-call(s32[4]{0:T(128)S(1)} %gather_fusion, bf16[4,576,128]{2,1,0:T(8,128)(2,1)S(1)} %all-to-all-done.2.parts_ref), custom_call_target="tpu_custom_call" | custom-call | tf_op jit(solution)/shard_map/combine/pallas_call | solution.py:236
  (72 shorter events, 25.4 us)
Async XLA Ops:
  6.5 128.9 %copy-start = (bf16[1,226,3072]{2,1,0:T(8,128)(2,1)S(1)}, bf16[1,226,3072]{2,1,0:T(8,128)(2,1)}, u32[]{:S(2)}) copy-start(bf16[1,226,3072]{2,1,0:T(8,128)(2,1)} %param.9) | copy-start | bytes 4165636
  6.5 26.6 %copy-start.9 = (bf16[1,2,4,4,3072]{4,3,2,1,0:T(4,128)(2,1)S(1)}, bf16[1,2,4,4,3072]{4,3,2,1,0:T(4,128)(2,1)}, u32[]{:S(2)}) copy-start(bf16[1,2,4,4,3072]{4,3,2,1,0:T(4,128)(2,1)} %param.8) | copy-start | bytes 589828
  6.5 38.2 %copy-start.10 = (bf16[3,3,3072]{2,1,0:T(4,128)(2,1)S(1)}, bf16[3,3,3072]{2,1,0:T(4,128)(2,1)}, u32[]{:S(2)}) copy-start(bf16[3,3,3072]{2,1,0:T(4,128)(2,1)} %param.10) | copy-start | bytes 165892
  6.5 79.0 %all-gather.2.cloned.1.call-start = ((), (), s32[]{:S(2)}) async-start(), calls=%async_computation.3 | async-start | bytes 2506752 | tf_op jit(solution)/shard_map/all_gather | solution.py:261
  7.6 8.7 %collective-permute-start.4 = (bf16[96,384]{1,0:T(8,128)(2,1)S(1)}, bf16[96,384]{1,0:T(8,128)(2,1)S(1)}, u32[]{:S(2)}, u32[]{:S(2)}) collective-permute-start(bf16[96,384]{1,0:T(8,128)(2,1)S(1)} %copy_bitcast_fusion), channel_id=1, source_target_pairs={{0,16},{16,0},{1,17},{17,1},{2,18},{18,2},{3,19},{19,3},{4,20},{20... | collective-permute-start | bytes 221192 | tf_op jit(solution)/shard_map/ppermute | solution.py:257
  12.7 20.4 %collective-permute-start = (bf16[1,2,1,4,3072]{4,3,2,1,0:T(4,128)(2,1)S(1)}, bf16[1,2,1,4,3072]{4,3,2,1,0:T(4,128)(2,1)S(1)}, u32[]{:S(2)}, u32[]{:S(2)}) collective-permute-start(bf16[1,2,1,4,3072]{4,3,2,1,0:T(4,128)(2,1)S(1)} %get-tuple-element.32), channel_id=1, source_target_pairs={{0,16},{16,32},{32,48},{48,64},{64,80},{80,96},{96,112},{112,128},... | collective-permute-start | bytes 147464 | tf_op jit(solution)/shard_map/ppermute | solution.py:33
  18.9 25.9 %all-to-all-start = ((f32[16,1,384]{2,1,0:T(1,128)}), f32[16,1,384]{2,1,0:T(1,128)S(1)}, u32[]{:S(2)}, u32[]{:S(2)}) async-start(f32[16,1,384]{2,1,0:T(1,128)} %broadcast_in_dim.4), calls=%async_computation | async-start | bytes 49152 | tf_op jit(solution)/shard_map/all_to_all | solution.py:248
  31.8 6.5 %collective-permute-start.1 = (bf16[1,2,1,4,3072]{4,3,2,1,0:T(4,128)(2,1)S(1)}, bf16[1,2,1,4,3072]{4,3,2,1,0:T(4,128)(2,1)S(1)}, u32[]{:S(2)}, u32[]{:S(2)}) collective-permute-start(bf16[1,2,1,4,3072]{4,3,2,1,0:T(4,128)(2,1)S(1)} %get-tuple-element.31), channel_id=1, source_target_pairs={{16,0},{32,16},{48,32},{64,48},{80,64},{96,80},{112,96},{128,112},... | collective-permute-start | bytes 147464 | tf_op jit(solution)/shard_map/ppermute | solution.py:36
  38.6 7.0 %collective-permute-start.2 = (bf16[1,2,6,1,3072]{4,3,2,1,0:T(2,128)(2,1)S(1)}, bf16[1,2,6,1,3072]{4,3,2,1,0:T(2,128)(2,1)S(1)}, u32[]{:S(2)}, u32[]{:S(2)}) collective-permute-start(bf16[1,2,6,1,3072]{4,3,2,1,0:T(2,128)(2,1)S(1)} %get-tuple-element.29), channel_id=1, source_target_pairs={{0,1},{1,2},{2,3},{3,4},{4,5},{5,6},{6,7},{7,8},{8,9},{9,10},{10,1... | collective-permute-start | bytes 221192 | tf_op jit(solution)/shard_map/ppermute | solution.py:33
  42.8 10.6 %collective-permute-start.3 = (bf16[1,2,6,1,3072]{4,3,2,1,0:T(2,128)(2,1)S(1)}, bf16[1,2,6,1,3072]{4,3,2,1,0:T(2,128)(2,1)S(1)}, u32[]{:S(2)}, u32[]{:S(2)}) collective-permute-start(bf16[1,2,6,1,3072]{4,3,2,1,0:T(2,128)(2,1)S(1)} %get-tuple-element.30), channel_id=1, source_target_pairs={{1,0},{2,1},{3,2},{4,3},{5,4},{6,5},{7,6},{8,7},{9,8},{10,9},{11,1... | collective-permute-start | bytes 221192 | tf_op jit(solution)/shard_map/ppermute | solution.py:36
  76.5 19.5 %collective-permute-start.6 = (bf16[128,3072]{1,0:T(8,128)(2,1)S(1)}, bf16[128,3072]{1,0:T(8,128)(2,1)}, u32[]{:S(2)}, u32[]{:S(2)}) collective-permute-start(bf16[128,3072]{1,0:T(8,128)(2,1)S(1)} %all_gather.6.x_ref), channel_id=1, source_target_pairs={{0,3},{1,0},{2,1},{3,2},{4,7},{5,4},{6,5},{7,6},{8,11},{9,8},{10,9... | collective-permute-start | bytes 2359304 | tf_op jit(solution)/shard_map/ppermute | solution.py:276
  78.4 30.6 %collective-permute-start.5 = (bf16[128,3072]{1,0:T(8,128)(2,1)S(1)}, bf16[128,3072]{1,0:T(8,128)(2,1)}, u32[]{:S(2)}, u32[]{:S(2)}) collective-permute-start(bf16[128,3072]{1,0:T(8,128)(2,1)S(1)} %all_gather.6.x_ref), channel_id=1, source_target_pairs={{0,1},{1,2},{2,3},{3,0},{4,5},{5,6},{6,7},{7,4},{8,9},{9,10},{10,1... | collective-permute-start | bytes 2359304 | tf_op jit(solution)/shard_map/ppermute | solution.py:276
  83.6 27.6 %collective-permute-start.7 = (bf16[128,3072]{1,0:T(8,128)(2,1)S(1)}, bf16[128,3072]{1,0:T(8,128)(2,1)}, u32[]{:S(2)}, u32[]{:S(2)}) collective-permute-start(bf16[128,3072]{1,0:T(8,128)(2,1)S(1)} %all_gather.6.x_ref), channel_id=1, source_target_pairs={{0,2},{1,3},{2,0},{3,1},{4,6},{5,7},{6,4},{7,5},{8,10},{9,11},{10,... | collective-permute-start | bytes 2359304 | tf_op jit(solution)/shard_map/ppermute | solution.py:276
  85.5 1.7 copy-start.1
  87.2 8.8 %copy-start.2 = (bf16[3072,384]{1,0:T(8,128)(2,1)S(1)}, bf16[3072,384]{1,0:T(8,128)(2,1)}, u32[]{:S(2)}) copy-start(bf16[3072,384]{1,0:T(8,128)(2,1)} %all-gather.2.cloned.1.call-done.w_ref) | copy-start | bytes 7077892
  114.4 52.8 %all-to-all-start.1 = ((bf16[4,512,256]{2,1,0:T(8,128)(2,1)}), bf16[4,512,256]{2,1,0:T(8,128)(2,1)S(1)}, u32[]{:S(2)}, u32[]{:S(2)}) async-start(bf16[4,512,256]{2,1,0:T(8,128)(2,1)} %broadcast_in_dim.5), calls=%async_computation.1 | async-start | bytes 2097152 | tf_op jit(solution)/shard_map/all_to_all | solution.py:248
  125.8 28.1 %collective-permute-start.10 = (bf16[512,128]{1,0:T(8,128)(2,1)S(1)}, bf16[512,128]{1,0:T(8,128)(2,1)S(1)}, u32[]{:S(2)}, u32[]{:S(2)}) collective-permute-start(bf16[512,128]{1,0:T(8,128)(2,1)S(1)} %constant_dynamic-update-slice_fusion.3.q0), channel_id=1, source_target_pairs={{0,48},{48,0},{16,32},{32,16},{1,49},{49,1},{17,33},{33,17},{2,50}... | collective-permute-start | bytes 393224 | tf_op jit(solution)/shard_map/ppermute | solution.py:292
  130.8 23.1 %collective-permute-start.9 = (bf16[512,128]{1,0:T(8,128)(2,1)S(1)}, bf16[512,128]{1,0:T(8,128)(2,1)}, u32[]{:S(2)}, u32[]{:S(2)}) collective-permute-start(bf16[512,128]{1,0:T(8,128)(2,1)S(1)} %constant_dynamic-update-slice_fusion.3.q0), channel_id=1, source_target_pairs={{0,32},{32,0},{1,33},{33,1},{2,34},{34,2},{3,35},{35,3},{4,36},{36... | collective-permute-start | bytes 393224 | tf_op jit(solution)/shard_map/ppermute | solution.py:292
  132.7 21.2 %collective-permute-start.8 = (bf16[512,128]{1,0:T(8,128)(2,1)S(1)}, bf16[512,128]{1,0:T(8,128)(2,1)}, u32[]{:S(2)}, u32[]{:S(2)}) collective-permute-start(bf16[512,128]{1,0:T(8,128)(2,1)S(1)} %constant_dynamic-update-slice_fusion.3.q0), channel_id=1, source_target_pairs={{0,16},{16,0},{1,17},{17,1},{2,18},{18,2},{3,19},{19,3},{4,20},{20... | collective-permute-start | bytes 393224 | tf_op jit(solution)/shard_map/ppermute | solution.py:292
  136.3 1.7 copy-start.3
  167.1 1.2 copy-start.5
  168.4 1.2 copy-start.7
  189.0 3.7 %copy-start.8 = (s32[4]{0:T(128)S(1)}, s32[4]{0:T(128)}, u32[]{:S(2)}) copy-start(s32[4]{0:T(128)} %constant.58.clone) | copy-start | bytes 52
  189.0 11.5 %all-to-all-start.2 = ((bf16[4,576,128]{2,1,0:T(8,128)(2,1)}), bf16[4,576,128]{2,1,0:T(8,128)(2,1)S(1)}, u32[]{:S(2)}, u32[]{:S(2)}) async-start(bf16[4,576,128]{2,1,0:T(8,128)(2,1)} %attend_rest.1), calls=%async_computation.2 | async-start | bytes 1179648 | tf_op jit(solution)/shard_map/all_to_all | solution.py:299
  (2 other events, 2.0 us)
Sparse Core Ops, SparseCore 0:
  17.1 46.6 all-gather.1

commit v3 on v2

v3 whole, which is shorter than its diff:
```python
import functools
import math

import jax
import jax.numpy as jnp
from jax import lax
from jax.experimental import pallas as pl
from jax.experimental.pallas import tpu as pltpu
from jax.sharding import Mesh, PartitionSpec as P

HD = 64
LOG2E = 1.4426950408889634
SCALE2 = 0.125 * LOG2E
BF = jnp.bfloat16
F32 = jnp.float32
TEXT_PART = 64
STAT_ROWS = 16


def vmem(*shape):
    return pl.BlockSpec(memory_space=pltpu.VMEM)


def params(mib):
    return pltpu.CompilerParams(vmem_limit_bytes=mib << 20)


def with_halo(block, sides, width):
    for axis, dim in sides:
        count = lax.axis_size(axis)
        forward = [(i, i + 1) for i in range(count - 1)]
        backward = [(target, source) for source, target in forward]
        low = lax.ppermute(
            lax.slice_in_dim(block, block.shape[dim] - width, None, axis=dim), axis, forward
        )
        high = lax.ppermute(lax.slice_in_dim(block, 0, width, axis=dim), axis, backward)
        block = jnp.concatenate([low, block, high], axis=dim)
    return block


def time_angles(step, count):
    half = count // 2
    freqs = jnp.exp(-math.log(10000.0) * jnp.arange(half, dtype=F32) / half)
    angle = step.astype(F32) * freqs
    return jnp.concatenate([jnp.cos(angle), jnp.sin(angle)])


def project_kernel(slots, x0, x1, x2, x3, text, w_ref, q_out, kv_out, text_out, mod, extra):
    blocks = (x0, x1, x2, x3)
    rows = x0.shape[0]
    width = text.shape[1]
    tile = rows // 4
    for slot, block in enumerate(blocks):
        extra[slot] = block[:, width:].astype(F32)
    for place in range(4):
        for far in range(4):
            for chunk in range(3):
                at = (far * 4 + place) * 3 + chunk
                kind, first = divmod(at * 128, width)
                row = far * tile + chunk
                mod[kind : kind + 1, first : first + 128] = (
                    extra[slots[place], row : row + 1, :]
                    + extra[slots[place], row + 3 : row + 4, :]
                    + extra[slots[place], row + 6 : row + 7, :]
                )
    shift = mod[0:1, :]
    gain = 1.0 + mod[1:2, :]

    def projected(x):
        values = x.astype(F32)
        center = jnp.sum(values, axis=1, keepdims=True) * (1.0 / width)
        centered = values - center
        spread = jnp.sum(centered * centered, axis=1, keepdims=True) * (1.0 / width)
        normed = centered * lax.rsqrt(spread + 1e-06) * gain + shift
        return jnp.dot(normed.astype(BF), w_ref[...], preferred_element_type=F32).astype(BF)

    text_out[...] = projected(text[...])[:, 128:]
    for slot, block in enumerate(blocks):
        out = projected(block[:, :width])
        q_out[slot * rows : (slot + 1) * rows, :] = out[:, :128]
        kv_out[slot * rows : (slot + 1) * rows, :] = out[:, 128:]


def project(slots, blocks, text, weight):
    rows, lanes = blocks[0].shape
    width = text.shape[1]
    return pl.pallas_call(
        project_kernel,
        out_shape=[
            jax.ShapeDtypeStruct((4 * rows, 128), BF),
            jax.ShapeDtypeStruct((4 * rows, 256), BF),
            jax.ShapeDtypeStruct((text.shape[0], 256), BF),
        ],
        in_specs=[pl.BlockSpec(memory_space=pltpu.SMEM)] + [vmem()] * 6,
        out_specs=[vmem()] * 3,
        scratch_shapes=[pltpu.VMEM((2, width), F32), pltpu.VMEM((4, rows, 128), F32)],
        compiler_params=params(20),
        cost_estimate=pl.CostEstimate(
            flops=8 * rows * width * weight.shape[1],
            bytes_accessed=2 * (4 * rows * lanes + weight.size),
            transcendentals=4 * rows,
        ),
        name="project",
    )(slots, *blocks, text, weight)


def softmax_tile(q, keys, values, text, valid):
    contract = (((1,), (1,)), ((), ()))
    lane = lax.broadcasted_iota(jnp.int32, (q.shape[0], 128), 1)
    outs, sums = [], []
    for head in range(2):
        own = jnp.where(lane // HD == head, q, 0.0).astype(BF)
        s = lax.dot_general(own, keys, contract, preferred_element_type=F32)
        top = jnp.max(s, axis=1, keepdims=True)
        if text is not None:
            t = lax.dot_general(own, text[0], contract, preferred_element_type=F32)
            t = jnp.where(valid, t, -1e30)
            top = jnp.maximum(top, jnp.max(t, axis=1, keepdims=True))
        top = top * SCALE2
        p = jnp.exp2(s * SCALE2 - top).astype(BF)
        acc = jnp.dot(p, values, preferred_element_type=F32)
        if text is not None:
            pt = jnp.where(valid, jnp.exp2(t * SCALE2 - top), 0.0).astype(BF)
            acc = acc + jnp.dot(pt, text[1], preferred_element_type=F32)
        total = acc[:, 128:]
        outs.append(acc[:, :128] / total)
        sums.append(top + jnp.log(total) * LOG2E)
    return jnp.where(lane < HD, outs[0], outs[1]), jnp.where(lane < HD, sums[0], sums[1])


def attend_kernel(info, q_ref, kv, text_kv, o_ref, values, text_values, *, tile):
    members, count = q_ref.shape[:2]
    values[:, :128] = kv[:, 128:]
    values[:, 128:] = jnp.ones((kv.shape[0], 128), BF)
    text_values[:, :128] = text_kv[:, 128:]
    text_values[:, 128:] = jnp.ones((TEXT_PART, 128), BF)
    lane = lax.broadcasted_iota(jnp.int32, (tile, 128), 1)
    position = info[0] + lax.broadcasted_iota(jnp.int32, (tile, TEXT_PART), 1)
    valid = (position >= info[1]) & (position < info[2])
    for member in range(members):

        @pl.loop(0, count // tile)
        def _(step):
            rows = pl.ds(pl.multiple_of(step * tile, tile), tile)
            out, rest = softmax_tile(
                q_ref[member, rows, :].astype(F32),
                kv[:, :128],
                values[...],
                (text_kv[:, :128], text_values[...]),
                valid,
            )
            o_ref[member, rows, :] = out.astype(BF)
            stats = jnp.zeros((tile, 128), F32)
            for part in range(3):
                piece = rest.astype(BF).astype(F32)
                stats = jnp.where(lane % HD == part, piece, stats)
                rest = rest - piece
            across = jnp.transpose(stats)
            across = jnp.concatenate([across[:8], across[HD : HD + 8]], axis=0)
            at = pl.multiple_of(count + step * STAT_ROWS, STAT_ROWS)
            o_ref[member, pl.ds(at, STAT_ROWS), :] = across.astype(BF)


def attend(info, qs, kv, text_kv):
    members, count = qs.shape[:2]
    keys = kv.shape[0]
    tile = 128
    rows = count + count // tile * STAT_ROWS
    return pl.pallas_call(
        functools.partial(attend_kernel, tile=tile),
        out_shape=jax.ShapeDtypeStruct((members, rows, 128), BF),
        in_specs=[pl.BlockSpec(memory_space=pltpu.SMEM)] + [vmem()] * 3,
        out_specs=vmem(),
        scratch_shapes=[pltpu.VMEM((keys, 256), BF), pltpu.VMEM((TEXT_PART, 256), BF)],
        compiler_params=params(24),
        cost_estimate=pl.CostEstimate(
            flops=4 * 4 * count * (keys + TEXT_PART) * 256,
            bytes_accessed=2 * 256 * (6 * count + keys),
            transcendentals=8 * count * (keys + TEXT_PART),
        ),
        name="attend",
    )(info, qs, kv, text_kv)


def combine_kernel(slots, parts_ref, out):
    members = parts_ref.shape[0]
    block = 128
    count = out.shape[0] * block
    lane = lax.broadcasted_iota(jnp.int32, (block, 128), 1)
    for place in range(out.shape[0]):
        slot = slots[place]
        rows = pl.ds(pl.multiple_of(slot * block, block), block)
        at = pl.ds(pl.multiple_of(count + slot * STAT_ROWS, STAT_ROWS), STAT_ROWS)
        lses = []
        for member in range(members):
            across = parts_ref[member, at, :].astype(F32)
            across = jnp.concatenate([across, jnp.zeros((128 - STAT_ROWS, 128), F32)], axis=0)
            stats = jnp.transpose(across)
            heads = [
                stats[:, 8 * h : 8 * h + 1]
                + stats[:, 8 * h + 1 : 8 * h + 2]
                + stats[:, 8 * h + 2 : 8 * h + 3]
                for h in range(2)
            ]
            lses.append(jnp.where(lane < HD, heads[0], heads[1]))
        top = functools.reduce(jnp.maximum, lses)
        shares = [jnp.exp2(lse - top) for lse in lses]
        weighted = sum(
            share * parts_ref[member, rows, :].astype(F32) for member, share in enumerate(shares)
        )
        out[place] = (weighted / sum(shares)).astype(BF)


def combine(slots, parts):
    return pl.pallas_call(
        combine_kernel,
        out_shape=jax.ShapeDtypeStruct((4, 128, 128), BF),
        in_specs=[pl.BlockSpec(memory_space=pltpu.SMEM), vmem()],
        out_specs=vmem(),
        compiler_params=params(8),
        name="combine",
    )(slots, parts)


def share(block, axis, count):
    copies = jnp.broadcast_to(block[None], (count,) + block.shape)
    return lax.all_to_all(copies, axis, split_axis=0, concat_axis=0, tiled=True)


def on_device(latents, prompt_rows, peg_weight, modulation_weight, qkv_weight, text_len, timestep):
    frames, tile_h, tile_w, width = latents.shape[1:]
    head_width = qkv_weight.shape[2]
    zl_at = lax.axis_index("zl")
    x_at = lax.axis_index("x")
    member = lax.axis_index("v") * 2 + zl_at

    rows = with_halo(latents, ((("u", "v", "zl"), 2),), 1)
    shard = qkv_weight.reshape(qkv_weight.shape[0], 3 * head_width)
    rows, shard = lax.optimization_barrier((rows, shard))
    other = lax.ppermute(shard, "zl", [(0, 1), (1, 0)])
    shards = jnp.where(
        zl_at == 0, jnp.stack([shard, other]), jnp.stack([other, shard])
    ).reshape(2 * shard.shape[0], shard.shape[1])
    weight = lax.all_gather(shards, ("item", "u", "v"), axis=0, tiled=True)
    padded = with_halo(rows, ((("zh", "x"), 3),), 1)
    summed = latents.astype(F32)
    for row_tap in range(3):
        for col_tap in range(3):
            summed = summed + padded[
                :, :, row_tap : row_tap + tile_h, col_tap : col_tap + tile_w, :
            ].astype(F32) * peg_weight[row_tap, col_tap].astype(F32)
    peg = summed.astype(BF).reshape(frames * tile_h * tile_w, width)

    activation = jax.nn.silu(time_angles(timestep[0], modulation_weight.shape[0])).astype(BF)
    own_columns = jnp.dot(activation[None, :], modulation_weight, preferred_element_type=F32)
    rest = own_columns.reshape(3, 128)
    pieces = []
    for _ in range(3):
        pieces.append(lax.reduce_precision(rest, 8, 7))
        rest = rest - pieces[-1]
    extra = jnp.concatenate(pieces).astype(BF)
    extra = jnp.pad(extra, ((0, peg.shape[0] - 9), (0, 0)))
    peg = jnp.concatenate([peg, extra], axis=1)

    tokens = lax.all_gather(peg, "zh", axis=0, tiled=True)
    blocks = [tokens] + [
        lax.ppermute(tokens, "x", [(i, (i + k) % 4) for i in range(4)]) for k in (1, 3, 2)
    ]
    distance = (jnp.arange(4, dtype=jnp.int32) - x_at) % 4
    slots = jnp.where(distance == 0, 0, jnp.where(distance == 3, 1, distance + 1))

    lower = member * TEXT_PART
    start = jnp.minimum(lower, prompt_rows.shape[1] - TEXT_PART)
    text_rows = lax.dynamic_slice_in_dim(prompt_rows[0], start, TEXT_PART, axis=0)
    queries, kv, text_kv = project(slots, blocks, text_rows, weight)

    all_kv = lax.all_gather(kv, "u", axis=0, tiled=True)
    qs = share(queries, ("v", "zl"), 4)
    info = jnp.stack([start, lower, text_len[0]])
    parts = attend(info, qs, all_kv, text_kv)
    parts = lax.all_to_all(parts, ("v", "zl"), split_axis=0, concat_axis=0, tiled=True)
    attended = combine(slots, parts)
    attended = attended.reshape(4, 4, frames, tile_h, tile_w, head_width)
    attended = attended.transpose(2, 3, 1, 0, 4, 5)
    return attended.reshape(1, frames, tile_h, 16 * tile_w, head_width)


def solution(mesh):
    fine = Mesh(mesh.devices.reshape(2, 4, 2, 2, 4, 4), ("item", "u", "v", "zl", "zh", "x"))
    row = ("u", "v", "zl")
    col = ("zh", "x")
    in_specs = (
        P("item", None, row, col, None),
        P("item", None, None),
        P(),
        P(None, col),
        P(("item",) + row, None, col),
        P("item"),
        P("item"),
    )
    out_specs = P("item", None, row, None, col)
    return jax.shard_map(
        on_device, mesh=fine, in_specs=in_specs, out_specs=out_specs, check_vma=False
    )
```

time: 212 us -> 196 us (0.925)
  starting transfers between devices: 60 us -> 29.6 us
  waiting for transfers between devices: 54.7 us -> 73.4 us
  blocking collectives: 21.6 us -> 33.7 us
  Pallas kernels: 41.7 us -> 30.6 us
  local copies, waits for them, and re-layouts: 14.3 us -> 9.21 us
    all_gather x0 -> x1, waiting for transfers between devices: none -> 23.1 us  [on_device(): all_kv = lax.all_gather(kv, 'u', axis=0, tiled=True)]
    all_to_all x2 -> x1, starting transfers between devices: 24.3 us -> 3.65 us  [share(): return lax.all_to_all(copies, axis, split_axis=0, concat_axis=0, tiled=True)]
    ppermute x3 -> x0, waiting for transfers between devices: 15.2 us -> none  [on_device(): qs = [queries] + [lax.ppermute(queries, axis, swap) for axis, swap in swaps]]
    all_to_all x0 -> x1, blocking collectives: none -> 12.2 us  [on_device(): lax.all_to_all(parts, ('v', 'zl'), split_axis=0, concat_axis=0, tiled=True)]
    pallas_call x7 -> x2, Pallas kernels: 38.8 us -> 27.7 us  [the longest x1 22.3 us: attend(): pl.pallas_call(functools.partial(attend_kernel, tile=tile), out_shape=jax...]
    ppermute x3 -> x0, starting transfers between devices: 9.58 us -> none  [on_device(): qs = [queries] + [lax.ppermute(queries, axis, swap) for axis, swap in swaps]]
    ppermute x3, waiting for transfers between devices: 18.7 us -> 27.2 us  [on_device(): lax.ppermute(tokens, 'x', [(i, (i + k) % 4) for i in range(4)])]
    all_to_all x2 -> x1, waiting for transfers between devices: 0.01 us -> 8.05 us  [share(): return lax.all_to_all(copies, axis, split_axis=0, concat_axis=0, tiled=True)]
  transfers between devices with their start and end apart: 15 -> 11, of which waited for: 7 -> 8; matrix products, arithmetic and copies ran while one was open for 3% -> 3% of each run, Pallas kernels for 8% -> 0%
where the time goes in v3:
time: 196 us; the launch traced here: 195 us
  waiting for transfers between devices  73.4 us (37%)
  blocking collectives  33.7 us (17%)
  Pallas kernels  30.6 us (16%)
  starting transfers between devices  29.6 us (15%)
  between operations  14.9 us (8%)
  local copies, waits for them, and re-layouts  9.21 us (5%)
  other arithmetic  3.5 us (2%)
    ppermute x3, waiting for transfers between devices, on_device(): lax.ppermute(tokens, 'x', [(i, (i + k) % 4) for i in range(4)])  27.2 us
    all_gather x1, waiting for transfers between devices, on_device(): all_kv = lax.all_gather(kv, 'u', axis=0, tiled=True)  23.1 us
    pallas_call x1, Pallas kernels, attend(): pl.pallas_call(functools.partial(attend_kernel, tile=tile), out_shape=jax...  22.3 us
    all_gather x1, blocking collectives, on_device(): tokens = lax.all_gather(peg, 'zh', axis=0, tiled=True)  21.5 us
    all_to_all x1, blocking collectives, on_device(): lax.all_to_all(parts, ('v', 'zl'), split_axis=0, concat_axis=0, tiled=True)  12.2 us
    ppermute x2, waiting for transfers between devices, with_halo(): lax.ppermute(lax.slice_in_dim(block, 0, width, axis=dim), axis, backward)  12.1 us
    ppermute x2, starting transfers between devices, with_halo(): lax.ppermute(lax.slice_in_dim(block, block.shape[dim] - width, None, axis...  10.3 us
    ppermute x3, starting transfers between devices, on_device(): lax.ppermute(tokens, 'x', [(i, (i + k) % 4) for i in range(4)])  8.96 us
  transfers between devices with their start and end apart: 11, of which 8 were waited for; matrix products, arithmetic and copies ran while one was open for 3% of the time, Pallas kernels for 0%

profile of v3, /device:TPU:6, one launch (start us, length us, event | category | flops | bytes accessed | tf_op | source)
XLA Modules:
  0.0 195.2 jit_solution(10655774496340661142)
XLA Ops:
  7.5 4.3 %collective-permute-start = (bf16[1,2,1,4,3072]{4,3,2,1,0:T(4,128)(2,1)S(1)}, bf16[1,2,1,4,3072]{4,3,2,1,0:T(4,128)(2,1)S(1)}, u32[]{:S(2)}, u32[]{:S(2)}) collective-permute-start(bf16[1,2,1,4,3072]{4,3,2,1,0:T(4,128)(2,1)S(1)} %get-tuple-element.17), channel_id=1, source_target_pairs={{0,16},{16,32},{32,48},{48,64},{64,80},{80,96},{96,112},{112,128},... | collective-permute-start | bytes 147464 | tf_op jit(solution)/shard_map/ppermute | solution.py:33
  11.8 1.3 collective-permute-start.1
  14.0 3.8 %collective-permute-done.1 = bf16[1,2,1,4,3072]{4,3,2,1,0:T(4,128)(2,1)S(1)} collective-permute-done((bf16[1,2,1,4,3072]{4,3,2,1,0:T(4,128)(2,1)S(1)}, bf16[1,2,1,4,3072]{4,3,2,1,0:T(4,128)(2,1)S(1)}, u32[]{:S(2)}, u32[]{:S(2)}) %collective-permute-start.1) | collective-permute-done | bytes 49184 | tf_op jit(solution)/shard_map/ppermute | solution.py:36
  19.0 3.5 %collective-permute-start.7 = (bf16[96,384]{1,0:T(8,128)(2,1)S(1)}, bf16[96,384]{1,0:T(8,128)(2,1)S(1)}, u32[]{:S(2)}, u32[]{:S(2)}) collective-permute-start(bf16[96,384]{1,0:T(8,128)(2,1)S(1)} %copy_bitcast_fusion), channel_id=1, source_target_pairs={{0,16},{16,0},{1,17},{17,1},{2,18},{18,2},{3,19},{19,3},{4,20},{20... | collective-permute-start | bytes 221192 | tf_op jit(solution)/shard_map/ppermute | solution.py:240
  23.1 2.1 %collective-permute-done.7 = bf16[96,384]{1,0:T(8,128)(2,1)S(1)} collective-permute-done((bf16[96,384]{1,0:T(8,128)(2,1)S(1)}, bf16[96,384]{1,0:T(8,128)(2,1)S(1)}, u32[]{:S(2)}, u32[]{:S(2)}) %collective-permute-start.7) | collective-permute-done | bytes 73760 | tf_op jit(solution)/shard_map/ppermute | solution.py:240
  26.8 6.0 %collective-permute-start.2 = (bf16[1,2,6,1,3072]{4,3,2,1,0:T(2,128)(2,1)S(1)}, bf16[1,2,6,1,3072]{4,3,2,1,0:T(2,128)(2,1)S(1)}, u32[]{:S(2)}, u32[]{:S(2)}) collective-permute-start(bf16[1,2,6,1,3072]{4,3,2,1,0:T(2,128)(2,1)S(1)} %get-tuple-element.15), channel_id=1, source_target_pairs={{0,1},{1,2},{2,3},{3,4},{4,5},{5,6},{6,7},{7,8},{8,9},{9,10},{10,1... | collective-permute-start | bytes 221192 | tf_op jit(solution)/shard_map/ppermute | solution.py:33
  32.8 1.9 collective-permute-start.3
  35.5 8.4 %collective-permute-done.3 = bf16[1,2,6,1,3072]{4,3,2,1,0:T(2,128)(2,1)S(1)} collective-permute-done((bf16[1,2,6,1,3072]{4,3,2,1,0:T(2,128)(2,1)S(1)}, bf16[1,2,6,1,3072]{4,3,2,1,0:T(2,128)(2,1)S(1)}, u32[]{:S(2)}, u32[]{:S(2)}) %collective-permute-start.3) | collective-permute-done | bytes 73760 | tf_op jit(solution)/shard_map/ppermute | solution.py:36
  43.9 1.4 add_convert_fusion
  45.3 21.5 %all_gather.9.x0 = bf16[128,3200]{1,0:T(8,128)(2,1)S(1)} all-gather(bf16[32,3200]{1,0:T(8,128)(2,1)S(1)} %pad_maximum_fusion.1), channel_id=1, replica_groups=mesh['item'=2,'u'=4,'v'=2,'zl'=2,'zh'=4,'x'=4] {'zh'}, dimensions={0}, use_global_device_ids=true | all-gather | bytes 1024000 | tf_op jit(solution)/shard_map/all_gather | solution.py:265
  66.9 1.9 collective-permute-start.6
  68.8 1.9 collective-permute-start.5
  70.7 5.1 %collective-permute-start.4 = (bf16[128,3200]{1,0:T(8,128)(2,1)S(1)}, bf16[128,3200]{1,0:T(8,128)(2,1)}, u32[]{:S(2)}, u32[]{:S(2)}) collective-permute-start(bf16[128,3200]{1,0:T(8,128)(2,1)S(1)} %all_gather.9.x0), channel_id=1, source_target_pairs={{0,1},{1,2},{2,3},{3,0},{4,5},{5,6},{6,7},{7,4},{8,9},{9,10},{10,1... | collective-permute-start | bytes 2457608 | tf_op jit(solution)/shard_map/ppermute | solution.py:267
  76.0 15.4 %collective-permute-done.6.x3 = bf16[128,3200]{1,0:T(8,128)(2,1)S(1)} collective-permute-done((bf16[128,3200]{1,0:T(8,128)(2,1)S(1)}, bf16[128,3200]{1,0:T(8,128)(2,1)S(1)}, u32[]{:S(2)}, u32[]{:S(2)}) %collective-permute-start.6) | collective-permute-done | bytes 819232 | tf_op jit(solution)/shard_map/ppermute | solution.py:267
  91.5 11.8 %collective-permute-done.5.x2 = bf16[128,3200]{1,0:T(8,128)(2,1)} collective-permute-done((bf16[128,3200]{1,0:T(8,128)(2,1)S(1)}, bf16[128,3200]{1,0:T(8,128)(2,1)}, u32[]{:S(2)}, u32[]{:S(2)}) %collective-permute-start.5) | collective-permute-done | bytes 819232 | tf_op jit(solution)/shard_map/ppermute | solution.py:267
  103.3 1.7 copy-done.1
  104.9 5.4 %project.1 = (bf16[512,128]{1,0:T(8,128)(2,1)S(1)}, bf16[512,256]{1,0:T(8,128)(2,1)S(1)}, bf16[64,256]{1,0:T(8,128)(2,1)S(1)}) custom-call(s32[4]{0:T(128)S(1)} %compare_select_fusion.3.slots, bf16[128,3200]{1,0:T(8,128)(2,1)S(1)} %all_gather.9.x0, bf16[128,3200]{1,0:T(8,128)(2,1)} %collective-permute-done.4.x1, ...), custom_call_target="tpu_custom_call" | custom-call | flops 1207959552 | bytes 5636096 | tf_op jit(solution)/shard_map/project/pallas_call | solution.py:87
  111.7 1.8 broadcast_in_dim.7
  113.5 3.6 %all-to-all-start = ((bf16[4,512,128]{2,1,0:T(8,128)(2,1)}), bf16[4,512,128]{2,1,0:T(8,128)(2,1)S(1)}, u32[]{:S(2)}, u32[]{:S(2)}) async-start(bf16[4,512,128]{2,1,0:T(8,128)(2,1)} %broadcast_in_dim.7), calls=%async_computation | async-start | bytes 1048576 | tf_op jit(solution)/shard_map/all_to_all | solution.py:227
  117.9 8.0 %all-to-all-done.q_ref = bf16[4,512,128]{2,1,0:T(8,128)(2,1)S(1)} async-done(((bf16[4,512,128]{2,1,0:T(8,128)(2,1)}), bf16[4,512,128]{2,1,0:T(8,128)(2,1)S(1)}, u32[]{:S(2)}, u32[]{:S(2)}) %all-to-all-start) | async-done | bytes 524320 | tf_op jit(solution)/shard_map/all_to_all | solution.py:227
  125.9 23.1 %all-gather.5.cloned.1.call-done.kv = bf16[2048,256]{1,0:T(8,128)(2,1)} async-done(((bf16[512,256]{1,0:T(8,128)(2,1)}), bf16[2048,256]{1,0:T(8,128)(2,1)}) %all-gather.5.cloned.1.call-update) | async-done | bytes 1048592 | tf_op jit(solution)/shard_map/all_gather | solution.py:277
  150.2 22.3 %attend.1 = bf16[4,576,128]{2,1,0:T(8,128)(2,1)S(1)} custom-call(s32[3]{0:T(128)S(1)} %pad_add_fusion.info, bf16[4,512,128]{2,1,0:T(8,128)(2,1)S(1)} %all-to-all-done.q_ref, bf16[2048,256]{1,0:T(8,128)(2,1)S(1)} %copy-done.4, bf16[64,256]{1,0:T(8,128)(2,1)S(1)} %get-tuple-element.14.text_kv), custom_call_target="tpu_custom_call" | custom-call | flops 4429185024 | bytes 2621440 | tf_op jit(solution)/shard_map/attend/pallas_call | solution.py:169
  172.6 12.2 %all_to_all.10.parts_ref = bf16[4,576,128]{2,1,0:T(8,128)(2,1)S(1)} all-to-all(bf16[4,576,128]{2,1,0:T(8,128)(2,1)S(1)} %attend.1), channel_id=1, replica_groups=mesh['item'=2,'u'=4,'v'=2,'zl'=2,'zh'=4,'x'=4] {'v','zl'}, dimensions={0} | all-to-all | bytes 1179648 | tf_op jit(solution)/shard_map/all_to_all | solution.py:281
  184.8 2.9 %combine.1 = bf16[4,128,128]{2,1,0:T(8,128)(2,1)S(1)} custom-call(s32[4]{0:T(128)S(1)} %compare_select_fusion.3.slots, bf16[4,576,128]{2,1,0:T(8,128)(2,1)S(1)} %all_to_all.10.parts_ref), custom_call_target="tpu_custom_call" | custom-call | tf_op jit(solution)/shard_map/combine/pallas_call | solution.py:215
  (42 shorter events, 8.9 us)
Async XLA Ops:
  6.5 69.4 %copy-start = (bf16[1,226,3072]{2,1,0:T(8,128)(2,1)S(1)}, bf16[1,226,3072]{2,1,0:T(8,128)(2,1)}, u32[]{:S(2)}) copy-start(bf16[1,226,3072]{2,1,0:T(8,128)(2,1)} %param.8) | copy-start | bytes 4165636
  6.5 19.5 %copy-start.6 = (bf16[512,384]{1,0:T(8,128)(2,1)S(1)}, bf16[512,384]{1,0:T(8,128)(2,1)}, u32[]{:S(2)}) copy-start(bf16[512,384]{1,0:T(8,128)(2,1)} %param.10) | copy-start | bytes 1179652
  6.5 20.0 %copy-start.7 = (bf16[3,3,3072]{2,1,0:T(4,128)(2,1)S(1)}, bf16[3,3,3072]{2,1,0:T(4,128)(2,1)}, u32[]{:S(2)}) copy-start(bf16[3,3,3072]{2,1,0:T(4,128)(2,1)} %param.9) | copy-start | bytes 165892
  6.5 96.7 %all-gather.3.cloned.1.call-start = ((), (), s32[]{:S(2)}) async-start(), calls=%async_computation.2 | async-start | bytes 2506752 | tf_op jit(solution)/shard_map/all_gather | solution.py:244
  7.5 6.5 %collective-permute-start = (bf16[1,2,1,4,3072]{4,3,2,1,0:T(4,128)(2,1)S(1)}, bf16[1,2,1,4,3072]{4,3,2,1,0:T(4,128)(2,1)S(1)}, u32[]{:S(2)}, u32[]{:S(2)}) collective-permute-start(bf16[1,2,1,4,3072]{4,3,2,1,0:T(4,128)(2,1)S(1)} %get-tuple-element.17), channel_id=1, source_target_pairs={{0,16},{16,32},{32,48},{48,64},{64,80},{80,96},{96,112},{112,128},... | collective-permute-start | bytes 147464 | tf_op jit(solution)/shard_map/ppermute | solution.py:33
  11.8 6.0 %collective-permute-start.1 = (bf16[1,2,1,4,3072]{4,3,2,1,0:T(4,128)(2,1)S(1)}, bf16[1,2,1,4,3072]{4,3,2,1,0:T(4,128)(2,1)S(1)}, u32[]{:S(2)}, u32[]{:S(2)}) collective-permute-start(bf16[1,2,1,4,3072]{4,3,2,1,0:T(4,128)(2,1)S(1)} %get-tuple-element.18), channel_id=1, source_target_pairs={{16,0},{32,16},{48,32},{64,48},{80,64},{96,80},{112,96},{128,112},... | collective-permute-start | bytes 147464 | tf_op jit(solution)/shard_map/ppermute | solution.py:36
  14.0 29.8 %copy-start.5 = (bf16[1,2,4,4,3072]{4,3,2,1,0:T(4,128)(2,1)S(1)}, bf16[1,2,4,4,3072]{4,3,2,1,0:T(4,128)(2,1)}, u32[]{:S(2)}) copy-start(bf16[1,2,4,4,3072]{4,3,2,1,0:T(4,128)(2,1)} %param.7) | copy-start | bytes 589828
  19.0 6.2 %collective-permute-start.7 = (bf16[96,384]{1,0:T(8,128)(2,1)S(1)}, bf16[96,384]{1,0:T(8,128)(2,1)S(1)}, u32[]{:S(2)}, u32[]{:S(2)}) collective-permute-start(bf16[96,384]{1,0:T(8,128)(2,1)S(1)} %copy_bitcast_fusion), channel_id=1, source_target_pairs={{0,16},{16,0},{1,17},{17,1},{2,18},{18,2},{3,19},{19,3},{4,20},{20... | collective-permute-start | bytes 221192 | tf_op jit(solution)/shard_map/ppermute | solution.py:240
  25.9 123.1 %all-gather.5.cloned.1.call-start = ((), (), s32[]{:S(2)}) async-start(), calls=%async_computation.3 | async-start | bytes 1310720 | tf_op jit(solution)/shard_map/all_gather | solution.py:277
  26.8 8.7 %collective-permute-start.2 = (bf16[1,2,6,1,3072]{4,3,2,1,0:T(2,128)(2,1)S(1)}, bf16[1,2,6,1,3072]{4,3,2,1,0:T(2,128)(2,1)S(1)}, u32[]{:S(2)}, u32[]{:S(2)}) collective-permute-start(bf16[1,2,6,1,3072]{4,3,2,1,0:T(2,128)(2,1)S(1)} %get-tuple-element.15), channel_id=1, source_target_pairs={{0,1},{1,2},{2,3},{3,4},{4,5},{5,6},{6,7},{7,8},{8,9},{9,10},{10,1... | collective-permute-start | bytes 221192 | tf_op jit(solution)/shard_map/ppermute | solution.py:33
  32.8 11.0 %collective-permute-start.3 = (bf16[1,2,6,1,3072]{4,3,2,1,0:T(2,128)(2,1)S(1)}, bf16[1,2,6,1,3072]{4,3,2,1,0:T(2,128)(2,1)S(1)}, u32[]{:S(2)}, u32[]{:S(2)}) collective-permute-start(bf16[1,2,6,1,3072]{4,3,2,1,0:T(2,128)(2,1)S(1)} %get-tuple-element.16), channel_id=1, source_target_pairs={{1,0},{2,1},{3,2},{4,3},{5,4},{6,5},{7,6},{8,7},{9,8},{10,9},{11,1... | collective-permute-start | bytes 221192 | tf_op jit(solution)/shard_map/ppermute | solution.py:36
  66.9 24.6 %collective-permute-start.6 = (bf16[128,3200]{1,0:T(8,128)(2,1)S(1)}, bf16[128,3200]{1,0:T(8,128)(2,1)S(1)}, u32[]{:S(2)}, u32[]{:S(2)}) collective-permute-start(bf16[128,3200]{1,0:T(8,128)(2,1)S(1)} %all_gather.9.x0), channel_id=1, source_target_pairs={{0,2},{1,3},{2,0},{3,1},{4,6},{5,7},{6,4},{7,5},{8,10},{9,11},{10,... | collective-permute-start | bytes 2457608 | tf_op jit(solution)/shard_map/ppermute | solution.py:267
  68.8 34.5 %collective-permute-start.5 = (bf16[128,3200]{1,0:T(8,128)(2,1)S(1)}, bf16[128,3200]{1,0:T(8,128)(2,1)}, u32[]{:S(2)}, u32[]{:S(2)}) collective-permute-start(bf16[128,3200]{1,0:T(8,128)(2,1)S(1)} %all_gather.9.x0), channel_id=1, source_target_pairs={{0,3},{1,0},{2,1},{3,2},{4,7},{5,4},{6,5},{7,6},{8,11},{9,8},{10,9... | collective-permute-start | bytes 2457608 | tf_op jit(solution)/shard_map/ppermute | solution.py:267
  70.7 32.5 %collective-permute-start.4 = (bf16[128,3200]{1,0:T(8,128)(2,1)S(1)}, bf16[128,3200]{1,0:T(8,128)(2,1)}, u32[]{:S(2)}, u32[]{:S(2)}) collective-permute-start(bf16[128,3200]{1,0:T(8,128)(2,1)S(1)} %all_gather.9.x0), channel_id=1, source_target_pairs={{0,1},{1,2},{2,3},{3,0},{4,5},{5,6},{6,7},{7,4},{8,9},{9,10},{10,1... | collective-permute-start | bytes 2457608 | tf_op jit(solution)/shard_map/ppermute | solution.py:267
  103.3 1.7 copy-start.1
  110.3 0.7 copy-start.2
  111.0 0.7 copy-start.3
  113.5 12.4 %all-to-all-start = ((bf16[4,512,128]{2,1,0:T(8,128)(2,1)}), bf16[4,512,128]{2,1,0:T(8,128)(2,1)S(1)}, u32[]{:S(2)}, u32[]{:S(2)}) async-start(bf16[4,512,128]{2,1,0:T(8,128)(2,1)} %broadcast_in_dim.7), calls=%async_computation | async-start | bytes 1048576 | tf_op jit(solution)/shard_map/all_to_all | solution.py:227
  149.0 1.2 copy-start.4
Sparse Core Ops, SparseCore 0:
  26.0 47.2 all-gather.2
  111.8 37.1 all-gather.4

commit v4 on v3

v4 whole, which is shorter than its diff:
```python
import functools
import math

import jax
import jax.numpy as jnp
from jax import lax
from jax.experimental import pallas as pl
from jax.experimental.pallas import tpu as pltpu
from jax.sharding import Mesh, PartitionSpec as P

HD = 64
LOG2E = 1.4426950408889634
SCALE2 = 0.125 * LOG2E
BF = jnp.bfloat16
F32 = jnp.float32
TEXT_PART = 64
STAT_ROWS = 16


def vmem(*shape):
    return pl.BlockSpec(memory_space=pltpu.VMEM)


def params(mib):
    return pltpu.CompilerParams(vmem_limit_bytes=mib << 20)


def with_halo(block, sides, width):
    for axis, dim in sides:
        count = lax.axis_size(axis)
        forward = [(i, i + 1) for i in range(count - 1)]
        backward = [(target, source) for source, target in forward]
        low = lax.ppermute(
            lax.slice_in_dim(block, block.shape[dim] - width, None, axis=dim), axis, forward
        )
        high = lax.ppermute(lax.slice_in_dim(block, 0, width, axis=dim), axis, backward)
        block = jnp.concatenate([low, block, high], axis=dim)
    return block


def time_angles(step, count):
    half = count // 2
    freqs = jnp.exp(-math.log(10000.0) * jnp.arange(half, dtype=F32) / half)
    angle = step.astype(F32) * freqs
    return jnp.concatenate([jnp.cos(angle), jnp.sin(angle)])


def project_kernel(
    slots, x0, x1, x2, x3, text, w_ref, q_out, text_out, q_copies, kv_copies, mod, extra, kv_out, sems
):
    blocks = (x0, x1, x2, x3)
    rows = x0.shape[0]
    width = text.shape[1]
    tile = rows // 4
    for slot, block in enumerate(blocks):
        extra[slot] = block[:, width:].astype(F32)
    for place in range(4):
        for far in range(4):
            for chunk in range(3):
                at = (far * 4 + place) * 3 + chunk
                kind, first = divmod(at * 128, width)
                row = far * tile + chunk
                mod[kind : kind + 1, first : first + 128] = (
                    extra[slots[place], row : row + 1, :]
                    + extra[slots[place], row + 3 : row + 4, :]
                    + extra[slots[place], row + 6 : row + 7, :]
                )
    shift = mod[0:1, :]
    gain = 1.0 + mod[1:2, :]

    def projected(x):
        values = x.astype(F32)
        center = jnp.sum(values, axis=1, keepdims=True) * (1.0 / width)
        centered = values - center
        spread = jnp.sum(centered * centered, axis=1, keepdims=True) * (1.0 / width)
        normed = centered * lax.rsqrt(spread + 1e-06) * gain + shift
        return jnp.dot(normed.astype(BF), w_ref[...], preferred_element_type=F32).astype(BF)

    text_out[...] = projected(text[...])[:, 128:]
    for slot, block in enumerate(blocks):
        out = projected(block[:, :width])
        q_out[slot * rows : (slot + 1) * rows, :] = out[:, :128]
        kv_out[slot * rows : (slot + 1) * rows, :] = out[:, 128:]
    copies = [
        pltpu.make_async_copy(block, copies.at[i], sems.at[kind, i])
        for kind, (block, copies) in enumerate(((q_out, q_copies), (kv_out, kv_copies)))
        for i in range(4)
    ]
    for copy in copies:
        copy.start()
    for copy in copies:
        copy.wait()


def project(slots, blocks, text, weight):
    rows, lanes = blocks[0].shape
    width = text.shape[1]
    return pl.pallas_call(
        project_kernel,
        out_shape=[
            jax.ShapeDtypeStruct((4 * rows, 128), BF),
            jax.ShapeDtypeStruct((text.shape[0], 256), BF),
            jax.ShapeDtypeStruct((4, 4 * rows, 128), BF),
            jax.ShapeDtypeStruct((4, 4 * rows, 256), BF),
        ],
        in_specs=[pl.BlockSpec(memory_space=pltpu.SMEM)] + [vmem()] * 6,
        out_specs=[vmem()] * 2 + [pl.BlockSpec(memory_space=pl.ANY)] * 2,
        scratch_shapes=[
            pltpu.VMEM((2, width), F32),
            pltpu.VMEM((4, rows, 128), F32),
            pltpu.VMEM((4 * rows, 256), BF),
            pltpu.SemaphoreType.DMA((2, 4)),
        ],
        compiler_params=params(20),
        cost_estimate=pl.CostEstimate(
            flops=8 * rows * width * weight.shape[1],
            bytes_accessed=2 * (4 * rows * lanes + weight.size),
            transcendentals=4 * rows,
        ),
        name="project",
    )(slots, *blocks, text, weight)


def load_keys(kv, text_kv, keys, values):
    blocks, size = kv.shape[:2]
    for block in range(blocks):
        rows = pl.ds(block * size, size)
        keys[rows, :] = kv[block, :, :128]
        values[rows, :128] = kv[block, :, 128:]
    at = blocks * size
    pad = 128 - TEXT_PART
    keys[at : at + TEXT_PART, :] = text_kv[:, :128]
    keys[at + TEXT_PART :, :] = jnp.zeros((pad, 128), BF)
    values[at : at + TEXT_PART, :128] = text_kv[:, 128:]
    values[at + TEXT_PART :, :128] = jnp.zeros((pad, 128), BF)
    values[:, 128:] = jnp.ones((values.shape[0], 128), BF)


def softmax_block(info, q, keys, values):
    rows = q.shape[0]
    latent = keys.shape[0] - 128
    lane = lax.broadcasted_iota(jnp.int32, (rows, 128), 1)
    position = info[0] + lane
    valid = (position >= info[1]) & (position < info[2]) & (lane < TEXT_PART)
    q = q.astype(F32)
    outs, sums = [], []
    for head in range(2):
        own = jnp.where(lane // HD == head, q, 0.0).astype(BF)
        s = lax.dot_general(
            own, keys[...], (((1,), (1,)), ((), ())), preferred_element_type=F32
        )
        text = jnp.where(valid, s[:, latent:], -1e30)
        top = jnp.maximum(
            jnp.max(s[:, :latent], axis=1, keepdims=True), jnp.max(text, axis=1, keepdims=True)
        )
        top = top * SCALE2
        p = jnp.exp2(s[:, :latent] * SCALE2 - top).astype(BF)
        p_text = jnp.where(valid, jnp.exp2(text * SCALE2 - top), 0.0).astype(BF)
        p = jnp.concatenate([p, p_text], axis=1)
        acc = jnp.dot(p, values[...], preferred_element_type=F32)
        total = acc[:, 128:]
        outs.append(acc[:, :128] / total)
        sums.append(top + jnp.log(total) * LOG2E)
    return jnp.where(lane < HD, outs[0], outs[1]), jnp.where(lane < HD, sums[0], sums[1])


def peers_kernel(info, q_ref, kv, text_kv, o_ref, keys, values):
    members, count = q_ref.shape[:2]
    load_keys(kv, text_kv, keys, values)
    lane = lax.broadcasted_iota(jnp.int32, (128, 128), 1)

    @pl.loop(1, members)
    def _(step):
        member = jnp.bitwise_xor(info[3], step)
        out, lse = softmax_block(info, q_ref[member], keys, values)
        o_ref[member, :count, :] = out.astype(BF)
        for tile in range(count // 128):
            rest = lse[tile * 128 : (tile + 1) * 128]
            stats = jnp.zeros((128, 128), F32)
            for part in range(3):
                piece = rest.astype(BF).astype(F32)
                stats = jnp.where(lane % HD == part, piece, stats)
                rest = rest - piece
            across = jnp.transpose(stats)
            across = jnp.concatenate([across[:8], across[HD : HD + 8]], axis=0)
            at = count + tile * STAT_ROWS
            o_ref[member, at : at + STAT_ROWS, :] = across.astype(BF)


def own_kernel(info, q_ref, kv, text_kv, o_ref, l_ref, keys, values):
    load_keys(kv, text_kv, keys, values)
    out, lse = softmax_block(info, q_ref[...], keys, values)
    o_ref[...] = out
    l_ref[...] = lse


def attend(kernel, name, blocks, out_shape, info, q, kv, text_kv):
    keys = kv.shape[0] * kv.shape[1] + 128
    count = q.shape[-2]
    return pl.pallas_call(
        kernel,
        out_shape=out_shape,
        in_specs=[pl.BlockSpec(memory_space=pltpu.SMEM)] + [vmem()] * 3,
        out_specs=jax.tree.map(lambda _: vmem(), out_shape),
        scratch_shapes=[pltpu.VMEM((keys, 128), BF), pltpu.VMEM((keys, 256), BF)],
        compiler_params=params(32),
        cost_estimate=pl.CostEstimate(
            flops=4 * blocks * count * keys * 256,
            bytes_accessed=2 * (q.size + kv.size),
            transcendentals=2 * blocks * count * keys,
        ),
        name=name,
    )(info, q, kv, text_kv)


def combine_kernel(slots, info, parts_ref, o_ref, l_ref, out):
    members = parts_ref.shape[0]
    block = 128
    count = o_ref.shape[0]
    lane = lax.broadcasted_iota(jnp.int32, (block, 128), 1)
    for place in range(out.shape[0]):
        slot = slots[place]
        rows = pl.ds(pl.multiple_of(slot * block, block), block)
        at = pl.ds(pl.multiple_of(count + slot * STAT_ROWS, STAT_ROWS), STAT_ROWS)
        lses = [l_ref[rows, :]]
        outs = [o_ref[rows, :]]
        for step in range(1, members):
            member = jnp.bitwise_xor(info[3], step)
            across = parts_ref[member, at, :].astype(F32)
            across = jnp.concatenate([across, jnp.zeros((128 - STAT_ROWS, 128), F32)], axis=0)
            stats = jnp.transpose(across)
            heads = [
                stats[:, 8 * h : 8 * h + 1]
                + stats[:, 8 * h + 1 : 8 * h + 2]
                + stats[:, 8 * h + 2 : 8 * h + 3]
                for h in range(2)
            ]
            lses.append(jnp.where(lane < HD, heads[0], heads[1]))
            outs.append(parts_ref[member, rows, :].astype(F32))
        top = functools.reduce(jnp.maximum, lses)
        shares = [jnp.exp2(lse - top) for lse in lses]
        weighted = sum(share * part for share, part in zip(shares, outs))
        out[place] = (weighted / sum(shares)).astype(BF)


def combine(slots, info, parts, own):
    smem = pl.BlockSpec(memory_space=pltpu.SMEM)
    return pl.pallas_call(
        combine_kernel,
        out_shape=jax.ShapeDtypeStruct((4, 128, 128), BF),
        in_specs=[smem, smem] + [vmem()] * 3,
        out_specs=vmem(),
        compiler_params=params(8),
        name="combine",
    )(slots, info, parts, *own)


def on_device(latents, prompt_rows, peg_weight, modulation_weight, qkv_weight, text_len, timestep):
    frames, tile_h, tile_w, width = latents.shape[1:]
    head_width = qkv_weight.shape[2]
    zl_at = lax.axis_index("zl")
    x_at = lax.axis_index("x")
    member = lax.axis_index("v") * 2 + zl_at

    shard = qkv_weight.reshape(qkv_weight.shape[0], 3 * head_width)
    half = lax.all_gather(shard, ("item", "u", "v"), axis=0, tiled=True)
    padded = with_halo(latents, ((("u", "v", "zl"), 2), (("zh", "x"), 3)), 1)
    summed = latents.astype(F32)
    for row_tap in range(3):
        for col_tap in range(3):
            summed = summed + padded[
                :, :, row_tap : row_tap + tile_h, col_tap : col_tap + tile_w, :
            ].astype(F32) * peg_weight[row_tap, col_tap].astype(F32)
    peg = summed.astype(BF).reshape(frames * tile_h * tile_w, width)

    activation = jax.nn.silu(time_angles(timestep[0], modulation_weight.shape[0])).astype(BF)
    own_columns = jnp.dot(activation[None, :], modulation_weight, preferred_element_type=F32)
    rest = own_columns.reshape(3, 128)
    pieces = []
    for _ in range(3):
        pieces.append(lax.reduce_precision(rest, 8, 7))
        rest = rest - pieces[-1]
    extra = jnp.concatenate(pieces).astype(BF)
    extra = jnp.pad(extra, ((0, peg.shape[0] - 9), (0, 0)))
    peg = jnp.concatenate([peg, extra], axis=1)

    tokens = lax.all_gather(peg, "zh", axis=0, tiled=True)
    tokens, half = lax.optimization_barrier((tokens, half))
    blocks = [tokens] + [
        lax.ppermute(tokens, "x", [(i, (i + k) % 4) for i in range(4)]) for k in (1, 3, 2)
    ]
    other = lax.ppermute(half, "zl", [(0, 1), (1, 0)])
    pieces = (-1, shard.shape[0], shard.shape[1])
    half, other = half.reshape(pieces), other.reshape(pieces)
    weight = jnp.where(
        zl_at == 0, jnp.stack([half, other], axis=1), jnp.stack([other, half], axis=1)
    ).reshape(width, 3 * head_width)
    distance = (jnp.arange(4, dtype=jnp.int32) - x_at) % 4
    slots = jnp.where(distance == 0, 0, jnp.where(distance == 3, 1, distance + 1))

    lower = member * TEXT_PART
    start = jnp.minimum(lower, prompt_rows.shape[1] - TEXT_PART)
    text_rows = lax.dynamic_slice_in_dim(prompt_rows[0], start, TEXT_PART, axis=0)
    queries, text_kv, q_copies, kv_copies = project(slots, blocks, text_rows, weight)
    group = ("v", "zl")
    qs = lax.all_to_all(q_copies, group, split_axis=0, concat_axis=0, tiled=True)
    kv = lax.all_to_all(kv_copies, "u", split_axis=0, concat_axis=0, tiled=True)
    info = jnp.stack([start, lower, text_len[0], member])
    count = queries.shape[0]
    part = jax.ShapeDtypeStruct((4, count + count // 128 * STAT_ROWS, 128), BF)
    parts = attend(peers_kernel, "peers", 3, part, info, qs, kv, text_kv)
    parts = lax.all_to_all(parts, group, split_axis=0, concat_axis=0, tiled=True)
    plain = jax.ShapeDtypeStruct((count, 128), F32)
    own = attend(own_kernel, "own", 1, [plain, plain], info, queries, kv, text_kv)
    attended = combine(slots, info, parts, own)
    attended = attended.reshape(4, 4, frames, tile_h, tile_w, head_width)
    attended = attended.transpose(2, 3, 1, 0, 4, 5)
    return attended.reshape(1, frames, tile_h, 16 * tile_w, head_width)


def solution(mesh):
    fine = Mesh(mesh.devices.reshape(2, 4, 2, 2, 4, 4), ("item", "u", "v", "zl", "zh", "x"))
    row = ("u", "v", "zl")
    col = ("zh", "x")
    in_specs = (
        P("item", None, row, col, None),
        P("item", None, None),
        P(),
        P(None, col),
        P(("item",) + row, None, col),
        P("item"),
        P("item"),
    )
    out_specs = P("item", None, row, None, col)
    return jax.shard_map(
        on_device, mesh=fine, in_specs=in_specs, out_specs=out_specs, check_vma=False
    )
```

time: 196 us -> 189 us (0.964)
  starting transfers between devices: 29.6 us -> 39.9 us
  waiting for transfers between devices: 73.4 us -> 64 us
  Pallas kernels: 30.6 us -> 21.9 us
  other arithmetic: 3.5 us -> 5.51 us
    all_gather x2 -> x1, waiting for transfers between devices: 23.1 us -> 0.01 us  [on_device(): half = lax.all_gather(shard, ('item', 'u', 'v'), axis=0, tiled=True)]
    ppermute x1, waiting for transfers between devices: 2.11 us -> 17.5 us  [on_device(): other = lax.ppermute(half, 'zl', [(0, 1), (1, 0)])]
    all_to_all x1 -> x2, waiting for transfers between devices: 8.05 us -> 22 us  [the longest x1 17.3 us: on_device(): kv = lax.all_to_all(kv_copies, 'u', split_axis=0, concat_axis=0, tiled=True)]
    ppermute x3, waiting for transfers between devices: 27.2 us -> 13.4 us  [on_device(): lax.ppermute(tokens, 'x', [(i, (i + k) % 4) for i in range(4)])]
    all_to_all x1 -> x2, starting transfers between devices: 3.65 us -> 14.2 us  [the longest x1 9.74 us: on_device(): lax.all_to_all(parts, group, split_axis=0, concat_axis=0, tiled=True)]
    pallas_call x1 -> x2, Pallas kernels: 22.3 us -> 12.9 us  [attend(): pl.pallas_call(kernel, out_shape=out_shape, in_specs=[pl.BlockSpec(memory...]
    all_to_all x1, blocking collectives: 12.2 us -> 9.82 us  [on_device(): lax.all_to_all(q_copies, group, split_axis=0, concat_axis=0, tiled=True)]
    select_n x1, other arithmetic: 0.69 us -> 2.85 us  [on_device(): jnp.where(zl_at == 0, jnp.stack([half, other], axis=1), jnp.stack([other,...]
  transfers between devices with their start and end apart: 11 -> 11, of which waited for: 8 -> 6; matrix products, arithmetic and copies ran while one was open for 3% -> 5% of each run, Pallas kernels for 0% -> 2%
where the time goes in v4:
time: 189 us; the launch traced here: 188 us
  waiting for transfers between devices  64 us (34%)
  starting transfers between devices  39.9 us (21%)
  blocking collectives  33.4 us (18%)
  Pallas kernels  21.9 us (12%)
  between operations  14.9 us (8%)
  local copies, waits for them, and re-layouts  8.36 us (4%)
  other arithmetic  5.51 us (3%)
    all_gather x1, blocking collectives, on_device(): tokens = lax.all_gather(peg, 'zh', axis=0, tiled=True)  23.6 us
    ppermute x1, waiting for transfers between devices, on_device(): other = lax.ppermute(half, 'zl', [(0, 1), (1, 0)])  17.5 us
    all_to_all x1, waiting for transfers between devices, on_device(): kv = lax.all_to_all(kv_copies, 'u', split_axis=0, concat_axis=0, tiled=True)  17.3 us
    ppermute x3, waiting for transfers between devices, on_device(): lax.ppermute(tokens, 'x', [(i, (i + k) % 4) for i in range(4)])  13.4 us
    pallas_call x2, Pallas kernels, attend(): pl.pallas_call(kernel, out_shape=out_shape, in_specs=[pl.BlockSpec(memory...  12.9 us
    ppermute x2, starting transfers between devices, with_halo(): lax.ppermute(lax.slice_in_dim(block, block.shape[dim] - width, None, axis...  10.3 us
    ppermute x2, waiting for transfers between devices, with_halo(): lax.ppermute(lax.slice_in_dim(block, 0, width, axis=dim), axis, backward)  10.2 us
    all_to_all x1, blocking collectives, on_device(): lax.all_to_all(q_copies, group, split_axis=0, concat_axis=0, tiled=True)  9.82 us
  transfers between devices with their start and end apart: 11, of which 6 were waited for; matrix products, arithmetic and copies ran while one was open for 5% of the time, Pallas kernels for 2%

profile of v4, /device:TPU:6, one launch (start us, length us, event | category | flops | bytes accessed | tf_op | source)
XLA Modules:
  0.0 188.2 jit_solution(8693261735087875913)
XLA Ops:
  7.5 4.3 %collective-permute-start = (bf16[1,2,1,4,3072]{4,3,2,1,0:T(4,128)(2,1)S(1)}, bf16[1,2,1,4,3072]{4,3,2,1,0:T(4,128)(2,1)S(1)}, u32[]{:S(2)}, u32[]{:S(2)}) collective-permute-start(bf16[1,2,1,4,3072]{4,3,2,1,0:T(4,128)(2,1)S(1)} %get-tuple-element.24), channel_id=1, source_target_pairs={{0,16},{16,32},{32,48},{48,64},{64,80},{80,96},{96,112},{112,128},... | collective-permute-start | bytes 147464 | tf_op jit(solution)/shard_map/ppermute | solution.py:33
  11.8 1.3 collective-permute-start.1
  13.1 1.5 copy_bitcast_fusion
  19.2 6.0 %collective-permute-start.2 = (bf16[1,2,6,1,3072]{4,3,2,1,0:T(2,128)(2,1)S(1)}, bf16[1,2,6,1,3072]{4,3,2,1,0:T(2,128)(2,1)S(1)}, u32[]{:S(2)}, u32[]{:S(2)}) collective-permute-start(bf16[1,2,6,1,3072]{4,3,2,1,0:T(2,128)(2,1)S(1)} %get-tuple-element.21), channel_id=1, source_target_pairs={{0,1},{1,2},{2,3},{3,4},{4,5},{5,6},{6,7},{7,8},{8,9},{9,10},{10,1... | collective-permute-start | bytes 221192 | tf_op jit(solution)/shard_map/ppermute | solution.py:33
  25.2 1.9 %collective-permute-start.3 = (bf16[1,2,6,1,3072]{4,3,2,1,0:T(2,128)(2,1)S(1)}, bf16[1,2,6,1,3072]{4,3,2,1,0:T(2,128)(2,1)S(1)}, u32[]{:S(2)}, u32[]{:S(2)}) collective-permute-start(bf16[1,2,6,1,3072]{4,3,2,1,0:T(2,128)(2,1)S(1)} %get-tuple-element.22), channel_id=1, source_target_pairs={{1,0},{2,1},{3,2},{4,3},{5,4},{6,5},{7,6},{8,7},{9,8},{10,9},{11,1... | collective-permute-start | bytes 221192 | tf_op jit(solution)/shard_map/ppermute | solution.py:36
  28.0 10.2 %collective-permute-done.3 = bf16[1,2,6,1,3072]{4,3,2,1,0:T(2,128)(2,1)S(1)} collective-permute-done((bf16[1,2,6,1,3072]{4,3,2,1,0:T(2,128)(2,1)S(1)}, bf16[1,2,6,1,3072]{4,3,2,1,0:T(2,128)(2,1)S(1)}, u32[]{:S(2)}, u32[]{:S(2)}) %collective-permute-start.3) | collective-permute-done | bytes 73760 | tf_op jit(solution)/shard_map/ppermute | solution.py:36
  38.3 1.4 fusion.8
  39.8 23.6 %all_gather.6.x0 = bf16[128,3200]{1,0:T(8,128)(2,1)S(1)} all-gather(bf16[32,3200]{1,0:T(8,128)(2,1)S(1)} %pad_maximum_fusion), channel_id=1, replica_groups=mesh['item'=2,'u'=4,'v'=2,'zl'=2,'zh'=4,'x'=4] {'zh'}, dimensions={0}, use_global_device_ids=true | all-gather | bytes 1024000 | tf_op jit(solution)/shard_map/all_gather | solution.py:287
  63.4 3.0 %collective-permute-start.7 = (bf16[1536,384]{1,0:T(8,128)(2,1)}, bf16[1536,384]{1,0:T(8,128)(2,1)}, u32[]{:S(2)}, u32[]{:S(2)}) collective-permute-start(bf16[1536,384]{1,0:T(8,128)(2,1)} %all-gather.2.cloned.1.call-done), channel_id=1, source_target_pairs={{0,16},{16,0},{1,17},{17,1},{2,18},{18,2},{3,19},{19,3},{4,20},{20... | collective-permute-start | bytes 3538952 | tf_op jit(solution)/shard_map/ppermute | solution.py:292
  66.3 2.5 %collective-permute-start.4 = (bf16[128,3200]{1,0:T(8,128)(2,1)S(1)}, bf16[128,3200]{1,0:T(8,128)(2,1)S(1)}, u32[]{:S(2)}, u32[]{:S(2)}) collective-permute-start(bf16[128,3200]{1,0:T(8,128)(2,1)S(1)} %all_gather.6.x0), channel_id=1, source_target_pairs={{0,1},{1,2},{2,3},{3,0},{4,5},{5,6},{6,7},{7,4},{8,9},{9,10},{10,1... | collective-permute-start | bytes 2457608 | tf_op jit(solution)/shard_map/ppermute | solution.py:290
  68.9 3.3 %collective-permute-start.5 = (bf16[128,3200]{1,0:T(8,128)(2,1)S(1)}, bf16[128,3200]{1,0:T(8,128)(2,1)}, u32[]{:S(2)}, u32[]{:S(2)}) collective-permute-start(bf16[128,3200]{1,0:T(8,128)(2,1)S(1)} %all_gather.6.x0), channel_id=1, source_target_pairs={{0,3},{1,0},{2,1},{3,2},{4,7},{5,4},{6,5},{7,6},{8,11},{9,8},{10,9... | collective-permute-start | bytes 2457608 | tf_op jit(solution)/shard_map/ppermute | solution.py:290
  72.2 3.4 %collective-permute-start.6 = (bf16[128,3200]{1,0:T(8,128)(2,1)S(1)}, bf16[128,3200]{1,0:T(8,128)(2,1)}, u32[]{:S(2)}, u32[]{:S(2)}) collective-permute-start(bf16[128,3200]{1,0:T(8,128)(2,1)S(1)} %all_gather.6.x0), channel_id=1, source_target_pairs={{0,2},{1,3},{2,0},{3,1},{4,6},{5,7},{6,4},{7,5},{8,10},{9,11},{10,... | collective-permute-start | bytes 2457608 | tf_op jit(solution)/shard_map/ppermute | solution.py:290
  75.7 17.5 %collective-permute-done.7 = bf16[1536,384]{1,0:T(8,128)(2,1)} collective-permute-done((bf16[1536,384]{1,0:T(8,128)(2,1)}, bf16[1536,384]{1,0:T(8,128)(2,1)}, u32[]{:S(2)}, u32[]{:S(2)}) %collective-permute-start.7) | collective-permute-done | bytes 1179680 | tf_op jit(solution)/shard_map/ppermute | solution.py:292
  93.2 2.9 %maximum_select_fusion = bf16[16,2,96,384]{3,2,1,0:T(8,128)(2,1)S(1)} fusion(bf16[16,1,96,384]{3,2,1,0:T(8,128)(2,1)} %bitcast.20, bf16[16,1,96,384]{3,2,1,0:T(8,128)(2,1)} %bitcast.48, pred[]{:T(512)S(6)} %eq.13), kind=kLoop, calls=%fused_computation | loop fusion | flops 3538944 | bytes 4718593 | tf_op jit(solution)/shard_map/jit(_where)/select_n | solution.py:295
  96.1 13.4 %collective-permute-done.5.x2 = bf16[128,3200]{1,0:T(8,128)(2,1)} collective-permute-done((bf16[128,3200]{1,0:T(8,128)(2,1)S(1)}, bf16[128,3200]{1,0:T(8,128)(2,1)}, u32[]{:S(2)}, u32[]{:S(2)}) %collective-permute-start.5) | collective-permute-done | bytes 819232 | tf_op jit(solution)/shard_map/ppermute | solution.py:290
  109.5 6.7 %project.1 = (bf16[512,128]{1,0:T(8,128)(2,1)S(1)}, bf16[64,256]{1,0:T(8,128)(2,1)S(1)}, bf16[4,512,128]{2,1,0:T(8,128)(2,1)S(1)}, bf16[4,512,256]{2,1,0:T(8,128)(2,1)}) custom-call(s32[4]{0:T(128)S(1)} %compare_select_fusion.3.slots, bf16[128,3200]{1,0:T(8,128)(2,1)S(1)} %all_gather.6.x0, bf16[128,3200]{1,0:T(8,128)(2,1)S(1)} %collective-permute-done.4.x1, ...), custom_call_target="tpu_custom_call" | custom-call | flops 1207959552 | bytes 5636096 | tf_op jit(solution)/shard_map/project/pallas_call | solution.py:98
  116.2 9.8 %all_to_all.15.q_ref = bf16[4,512,128]{2,1,0:T(8,128)(2,1)S(1)} all-to-all(bf16[4,512,128]{2,1,0:T(8,128)(2,1)S(1)} %get-tuple-element.15), channel_id=1, replica_groups=mesh['item'=2,'u'=4,'v'=2,'zl'=2,'zh'=4,'x'=4] {'v','zl'}, dimensions={0} | all-to-all | bytes 1048576 | tf_op jit(solution)/shard_map/all_to_all | solution.py:306
  126.1 4.5 %all-to-all-start.1 = ((bf16[4,512,256]{2,1,0:T(8,128)(2,1)}), bf16[4,512,256]{2,1,0:T(8,128)(2,1)S(1)}, u32[]{:S(2)}, u32[]{:S(2)}) async-start(bf16[4,512,256]{2,1,0:T(8,128)(2,1)} %get-tuple-element.16), calls=%async_computation.1 | async-start | bytes 2097152 | tf_op jit(solution)/shard_map/all_to_all | solution.py:307
  131.3 17.3 %all-to-all-done.1.kv = bf16[4,512,256]{2,1,0:T(8,128)(2,1)S(1)} async-done(((bf16[4,512,256]{2,1,0:T(8,128)(2,1)}), bf16[4,512,256]{2,1,0:T(8,128)(2,1)S(1)}, u32[]{:S(2)}, u32[]{:S(2)}) %all-to-all-start.1) | async-done | bytes 1048608 | tf_op jit(solution)/shard_map/all_to_all | solution.py:307
  148.6 9.4 %peers.1 = bf16[4,576,128]{2,1,0:T(8,128)(2,1)S(1)} custom-call(s32[4]{0:T(128)S(1)} %pad_add_fusion.info, bf16[4,512,128]{2,1,0:T(8,128)(2,1)S(1)} %all_to_all.15.q_ref, bf16[4,512,256]{2,1,0:T(8,128)(2,1)S(1)} %all-to-all-done.1.kv, bf16[64,256]{1,0:T(8,128)(2,1)S(1)} %get-tuple-element.17.text_kv), custom_call_target="tpu_custom_call" | custom-call | flops 3422552064 | bytes 1572864 | tf_op jit(solution)/shard_map/peers/pallas_call | solution.py:200
  158.9 9.7 %all-to-all-start.2 = ((bf16[4,576,128]{2,1,0:T(8,128)(2,1)}), bf16[4,576,128]{2,1,0:T(8,128)(2,1)S(1)}, u32[]{:S(2)}, u32[]{:S(2)}) async-start(bf16[4,576,128]{2,1,0:T(8,128)(2,1)} %copy-done.1), calls=%async_computation.2 | async-start | bytes 1179648 | tf_op jit(solution)/shard_map/all_to_all | solution.py:312
  168.6 3.5 %own.1 = (f32[512,128]{1,0:T(8,128)S(1)}, f32[512,128]{1,0:T(8,128)S(1)}) custom-call(s32[4]{0:T(128)S(1)} %pad_add_fusion.info, bf16[512,128]{1,0:T(8,128)(2,1)S(1)} %get-tuple-element.18.q_ref, bf16[4,512,256]{2,1,0:T(8,128)(2,1)S(1)} %all-to-all-done.1.kv, bf16[64,256]{1,0:T(8,128)(2,1)S(1)} %get-tuple-element.17.text_kv), custom_call_target="tpu_custom_call" | custom-call | flops 1140850688 | bytes 1179648 | tf_op jit(solution)/shard_map/own/pallas_call | solution.py:200
  172.8 4.6 %all-to-all-done.2.parts_ref = bf16[4,576,128]{2,1,0:T(8,128)(2,1)S(1)} async-done(((bf16[4,576,128]{2,1,0:T(8,128)(2,1)}), bf16[4,576,128]{2,1,0:T(8,128)(2,1)S(1)}, u32[]{:S(2)}, u32[]{:S(2)}) %all-to-all-start.2) | async-done | bytes 589856 | tf_op jit(solution)/shard_map/all_to_all | solution.py:312
  178.4 2.3 %combine.1 = bf16[4,128,128]{2,1,0:T(8,128)(2,1)S(1)} custom-call(s32[4]{0:T(128)S(1)} %compare_select_fusion.3.slots, s32[4]{0:T(128)S(1)} %pad_add_fusion.info, bf16[4,576,128]{2,1,0:T(8,128)(2,1)S(1)} %all-to-all-done.2.parts_ref, f32[512,128]{1,0:T(8,128)S(1)} %get-tuple-element.19.o_ref, f32[512,128]{1,0:T(8,128)S(1)} %copy-done.3), custom_call_target="tpu_custom_call" | custom-call | tf_op jit(solution)/shard_map/combine/pallas_call | solution.py:248
  (37 shorter events, 9.2 us)
Async XLA Ops:
  6.5 69.1 %copy-start = (bf16[1,226,3072]{2,1,0:T(8,128)(2,1)S(1)}, bf16[1,226,3072]{2,1,0:T(8,128)(2,1)}, u32[]{:S(2)}) copy-start(bf16[1,226,3072]{2,1,0:T(8,128)(2,1)} %param.8) | copy-start | bytes 4165636
  6.5 31.7 %copy-start.4 = (bf16[1,2,4,4,3072]{4,3,2,1,0:T(4,128)(2,1)S(1)}, bf16[1,2,4,4,3072]{4,3,2,1,0:T(4,128)(2,1)}, u32[]{:S(2)}) copy-start(bf16[1,2,4,4,3072]{4,3,2,1,0:T(4,128)(2,1)} %param.7) | copy-start | bytes 589828
  6.5 56.8 %all-gather.2.cloned.1.call-start = ((), (), s32[]{:S(2)}) async-start(), calls=%async_computation.3 | async-start | bytes 1253376 | tf_op jit(solution)/shard_map/all_gather | solution.py:266
  7.5 10.3 %collective-permute-start = (bf16[1,2,1,4,3072]{4,3,2,1,0:T(4,128)(2,1)S(1)}, bf16[1,2,1,4,3072]{4,3,2,1,0:T(4,128)(2,1)S(1)}, u32[]{:S(2)}, u32[]{:S(2)}) collective-permute-start(bf16[1,2,1,4,3072]{4,3,2,1,0:T(4,128)(2,1)S(1)} %get-tuple-element.24), channel_id=1, source_target_pairs={{0,16},{16,32},{32,48},{48,64},{64,80},{80,96},{96,112},{112,128},... | collective-permute-start | bytes 147464 | tf_op jit(solution)/shard_map/ppermute | solution.py:33
  11.8 7.1 %collective-permute-start.1 = (bf16[1,2,1,4,3072]{4,3,2,1,0:T(4,128)(2,1)S(1)}, bf16[1,2,1,4,3072]{4,3,2,1,0:T(4,128)(2,1)S(1)}, u32[]{:S(2)}, u32[]{:S(2)}) collective-permute-start(bf16[1,2,1,4,3072]{4,3,2,1,0:T(4,128)(2,1)S(1)} %get-tuple-element.23), channel_id=1, source_target_pairs={{16,0},{32,16},{48,32},{64,48},{80,64},{96,80},{112,96},{128,112},... | collective-permute-start | bytes 147464 | tf_op jit(solution)/shard_map/ppermute | solution.py:36
  19.2 8.9 %collective-permute-start.2 = (bf16[1,2,6,1,3072]{4,3,2,1,0:T(2,128)(2,1)S(1)}, bf16[1,2,6,1,3072]{4,3,2,1,0:T(2,128)(2,1)S(1)}, u32[]{:S(2)}, u32[]{:S(2)}) collective-permute-start(bf16[1,2,6,1,3072]{4,3,2,1,0:T(2,128)(2,1)S(1)} %get-tuple-element.21), channel_id=1, source_target_pairs={{0,1},{1,2},{2,3},{3,4},{4,5},{5,6},{6,7},{7,8},{8,9},{9,10},{10,1... | collective-permute-start | bytes 221192 | tf_op jit(solution)/shard_map/ppermute | solution.py:33
  25.2 13.1 %collective-permute-start.3 = (bf16[1,2,6,1,3072]{4,3,2,1,0:T(2,128)(2,1)S(1)}, bf16[1,2,6,1,3072]{4,3,2,1,0:T(2,128)(2,1)S(1)}, u32[]{:S(2)}, u32[]{:S(2)}) collective-permute-start(bf16[1,2,6,1,3072]{4,3,2,1,0:T(2,128)(2,1)S(1)} %get-tuple-element.22), channel_id=1, source_target_pairs={{1,0},{2,1},{3,2},{4,3},{5,4},{6,5},{7,6},{8,7},{9,8},{10,9},{11,1... | collective-permute-start | bytes 221192 | tf_op jit(solution)/shard_map/ppermute | solution.py:36
  63.4 29.8 %collective-permute-start.7 = (bf16[1536,384]{1,0:T(8,128)(2,1)}, bf16[1536,384]{1,0:T(8,128)(2,1)}, u32[]{:S(2)}, u32[]{:S(2)}) collective-permute-start(bf16[1536,384]{1,0:T(8,128)(2,1)} %all-gather.2.cloned.1.call-done), channel_id=1, source_target_pairs={{0,16},{16,0},{1,17},{17,1},{2,18},{18,2},{3,19},{19,3},{4,20},{20... | collective-permute-start | bytes 3538952 | tf_op jit(solution)/shard_map/ppermute | solution.py:292
  66.3 29.7 %collective-permute-start.4 = (bf16[128,3200]{1,0:T(8,128)(2,1)S(1)}, bf16[128,3200]{1,0:T(8,128)(2,1)S(1)}, u32[]{:S(2)}, u32[]{:S(2)}) collective-permute-start(bf16[128,3200]{1,0:T(8,128)(2,1)S(1)} %all_gather.6.x0), channel_id=1, source_target_pairs={{0,1},{1,2},{2,3},{3,0},{4,5},{5,6},{6,7},{7,4},{8,9},{9,10},{10,1... | collective-permute-start | bytes 2457608 | tf_op jit(solution)/shard_map/ppermute | solution.py:290
  68.9 40.6 %collective-permute-start.5 = (bf16[128,3200]{1,0:T(8,128)(2,1)S(1)}, bf16[128,3200]{1,0:T(8,128)(2,1)}, u32[]{:S(2)}, u32[]{:S(2)}) collective-permute-start(bf16[128,3200]{1,0:T(8,128)(2,1)S(1)} %all_gather.6.x0), channel_id=1, source_target_pairs={{0,3},{1,0},{2,1},{3,2},{4,7},{5,4},{6,5},{7,6},{8,11},{9,8},{10,9... | collective-permute-start | bytes 2457608 | tf_op jit(solution)/shard_map/ppermute | solution.py:290
  72.2 37.3 %collective-permute-start.6 = (bf16[128,3200]{1,0:T(8,128)(2,1)S(1)}, bf16[128,3200]{1,0:T(8,128)(2,1)}, u32[]{:S(2)}, u32[]{:S(2)}) collective-permute-start(bf16[128,3200]{1,0:T(8,128)(2,1)S(1)} %all_gather.6.x0), channel_id=1, source_target_pairs={{0,2},{1,3},{2,0},{3,1},{4,6},{5,7},{6,4},{7,5},{8,10},{9,11},{10,... | collective-permute-start | bytes 2457608 | tf_op jit(solution)/shard_map/ppermute | solution.py:290
  126.1 22.6 %all-to-all-start.1 = ((bf16[4,512,256]{2,1,0:T(8,128)(2,1)}), bf16[4,512,256]{2,1,0:T(8,128)(2,1)S(1)}, u32[]{:S(2)}, u32[]{:S(2)}) async-start(bf16[4,512,256]{2,1,0:T(8,128)(2,1)} %get-tuple-element.16), calls=%async_computation.1 | async-start | bytes 2097152 | tf_op jit(solution)/shard_map/all_to_all | solution.py:307
  158.0 0.9 copy-start.1
  158.9 18.6 %all-to-all-start.2 = ((bf16[4,576,128]{2,1,0:T(8,128)(2,1)}), bf16[4,576,128]{2,1,0:T(8,128)(2,1)S(1)}, u32[]{:S(2)}, u32[]{:S(2)}) async-start(bf16[4,576,128]{2,1,0:T(8,128)(2,1)} %copy-done.1), calls=%async_computation.2 | async-start | bytes 1179648 | tf_op jit(solution)/shard_map/all_to_all | solution.py:312
  172.1 0.7 copy-start.2
  177.4 1.0 copy-start.3
Sparse Core Ops, SparseCore 0:
  14.8 48.0 all-gather.1

commit v5 on v4

--- a/solution.py
+++ b/solution.py
@@ -19,6 +19,14 @@
 
 def vmem(*shape):
     return pl.BlockSpec(memory_space=pltpu.VMEM)
+
+
+def hbm():
+    return pl.BlockSpec(memory_space=pltpu.MemorySpace.HBM)
+
+
+def keep(x):
+    return pltpu.with_memory_space_constraint(x, pltpu.MemorySpace.HBM)
 
 
 def params(mib):
@@ -46,14 +54,29 @@
 
 
 def project_kernel(
-    slots, x0, x1, x2, x3, text, w_ref, q_out, text_out, q_copies, kv_copies, mod, extra, kv_out, sems
+    slots, x0, a0, a1, b0, b1, c0, c1, text, w_hbm,
+    text_out, q_copies, kv_copies,
+    held, mod, extra, normed, w_ref, q_out, kv_out, sems, in_sems, w_sem,
 ):
-    blocks = (x0, x1, x2, x3)
     rows = x0.shape[0]
+    half = rows // 2
     width = text.shape[1]
     tile = rows // 4
-    for slot, block in enumerate(blocks):
-        extra[slot] = block[:, width:].astype(F32)
+    arrived = [(x0, 0)]
+    for slot, (low, high) in enumerate(((a0, a1), (b0, b1), (c0, c1))):
+        arrived += [(low, (slot + 1) * rows), (high, (slot + 1) * rows + half)]
+    fetches = []
+    for i, (piece, at) in enumerate(arrived):
+        fetches.append(
+            pltpu.make_async_copy(piece, held.at[pl.ds(at, piece.shape[0]), :], in_sems.at[i])
+        )
+        fetches[-1].start()
+    fetch = pltpu.make_async_copy(w_hbm, w_ref, w_sem)
+    fetch.start()
+    for copy in fetches:
+        copy.wait()
+    for slot in range(4):
+        extra[slot] = held[slot * rows : (slot + 1) * rows, width:].astype(F32)
     for place in range(4):
         for far in range(4):
             for chunk in range(3):
@@ -67,20 +90,20 @@
                 )
     shift = mod[0:1, :]
     gain = 1.0 + mod[1:2, :]
-
-    def projected(x):
-        values = x.astype(F32)
+    for block in range(5):
+        at = block * rows
+        count = rows if block < 4 else text.shape[0]
+        values = (held[at : at + rows, :width] if block < 4 else text[...]).astype(F32)
         center = jnp.sum(values, axis=1, keepdims=True) * (1.0 / width)
         centered = values - center
         spread = jnp.sum(centered * centered, axis=1, keepdims=True) * (1.0 / width)
-        normed = centered * lax.rsqrt(spread + 1e-06) * gain + shift
-        return jnp.dot(normed.astype(BF), w_ref[...], preferred_element_type=F32).astype(BF)
-
-    text_out[...] = projected(text[...])[:, 128:]
-    for slot, block in enumerate(blocks):
-        out = projected(block[:, :width])
-        q_out[slot * rows : (slot + 1) * rows, :] = out[:, :128]
-        kv_out[slot * rows : (slot + 1) * rows, :] = out[:, 128:]
+        result = centered * lax.rsqrt(spread + 1e-06) * gain + shift
+        normed[at : at + count, :] = result.astype(BF)
+    fetch.wait()
+    out = jnp.dot(normed[...], w_ref[...], preferred_element_type=F32).astype(BF)
+    q_out[...] = out[: 4 * rows, :128]
+    kv_out[...] = out[: 4 * rows, 128:]
+    text_out[...] = out[4 * rows :, 128:]
     copies = [
         pltpu.make_async_copy(block, copies.at[i], sems.at[kind, i])
         for kind, (block, copies) in enumerate(((q_out, q_copies), (kv_out, kv_copies)))
@@ -92,33 +115,38 @@
         copy.wait()
 
 
-def project(slots, blocks, text, weight):
-    rows, lanes = blocks[0].shape
+def project(slots, pieces, text, weight):
+    rows, lanes = pieces[0].shape
     width = text.shape[1]
     return pl.pallas_call(
         project_kernel,
         out_shape=[
-            jax.ShapeDtypeStruct((4 * rows, 128), BF),
             jax.ShapeDtypeStruct((text.shape[0], 256), BF),
-            jax.ShapeDtypeStruct((4, 4 * rows, 128), BF),
-            jax.ShapeDtypeStruct((4, 4 * rows, 256), BF),
+            pltpu.MemorySpace.HBM((4, 4 * rows, 128), BF),
+            pltpu.MemorySpace.HBM((4, 4 * rows, 256), BF),
         ],
-        in_specs=[pl.BlockSpec(memory_space=pltpu.SMEM)] + [vmem()] * 6,
-        out_specs=[vmem()] * 2 + [pl.BlockSpec(memory_space=pl.ANY)] * 2,
+        in_specs=[pl.BlockSpec(memory_space=pltpu.SMEM)] + [hbm()] * 7 + [vmem(), hbm()],
+        out_specs=[vmem()] + [hbm()] * 2,
         scratch_shapes=[
+            pltpu.VMEM((4 * rows, lanes), BF),
             pltpu.VMEM((2, width), F32),
             pltpu.VMEM((4, rows, 128), F32),
+            pltpu.VMEM((4 * rows + text.shape[0], width), BF),
+            pltpu.VMEM(weight.shape, BF),
+            pltpu.VMEM((4 * rows, 128), BF),
             pltpu.VMEM((4 * rows, 256), BF),
             pltpu.SemaphoreType.DMA((2, 4)),
+            pltpu.SemaphoreType.DMA((7,)),
+            pltpu.SemaphoreType.DMA,
         ],
-        compiler_params=params(20),
+        compiler_params=params(28),
         cost_estimate=pl.CostEstimate(
             flops=8 * rows * width * weight.shape[1],
             bytes_accessed=2 * (4 * rows * lanes + weight.size),
             transcendentals=4 * rows,
         ),
         name="project",
-    )(slots, *blocks, text, weight)
+    )(slots, *map(keep, pieces), text, keep(weight))
 
 
 def load_keys(kv, text_kv, keys, values):
@@ -164,16 +192,19 @@
     return jnp.where(lane < HD, outs[0], outs[1]), jnp.where(lane < HD, sums[0], sums[1])
 
 
-def peers_kernel(info, q_ref, kv, text_kv, o_ref, keys, values):
+def peers_kernel(info, q_ref, kv, text_kv, o_ref, keys, values, held, sems):
     members, count = q_ref.shape[:2]
     load_keys(kv, text_kv, keys, values)
     lane = lax.broadcasted_iota(jnp.int32, (128, 128), 1)
 
+    def send(step):
+        member = jnp.bitwise_xor(info[3], step)
+        return pltpu.make_async_copy(held.at[step], o_ref.at[member], sems.at[step])
+
     @pl.loop(1, members)
     def _(step):
-        member = jnp.bitwise_xor(info[3], step)
-        out, lse = softmax_block(info, q_ref[member], keys, values)
-        o_ref[member, :count, :] = out.astype(BF)
+        out, lse = softmax_block(info, q_ref[jnp.bitwise_xor(info[3], step)], keys, values)
+        held[step, :count, :] = out.astype(BF)
         for tile in range(count // 128):
             rest = lse[tile * 128 : (tile + 1) * 128]
             stats = jnp.zeros((128, 128), F32)
@@ -184,14 +215,21 @@
             across = jnp.transpose(stats)
             across = jnp.concatenate([across[:8], across[HD : HD + 8]], axis=0)
             at = count + tile * STAT_ROWS
-            o_ref[member, at : at + STAT_ROWS, :] = across.astype(BF)
-
-
-def own_kernel(info, q_ref, kv, text_kv, o_ref, l_ref, keys, values):
+            held[step, at : at + STAT_ROWS, :] = across.astype(BF)
+        send(step).start()
+
+    for step in range(1, members):
+        send(step).wait()
+
+
+def own_kernel(info, q_ref, kv, text_kv, o_ref, keys, values, held, sems):
     load_keys(kv, text_kv, keys, values)
-    out, lse = softmax_block(info, q_ref[...], keys, values)
-    o_ref[...] = out
-    l_ref[...] = lse
+    out, lse = softmax_block(info, q_ref[info[3]], keys, values)
+    held[0] = out
+    held[1] = lse
+    copy = pltpu.make_async_copy(held, o_ref, sems.at[0])
+    copy.start()
+    copy.wait()
 
 
 def attend(kernel, name, blocks, out_shape, info, q, kv, text_kv):
@@ -199,11 +237,16 @@
     count = q.shape[-2]
     return pl.pallas_call(
         kernel,
-        out_shape=out_shape,
+        out_shape=pltpu.MemorySpace.HBM(out_shape.shape, out_shape.dtype),
         in_specs=[pl.BlockSpec(memory_space=pltpu.SMEM)] + [vmem()] * 3,
-        out_specs=jax.tree.map(lambda _: vmem(), out_shape),
-        scratch_shapes=[pltpu.VMEM((keys, 128), BF), pltpu.VMEM((keys, 256), BF)],
-        compiler_params=params(32),
+        out_specs=hbm(),
+        scratch_shapes=[
+            pltpu.VMEM((keys, 128), BF),
+            pltpu.VMEM((keys, 256), BF),
+            pltpu.VMEM(out_shape.shape, out_shape.dtype),
+            pltpu.SemaphoreType.DMA((4,)),
+        ],
+        compiler_params=params(24),
         cost_estimate=pl.CostEstimate(
             flops=4 * blocks * count * keys * 256,
             bytes_accessed=2 * (q.size + kv.size),
@@ -213,12 +256,18 @@
     )(info, q, kv, text_kv)
 
 
-def combine_kernel(slots, info, parts_ref, o_ref, l_ref, out):
+def combine_kernel(slots, info, parts_ref, own_hbm, out, grid, own, sem):
+    copy = pltpu.make_async_copy(own_hbm, own, sem)
+    copy.start()
+    copy.wait()
+    o_ref, l_ref = own.at[0], own.at[1]
     members = parts_ref.shape[0]
     block = 128
     count = o_ref.shape[0]
     lane = lax.broadcasted_iota(jnp.int32, (block, 128), 1)
-    for place in range(out.shape[0]):
+    frames, tile_h, cells = out.shape[:3]
+    tile_w = cells // 16
+    for place in range(4):
         slot = slots[place]
         rows = pl.ds(pl.multiple_of(slot * block, block), block)
         at = pl.ds(pl.multiple_of(count + slot * STAT_ROWS, STAT_ROWS), STAT_ROWS)
@@ -240,19 +289,32 @@
         top = functools.reduce(jnp.maximum, lses)
         shares = [jnp.exp2(lse - top) for lse in lses]
         weighted = sum(share * part for share, part in zip(shares, outs))
-        out[place] = (weighted / sum(shares)).astype(BF)
-
-
-def combine(slots, info, parts, own):
+        merged = weighted / sum(shares)
+        at = 0
+        for far in range(4):
+            for frame in range(frames):
+                for row in range(tile_h):
+                    first = (far * 4 + place) * tile_w
+                    grid[frame, row, first : first + tile_w, :] = merged[at : at + tile_w]
+                    at += tile_w
+    out[...] = grid[...].astype(BF)
+
+
+def combine(slots, info, parts, own, shape):
     smem = pl.BlockSpec(memory_space=pltpu.SMEM)
     return pl.pallas_call(
         combine_kernel,
-        out_shape=jax.ShapeDtypeStruct((4, 128, 128), BF),
-        in_specs=[smem, smem] + [vmem()] * 3,
+        out_shape=jax.ShapeDtypeStruct(shape, BF),
+        in_specs=[smem, smem, vmem(), hbm()],
         out_specs=vmem(),
+        scratch_shapes=[
+            pltpu.VMEM(shape, F32),
+            pltpu.VMEM(own.shape, F32),
+            pltpu.SemaphoreType.DMA,
+        ],
         compiler_params=params(8),
         name="combine",
-    )(slots, info, parts, *own)
+    )(slots, info, parts, keep(own))
 
 
 def on_device(latents, prompt_rows, peg_weight, modulation_weight, qkv_weight, text_len, timestep):
@@ -263,7 +325,7 @@
     member = lax.axis_index("v") * 2 + zl_at
 
     shard = qkv_weight.reshape(qkv_weight.shape[0], 3 * head_width)
-    half = lax.all_gather(shard, ("item", "u", "v"), axis=0, tiled=True)
+    weight = lax.all_gather(shard, ("item", "u", "v", "zl"), axis=0, tiled=True)
     padded = with_halo(latents, ((("u", "v", "zl"), 2), (("zh", "x"), 3)), 1)
     summed = latents.astype(F32)
     for row_tap in range(3):
@@ -276,46 +338,43 @@
     activation = jax.nn.silu(time_angles(timestep[0], modulation_weight.shape[0])).astype(BF)
     own_columns = jnp.dot(activation[None, :], modulation_weight, preferred_element_type=F32)
     rest = own_columns.reshape(3, 128)
-    pieces = []
+    terms = []
     for _ in range(3):
-        pieces.append(lax.reduce_precision(rest, 8, 7))
-        rest = rest - pieces[-1]
-    extra = jnp.concatenate(pieces).astype(BF)
+        terms.append(lax.reduce_precision(rest, 8, 7))
+        rest = rest - terms[-1]
+    extra = jnp.concatenate(terms).astype(BF)
     extra = jnp.pad(extra, ((0, peg.shape[0] - 9), (0, 0)))
     peg = jnp.concatenate([peg, extra], axis=1)
 
     tokens = lax.all_gather(peg, "zh", axis=0, tiled=True)
-    tokens, half = lax.optimization_barrier((tokens, half))
-    blocks = [tokens] + [
-        lax.ppermute(tokens, "x", [(i, (i + k) % 4) for i in range(4)]) for k in (1, 3, 2)
-    ]
-    other = lax.ppermute(half, "zl", [(0, 1), (1, 0)])
-    pieces = (-1, shard.shape[0], shard.shape[1])
-    half, other = half.reshape(pieces), other.reshape(pieces)
-    weight = jnp.where(
-        zl_at == 0, jnp.stack([half, other], axis=1), jnp.stack([other, half], axis=1)
-    ).reshape(width, 3 * head_width)
+    half = tokens.shape[0] // 2
+    low, high = tokens[:half], tokens[half:]
+    up = [(i, (i + 1) % 4) for i in range(4)]
+    down = [(i, (i - 1) % 4) for i in range(4)]
+    a0, b1 = lax.ppermute(low, "x", up), lax.ppermute(high, "x", down)
+    a1, b0 = lax.ppermute(high, "x", up), lax.ppermute(low, "x", down)
+    a0, b1 = lax.optimization_barrier((a0, b1))
+    c0, c1 = lax.ppermute(a0, "x", up), lax.ppermute(b1, "x", down)
+    pieces = (tokens, a0, a1, b0, b1, c0, c1)
     distance = (jnp.arange(4, dtype=jnp.int32) - x_at) % 4
     slots = jnp.where(distance == 0, 0, jnp.where(distance == 3, 1, distance + 1))
 
     lower = member * TEXT_PART
     start = jnp.minimum(lower, prompt_rows.shape[1] - TEXT_PART)
     text_rows = lax.dynamic_slice_in_dim(prompt_rows[0], start, TEXT_PART, axis=0)
-    queries, text_kv, q_copies, kv_copies = project(slots, blocks, text_rows, weight)
+    text_kv, q_copies, kv_copies = project(slots, pieces, text_rows, weight)
     group = ("v", "zl")
     qs = lax.all_to_all(q_copies, group, split_axis=0, concat_axis=0, tiled=True)
     kv = lax.all_to_all(kv_copies, "u", split_axis=0, concat_axis=0, tiled=True)
     info = jnp.stack([start, lower, text_len[0], member])
-    count = queries.shape[0]
+    count = qs.shape[1]
     part = jax.ShapeDtypeStruct((4, count + count // 128 * STAT_ROWS, 128), BF)
     parts = attend(peers_kernel, "peers", 3, part, info, qs, kv, text_kv)
     parts = lax.all_to_all(parts, group, split_axis=0, concat_axis=0, tiled=True)
-    plain = jax.ShapeDtypeStruct((count, 128), F32)
-    own = attend(own_kernel, "own", 1, [plain, plain], info, queries, kv, text_kv)
-    attended = combine(slots, info, parts, own)
-    attended = attended.reshape(4, 4, frames, tile_h, tile_w, head_width)
-    attended = attended.transpose(2, 3, 1, 0, 4, 5)
-    return attended.reshape(1, frames, tile_h, 16 * tile_w, head_width)
+    plain = jax.ShapeDtypeStruct((2, count, 128), F32)
+    own = attend(own_kernel, "own", 1, plain, info, qs, kv, text_kv)
+    shape = (frames, tile_h, 16 * tile_w, head_width)
+    return combine(slots, info, parts, own, shape)[None]
 
 
 def solution(mesh):

time: 189 us -> 184 us (0.974)
  the two profiles are of different devices: /device:TPU:6 before, /device:TPU:17 now
where the time goes in v5:
time: 184 us; the launch traced here: 183 us
  starting transfers between devices  58.2 us (32%)
  blocking collectives  36.7 us (20%)
  waiting for transfers between devices  36.3 us (20%)
  Pallas kernels  26.5 us (14%)
  between operations  15 us (8%)
  local copies, waits for them, and re-layouts  7.08 us (4%)
  other arithmetic  2.63 us (1%)
    all_gather x1, blocking collectives, on_device(): tokens = lax.all_gather(peg, 'zh', axis=0, tiled=True)  23.5 us
    all_to_all x1, waiting for transfers between devices, on_device(): kv = lax.all_to_all(kv_copies, 'u', split_axis=0, concat_axis=0, tiled=True)  16.5 us
    all_to_all x1, starting transfers between devices, on_device(): kv = lax.all_to_all(kv_copies, 'u', split_axis=0, concat_axis=0, tiled=True)  14.8 us
    pallas_call x2, Pallas kernels, attend(): pl.pallas_call(kernel, out_shape=pltpu.MemorySpace.HBM(out_shape.shape, o...  14.4 us
    all_to_all x1, blocking collectives, on_device(): lax.all_to_all(q_copies, group, split_axis=0, concat_axis=0, tiled=True)  13.2 us
    all_to_all x1, starting transfers between devices, on_device(): lax.all_to_all(parts, group, split_axis=0, concat_axis=0, tiled=True)  11.9 us
    ppermute x2, starting transfers between devices, on_device(): a0, b1 = (lax.ppermute(low, 'x', up), lax.ppermute(high, 'x', down))  8.18 us
    pallas_call x1, Pallas kernels, project(): pl.pallas_call(project_kernel, out_shape=[jax.ShapeDtypeStruct((text.shap...  8.1 us
  transfers between devices with their start and end apart: 13, of which 9 were waited for; matrix products, arithmetic and copies ran while one was open for 4% of the time, Pallas kernels for 2%

profile of v5, /device:TPU:17, one launch (start us, length us, event | category | flops | bytes accessed | tf_op | source)
XLA Modules:
  0.0 182.7 jit_solution(13617612297097445526)
XLA Ops:
  6.5 1.6 copy_bitcast_fusion
  9.1 3.9 %collective-permute-start.1 = (bf16[1,2,1,4,3072]{4,3,2,1,0:T(4,128)(2,1)S(1)}, bf16[1,2,1,4,3072]{4,3,2,1,0:T(4,128)(2,1)S(1)}, u32[]{:S(2)}, u32[]{:S(2)}) collective-permute-start(bf16[1,2,1,4,3072]{4,3,2,1,0:T(4,128)(2,1)S(1)} %get-tuple-element.19), channel_id=1, source_target_pairs={{16,0},{32,16},{48,32},{64,48},{80,64},{96,80},{112,96},{128,112},... | collective-permute-start | bytes 147464 | tf_op jit(solution)/shard_map/ppermute | solution.py:44
  13.0 2.0 %collective-permute-start = (bf16[1,2,1,4,3072]{4,3,2,1,0:T(4,128)(2,1)S(1)}, bf16[1,2,1,4,3072]{4,3,2,1,0:T(4,128)(2,1)S(1)}, u32[]{:S(2)}, u32[]{:S(2)}) collective-permute-start(bf16[1,2,1,4,3072]{4,3,2,1,0:T(4,128)(2,1)S(1)} %get-tuple-element.20), channel_id=1, source_target_pairs={{0,16},{16,32},{32,48},{48,64},{64,80},{80,96},{96,112},{112,128},... | collective-permute-start | bytes 147464 | tf_op jit(solution)/shard_map/ppermute | solution.py:41
  19.1 3.1 %collective-permute-start.2 = (bf16[1,2,6,1,3072]{4,3,2,1,0:T(2,128)(2,1)S(1)}, bf16[1,2,6,1,3072]{4,3,2,1,0:T(2,128)(2,1)S(1)}, u32[]{:S(2)}, u32[]{:S(2)}) collective-permute-start(bf16[1,2,6,1,3072]{4,3,2,1,0:T(2,128)(2,1)S(1)} %get-tuple-element.17), channel_id=1, source_target_pairs={{0,1},{1,2},{2,3},{3,4},{4,5},{5,6},{6,7},{7,8},{8,9},{9,10},{10,1... | collective-permute-start | bytes 221192 | tf_op jit(solution)/shard_map/ppermute | solution.py:41
  24.3 3.8 %collective-permute-done.3 = bf16[1,2,6,1,3072]{4,3,2,1,0:T(2,128)(2,1)S(1)} collective-permute-done((bf16[1,2,6,1,3072]{4,3,2,1,0:T(2,128)(2,1)S(1)}, bf16[1,2,6,1,3072]{4,3,2,1,0:T(2,128)(2,1)S(1)}, u32[]{:S(2)}, u32[]{:S(2)}) %collective-permute-start.3) | collective-permute-done | bytes 73760 | tf_op jit(solution)/shard_map/ppermute | solution.py:44
  28.1 1.4 fusion.8
  29.6 23.5 %all_gather.6.x0 = bf16[128,3200]{1,0:T(8,128)(2,1)S(1)} all-gather(bf16[32,3200]{1,0:T(8,128)(2,1)S(1)} %pad_maximum_fusion), channel_id=1, replica_groups=mesh['item'=2,'u'=4,'v'=2,'zl'=2,'zh'=4,'x'=4] {'zh'}, dimensions={0}, use_global_device_ids=true | all-gather | bytes 1024000 | tf_op jit(solution)/shard_map/all_gather | solution.py:349
  54.2 6.3 %collective-permute-start.5 = (bf16[64,3200]{1,0:T(8,128)(2,1)}, bf16[64,3200]{1,0:T(8,128)(2,1)S(1)}, u32[]{:S(2)}, u32[]{:S(2)}) collective-permute-start(bf16[64,3200]{1,0:T(8,128)(2,1)} %get-tuple-element.15), channel_id=1, source_target_pairs={{0,3},{1,0},{2,1},{3,2},{4,7},{5,4},{6,5},{7,6},{8,11},{9,8},{10,9... | collective-permute-start | bytes 1228808 | tf_op jit(solution)/shard_map/ppermute | solution.py:354
  60.5 1.9 %collective-permute-start.4 = (bf16[64,3200]{1,0:T(8,128)(2,1)}, bf16[64,3200]{1,0:T(8,128)(2,1)S(1)}, u32[]{:S(2)}, u32[]{:S(2)}) collective-permute-start(bf16[64,3200]{1,0:T(8,128)(2,1)} %get-tuple-element.16), channel_id=1, source_target_pairs={{0,1},{1,2},{2,3},{3,0},{4,5},{5,6},{6,7},{7,4},{8,9},{9,10},{10,1... | collective-permute-start | bytes 1228808 | tf_op jit(solution)/shard_map/ppermute | solution.py:354
  62.4 1.9 %collective-permute-start.6 = (bf16[64,3200]{1,0:T(8,128)(2,1)}, bf16[64,3200]{1,0:T(8,128)(2,1)S(1)}, u32[]{:S(2)}, u32[]{:S(2)}) collective-permute-start(bf16[64,3200]{1,0:T(8,128)(2,1)} %get-tuple-element.15), channel_id=1, source_target_pairs={{0,1},{1,2},{2,3},{3,0},{4,5},{5,6},{6,7},{7,4},{8,9},{9,10},{10,1... | collective-permute-start | bytes 1228808 | tf_op jit(solution)/shard_map/ppermute | solution.py:355
  64.3 4.6 %collective-permute-start.7 = (bf16[64,3200]{1,0:T(8,128)(2,1)}, bf16[64,3200]{1,0:T(8,128)(2,1)S(1)}, u32[]{:S(2)}, u32[]{:S(2)}) collective-permute-start(bf16[64,3200]{1,0:T(8,128)(2,1)} %get-tuple-element.16), channel_id=1, source_target_pairs={{0,3},{1,0},{2,1},{3,2},{4,7},{5,4},{6,5},{7,6},{8,11},{9,8},{10,9... | collective-permute-start | bytes 1228808 | tf_op jit(solution)/shard_map/ppermute | solution.py:355
  68.9 1.6 collective-permute-done.4.a0
  70.6 1.9 %collective-permute-start.8 = (bf16[64,3200]{1,0:T(8,128)(2,1)S(1)}, bf16[64,3200]{1,0:T(8,128)(2,1)S(1)}, u32[]{:S(2)}, u32[]{:S(2)}) collective-permute-start(bf16[64,3200]{1,0:T(8,128)(2,1)S(1)} %collective-permute-done.4.a0), channel_id=1, source_target_pairs={{0,1},{1,2},{2,3},{3,0},{4,5},{5,6},{6,7},{7,4},{8,9},{9,10},{10,1... | collective-permute-start | bytes 1228808 | tf_op jit(solution)/shard_map/ppermute | solution.py:357
  72.5 4.6 %collective-permute-start.9 = (bf16[64,3200]{1,0:T(8,128)(2,1)S(1)}, bf16[64,3200]{1,0:T(8,128)(2,1)}, u32[]{:S(2)}, u32[]{:S(2)}) collective-permute-start(bf16[64,3200]{1,0:T(8,128)(2,1)S(1)} %collective-permute-done.5.b1), channel_id=1, source_target_pairs={{0,3},{1,0},{2,1},{3,2},{4,7},{5,4},{6,5},{7,6},{8,11},{9,8},{10,9... | collective-permute-start | bytes 1228808 | tf_op jit(solution)/shard_map/ppermute | solution.py:357
  78.1 7.0 %collective-permute-done.8.c0 = bf16[64,3200]{1,0:T(8,128)(2,1)S(1)} collective-permute-done((bf16[64,3200]{1,0:T(8,128)(2,1)S(1)}, bf16[64,3200]{1,0:T(8,128)(2,1)S(1)}, u32[]{:S(2)}, u32[]{:S(2)}) %collective-permute-start.8) | collective-permute-done | bytes 409632 | tf_op jit(solution)/shard_map/ppermute | solution.py:357
  86.4 8.1 %project.1 = (bf16[64,256]{1,0:T(8,128)(2,1)S(1)}, bf16[4,512,128]{2,1,0:T(8,128)(2,1)}, bf16[4,512,256]{2,1,0:T(8,128)(2,1)}) custom-call(s32[4]{0:T(128)S(1)} %compare_select_fusion.3.slots, bf16[128,3200]{1,0:T(8,128)(2,1)} %copy-done.3, bf16[64,3200]{1,0:T(8,128)(2,1)} %copy-done.6, bf16[64,3200]{1,0:T(8,128)(2,1)} %copy-done.7, ...), custom_call_target="tpu_custom_call" | custom-call | flops 1207959552 | bytes 5636096 | tf_op jit(solution)/shard_map/project/pallas_call | solution.py:121
  94.5 13.2 %all_to_all.15.q_ref = bf16[4,512,128]{2,1,0:T(8,128)(2,1)S(1)} all-to-all(bf16[4,512,128]{2,1,0:T(8,128)(2,1)} %get-tuple-element.12), channel_id=1, replica_groups=mesh['item'=2,'u'=4,'v'=2,'zl'=2,'zh'=4,'x'=4] {'v','zl'}, dimensions={0} | all-to-all | bytes 1048576 | tf_op jit(solution)/shard_map/all_to_all | solution.py:367
  107.7 14.8 %all-to-all-start.1 = ((bf16[4,512,256]{2,1,0:T(8,128)(2,1)}), bf16[4,512,256]{2,1,0:T(8,128)(2,1)S(1)}, u32[]{:S(2)}, u32[]{:S(2)}) async-start(bf16[4,512,256]{2,1,0:T(8,128)(2,1)} %get-tuple-element.13), calls=%async_computation.1 | async-start | bytes 2097152 | tf_op jit(solution)/shard_map/all_to_all | solution.py:368
  123.3 16.5 %all-to-all-done.1.kv = bf16[4,512,256]{2,1,0:T(8,128)(2,1)S(1)} async-done(((bf16[4,512,256]{2,1,0:T(8,128)(2,1)}), bf16[4,512,256]{2,1,0:T(8,128)(2,1)S(1)}, u32[]{:S(2)}, u32[]{:S(2)}) %all-to-all-start.1) | async-done | bytes 1048608 | tf_op jit(solution)/shard_map/all_to_all | solution.py:368
  139.7 10.1 %peers.1 = bf16[4,576,128]{2,1,0:T(8,128)(2,1)} custom-call(s32[4]{0:T(128)S(1)} %pad_add_fusion.info, bf16[4,512,128]{2,1,0:T(8,128)(2,1)S(1)} %all_to_all.15.q_ref, bf16[4,512,256]{2,1,0:T(8,128)(2,1)S(1)} %all-to-all-done.1.kv, bf16[64,256]{1,0:T(8,128)(2,1)S(1)} %get-tuple-element.14.text_kv), custom_call_target="tpu_custom_call" | custom-call | flops 3422552064 | bytes 1572864 | tf_op jit(solution)/shard_map/peers/pallas_call | solution.py:238
  149.8 11.9 %all-to-all-start.2 = ((bf16[4,576,128]{2,1,0:T(8,128)(2,1)}), bf16[4,576,128]{2,1,0:T(8,128)(2,1)S(1)}, u32[]{:S(2)}, u32[]{:S(2)}) async-start(bf16[4,576,128]{2,1,0:T(8,128)(2,1)} %peers.1), calls=%async_computation.2 | async-start | bytes 1179648 | tf_op jit(solution)/shard_map/all_to_all | solution.py:373
  162.8 4.3 %own.1.own_hbm = f32[2,512,128]{2,1,0:T(8,128)} custom-call(s32[4]{0:T(128)S(1)} %pad_add_fusion.info, bf16[4,512,128]{2,1,0:T(8,128)(2,1)S(1)} %copy-done.2, bf16[4,512,256]{2,1,0:T(8,128)(2,1)S(1)} %all-to-all-done.1.kv, bf16[64,256]{1,0:T(8,128)(2,1)S(1)} %get-tuple-element.14.text_kv), custom_call_target="tpu_custom_call" | custom-call | flops 1140850688 | bytes 1572864 | tf_op jit(solution)/shard_map/own/pallas_call | solution.py:238
  167.1 4.7 %all-to-all-done.2.parts_ref = bf16[4,576,128]{2,1,0:T(8,128)(2,1)S(1)} async-done(((bf16[4,576,128]{2,1,0:T(8,128)(2,1)}), bf16[4,576,128]{2,1,0:T(8,128)(2,1)S(1)}, u32[]{:S(2)}, u32[]{:S(2)}) %all-to-all-start.2) | async-done | bytes 589856 | tf_op jit(solution)/shard_map/all_to_all | solution.py:373
  171.8 4.0 %combine.1 = bf16[2,4,64,128]{3,2,1,0:T(8,128)(2,1)} custom-call(s32[4]{0:T(128)S(1)} %compare_select_fusion.3.slots, s32[4]{0:T(128)S(1)} %pad_add_fusion.info, bf16[4,576,128]{2,1,0:T(8,128)(2,1)S(1)} %all-to-all-done.2.parts_ref, f32[2,512,128]{2,1,0:T(8,128)} %own.1.own_hbm), custom_call_target="tpu_custom_call" | custom-call | tf_op jit(solution)/shard_map/combine/pallas_call | solution.py:305
  (50 shorter events, 10.9 us)
Async XLA Ops:
  6.5 70.6 %copy-start = (bf16[1,226,3072]{2,1,0:T(8,128)(2,1)S(1)}, bf16[1,226,3072]{2,1,0:T(8,128)(2,1)}, u32[]{:S(2)}) copy-start(bf16[1,226,3072]{2,1,0:T(8,128)(2,1)} %param.8) | copy-start | bytes 4165636
  6.5 12.2 %copy-start.4 = (bf16[1,2,4,4,3072]{4,3,2,1,0:T(4,128)(2,1)S(1)}, bf16[1,2,4,4,3072]{4,3,2,1,0:T(4,128)(2,1)}, u32[]{:S(2)}) copy-start(bf16[1,2,4,4,3072]{4,3,2,1,0:T(4,128)(2,1)} %param.7) | copy-start | bytes 589828
  6.5 79.9 %all-gather.2.cloned.1.call-start = ((), (), s32[]{:S(2)}) async-start(), calls=%async_computation.3 | async-start | bytes 2433024 | tf_op jit(solution)/shard_map/all_gather | solution.py:328
  9.1 9.8 %collective-permute-start.1 = (bf16[1,2,1,4,3072]{4,3,2,1,0:T(4,128)(2,1)S(1)}, bf16[1,2,1,4,3072]{4,3,2,1,0:T(4,128)(2,1)S(1)}, u32[]{:S(2)}, u32[]{:S(2)}) collective-permute-start(bf16[1,2,1,4,3072]{4,3,2,1,0:T(4,128)(2,1)S(1)} %get-tuple-element.19), channel_id=1, source_target_pairs={{16,0},{32,16},{48,32},{64,48},{80,64},{96,80},{112,96},{128,112},... | collective-permute-start | bytes 147464 | tf_op jit(solution)/shard_map/ppermute | solution.py:44
  13.0 5.7 %collective-permute-start = (bf16[1,2,1,4,3072]{4,3,2,1,0:T(4,128)(2,1)S(1)}, bf16[1,2,1,4,3072]{4,3,2,1,0:T(4,128)(2,1)S(1)}, u32[]{:S(2)}, u32[]{:S(2)}) collective-permute-start(bf16[1,2,1,4,3072]{4,3,2,1,0:T(4,128)(2,1)S(1)} %get-tuple-element.20), channel_id=1, source_target_pairs={{0,16},{16,32},{32,48},{48,64},{64,80},{80,96},{96,112},{112,128},... | collective-permute-start | bytes 147464 | tf_op jit(solution)/shard_map/ppermute | solution.py:41
  19.1 5.2 %collective-permute-start.2 = (bf16[1,2,6,1,3072]{4,3,2,1,0:T(2,128)(2,1)S(1)}, bf16[1,2,6,1,3072]{4,3,2,1,0:T(2,128)(2,1)S(1)}, u32[]{:S(2)}, u32[]{:S(2)}) collective-permute-start(bf16[1,2,6,1,3072]{4,3,2,1,0:T(2,128)(2,1)S(1)} %get-tuple-element.17), channel_id=1, source_target_pairs={{0,1},{1,2},{2,3},{3,4},{4,5},{5,6},{6,7},{7,8},{8,9},{9,10},{10,1... | collective-permute-start | bytes 221192 | tf_op jit(solution)/shard_map/ppermute | solution.py:41
  22.2 5.9 %collective-permute-start.3 = (bf16[1,2,6,1,3072]{4,3,2,1,0:T(2,128)(2,1)S(1)}, bf16[1,2,6,1,3072]{4,3,2,1,0:T(2,128)(2,1)S(1)}, u32[]{:S(2)}, u32[]{:S(2)}) collective-permute-start(bf16[1,2,6,1,3072]{4,3,2,1,0:T(2,128)(2,1)S(1)} %get-tuple-element.18), channel_id=1, source_target_pairs={{1,0},{2,1},{3,2},{4,3},{5,4},{6,5},{7,6},{8,7},{9,8},{10,9},{11,1... | collective-permute-start | bytes 221192 | tf_op jit(solution)/shard_map/ppermute | solution.py:44
  53.1 33.3 %copy-start.3 = (bf16[128,3200]{1,0:T(8,128)(2,1)}, bf16[128,3200]{1,0:T(8,128)(2,1)S(1)}, u32[]{:S(2)}) copy-start(bf16[128,3200]{1,0:T(8,128)(2,1)S(1)} %all_gather.6.x0) | copy-start | bytes 2457604
  54.2 14.7 %collective-permute-start.5 = (bf16[64,3200]{1,0:T(8,128)(2,1)}, bf16[64,3200]{1,0:T(8,128)(2,1)S(1)}, u32[]{:S(2)}, u32[]{:S(2)}) collective-permute-start(bf16[64,3200]{1,0:T(8,128)(2,1)} %get-tuple-element.15), channel_id=1, source_target_pairs={{0,3},{1,0},{2,1},{3,2},{4,7},{5,4},{6,5},{7,6},{8,11},{9,8},{10,9... | collective-permute-start | bytes 1228808 | tf_op jit(solution)/shard_map/ppermute | solution.py:354
  60.5 10.1 %collective-permute-start.4 = (bf16[64,3200]{1,0:T(8,128)(2,1)}, bf16[64,3200]{1,0:T(8,128)(2,1)S(1)}, u32[]{:S(2)}, u32[]{:S(2)}) collective-permute-start(bf16[64,3200]{1,0:T(8,128)(2,1)} %get-tuple-element.16), channel_id=1, source_target_pairs={{0,1},{1,2},{2,3},{3,0},{4,5},{5,6},{6,7},{7,4},{8,9},{9,10},{10,1... | collective-permute-start | bytes 1228808 | tf_op jit(solution)/shard_map/ppermute | solution.py:354
  62.4 14.8 %collective-permute-start.6 = (bf16[64,3200]{1,0:T(8,128)(2,1)}, bf16[64,3200]{1,0:T(8,128)(2,1)S(1)}, u32[]{:S(2)}, u32[]{:S(2)}) collective-permute-start(bf16[64,3200]{1,0:T(8,128)(2,1)} %get-tuple-element.15), channel_id=1, source_target_pairs={{0,1},{1,2},{2,3},{3,0},{4,5},{5,6},{6,7},{7,4},{8,9},{9,10},{10,1... | collective-permute-start | bytes 1228808 | tf_op jit(solution)/shard_map/ppermute | solution.py:355
  64.3 13.8 %collective-permute-start.7 = (bf16[64,3200]{1,0:T(8,128)(2,1)}, bf16[64,3200]{1,0:T(8,128)(2,1)S(1)}, u32[]{:S(2)}, u32[]{:S(2)}) collective-permute-start(bf16[64,3200]{1,0:T(8,128)(2,1)} %get-tuple-element.16), channel_id=1, source_target_pairs={{0,3},{1,0},{2,1},{3,2},{4,7},{5,4},{6,5},{7,6},{8,11},{9,8},{10,9... | collective-permute-start | bytes 1228808 | tf_op jit(solution)/shard_map/ppermute | solution.py:355
  68.9 17.5 %copy-start.5 = (bf16[64,3200]{1,0:T(8,128)(2,1)}, bf16[64,3200]{1,0:T(8,128)(2,1)S(1)}, u32[]{:S(2)}) copy-start(bf16[64,3200]{1,0:T(8,128)(2,1)S(1)} %collective-permute-done.5.b1) | copy-start | bytes 1228804
  70.6 15.8 %copy-start.6 = (bf16[64,3200]{1,0:T(8,128)(2,1)}, bf16[64,3200]{1,0:T(8,128)(2,1)S(1)}, u32[]{:S(2)}) copy-start(bf16[64,3200]{1,0:T(8,128)(2,1)S(1)} %collective-permute-done.4.a0) | copy-start | bytes 1228804
  70.6 14.5 %collective-permute-start.8 = (bf16[64,3200]{1,0:T(8,128)(2,1)S(1)}, bf16[64,3200]{1,0:T(8,128)(2,1)S(1)}, u32[]{:S(2)}, u32[]{:S(2)}) collective-permute-start(bf16[64,3200]{1,0:T(8,128)(2,1)S(1)} %collective-permute-done.4.a0), channel_id=1, source_target_pairs={{0,1},{1,2},{2,3},{3,0},{4,5},{5,6},{6,7},{7,4},{8,9},{9,10},{10,1... | collective-permute-start | bytes 1228808 | tf_op jit(solution)/shard_map/ppermute | solution.py:357
  72.5 13.9 %collective-permute-start.9 = (bf16[64,3200]{1,0:T(8,128)(2,1)S(1)}, bf16[64,3200]{1,0:T(8,128)(2,1)}, u32[]{:S(2)}, u32[]{:S(2)}) collective-permute-start(bf16[64,3200]{1,0:T(8,128)(2,1)S(1)} %collective-permute-done.5.b1), channel_id=1, source_target_pairs={{0,3},{1,0},{2,1},{3,2},{4,7},{5,4},{6,5},{7,6},{8,11},{9,8},{10,9... | collective-permute-start | bytes 1228808 | tf_op jit(solution)/shard_map/ppermute | solution.py:357
  77.2 7.9 %copy-start.7 = (bf16[64,3200]{1,0:T(8,128)(2,1)}, bf16[64,3200]{1,0:T(8,128)(2,1)S(1)}, u32[]{:S(2)}) copy-start(bf16[64,3200]{1,0:T(8,128)(2,1)S(1)} %collective-permute-done.6.a1) | copy-start | bytes 1228804
  78.1 7.0 %copy-start.8 = (bf16[64,3200]{1,0:T(8,128)(2,1)}, bf16[64,3200]{1,0:T(8,128)(2,1)S(1)}, u32[]{:S(2)}) copy-start(bf16[64,3200]{1,0:T(8,128)(2,1)S(1)} %collective-permute-done.7.b0) | copy-start | bytes 1228804
  85.1 0.7 copy-start.9
  107.7 42.1 %copy-start.1 = (bf16[4,512,128]{2,1,0:T(8,128)(2,1)}, bf16[4,512,128]{2,1,0:T(8,128)(2,1)S(1)}, u32[]{:S(2)}) copy-start(bf16[4,512,128]{2,1,0:T(8,128)(2,1)S(1)} %all_to_all.15.q_ref) | copy-start | bytes 1572868
  107.7 32.0 %all-to-all-start.1 = ((bf16[4,512,256]{2,1,0:T(8,128)(2,1)}), bf16[4,512,256]{2,1,0:T(8,128)(2,1)S(1)}, u32[]{:S(2)}, u32[]{:S(2)}) async-start(bf16[4,512,256]{2,1,0:T(8,128)(2,1)} %get-tuple-element.13), calls=%async_computation.1 | async-start | bytes 2097152 | tf_op jit(solution)/shard_map/all_to_all | solution.py:368
  149.8 21.9 %all-to-all-start.2 = ((bf16[4,576,128]{2,1,0:T(8,128)(2,1)}), bf16[4,576,128]{2,1,0:T(8,128)(2,1)S(1)}, u32[]{:S(2)}, u32[]{:S(2)}) async-start(bf16[4,576,128]{2,1,0:T(8,128)(2,1)} %peers.1), calls=%async_computation.2 | async-start | bytes 1179648 | tf_op jit(solution)/shard_map/all_to_all | solution.py:373
  161.7 1.0 copy-start.2
Sparse Core Ops, SparseCore 0:
  9.5 73.3 all-gather.1

commit v6 on v5

--- a/solution.py
+++ b/solution.py
@@ -55,8 +55,8 @@
 
 def project_kernel(
     slots, x0, a0, a1, b0, b1, c0, c1, text, w_hbm,
-    text_out, q_copies, kv_copies,
-    held, mod, extra, normed, w_ref, q_out, kv_out, sems, in_sems, w_sem,
+    q_out, kv_out, text_out,
+    held, mod, extra, normed, w_ref, kv, in_sems, w_sem, out_sems,
 ):
     rows = x0.shape[0]
     half = rows // 2
@@ -65,54 +65,76 @@
     arrived = [(x0, 0)]
     for slot, (low, high) in enumerate(((a0, a1), (b0, b1), (c0, c1))):
         arrived += [(low, (slot + 1) * rows), (high, (slot + 1) * rows + half)]
-    fetches = []
-    for i, (piece, at) in enumerate(arrived):
-        fetches.append(
-            pltpu.make_async_copy(piece, held.at[pl.ds(at, piece.shape[0]), :], in_sems.at[i])
-        )
-        fetches[-1].start()
+
+    def tail(i):
+        piece, at = arrived[i]
+        size = piece.shape[0]
+        return pltpu.make_async_copy(
+            piece.at[:, pl.ds(width, 128)], extra.at[pl.ds(at, size), :], in_sems.at[0, i]
+        )
+
+    def body(i):
+        piece, at = arrived[i]
+        size = piece.shape[0]
+        return pltpu.make_async_copy(
+            piece.at[:, pl.ds(0, width)], held.at[pl.ds(at, size), :], in_sems.at[1, i]
+        )
+
+    count = len(arrived)
+    for i in range(count):
+        tail(i).start()
+    for i in range(count):
+        body(i).start()
     fetch = pltpu.make_async_copy(w_hbm, w_ref, w_sem)
     fetch.start()
-    for copy in fetches:
-        copy.wait()
-    for slot in range(4):
-        extra[slot] = held[slot * rows : (slot + 1) * rows, width:].astype(F32)
+    for i in range(count):
+        tail(i).wait()
     for place in range(4):
+        base = pl.multiple_of(slots[place] * rows, rows)
+        terms = extra[pl.ds(base, rows), :].astype(F32)
         for far in range(4):
             for chunk in range(3):
                 at = (far * 4 + place) * 3 + chunk
                 kind, first = divmod(at * 128, width)
                 row = far * tile + chunk
                 mod[kind : kind + 1, first : first + 128] = (
-                    extra[slots[place], row : row + 1, :]
-                    + extra[slots[place], row + 3 : row + 4, :]
-                    + extra[slots[place], row + 6 : row + 7, :]
+                    terms[row : row + 1] + terms[row + 3 : row + 4] + terms[row + 6 : row + 7]
                 )
     shift = mod[0:1, :]
     gain = 1.0 + mod[1:2, :]
-    for block in range(5):
-        at = block * rows
-        count = rows if block < 4 else text.shape[0]
-        values = (held[at : at + rows, :width] if block < 4 else text[...]).astype(F32)
+
+    def norm(rows_in, at):
+        values = rows_in.astype(F32)
         center = jnp.sum(values, axis=1, keepdims=True) * (1.0 / width)
         centered = values - center
         spread = jnp.sum(centered * centered, axis=1, keepdims=True) * (1.0 / width)
         result = centered * lax.rsqrt(spread + 1e-06) * gain + shift
-        normed[at : at + count, :] = result.astype(BF)
-    fetch.wait()
-    out = jnp.dot(normed[...], w_ref[...], preferred_element_type=F32).astype(BF)
-    q_out[...] = out[: 4 * rows, :128]
-    kv_out[...] = out[: 4 * rows, 128:]
-    text_out[...] = out[4 * rows :, 128:]
-    copies = [
-        pltpu.make_async_copy(block, copies.at[i], sems.at[kind, i])
-        for kind, (block, copies) in enumerate(((q_out, q_copies), (kv_out, kv_copies)))
-        for i in range(4)
-    ]
-    for copy in copies:
-        copy.start()
-    for copy in copies:
-        copy.wait()
+        normed[at : at + rows_in.shape[0], :] = result.astype(BF)
+
+    sends = []
+    norm(text[...], 4 * rows)
+    for part in range(2):
+        first = 2 * rows * part
+        for i in range(count):
+            if first <= arrived[i][1] < first + 2 * rows:
+                body(i).wait()
+        for block in (2 * part, 2 * part + 1):
+            norm(held[block * rows : (block + 1) * rows, :], block * rows)
+        last = first + 2 * rows + (text.shape[0] if part else 0)
+        if part == 0:
+            fetch.wait()
+        out = jnp.dot(normed[first:last, :], w_ref[...], preferred_element_type=F32).astype(BF)
+        span = pl.ds(first, 2 * rows)
+        q_out[span, :] = out[: 2 * rows, :128]
+        kv[span, :] = out[: 2 * rows, 128:]
+        sends.append(
+            pltpu.make_async_copy(kv.at[span, :], kv_out.at[span, :], out_sems.at[part])
+        )
+        sends[-1].start()
+        if part:
+            text_out[...] = out[2 * rows :, 128:]
+    for send in sends:
+        send.wait()
 
 
 def project(slots, pieces, text, weight):
@@ -121,23 +143,22 @@
     return pl.pallas_call(
         project_kernel,
         out_shape=[
+            jax.ShapeDtypeStruct((4 * rows, 128), BF),
+            pltpu.MemorySpace.HBM((4 * rows, 256), BF),
             jax.ShapeDtypeStruct((text.shape[0], 256), BF),
-            pltpu.MemorySpace.HBM((4, 4 * rows, 128), BF),
-            pltpu.MemorySpace.HBM((4, 4 * rows, 256), BF),
         ],
         in_specs=[pl.BlockSpec(memory_space=pltpu.SMEM)] + [hbm()] * 7 + [vmem(), hbm()],
-        out_specs=[vmem()] + [hbm()] * 2,
+        out_specs=[vmem(), hbm(), vmem()],
         scratch_shapes=[
-            pltpu.VMEM((4 * rows, lanes), BF),
+            pltpu.VMEM((4 * rows, width), BF),
             pltpu.VMEM((2, width), F32),
-            pltpu.VMEM((4, rows, 128), F32),
+            pltpu.VMEM((4 * rows, 128), BF),
             pltpu.VMEM((4 * rows + text.shape[0], width), BF),
             pltpu.VMEM(weight.shape, BF),
-            pltpu.VMEM((4 * rows, 128), BF),
             pltpu.VMEM((4 * rows, 256), BF),
-            pltpu.SemaphoreType.DMA((2, 4)),
-            pltpu.SemaphoreType.DMA((7,)),
+            pltpu.SemaphoreType.DMA((2, 7)),
             pltpu.SemaphoreType.DMA,
+            pltpu.SemaphoreType.DMA((2,)),
         ],
         compiler_params=params(28),
         cost_estimate=pl.CostEstimate(
@@ -192,8 +213,8 @@
     return jnp.where(lane < HD, outs[0], outs[1]), jnp.where(lane < HD, sums[0], sums[1])
 
 
-def peers_kernel(info, q_ref, kv, text_kv, o_ref, keys, values, held, sems):
-    members, count = q_ref.shape[:2]
+def peers_kernel(info, q1, q2, q3, kv, text_kv, o_ref, keys, values, held, sems):
+    count = q1.shape[0]
     load_keys(kv, text_kv, keys, values)
     lane = lax.broadcasted_iota(jnp.int32, (128, 128), 1)
 
@@ -201,9 +222,8 @@
         member = jnp.bitwise_xor(info[3], step)
         return pltpu.make_async_copy(held.at[step], o_ref.at[member], sems.at[step])
 
-    @pl.loop(1, members)
-    def _(step):
-        out, lse = softmax_block(info, q_ref[jnp.bitwise_xor(info[3], step)], keys, values)
+    for step, q_ref in enumerate((q1, q2, q3), 1):
+        out, lse = softmax_block(info, q_ref[...], keys, values)
         held[step, :count, :] = out.astype(BF)
         for tile in range(count // 128):
             rest = lse[tile * 128 : (tile + 1) * 128]
@@ -218,13 +238,13 @@
             held[step, at : at + STAT_ROWS, :] = across.astype(BF)
         send(step).start()
 
-    for step in range(1, members):
+    for step in range(1, 4):
         send(step).wait()
 
 
 def own_kernel(info, q_ref, kv, text_kv, o_ref, keys, values, held, sems):
     load_keys(kv, text_kv, keys, values)
-    out, lse = softmax_block(info, q_ref[info[3]], keys, values)
+    out, lse = softmax_block(info, q_ref[...], keys, values)
     held[0] = out
     held[1] = lse
     copy = pltpu.make_async_copy(held, o_ref, sems.at[0])
@@ -232,13 +252,13 @@
     copy.wait()
 
 
-def attend(kernel, name, blocks, out_shape, info, q, kv, text_kv):
+def attend(kernel, name, out_shape, info, qs, kv, text_kv):
     keys = kv.shape[0] * kv.shape[1] + 128
-    count = q.shape[-2]
+    blocks, count = len(qs), qs[0].shape[0]
     return pl.pallas_call(
         kernel,
         out_shape=pltpu.MemorySpace.HBM(out_shape.shape, out_shape.dtype),
-        in_specs=[pl.BlockSpec(memory_space=pltpu.SMEM)] + [vmem()] * 3,
+        in_specs=[pl.BlockSpec(memory_space=pltpu.SMEM)] + [vmem()] * (blocks + 2),
         out_specs=hbm(),
         scratch_shapes=[
             pltpu.VMEM((keys, 128), BF),
@@ -249,24 +269,26 @@
         compiler_params=params(24),
         cost_estimate=pl.CostEstimate(
             flops=4 * blocks * count * keys * 256,
-            bytes_accessed=2 * (q.size + kv.size),
+            bytes_accessed=2 * (blocks * qs[0].size + kv.size),
             transcendentals=2 * blocks * count * keys,
         ),
         name=name,
-    )(info, q, kv, text_kv)
+    )(info, *qs, kv, text_kv)
 
 
 def combine_kernel(slots, info, parts_ref, own_hbm, out, grid, own, sem):
     copy = pltpu.make_async_copy(own_hbm, own, sem)
     copy.start()
-    copy.wait()
     o_ref, l_ref = own.at[0], own.at[1]
     members = parts_ref.shape[0]
     block = 128
     count = o_ref.shape[0]
-    lane = lax.broadcasted_iota(jnp.int32, (block, 128), 1)
+    term = lax.broadcasted_iota(jnp.int32, (STAT_ROWS, 128), 0)
+    head = lax.broadcasted_iota(jnp.int32, (STAT_ROWS, 128), 1) // HD
+    spread = jnp.where((term // 8 == head) & (term % 8 < 3), 1.0, 0.0).astype(BF)
     frames, tile_h, cells = out.shape[:3]
     tile_w = cells // 16
+    copy.wait()
     for place in range(4):
         slot = slots[place]
         rows = pl.ds(pl.multiple_of(slot * block, block), block)
@@ -275,16 +297,14 @@
         outs = [o_ref[rows, :]]
         for step in range(1, members):
             member = jnp.bitwise_xor(info[3], step)
-            across = parts_ref[member, at, :].astype(F32)
-            across = jnp.concatenate([across, jnp.zeros((128 - STAT_ROWS, 128), F32)], axis=0)
-            stats = jnp.transpose(across)
-            heads = [
-                stats[:, 8 * h : 8 * h + 1]
-                + stats[:, 8 * h + 1 : 8 * h + 2]
-                + stats[:, 8 * h + 2 : 8 * h + 3]
-                for h in range(2)
-            ]
-            lses.append(jnp.where(lane < HD, heads[0], heads[1]))
+            lses.append(
+                lax.dot_general(
+                    parts_ref[member, at, :],
+                    spread,
+                    (((0,), (0,)), ((), ())),
+                    preferred_element_type=F32,
+                )
+            )
             outs.append(parts_ref[member, rows, :].astype(F32))
         top = functools.reduce(jnp.maximum, lses)
         shares = [jnp.exp2(lse - top) for lse in lses]
@@ -324,9 +344,10 @@
     x_at = lax.axis_index("x")
     member = lax.axis_index("v") * 2 + zl_at
 
+    row_axes = ("u", "v", "zl")
+    padded = with_halo(latents, ((row_axes, 2), (("zh", "x"), 3)), 1)
     shard = qkv_weight.reshape(qkv_weight.shape[0], 3 * head_width)
-    weight = lax.all_gather(shard, ("item", "u", "v", "zl"), axis=0, tiled=True)
-    padded = with_halo(latents, ((("u", "v", "zl"), 2), (("zh", "x"), 3)), 1)
+    weight = lax.all_gather(shard, ("item",) + row_axes, axis=0, tiled=True)
     summed = latents.astype(F32)
     for row_tap in range(3):
         for col_tap in range(3):
@@ -362,17 +383,22 @@
     lower = member * TEXT_PART
     start = jnp.minimum(lower, prompt_rows.shape[1] - TEXT_PART)
     text_rows = lax.dynamic_slice_in_dim(prompt_rows[0], start, TEXT_PART, axis=0)
-    text_kv, q_copies, kv_copies = project(slots, pieces, text_rows, weight)
+    queries, kv, text_kv = project(slots, pieces, text_rows, weight)
     group = ("v", "zl")
-    qs = lax.all_to_all(q_copies, group, split_axis=0, concat_axis=0, tiled=True)
-    kv = lax.all_to_all(kv_copies, "u", split_axis=0, concat_axis=0, tiled=True)
+    swaps = (
+        ("zl", [(0, 1), (1, 0)]),
+        ("v", [(0, 1), (1, 0)]),
+        (group, [(0, 3), (3, 0), (1, 2), (2, 1)]),
+    )
+    qs = [lax.ppermute(queries, axis, swap) for axis, swap in swaps]
+    kv = lax.all_gather(kv, "u", axis=0)
     info = jnp.stack([start, lower, text_len[0], member])
-    count = qs.shape[1]
+    count = queries.shape[0]
     part = jax.ShapeDtypeStruct((4, count + count // 128 * STAT_ROWS, 128), BF)
-    parts = attend(peers_kernel, "peers", 3, part, info, qs, kv, text_kv)
+    parts = attend(peers_kernel, "peers", part, info, qs, kv, text_kv)
     parts = lax.all_to_all(parts, group, split_axis=0, concat_axis=0, tiled=True)
     plain = jax.ShapeDtypeStruct((2, count, 128), F32)
-    own = attend(own_kernel, "own", 1, plain, info, qs, kv, text_kv)
+    own = attend(own_kernel, "own", plain, info, [queries], kv, text_kv)
     shape = (frames, tile_h, 16 * tile_w, head_width)
     return combine(slots, info, parts, own, shape)[None]
 

time: 184 us -> 175 us (0.951)
  the two profiles are of different devices: /device:TPU:17 before, /device:TPU:6 now
where the time goes in v6:
time: 175 us; the launch traced here: 174 us
  waiting for transfers between devices  52.5 us (30%)
  starting transfers between devices  50.4 us (29%)
  blocking collectives  23.6 us (13%)
  Pallas kernels  23.5 us (13%)
  between operations  15 us (9%)
  local copies, waits for them, and re-layouts  6.45 us (4%)
  other arithmetic  2.63 us (2%)
    all_gather x1, blocking collectives, on_device(): tokens = lax.all_gather(peg, 'zh', axis=0, tiled=True)  23.6 us
    all_gather x1, waiting for transfers between devices, on_device(): kv = lax.all_gather(kv, 'u', axis=0)  20.6 us
    pallas_call x2, Pallas kernels, attend(): pl.pallas_call(kernel, out_shape=pltpu.MemorySpace.HBM(out_shape.shape, o...  14 us
    ppermute x3, starting transfers between devices, on_device(): qs = [lax.ppermute(queries, axis, swap) for axis, swap in swaps]  12.6 us
    ppermute x2, starting transfers between devices, with_halo(): lax.ppermute(lax.slice_in_dim(block, block.shape[dim] - width, None, axis...  10.9 us
    ppermute x2, waiting for transfers between devices, with_halo(): lax.ppermute(lax.slice_in_dim(block, 0, width, axis=dim), axis, backward)  9.67 us
    ppermute x2, waiting for transfers between devices, on_device(): c0, c1 = (lax.ppermute(a0, 'x', up), lax.ppermute(b1, 'x', down))  8.56 us
    ppermute x2, starting transfers between devices, on_device(): c0, c1 = (lax.ppermute(a0, 'x', up), lax.ppermute(b1, 'x', down))  7.3 us
  transfers between devices with their start and end apart: 16, of which 11 were waited for; matrix products, arithmetic and copies ran while one was open for 4% of the time, Pallas kernels for 2%

profile of v6, /device:TPU:6, one launch (start us, length us, event | category | flops | bytes accessed | tf_op | source)
XLA Modules:
  0.0 174.4 jit_solution(14394841322923488796)
XLA Ops:
  10.4 4.9 %collective-permute-start = (bf16[1,2,1,4,3072]{4,3,2,1,0:T(4,128)(2,1)S(1)}, bf16[1,2,1,4,3072]{4,3,2,1,0:T(4,128)(2,1)S(1)}, u32[]{:S(2)}, u32[]{:S(2)}) collective-permute-start(bf16[1,2,1,4,3072]{4,3,2,1,0:T(4,128)(2,1)S(1)} %get-tuple-element.20), channel_id=1, source_target_pairs={{0,16},{16,32},{32,48},{48,64},{64,80},{80,96},{96,112},{112,128},... | collective-permute-start | bytes 147464 | tf_op jit(solution)/shard_map/ppermute | solution.py:41
  18.9 6.0 %collective-permute-start.2 = (bf16[1,2,6,1,3072]{4,3,2,1,0:T(2,128)(2,1)S(1)}, bf16[1,2,6,1,3072]{4,3,2,1,0:T(2,128)(2,1)S(1)}, u32[]{:S(2)}, u32[]{:S(2)}) collective-permute-start(bf16[1,2,6,1,3072]{4,3,2,1,0:T(2,128)(2,1)S(1)} %get-tuple-element.17), channel_id=1, source_target_pairs={{0,1},{1,2},{2,3},{3,4},{4,5},{5,6},{6,7},{7,8},{8,9},{9,10},{10,1... | collective-permute-start | bytes 221192 | tf_op jit(solution)/shard_map/ppermute | solution.py:41
  24.9 1.9 %collective-permute-start.3 = (bf16[1,2,6,1,3072]{4,3,2,1,0:T(2,128)(2,1)S(1)}, bf16[1,2,6,1,3072]{4,3,2,1,0:T(2,128)(2,1)S(1)}, u32[]{:S(2)}, u32[]{:S(2)}) collective-permute-start(bf16[1,2,6,1,3072]{4,3,2,1,0:T(2,128)(2,1)S(1)} %get-tuple-element.18), channel_id=1, source_target_pairs={{1,0},{2,1},{3,2},{4,3},{5,4},{6,5},{7,6},{8,7},{9,8},{10,9},{11,1... | collective-permute-start | bytes 221192 | tf_op jit(solution)/shard_map/ppermute | solution.py:44
  27.8 9.7 %collective-permute-done.3 = bf16[1,2,6,1,3072]{4,3,2,1,0:T(2,128)(2,1)S(1)} collective-permute-done((bf16[1,2,6,1,3072]{4,3,2,1,0:T(2,128)(2,1)S(1)}, bf16[1,2,6,1,3072]{4,3,2,1,0:T(2,128)(2,1)S(1)}, u32[]{:S(2)}, u32[]{:S(2)}) %collective-permute-start.3) | collective-permute-done | bytes 73760 | tf_op jit(solution)/shard_map/ppermute | solution.py:44
  38.9 23.6 %all_gather.12.x0 = bf16[128,3200]{1,0:T(8,128)(2,1)S(1)} all-gather(bf16[32,3200]{1,0:T(8,128)(2,1)S(1)} %pad_maximum_fusion), channel_id=1, replica_groups=mesh['item'=2,'u'=4,'v'=2,'zl'=2,'zh'=4,'x'=4] {'zh'}, dimensions={0}, use_global_device_ids=true | all-gather | bytes 1024000 | tf_op jit(solution)/shard_map/all_gather | solution.py:370
  65.5 5.1 %collective-permute-start.4 = (bf16[64,3200]{1,0:T(8,128)(2,1)}, bf16[64,3200]{1,0:T(8,128)(2,1)}, u32[]{:S(2)}, u32[]{:S(2)}) collective-permute-start(bf16[64,3200]{1,0:T(8,128)(2,1)} %get-tuple-element.16), channel_id=1, source_target_pairs={{0,1},{1,2},{2,3},{3,0},{4,5},{5,6},{6,7},{7,4},{8,9},{9,10},{10,1... | collective-permute-start | bytes 1228808 | tf_op jit(solution)/shard_map/ppermute | solution.py:375
  70.7 3.2 %collective-permute-start.6 = (bf16[64,3200]{1,0:T(8,128)(2,1)}, bf16[64,3200]{1,0:T(8,128)(2,1)}, u32[]{:S(2)}, u32[]{:S(2)}) collective-permute-start(bf16[64,3200]{1,0:T(8,128)(2,1)} %get-tuple-element.15), channel_id=1, source_target_pairs={{0,1},{1,2},{2,3},{3,0},{4,5},{5,6},{6,7},{7,4},{8,9},{9,10},{10,1... | collective-permute-start | bytes 1228808 | tf_op jit(solution)/shard_map/ppermute | solution.py:376
  73.9 2.6 %collective-permute-start.7 = (bf16[64,3200]{1,0:T(8,128)(2,1)}, bf16[64,3200]{1,0:T(8,128)(2,1)}, u32[]{:S(2)}, u32[]{:S(2)}) collective-permute-start(bf16[64,3200]{1,0:T(8,128)(2,1)} %get-tuple-element.16), channel_id=1, source_target_pairs={{0,3},{1,0},{2,1},{3,2},{4,7},{5,4},{6,5},{7,6},{8,11},{9,8},{10,9... | collective-permute-start | bytes 1228808 | tf_op jit(solution)/shard_map/ppermute | solution.py:376
  77.2 3.0 %collective-permute-done.4.a0 = bf16[64,3200]{1,0:T(8,128)(2,1)} collective-permute-done((bf16[64,3200]{1,0:T(8,128)(2,1)}, bf16[64,3200]{1,0:T(8,128)(2,1)}, u32[]{:S(2)}, u32[]{:S(2)}) %collective-permute-start.4) | collective-permute-done | bytes 409632 | tf_op jit(solution)/shard_map/ppermute | solution.py:375
  80.2 5.4 %collective-permute-start.8 = (bf16[64,3200]{1,0:T(8,128)(2,1)}, bf16[64,3200]{1,0:T(8,128)(2,1)}, u32[]{:S(2)}, u32[]{:S(2)}) collective-permute-start(bf16[64,3200]{1,0:T(8,128)(2,1)} %collective-permute-done.4.a0), channel_id=1, source_target_pairs={{0,1},{1,2},{2,3},{3,0},{4,5},{5,6},{6,7},{7,4},{8,9},{9,10},{10,1... | collective-permute-start | bytes 1228808 | tf_op jit(solution)/shard_map/ppermute | solution.py:378
  85.5 1.9 %collective-permute-start.9 = (bf16[64,3200]{1,0:T(8,128)(2,1)S(1)}, bf16[64,3200]{1,0:T(8,128)(2,1)}, u32[]{:S(2)}, u32[]{:S(2)}) collective-permute-start(bf16[64,3200]{1,0:T(8,128)(2,1)S(1)} %collective-permute-done.5.b1), channel_id=1, source_target_pairs={{0,3},{1,0},{2,1},{3,2},{4,7},{5,4},{6,5},{7,6},{8,11},{9,8},{10,9... | collective-permute-start | bytes 1228808 | tf_op jit(solution)/shard_map/ppermute | solution.py:378
  88.1 3.2 %collective-permute-done.8.c0 = bf16[64,3200]{1,0:T(8,128)(2,1)} collective-permute-done((bf16[64,3200]{1,0:T(8,128)(2,1)}, bf16[64,3200]{1,0:T(8,128)(2,1)}, u32[]{:S(2)}, u32[]{:S(2)}) %collective-permute-start.8) | collective-permute-done | bytes 409632 | tf_op jit(solution)/shard_map/ppermute | solution.py:378
  91.3 5.4 %collective-permute-done.9.c1 = bf16[64,3200]{1,0:T(8,128)(2,1)} collective-permute-done((bf16[64,3200]{1,0:T(8,128)(2,1)S(1)}, bf16[64,3200]{1,0:T(8,128)(2,1)}, u32[]{:S(2)}, u32[]{:S(2)}) %collective-permute-start.9) | collective-permute-done | bytes 409632 | tf_op jit(solution)/shard_map/ppermute | solution.py:378
  96.7 6.8 %project.1 = (bf16[512,128]{1,0:T(8,128)(2,1)S(1)}, bf16[512,256]{1,0:T(8,128)(2,1)}, bf16[64,256]{1,0:T(8,128)(2,1)S(1)}) custom-call(s32[4]{0:T(128)S(1)} %compare_select_fusion.3.slots, bf16[128,3200]{1,0:T(8,128)(2,1)} %copy-done.3, bf16[64,3200]{1,0:T(8,128)(2,1)} %collective-permute-done.4.a0, bf16[64,3200]{1,0:T(8,128)(2,1)} %collective-permute-done.6.a1, ...), custom_call_target="tpu_custom_call" | custom-call | flops 1207959552 | bytes 5636096 | tf_op jit(solution)/shard_map/project/pallas_call | solution.py:143
  103.6 2.1 %collective-permute-start.12 = (bf16[512,128]{1,0:T(8,128)(2,1)S(1)}, bf16[512,128]{1,0:T(8,128)(2,1)S(1)}, u32[]{:S(2)}, u32[]{:S(2)}) collective-permute-start(bf16[512,128]{1,0:T(8,128)(2,1)S(1)} %get-tuple-element.12.q_ref), channel_id=1, source_target_pairs={{0,48},{48,0},{16,32},{32,16},{1,49},{49,1},{17,33},{33,17},{2,50}... | collective-permute-start | bytes 393224 | tf_op jit(solution)/shard_map/ppermute | solution.py:393
  105.7 8.4 %collective-permute-start.11 = (bf16[512,128]{1,0:T(8,128)(2,1)S(1)}, bf16[512,128]{1,0:T(8,128)(2,1)S(1)}, u32[]{:S(2)}, u32[]{:S(2)}) collective-permute-start(bf16[512,128]{1,0:T(8,128)(2,1)S(1)} %get-tuple-element.12.q_ref), channel_id=1, source_target_pairs={{0,32},{32,0},{1,33},{33,1},{2,34},{34,2},{3,35},{35,3},{4,36},{36... | collective-permute-start | bytes 393224 | tf_op jit(solution)/shard_map/ppermute | solution.py:393
  114.1 2.1 %collective-permute-start.10 = (bf16[512,128]{1,0:T(8,128)(2,1)S(1)}, bf16[512,128]{1,0:T(8,128)(2,1)S(1)}, u32[]{:S(2)}, u32[]{:S(2)}) collective-permute-start(bf16[512,128]{1,0:T(8,128)(2,1)S(1)} %get-tuple-element.12.q_ref), channel_id=1, source_target_pairs={{0,16},{16,0},{1,17},{17,1},{2,18},{18,2},{3,19},{19,3},{4,20},{20... | collective-permute-start | bytes 393224 | tf_op jit(solution)/shard_map/ppermute | solution.py:393
  117.0 3.9 %collective-permute-done.10.q1 = bf16[512,128]{1,0:T(8,128)(2,1)S(1)} collective-permute-done((bf16[512,128]{1,0:T(8,128)(2,1)S(1)}, bf16[512,128]{1,0:T(8,128)(2,1)S(1)}, u32[]{:S(2)}, u32[]{:S(2)}) %collective-permute-start.10) | collective-permute-done | bytes 131104 | tf_op jit(solution)/shard_map/ppermute | solution.py:393
  120.9 20.6 %all-gather.6.cloned.1.call-done = bf16[2048,256]{1,0:T(8,128)(2,1)} async-done(((bf16[512,256]{1,0:T(8,128)(2,1)}), bf16[2048,256]{1,0:T(8,128)(2,1)}) %all-gather.6.cloned.1.call-update) | async-done | bytes 1048592 | tf_op jit(solution)/shard_map/all_gather | solution.py:394
  142.7 9.6 %peers.1 = bf16[4,576,128]{2,1,0:T(8,128)(2,1)} custom-call(s32[4]{0:T(128)S(1)} %pad_add_fusion.info, bf16[512,128]{1,0:T(8,128)(2,1)S(1)} %collective-permute-done.10.q1, bf16[512,128]{1,0:T(8,128)(2,1)S(1)} %collective-permute-done.11.q2, bf16[512,128]{1,0:T(8,128)(2,1)S(1)} %collective-permute-done.12.q3, bf16[4,512,256]{2,1,0:T(8,128)(2,1)S(1)} %bitcast.34, ...), custom_call_target="tpu_custom_call" | custom-call | flops 3422552064 | bytes 1441792 | tf_op jit(solution)/shard_map/peers/pallas_call | solution.py:258
  152.4 3.5 %all-to-all-start = ((bf16[4,576,128]{2,1,0:T(8,128)(2,1)}), bf16[4,576,128]{2,1,0:T(8,128)(2,1)S(1)}, u32[]{:S(2)}, u32[]{:S(2)}) async-start(bf16[4,576,128]{2,1,0:T(8,128)(2,1)} %peers.1), calls=%async_computation | async-start | bytes 1179648 | tf_op jit(solution)/shard_map/all_to_all | solution.py:399
  155.9 4.3 %own.1.own_hbm = f32[2,512,128]{2,1,0:T(8,128)} custom-call(s32[4]{0:T(128)S(1)} %pad_add_fusion.info, bf16[512,128]{1,0:T(8,128)(2,1)S(1)} %get-tuple-element.12.q_ref, bf16[4,512,256]{2,1,0:T(8,128)(2,1)S(1)} %bitcast.35, bf16[64,256]{1,0:T(8,128)(2,1)S(1)} %get-tuple-element.14.text_kv), custom_call_target="tpu_custom_call" | custom-call | flops 1140850688 | bytes 1179648 | tf_op jit(solution)/shard_map/own/pallas_call | solution.py:258
  160.2 4.6 %all-to-all-done.parts_ref = bf16[4,576,128]{2,1,0:T(8,128)(2,1)S(1)} async-done(((bf16[4,576,128]{2,1,0:T(8,128)(2,1)}), bf16[4,576,128]{2,1,0:T(8,128)(2,1)S(1)}, u32[]{:S(2)}, u32[]{:S(2)}) %all-to-all-start) | async-done | bytes 589856 | tf_op jit(solution)/shard_map/all_to_all | solution.py:399
  164.8 2.7 %combine.1 = bf16[2,4,64,128]{3,2,1,0:T(8,128)(2,1)} custom-call(s32[4]{0:T(128)S(1)} %compare_select_fusion.3.slots, s32[4]{0:T(128)S(1)} %pad_add_fusion.info, bf16[4,576,128]{2,1,0:T(8,128)(2,1)S(1)} %all-to-all-done.parts_ref, f32[2,512,128]{2,1,0:T(8,128)} %own.1.own_hbm), custom_call_target="tpu_custom_call" | custom-call | tf_op jit(solution)/shard_map/combine/pallas_call | solution.py:325
  (48 shorter events, 14.8 us)
Async XLA Ops:
  6.5 81.0 %copy-start = (bf16[1,226,3072]{2,1,0:T(8,128)(2,1)S(1)}, bf16[1,226,3072]{2,1,0:T(8,128)(2,1)}, u32[]{:S(2)}) copy-start(bf16[1,226,3072]{2,1,0:T(8,128)(2,1)} %param.8) | copy-start | bytes 4165636
  6.5 12.0 %copy-start.4 = (bf16[1,2,4,4,3072]{4,3,2,1,0:T(4,128)(2,1)S(1)}, bf16[1,2,4,4,3072]{4,3,2,1,0:T(4,128)(2,1)}, u32[]{:S(2)}) copy-start(bf16[1,2,4,4,3072]{4,3,2,1,0:T(4,128)(2,1)} %param.7) | copy-start | bytes 589828
  6.5 90.2 %all-gather.4.cloned.1.call-start = ((), (), s32[]{:S(2)}) async-start(), calls=%async_computation.1 | async-start | bytes 2433024 | tf_op jit(solution)/shard_map/all_gather | solution.py:350
  8.2 133.3 %all-gather.6.cloned.1.call-start = ((), (), s32[]{:S(2)}) async-start(), calls=%async_computation.2 | async-start | bytes 1310720 | tf_op jit(solution)/shard_map/all_gather | solution.py:394
  9.1 9.5 %collective-permute-start.1 = (bf16[1,2,1,4,3072]{4,3,2,1,0:T(4,128)(2,1)S(1)}, bf16[1,2,1,4,3072]{4,3,2,1,0:T(4,128)(2,1)S(1)}, u32[]{:S(2)}, u32[]{:S(2)}) collective-permute-start(bf16[1,2,1,4,3072]{4,3,2,1,0:T(4,128)(2,1)S(1)} %get-tuple-element.19), channel_id=1, source_target_pairs={{16,0},{32,16},{48,32},{64,48},{80,64},{96,80},{112,96},{128,112},... | collective-permute-start | bytes 147464 | tf_op jit(solution)/shard_map/ppermute | solution.py:44
  10.4 8.1 %collective-permute-start = (bf16[1,2,1,4,3072]{4,3,2,1,0:T(4,128)(2,1)S(1)}, bf16[1,2,1,4,3072]{4,3,2,1,0:T(4,128)(2,1)S(1)}, u32[]{:S(2)}, u32[]{:S(2)}) collective-permute-start(bf16[1,2,1,4,3072]{4,3,2,1,0:T(4,128)(2,1)S(1)} %get-tuple-element.20), channel_id=1, source_target_pairs={{0,16},{16,32},{32,48},{48,64},{64,80},{80,96},{96,112},{112,128},... | collective-permute-start | bytes 147464 | tf_op jit(solution)/shard_map/ppermute | solution.py:41
  18.9 8.9 %collective-permute-start.2 = (bf16[1,2,6,1,3072]{4,3,2,1,0:T(2,128)(2,1)S(1)}, bf16[1,2,6,1,3072]{4,3,2,1,0:T(2,128)(2,1)S(1)}, u32[]{:S(2)}, u32[]{:S(2)}) collective-permute-start(bf16[1,2,6,1,3072]{4,3,2,1,0:T(2,128)(2,1)S(1)} %get-tuple-element.17), channel_id=1, source_target_pairs={{0,1},{1,2},{2,3},{3,4},{4,5},{5,6},{6,7},{7,8},{8,9},{9,10},{10,1... | collective-permute-start | bytes 221192 | tf_op jit(solution)/shard_map/ppermute | solution.py:41
  24.9 12.5 %collective-permute-start.3 = (bf16[1,2,6,1,3072]{4,3,2,1,0:T(2,128)(2,1)S(1)}, bf16[1,2,6,1,3072]{4,3,2,1,0:T(2,128)(2,1)S(1)}, u32[]{:S(2)}, u32[]{:S(2)}) collective-permute-start(bf16[1,2,6,1,3072]{4,3,2,1,0:T(2,128)(2,1)S(1)} %get-tuple-element.18), channel_id=1, source_target_pairs={{1,0},{2,1},{3,2},{4,3},{5,4},{6,5},{7,6},{8,7},{9,8},{10,9},{11,1... | collective-permute-start | bytes 221192 | tf_op jit(solution)/shard_map/ppermute | solution.py:44
  62.6 34.1 %copy-start.3 = (bf16[128,3200]{1,0:T(8,128)(2,1)}, bf16[128,3200]{1,0:T(8,128)(2,1)S(1)}, u32[]{:S(2)}) copy-start(bf16[128,3200]{1,0:T(8,128)(2,1)S(1)} %all_gather.12.x0) | copy-start | bytes 2457604
  63.6 13.6 %collective-permute-start.5 = (bf16[64,3200]{1,0:T(8,128)(2,1)}, bf16[64,3200]{1,0:T(8,128)(2,1)S(1)}, u32[]{:S(2)}, u32[]{:S(2)}) collective-permute-start(bf16[64,3200]{1,0:T(8,128)(2,1)} %get-tuple-element.15), channel_id=1, source_target_pairs={{0,3},{1,0},{2,1},{3,2},{4,7},{5,4},{6,5},{7,6},{8,11},{9,8},{10,9... | collective-permute-start | bytes 1228808 | tf_op jit(solution)/shard_map/ppermute | solution.py:375
  65.5 14.6 %collective-permute-start.4 = (bf16[64,3200]{1,0:T(8,128)(2,1)}, bf16[64,3200]{1,0:T(8,128)(2,1)}, u32[]{:S(2)}, u32[]{:S(2)}) collective-permute-start(bf16[64,3200]{1,0:T(8,128)(2,1)} %get-tuple-element.16), channel_id=1, source_target_pairs={{0,1},{1,2},{2,3},{3,0},{4,5},{5,6},{6,7},{7,4},{8,9},{9,10},{10,1... | collective-permute-start | bytes 1228808 | tf_op jit(solution)/shard_map/ppermute | solution.py:375
  70.7 16.9 %collective-permute-start.6 = (bf16[64,3200]{1,0:T(8,128)(2,1)}, bf16[64,3200]{1,0:T(8,128)(2,1)}, u32[]{:S(2)}, u32[]{:S(2)}) collective-permute-start(bf16[64,3200]{1,0:T(8,128)(2,1)} %get-tuple-element.15), channel_id=1, source_target_pairs={{0,1},{1,2},{2,3},{3,0},{4,5},{5,6},{6,7},{7,4},{8,9},{9,10},{10,1... | collective-permute-start | bytes 1228808 | tf_op jit(solution)/shard_map/ppermute | solution.py:376
  73.9 14.2 %collective-permute-start.7 = (bf16[64,3200]{1,0:T(8,128)(2,1)}, bf16[64,3200]{1,0:T(8,128)(2,1)}, u32[]{:S(2)}, u32[]{:S(2)}) collective-permute-start(bf16[64,3200]{1,0:T(8,128)(2,1)} %get-tuple-element.16), channel_id=1, source_target_pairs={{0,3},{1,0},{2,1},{3,2},{4,7},{5,4},{6,5},{7,6},{8,11},{9,8},{10,9... | collective-permute-start | bytes 1228808 | tf_op jit(solution)/shard_map/ppermute | solution.py:376
  77.2 19.5 %copy-start.5 = (bf16[64,3200]{1,0:T(8,128)(2,1)}, bf16[64,3200]{1,0:T(8,128)(2,1)S(1)}, u32[]{:S(2)}) copy-start(bf16[64,3200]{1,0:T(8,128)(2,1)S(1)} %collective-permute-done.5.b1) | copy-start | bytes 1228804
  80.2 11.2 %collective-permute-start.8 = (bf16[64,3200]{1,0:T(8,128)(2,1)}, bf16[64,3200]{1,0:T(8,128)(2,1)}, u32[]{:S(2)}, u32[]{:S(2)}) collective-permute-start(bf16[64,3200]{1,0:T(8,128)(2,1)} %collective-permute-done.4.a0), channel_id=1, source_target_pairs={{0,1},{1,2},{2,3},{3,0},{4,5},{5,6},{6,7},{7,4},{8,9},{9,10},{10,1... | collective-permute-start | bytes 1228808 | tf_op jit(solution)/shard_map/ppermute | solution.py:378
  85.5 11.2 %collective-permute-start.9 = (bf16[64,3200]{1,0:T(8,128)(2,1)S(1)}, bf16[64,3200]{1,0:T(8,128)(2,1)}, u32[]{:S(2)}, u32[]{:S(2)}) collective-permute-start(bf16[64,3200]{1,0:T(8,128)(2,1)S(1)} %collective-permute-done.5.b1), channel_id=1, source_target_pairs={{0,3},{1,0},{2,1},{3,2},{4,7},{5,4},{6,5},{7,6},{8,11},{9,8},{10,9... | collective-permute-start | bytes 1228808 | tf_op jit(solution)/shard_map/ppermute | solution.py:378
  103.6 13.3 %collective-permute-start.12 = (bf16[512,128]{1,0:T(8,128)(2,1)S(1)}, bf16[512,128]{1,0:T(8,128)(2,1)S(1)}, u32[]{:S(2)}, u32[]{:S(2)}) collective-permute-start(bf16[512,128]{1,0:T(8,128)(2,1)S(1)} %get-tuple-element.12.q_ref), channel_id=1, source_target_pairs={{0,48},{48,0},{16,32},{32,16},{1,49},{49,1},{17,33},{33,17},{2,50}... | collective-permute-start | bytes 393224 | tf_op jit(solution)/shard_map/ppermute | solution.py:393
  105.7 11.3 %collective-permute-start.11 = (bf16[512,128]{1,0:T(8,128)(2,1)S(1)}, bf16[512,128]{1,0:T(8,128)(2,1)S(1)}, u32[]{:S(2)}, u32[]{:S(2)}) collective-permute-start(bf16[512,128]{1,0:T(8,128)(2,1)S(1)} %get-tuple-element.12.q_ref), channel_id=1, source_target_pairs={{0,32},{32,0},{1,33},{33,1},{2,34},{34,2},{3,35},{35,3},{4,36},{36... | collective-permute-start | bytes 393224 | tf_op jit(solution)/shard_map/ppermute | solution.py:393
  114.1 6.9 %collective-permute-start.10 = (bf16[512,128]{1,0:T(8,128)(2,1)S(1)}, bf16[512,128]{1,0:T(8,128)(2,1)S(1)}, u32[]{:S(2)}, u32[]{:S(2)}) collective-permute-start(bf16[512,128]{1,0:T(8,128)(2,1)S(1)} %get-tuple-element.12.q_ref), channel_id=1, source_target_pairs={{0,16},{16,0},{1,17},{17,1},{2,18},{18,2},{3,19},{19,3},{4,20},{20... | collective-permute-start | bytes 393224 | tf_op jit(solution)/shard_map/ppermute | solution.py:393
  141.5 1.2 copy-start.1
  142.7 13.1 %copy-start.2 = (bf16[2048,256]{1,0:T(8,128)(2,1)S(1)}, bf16[2048,256]{1,0:T(8,128)(2,1)}, u32[]{:S(2)}) copy-start(bf16[2048,256]{1,0:T(8,128)(2,1)} %all-gather.6.cloned.1.call-done) | copy-start | bytes 3145732
  152.4 12.5 %all-to-all-start = ((bf16[4,576,128]{2,1,0:T(8,128)(2,1)}), bf16[4,576,128]{2,1,0:T(8,128)(2,1)S(1)}, u32[]{:S(2)}, u32[]{:S(2)}) async-start(bf16[4,576,128]{2,1,0:T(8,128)(2,1)} %peers.1), calls=%async_computation | async-start | bytes 1179648 | tf_op jit(solution)/shard_map/all_to_all | solution.py:399
Sparse Core Ops, SparseCore 0:
  9.5 73.4 all-gather.3
  103.7 37.7 all-gather.5

commit v7 on v6

--- a/solution.py
+++ b/solution.py
@@ -170,24 +170,25 @@
     )(slots, *map(keep, pieces), text, keep(weight))
 
 
-def load_keys(kv, text_kv, keys, values):
-    blocks, size = kv.shape[:2]
-    for block in range(blocks):
-        rows = pl.ds(block * size, size)
-        keys[rows, :] = kv[block, :, :128]
-        values[rows, :128] = kv[block, :, 128:]
-    at = blocks * size
-    pad = 128 - TEXT_PART
-    keys[at : at + TEXT_PART, :] = text_kv[:, :128]
-    keys[at + TEXT_PART :, :] = jnp.zeros((pad, 128), BF)
-    values[at : at + TEXT_PART, :128] = text_kv[:, 128:]
-    values[at + TEXT_PART :, :128] = jnp.zeros((pad, 128), BF)
+def load_keys(blocks, text_kv, keys, values):
+    at = 0
+    for block in blocks:
+        size = block.shape[0]
+        keys[at : at + size, :] = block[:, :128]
+        values[at : at + size, :128] = block[:, 128:]
+        at += size
+    if text_kv is not None:
+        pad = 128 - TEXT_PART
+        keys[at : at + TEXT_PART, :] = text_kv[:, :128]
+        keys[at + TEXT_PART :, :] = jnp.zeros((pad, 128), BF)
+        values[at : at + TEXT_PART, :128] = text_kv[:, 128:]
+        values[at + TEXT_PART :, :128] = jnp.zeros((pad, 128), BF)
     values[:, 128:] = jnp.ones((values.shape[0], 128), BF)
 
 
-def softmax_block(info, q, keys, values):
+def softmax_block(info, q, keys, values, has_text):
     rows = q.shape[0]
-    latent = keys.shape[0] - 128
+    latent = keys.shape[0] - (128 if has_text else 0)
     lane = lax.broadcasted_iota(jnp.int32, (rows, 128), 1)
     position = info[0] + lane
     valid = (position >= info[1]) & (position < info[2]) & (lane < TEXT_PART)
@@ -198,14 +199,15 @@
         s = lax.dot_general(
             own, keys[...], (((1,), (1,)), ((), ())), preferred_element_type=F32
         )
-        text = jnp.where(valid, s[:, latent:], -1e30)
-        top = jnp.maximum(
-            jnp.max(s[:, :latent], axis=1, keepdims=True), jnp.max(text, axis=1, keepdims=True)
-        )
+        top = jnp.max(s[:, :latent], axis=1, keepdims=True)
+        if has_text:
+            text = jnp.where(valid, s[:, latent:], -1e30)
+            top = jnp.maximum(top, jnp.max(text, axis=1, keepdims=True))
         top = top * SCALE2
         p = jnp.exp2(s[:, :latent] * SCALE2 - top).astype(BF)
-        p_text = jnp.where(valid, jnp.exp2(text * SCALE2 - top), 0.0).astype(BF)
-        p = jnp.concatenate([p, p_text], axis=1)
+        if has_text:
+            p_text = jnp.where(valid, jnp.exp2(text * SCALE2 - top), 0.0).astype(BF)
+            p = jnp.concatenate([p, p_text], axis=1)
         acc = jnp.dot(p, values[...], preferred_element_type=F32)
         total = acc[:, 128:]
         outs.append(acc[:, :128] / total)
@@ -213,18 +215,38 @@
     return jnp.where(lane < HD, outs[0], outs[1]), jnp.where(lane < HD, sums[0], sums[1])
 
 
-def peers_kernel(info, q1, q2, q3, kv, text_kv, o_ref, keys, values, held, sems):
+def first_kernel(info, q1, q2, q3, kv0, kv1, kv2, text_kv, o_ref, keys, values, held, sems):
+    load_keys((kv0, kv1, kv2), text_kv, keys, values)
+    sends = []
+    for i, q_ref in enumerate((q1, q2, q3)):
+        held[i, 0], held[i, 1] = softmax_block(info, q_ref[...], keys, values, True)
+        sends.append(pltpu.make_async_copy(held.at[i], o_ref.at[i], sems.at[i]))
+        sends[-1].start()
+    for send in sends:
+        send.wait()
+
+
+def rest_kernel(
+    info, q1, q2, q3, kv3, kv4, before_hbm, o_ref, keys, values, held, before, sems, in_sems
+):
+    fetches = [
+        pltpu.make_async_copy(before_hbm.at[i], before.at[i], in_sems.at[i]) for i in range(3)
+    ]
+    for fetch in fetches:
+        fetch.start()
     count = q1.shape[0]
-    load_keys(kv, text_kv, keys, values)
+    load_keys((kv3, kv4), None, keys, values)
     lane = lax.broadcasted_iota(jnp.int32, (128, 128), 1)
-
-    def send(step):
-        member = jnp.bitwise_xor(info[3], step)
-        return pltpu.make_async_copy(held.at[step], o_ref.at[member], sems.at[step])
-
-    for step, q_ref in enumerate((q1, q2, q3), 1):
-        out, lse = softmax_block(info, q_ref[...], keys, values)
-        held[step, :count, :] = out.astype(BF)
+    sends = []
+    for i, q_ref in enumerate((q1, q2, q3)):
+        out, lse = softmax_block(info, q_ref[...], keys, values, False)
+        fetches[i].wait()
+        earlier = before[i, 1]
+        top = jnp.maximum(lse, earlier)
+        new, old = jnp.exp2(lse - top), jnp.exp2(earlier - top)
+        total = new + old
+        held[i, :count, :] = ((new * out + old * before[i, 0]) / total).astype(BF)
+        lse = top + jnp.log(total) * LOG2E
         for tile in range(count // 128):
             rest = lse[tile * 128 : (tile + 1) * 128]
             stats = jnp.zeros((128, 128), F32)
@@ -235,45 +257,52 @@
             across = jnp.transpose(stats)
             across = jnp.concatenate([across[:8], across[HD : HD + 8]], axis=0)
             at = count + tile * STAT_ROWS
-            held[step, at : at + STAT_ROWS, :] = across.astype(BF)
-        send(step).start()
-
-    for step in range(1, 4):
-        send(step).wait()
-
-
-def own_kernel(info, q_ref, kv, text_kv, o_ref, keys, values, held, sems):
-    load_keys(kv, text_kv, keys, values)
-    out, lse = softmax_block(info, q_ref[...], keys, values)
-    held[0] = out
-    held[1] = lse
+            held[i, at : at + STAT_ROWS, :] = across.astype(BF)
+        member = jnp.bitwise_xor(info[3], i + 1)
+        sends.append(pltpu.make_async_copy(held.at[i], o_ref.at[member], sems.at[i]))
+        sends[-1].start()
+    for send in sends:
+        send.wait()
+
+
+def own_kernel(info, q_ref, kv0, kv1, kv2, kv3, kv4, text_kv, o_ref, keys, values, held, sems):
+    load_keys((kv0, kv1, kv2, kv3, kv4), text_kv, keys, values)
+    held[0], held[1] = softmax_block(info, q_ref[...], keys, values, True)
     copy = pltpu.make_async_copy(held, o_ref, sems.at[0])
     copy.start()
     copy.wait()
 
 
-def attend(kernel, name, out_shape, info, qs, kv, text_kv):
-    keys = kv.shape[0] * kv.shape[1] + 128
-    blocks, count = len(qs), qs[0].shape[0]
+def attend(kernel, name, out_shape, held, info, qs, blocks, text_kv=None, before=None):
+    keys = sum(block.shape[0] for block in blocks) + (0 if text_kv is None else 128)
+    count = qs[0].shape[0]
+    operands = [*qs, *blocks] + ([] if text_kv is None else [text_kv])
+    specs = [pl.BlockSpec(memory_space=pltpu.SMEM)] + [vmem()] * len(operands)
+    scratch = [
+        pltpu.VMEM((keys, 128), BF),
+        pltpu.VMEM((keys, 256), BF),
+        pltpu.VMEM(held, out_shape.dtype),
+    ]
+    sems = [pltpu.SemaphoreType.DMA((3,))]
+    if before is not None:
+        operands.append(keep(before))
+        specs.append(hbm())
+        scratch.append(pltpu.VMEM(before.shape, before.dtype))
+        sems = sems * 2
     return pl.pallas_call(
         kernel,
         out_shape=pltpu.MemorySpace.HBM(out_shape.shape, out_shape.dtype),
-        in_specs=[pl.BlockSpec(memory_space=pltpu.SMEM)] + [vmem()] * (blocks + 2),
+        in_specs=specs,
         out_specs=hbm(),
-        scratch_shapes=[
-            pltpu.VMEM((keys, 128), BF),
-            pltpu.VMEM((keys, 256), BF),
-            pltpu.VMEM(out_shape.shape, out_shape.dtype),
-            pltpu.SemaphoreType.DMA((4,)),
-        ],
+        scratch_shapes=scratch + sems,
         compiler_params=params(24),
         cost_estimate=pl.CostEstimate(
-            flops=4 * blocks * count * keys * 256,
-            bytes_accessed=2 * (blocks * qs[0].size + kv.size),
-            transcendentals=2 * blocks * count * keys,
+            flops=4 * len(qs) * count * keys * 256,
+            bytes_accessed=512 * (len(qs) * count + keys),
+            transcendentals=2 * len(qs) * count * keys,
         ),
         name=name,
-    )(info, *qs, kv, text_kv)
+    )(info, *operands)
 
 
 def combine_kernel(slots, info, parts_ref, own_hbm, out, grid, own, sem):
@@ -345,7 +374,11 @@
     member = lax.axis_index("v") * 2 + zl_at
 
     row_axes = ("u", "v", "zl")
-    padded = with_halo(latents, ((row_axes, 2), (("zh", "x"), 3)), 1)
+    padded = with_halo(latents, ((row_axes, 2),), 1)
+    padded, peg_weight, modulation_weight = lax.optimization_barrier(
+        (padded, peg_weight, modulation_weight)
+    )
+    padded = with_halo(padded, ((("zh", "x"), 3),), 1)
     shard = qkv_weight.reshape(qkv_weight.shape[0], 3 * head_width)
     weight = lax.all_gather(shard, ("item",) + row_axes, axis=0, tiled=True)
     summed = latents.astype(F32)
@@ -391,14 +424,24 @@
         (group, [(0, 3), (3, 0), (1, 2), (2, 1)]),
     )
     qs = [lax.ppermute(queries, axis, swap) for axis, swap in swaps]
-    kv = lax.all_gather(kv, "u", axis=0)
+    near = [lax.ppermute(kv, "u", up), lax.ppermute(kv, "u", down)]
+    near = lax.optimization_barrier(near)
+    count = kv.shape[0]
+    far = [
+        lax.ppermute(near[0][: count // 2], "u", up),
+        lax.ppermute(near[1][count // 2 :], "u", down),
+    ]
     info = jnp.stack([start, lower, text_len[0], member])
-    count = queries.shape[0]
-    part = jax.ShapeDtypeStruct((4, count + count // 128 * STAT_ROWS, 128), BF)
-    parts = attend(peers_kernel, "peers", part, info, qs, kv, text_kv)
+    shape = (3, 2, count, 128)
+    first = jax.ShapeDtypeStruct(shape, F32)
+    first = attend(first_kernel, "first", first, shape, info, qs, [kv, *near], text_kv)
+    shape = (4, count + count // 128 * STAT_ROWS, 128)
+    parts = jax.ShapeDtypeStruct(shape, BF)
+    parts = attend(rest_kernel, "rest", parts, (3,) + shape[1:], info, qs, far, None, first)
     parts = lax.all_to_all(parts, group, split_axis=0, concat_axis=0, tiled=True)
-    plain = jax.ShapeDtypeStruct((2, count, 128), F32)
-    own = attend(own_kernel, "own", plain, info, [queries], kv, text_kv)
+    shape = (2, count, 128)
+    own = jax.ShapeDtypeStruct(shape, F32)
+    own = attend(own_kernel, "own", own, shape, info, [queries], [kv, *near, *far], text_kv)
     shape = (frames, tile_h, 16 * tile_w, head_width)
     return combine(slots, info, parts, own, shape)[None]
 

time: 175 us -> 170 us (0.971)
  waiting for transfers between devices: 52.5 us -> 28.7 us
  starting transfers between devices: 50.4 us -> 65.1 us
  Pallas kernels: 23.5 us -> 27.5 us
    all_gather x1 -> x0, waiting for transfers between devices: 20.6 us -> none  [on_device(): kv = lax.all_gather(kv, 'u', axis=0)]
    ppermute x0 -> x4, starting transfers between devices: none -> 15.7 us  [the longest x2 8.09 us: on_device(): near = [lax.ppermute(kv, 'u', up), lax.ppermute(kv, 'u', down)]]
    ppermute x3, waiting for transfers between devices: 4.03 us -> 0.01 us  [on_device(): qs = [lax.ppermute(queries, axis, swap) for axis, swap in swaps]]
    pallas_call x2 -> x3, Pallas kernels: 14 us -> 17.9 us  [attend(): pl.pallas_call(kernel, out_shape=pltpu.MemorySpace.HBM(out_shape.shape, o...]
    ppermute x2, waiting for transfers between devices: 9.67 us -> 11.9 us  [with_halo(): lax.ppermute(lax.slice_in_dim(block, 0, width, axis=dim), axis, backward)]
    all_to_all x1, waiting for transfers between devices: 4.64 us -> 2.64 us  [on_device(): lax.all_to_all(parts, group, split_axis=0, concat_axis=0, tiled=True)]
  transfers between devices with their start and end apart: 16 -> 19, of which waited for: 11 -> 9; matrix products, arithmetic and copies ran while one was open for 4% -> 3% of each run, Pallas kernels for 2% -> 7%
where the time goes in v7:
time: 170 us; the launch traced here: 169 us
  starting transfers between devices  65.1 us (38%)
  waiting for transfers between devices  28.7 us (17%)
  Pallas kernels  27.5 us (16%)
  blocking collectives  22.5 us (13%)
  between operations  15.1 us (9%)
  local copies, waits for them, and re-layouts  6.71 us (4%)
  other arithmetic  2.82 us (2%)
    all_gather x1, blocking collectives, on_device(): tokens = lax.all_gather(peg, 'zh', axis=0, tiled=True)  22.5 us
    pallas_call x3, Pallas kernels, attend(): pl.pallas_call(kernel, out_shape=pltpu.MemorySpace.HBM(out_shape.shape, o...  17.9 us
    ppermute x2, waiting for transfers between devices, with_halo(): lax.ppermute(lax.slice_in_dim(block, 0, width, axis=dim), axis, backward)  11.9 us
    ppermute x3, starting transfers between devices, on_device(): qs = [lax.ppermute(queries, axis, swap) for axis, swap in swaps]  11.1 us
    ppermute x2, starting transfers between devices, with_halo(): lax.ppermute(lax.slice_in_dim(block, block.shape[dim] - width, None, axis...  10.3 us
    ppermute x2, starting transfers between devices, on_device(): near = [lax.ppermute(kv, 'u', up), lax.ppermute(kv, 'u', down)]  8.09 us
    ppermute x2, waiting for transfers between devices, on_device(): c0, c1 = (lax.ppermute(a0, 'x', up), lax.ppermute(b1, 'x', down))  7.91 us
    ppermute x2, starting transfers between devices, on_device(): c0, c1 = (lax.ppermute(a0, 'x', up), lax.ppermute(b1, 'x', down))  7.4 us
  transfers between devices with their start and end apart: 19, of which 9 were waited for; matrix products, arithmetic and copies ran while one was open for 3% of the time, Pallas kernels for 7%

profile of v7, /device:TPU:6, one launch (start us, length us, event | category | flops | bytes accessed | tf_op | source)
XLA Modules:
  0.0 168.6 jit_solution(3625290459286717597)
XLA Ops:
  9.1 4.3 %collective-permute-start = (bf16[1,2,1,4,3072]{4,3,2,1,0:T(4,128)(2,1)S(1)}, bf16[1,2,1,4,3072]{4,3,2,1,0:T(4,128)(2,1)S(1)}, u32[]{:S(2)}, u32[]{:S(2)}) collective-permute-start(bf16[1,2,1,4,3072]{4,3,2,1,0:T(4,128)(2,1)S(1)} %get-tuple-element.29), channel_id=1, source_target_pairs={{0,16},{16,32},{32,48},{48,64},{64,80},{80,96},{96,112},{112,128},... | collective-permute-start | bytes 147464 | tf_op jit(solution)/shard_map/ppermute | solution.py:41
  15.5 3.9 %collective-permute-done.1 = bf16[1,2,1,4,3072]{4,3,2,1,0:T(4,128)(2,1)S(1)} collective-permute-done((bf16[1,2,1,4,3072]{4,3,2,1,0:T(4,128)(2,1)S(1)}, bf16[1,2,1,4,3072]{4,3,2,1,0:T(4,128)(2,1)S(1)}, u32[]{:S(2)}, u32[]{:S(2)}) %collective-permute-start.1) | collective-permute-done | bytes 49184 | tf_op jit(solution)/shard_map/ppermute | solution.py:44
  20.8 6.0 %collective-permute-start.2 = (bf16[1,2,6,1,3072]{4,3,2,1,0:T(2,128)(2,1)S(1)}, bf16[1,2,6,1,3072]{4,3,2,1,0:T(2,128)(2,1)S(1)}, u32[]{:S(2)}, u32[]{:S(2)}) collective-permute-start(bf16[1,2,6,1,3072]{4,3,2,1,0:T(2,128)(2,1)S(1)} %get-tuple-element.27), channel_id=1, source_target_pairs={{0,1},{1,2},{2,3},{3,4},{4,5},{5,6},{6,7},{7,8},{8,9},{9,10},{10,1... | collective-permute-start | bytes 221192 | tf_op jit(solution)/shard_map/ppermute | solution.py:41
  30.2 8.0 %collective-permute-done.3 = bf16[1,2,6,1,3072]{4,3,2,1,0:T(2,128)(2,1)S(1)} collective-permute-done((bf16[1,2,6,1,3072]{4,3,2,1,0:T(2,128)(2,1)S(1)}, bf16[1,2,6,1,3072]{4,3,2,1,0:T(2,128)(2,1)S(1)}, u32[]{:S(2)}, u32[]{:S(2)}) %collective-permute-start.3) | collective-permute-done | bytes 73760 | tf_op jit(solution)/shard_map/ppermute | solution.py:44
  39.6 22.5 %all_gather.6.x0 = bf16[128,3200]{1,0:T(8,128)(2,1)S(1)} all-gather(bf16[32,3200]{1,0:T(8,128)(2,1)S(1)} %pad_maximum_fusion.1), channel_id=1, replica_groups=mesh['item'=2,'u'=4,'v'=2,'zl'=2,'zh'=4,'x'=4] {'zh'}, dimensions={0}, use_global_device_ids=true | all-gather | bytes 1024000 | tf_op jit(solution)/shard_map/all_gather | solution.py:403
  65.9 5.4 %collective-permute-start.4 = (bf16[64,3200]{1,0:T(8,128)(2,1)}, bf16[64,3200]{1,0:T(8,128)(2,1)S(1)}, u32[]{:S(2)}, u32[]{:S(2)}) collective-permute-start(bf16[64,3200]{1,0:T(8,128)(2,1)} %get-tuple-element.26), channel_id=1, source_target_pairs={{0,1},{1,2},{2,3},{3,0},{4,5},{5,6},{6,7},{7,4},{8,9},{9,10},{10,1... | collective-permute-start | bytes 1228808 | tf_op jit(solution)/shard_map/ppermute | solution.py:408
  71.4 3.9 %collective-permute-start.6 = (bf16[64,3200]{1,0:T(8,128)(2,1)}, bf16[64,3200]{1,0:T(8,128)(2,1)S(1)}, u32[]{:S(2)}, u32[]{:S(2)}) collective-permute-start(bf16[64,3200]{1,0:T(8,128)(2,1)} %get-tuple-element.25), channel_id=1, source_target_pairs={{0,1},{1,2},{2,3},{3,0},{4,5},{5,6},{6,7},{7,4},{8,9},{9,10},{10,1... | collective-permute-start | bytes 1228808 | tf_op jit(solution)/shard_map/ppermute | solution.py:409
  77.3 4.3 %collective-permute-done.4.a0 = bf16[64,3200]{1,0:T(8,128)(2,1)S(1)} collective-permute-done((bf16[64,3200]{1,0:T(8,128)(2,1)}, bf16[64,3200]{1,0:T(8,128)(2,1)S(1)}, u32[]{:S(2)}, u32[]{:S(2)}) %collective-permute-start.4) | collective-permute-done | bytes 409632 | tf_op jit(solution)/shard_map/ppermute | solution.py:408
  81.6 5.5 %collective-permute-start.8 = (bf16[64,3200]{1,0:T(8,128)(2,1)S(1)}, bf16[64,3200]{1,0:T(8,128)(2,1)S(1)}, u32[]{:S(2)}, u32[]{:S(2)}) collective-permute-start(bf16[64,3200]{1,0:T(8,128)(2,1)S(1)} %collective-permute-done.4.a0), channel_id=1, source_target_pairs={{0,1},{1,2},{2,3},{3,0},{4,5},{5,6},{6,7},{7,4},{8,9},{9,10},{10,1... | collective-permute-start | bytes 1228808 | tf_op jit(solution)/shard_map/ppermute | solution.py:411
  87.1 1.9 %collective-permute-start.9 = (bf16[64,3200]{1,0:T(8,128)(2,1)S(1)}, bf16[64,3200]{1,0:T(8,128)(2,1)}, u32[]{:S(2)}, u32[]{:S(2)}) collective-permute-start(bf16[64,3200]{1,0:T(8,128)(2,1)S(1)} %collective-permute-done.5.b1), channel_id=1, source_target_pairs={{0,3},{1,0},{2,1},{3,2},{4,7},{5,4},{6,5},{7,6},{8,11},{9,8},{10,9... | collective-permute-start | bytes 1228808 | tf_op jit(solution)/shard_map/ppermute | solution.py:411
  89.6 3.0 %collective-permute-done.8.c0 = bf16[64,3200]{1,0:T(8,128)(2,1)S(1)} collective-permute-done((bf16[64,3200]{1,0:T(8,128)(2,1)S(1)}, bf16[64,3200]{1,0:T(8,128)(2,1)S(1)}, u32[]{:S(2)}, u32[]{:S(2)}) %collective-permute-start.8) | collective-permute-done | bytes 409632 | tf_op jit(solution)/shard_map/ppermute | solution.py:411
  93.3 4.9 %collective-permute-done.9.c1 = bf16[64,3200]{1,0:T(8,128)(2,1)} collective-permute-done((bf16[64,3200]{1,0:T(8,128)(2,1)S(1)}, bf16[64,3200]{1,0:T(8,128)(2,1)}, u32[]{:S(2)}, u32[]{:S(2)}) %collective-permute-start.9) | collective-permute-done | bytes 409632 | tf_op jit(solution)/shard_map/ppermute | solution.py:411
  98.3 6.9 %project.1 = (bf16[512,128]{1,0:T(8,128)(2,1)S(1)}, bf16[512,256]{1,0:T(8,128)(2,1)}, bf16[64,256]{1,0:T(8,128)(2,1)S(1)}) custom-call(s32[4]{0:T(128)S(1)} %compare_select_fusion.3.slots, bf16[128,3200]{1,0:T(8,128)(2,1)} %copy-done.3, bf16[64,3200]{1,0:T(8,128)(2,1)} %copy-done.6, bf16[64,3200]{1,0:T(8,128)(2,1)} %copy-done.7, bf16[64,3200]{1,0:T(8,128)(2,1)} %copy-done.8, ...), custom_call_target="tpu_custom_call" | custom-call | flops 1207959552 | bytes 5636096 | tf_op jit(solution)/shard_map/project/pallas_call | solution.py:143
  105.1 6.2 %collective-permute-start.14 = (bf16[512,256]{1,0:T(8,128)(2,1)}, bf16[512,256]{1,0:T(8,128)(2,1)S(1)}, u32[]{:S(2)}, u32[]{:S(2)}) collective-permute-start(bf16[512,256]{1,0:T(8,128)(2,1)} %get-tuple-element.21.kv0), channel_id=1, source_target_pairs={{0,192},{64,0},{128,64},{192,128},{1,193},{65,1},{129,65},{193,129... | collective-permute-start | bytes 786440 | tf_op jit(solution)/shard_map/ppermute | solution.py:427
  113.2 6.7 %collective-permute-start.12 = (bf16[512,128]{1,0:T(8,128)(2,1)S(1)}, bf16[512,128]{1,0:T(8,128)(2,1)S(1)}, u32[]{:S(2)}, u32[]{:S(2)}) collective-permute-start(bf16[512,128]{1,0:T(8,128)(2,1)S(1)} %get-tuple-element.20.q_ref), channel_id=1, source_target_pairs={{0,48},{48,0},{16,32},{32,16},{1,49},{49,1},{17,33},{33,17},{2,50}... | collective-permute-start | bytes 393224 | tf_op jit(solution)/shard_map/ppermute | solution.py:426
  121.9 2.5 %collective-permute-start.10 = (bf16[512,128]{1,0:T(8,128)(2,1)S(1)}, bf16[512,128]{1,0:T(8,128)(2,1)S(1)}, u32[]{:S(2)}, u32[]{:S(2)}) collective-permute-start(bf16[512,128]{1,0:T(8,128)(2,1)S(1)} %get-tuple-element.20.q_ref), channel_id=1, source_target_pairs={{0,16},{16,0},{1,17},{17,1},{2,18},{18,2},{3,19},{19,3},{4,20},{20... | collective-permute-start | bytes 393224 | tf_op jit(solution)/shard_map/ppermute | solution.py:426
  125.7 5.5 %collective-permute-start.16 = (bf16[256,256]{1,0:T(8,128)(2,1)S(1)}, bf16[256,256]{1,0:T(8,128)(2,1)S(1)}, u32[]{:S(2)}, u32[]{:S(2)}) collective-permute-start(bf16[256,256]{1,0:T(8,128)(2,1)S(1)} %slice.109), channel_id=1, source_target_pairs={{0,192},{64,0},{128,64},{192,128},{1,193},{65,1},{129,65},{193,129... | collective-permute-start | bytes 393224 | tf_op jit(solution)/shard_map/ppermute | solution.py:432
  131.2 2.1 %collective-permute-start.15 = (bf16[256,256]{1,0:T(8,128)(2,1)S(1)}, bf16[256,256]{1,0:T(8,128)(2,1)S(1)}, u32[]{:S(2)}, u32[]{:S(2)}) collective-permute-start(bf16[256,256]{1,0:T(8,128)(2,1)S(1)} %slice.108), channel_id=1, source_target_pairs={{0,64},{64,128},{128,192},{192,0},{1,65},{65,129},{129,193},{193,1... | collective-permute-start | bytes 393224 | tf_op jit(solution)/shard_map/ppermute | solution.py:431
  134.3 7.8 %first.1.before_hbm = f32[3,2,512,128]{3,2,1,0:T(8,128)} custom-call(s32[4]{0:T(128)S(1)} %pad_add_fusion.info, bf16[512,128]{1,0:T(8,128)(2,1)S(1)} %collective-permute-done.10.q1, bf16[512,128]{1,0:T(8,128)(2,1)S(1)} %collective-permute-done.11.q2, bf16[512,128]{1,0:T(8,128)(2,1)S(1)} %collective-permute-done.12.q3, bf16[512,256]{1,0:T(8,128)(2,1)S(1)} %copy-done.1, ...), custom_call_target="tpu_custom_call" | custom-call | flops 2617245696 | bytes 1638400 | tf_op jit(solution)/shard_map/first/pallas_call | solution.py:292
  142.1 5.7 %rest.1 = bf16[4,576,128]{2,1,0:T(8,128)(2,1)} custom-call(s32[4]{0:T(128)S(1)} %pad_add_fusion.info, bf16[512,128]{1,0:T(8,128)(2,1)S(1)} %collective-permute-done.10.q1, bf16[512,128]{1,0:T(8,128)(2,1)S(1)} %collective-permute-done.11.q2, bf16[512,128]{1,0:T(8,128)(2,1)S(1)} %collective-permute-done.12.q3, ...), custom_call_target="tpu_custom_call" | custom-call | flops 805306368 | bytes 1048576 | tf_op jit(solution)/shard_map/rest/pallas_call | solution.py:292
  147.9 4.2 %all-to-all-start = ((bf16[4,576,128]{2,1,0:T(8,128)(2,1)}), bf16[4,576,128]{2,1,0:T(8,128)(2,1)S(1)}, u32[]{:S(2)}, u32[]{:S(2)}) async-start(bf16[4,576,128]{2,1,0:T(8,128)(2,1)} %rest.1), calls=%async_computation | async-start | bytes 1179648 | tf_op jit(solution)/shard_map/all_to_all | solution.py:441
  152.1 4.3 %own.1.own_hbm = f32[2,512,128]{2,1,0:T(8,128)} custom-call(s32[4]{0:T(128)S(1)} %pad_add_fusion.info, bf16[512,128]{1,0:T(8,128)(2,1)S(1)} %get-tuple-element.20.q_ref, bf16[512,256]{1,0:T(8,128)(2,1)S(1)} %copy-done.2, bf16[512,256]{1,0:T(8,128)(2,1)S(1)} %collective-permute-done.13.kv1, bf16[512,256]{1,0:T(8,128)(2,1)S(1)} %collective-permute-done.14.kv2, ...), custom_call_target="tpu_custom_call" | custom-call | flops 1140850688 | bytes 1376256 | tf_op jit(solution)/shard_map/own/pallas_call | solution.py:292
  156.4 2.6 %all-to-all-done.parts_ref = bf16[4,576,128]{2,1,0:T(8,128)(2,1)S(1)} async-done(((bf16[4,576,128]{2,1,0:T(8,128)(2,1)}), bf16[4,576,128]{2,1,0:T(8,128)(2,1)S(1)}, u32[]{:S(2)}, u32[]{:S(2)}) %all-to-all-start) | async-done | bytes 589856 | tf_op jit(solution)/shard_map/all_to_all | solution.py:441
  159.0 2.7 %combine.1 = bf16[2,4,64,128]{3,2,1,0:T(8,128)(2,1)} custom-call(s32[4]{0:T(128)S(1)} %compare_select_fusion.3.slots, s32[4]{0:T(128)S(1)} %pad_add_fusion.info, bf16[4,576,128]{2,1,0:T(8,128)(2,1)S(1)} %all-to-all-done.parts_ref, f32[2,512,128]{2,1,0:T(8,128)} %own.1.own_hbm), custom_call_target="tpu_custom_call" | custom-call | tf_op jit(solution)/shard_map/combine/pallas_call | solution.py:354
  (66 shorter events, 22.6 us)
Async XLA Ops:
  6.5 82.5 %copy-start = (bf16[1,226,3072]{2,1,0:T(8,128)(2,1)S(1)}, bf16[1,226,3072]{2,1,0:T(8,128)(2,1)}, u32[]{:S(2)}) copy-start(bf16[1,226,3072]{2,1,0:T(8,128)(2,1)} %param.8) | copy-start | bytes 4165636
  6.5 31.6 %copy-start.4 = (bf16[1,2,4,4,3072]{4,3,2,1,0:T(4,128)(2,1)S(1)}, bf16[1,2,4,4,3072]{4,3,2,1,0:T(4,128)(2,1)}, u32[]{:S(2)}) copy-start(bf16[1,2,4,4,3072]{4,3,2,1,0:T(4,128)(2,1)} %param.7) | copy-start | bytes 589828
  6.5 22.2 %copy-start.10 = (bf16[512,384]{1,0:T(8,128)(2,1)S(1)}, bf16[512,384]{1,0:T(8,128)(2,1)}, u32[]{:S(2)}) copy-start(bf16[512,384]{1,0:T(8,128)(2,1)} %param.10) | copy-start | bytes 1179652
  6.5 22.6 %copy-start.11 = (bf16[3,3,3072]{2,1,0:T(4,128)(2,1)S(1)}, bf16[3,3,3072]{2,1,0:T(4,128)(2,1)}, u32[]{:S(2)}) copy-start(bf16[3,3,3072]{2,1,0:T(4,128)(2,1)} %param.9) | copy-start | bytes 165892
  6.5 91.7 %all-gather.2.cloned.1.call-start = ((), (), s32[]{:S(2)}) async-start(), calls=%async_computation.1 | async-start | bytes 2433024 | tf_op jit(solution)/shard_map/all_gather | solution.py:383
  9.1 6.3 %collective-permute-start = (bf16[1,2,1,4,3072]{4,3,2,1,0:T(4,128)(2,1)S(1)}, bf16[1,2,1,4,3072]{4,3,2,1,0:T(4,128)(2,1)S(1)}, u32[]{:S(2)}, u32[]{:S(2)}) collective-permute-start(bf16[1,2,1,4,3072]{4,3,2,1,0:T(4,128)(2,1)S(1)} %get-tuple-element.29), channel_id=1, source_target_pairs={{0,16},{16,32},{32,48},{48,64},{64,80},{80,96},{96,112},{112,128},... | collective-permute-start | bytes 147464 | tf_op jit(solution)/shard_map/ppermute | solution.py:41
  13.4 6.0 %collective-permute-start.1 = (bf16[1,2,1,4,3072]{4,3,2,1,0:T(4,128)(2,1)S(1)}, bf16[1,2,1,4,3072]{4,3,2,1,0:T(4,128)(2,1)S(1)}, u32[]{:S(2)}, u32[]{:S(2)}) collective-permute-start(bf16[1,2,1,4,3072]{4,3,2,1,0:T(4,128)(2,1)S(1)} %get-tuple-element.30), channel_id=1, source_target_pairs={{16,0},{32,16},{48,32},{64,48},{80,64},{96,80},{112,96},{128,112},... | collective-permute-start | bytes 147464 | tf_op jit(solution)/shard_map/ppermute | solution.py:44
  20.8 9.4 %collective-permute-start.2 = (bf16[1,2,6,1,3072]{4,3,2,1,0:T(2,128)(2,1)S(1)}, bf16[1,2,6,1,3072]{4,3,2,1,0:T(2,128)(2,1)S(1)}, u32[]{:S(2)}, u32[]{:S(2)}) collective-permute-start(bf16[1,2,6,1,3072]{4,3,2,1,0:T(2,128)(2,1)S(1)} %get-tuple-element.27), channel_id=1, source_target_pairs={{0,1},{1,2},{2,3},{3,4},{4,5},{5,6},{6,7},{7,8},{8,9},{9,10},{10,1... | collective-permute-start | bytes 221192 | tf_op jit(solution)/shard_map/ppermute | solution.py:41
  26.8 11.4 %collective-permute-start.3 = (bf16[1,2,6,1,3072]{4,3,2,1,0:T(2,128)(2,1)S(1)}, bf16[1,2,6,1,3072]{4,3,2,1,0:T(2,128)(2,1)S(1)}, u32[]{:S(2)}, u32[]{:S(2)}) collective-permute-start(bf16[1,2,6,1,3072]{4,3,2,1,0:T(2,128)(2,1)S(1)} %get-tuple-element.28), channel_id=1, source_target_pairs={{1,0},{2,1},{3,2},{4,3},{5,4},{6,5},{7,6},{8,7},{9,8},{10,9},{11,1... | collective-permute-start | bytes 221192 | tf_op jit(solution)/shard_map/ppermute | solution.py:44
  64.0 13.2 %collective-permute-start.5 = (bf16[64,3200]{1,0:T(8,128)(2,1)}, bf16[64,3200]{1,0:T(8,128)(2,1)S(1)}, u32[]{:S(2)}, u32[]{:S(2)}) collective-permute-start(bf16[64,3200]{1,0:T(8,128)(2,1)} %get-tuple-element.25), channel_id=1, source_target_pairs={{0,3},{1,0},{2,1},{3,2},{4,7},{5,4},{6,5},{7,6},{8,11},{9,8},{10,9... | collective-permute-start | bytes 1228808 | tf_op jit(solution)/shard_map/ppermute | solution.py:408
  65.9 15.6 %collective-permute-start.4 = (bf16[64,3200]{1,0:T(8,128)(2,1)}, bf16[64,3200]{1,0:T(8,128)(2,1)S(1)}, u32[]{:S(2)}, u32[]{:S(2)}) collective-permute-start(bf16[64,3200]{1,0:T(8,128)(2,1)} %get-tuple-element.26), channel_id=1, source_target_pairs={{0,1},{1,2},{2,3},{3,0},{4,5},{5,6},{6,7},{7,4},{8,9},{9,10},{10,1... | collective-permute-start | bytes 1228808 | tf_op jit(solution)/shard_map/ppermute | solution.py:408
  71.4 17.8 %collective-permute-start.6 = (bf16[64,3200]{1,0:T(8,128)(2,1)}, bf16[64,3200]{1,0:T(8,128)(2,1)S(1)}, u32[]{:S(2)}, u32[]{:S(2)}) collective-permute-start(bf16[64,3200]{1,0:T(8,128)(2,1)} %get-tuple-element.25), channel_id=1, source_target_pairs={{0,1},{1,2},{2,3},{3,0},{4,5},{5,6},{6,7},{7,4},{8,9},{9,10},{10,1... | collective-permute-start | bytes 1228808 | tf_op jit(solution)/shard_map/ppermute | solution.py:409
  75.3 14.2 %collective-permute-start.7 = (bf16[64,3200]{1,0:T(8,128)(2,1)}, bf16[64,3200]{1,0:T(8,128)(2,1)S(1)}, u32[]{:S(2)}, u32[]{:S(2)}) collective-permute-start(bf16[64,3200]{1,0:T(8,128)(2,1)} %get-tuple-element.26), channel_id=1, source_target_pairs={{0,3},{1,0},{2,1},{3,2},{4,7},{5,4},{6,5},{7,6},{8,11},{9,8},{10,9... | collective-permute-start | bytes 1228808 | tf_op jit(solution)/shard_map/ppermute | solution.py:409
  77.2 21.0 %copy-start.5 = (bf16[64,3200]{1,0:T(8,128)(2,1)}, bf16[64,3200]{1,0:T(8,128)(2,1)S(1)}, u32[]{:S(2)}) copy-start(bf16[64,3200]{1,0:T(8,128)(2,1)S(1)} %collective-permute-done.5.b1) | copy-start | bytes 1228804
  81.6 10.9 %collective-permute-start.8 = (bf16[64,3200]{1,0:T(8,128)(2,1)S(1)}, bf16[64,3200]{1,0:T(8,128)(2,1)S(1)}, u32[]{:S(2)}, u32[]{:S(2)}) collective-permute-start(bf16[64,3200]{1,0:T(8,128)(2,1)S(1)} %collective-permute-done.4.a0), channel_id=1, source_target_pairs={{0,1},{1,2},{2,3},{3,0},{4,5},{5,6},{6,7},{7,4},{8,9},{9,10},{10,1... | collective-permute-start | bytes 1228808 | tf_op jit(solution)/shard_map/ppermute | solution.py:411
  87.1 11.2 %collective-permute-start.9 = (bf16[64,3200]{1,0:T(8,128)(2,1)S(1)}, bf16[64,3200]{1,0:T(8,128)(2,1)}, u32[]{:S(2)}, u32[]{:S(2)}) collective-permute-start(bf16[64,3200]{1,0:T(8,128)(2,1)S(1)} %collective-permute-done.5.b1), channel_id=1, source_target_pairs={{0,3},{1,0},{2,1},{3,2},{4,7},{5,4},{6,5},{7,6},{8,11},{9,8},{10,9... | collective-permute-start | bytes 1228808 | tf_op jit(solution)/shard_map/ppermute | solution.py:411
  105.1 20.0 %collective-permute-start.14 = (bf16[512,256]{1,0:T(8,128)(2,1)}, bf16[512,256]{1,0:T(8,128)(2,1)S(1)}, u32[]{:S(2)}, u32[]{:S(2)}) collective-permute-start(bf16[512,256]{1,0:T(8,128)(2,1)} %get-tuple-element.21.kv0), channel_id=1, source_target_pairs={{0,192},{64,0},{128,64},{192,128},{1,193},{65,1},{129,65},{193,129... | collective-permute-start | bytes 786440 | tf_op jit(solution)/shard_map/ppermute | solution.py:427
  111.3 14.4 %collective-permute-start.13 = (bf16[512,256]{1,0:T(8,128)(2,1)}, bf16[512,256]{1,0:T(8,128)(2,1)S(1)}, u32[]{:S(2)}, u32[]{:S(2)}) collective-permute-start(bf16[512,256]{1,0:T(8,128)(2,1)} %get-tuple-element.21.kv0), channel_id=1, source_target_pairs={{0,64},{64,128},{128,192},{192,0},{1,65},{65,129},{129,193},{193,1... | collective-permute-start | bytes 786440 | tf_op jit(solution)/shard_map/ppermute | solution.py:427
  113.2 20.1 %collective-permute-start.12 = (bf16[512,128]{1,0:T(8,128)(2,1)S(1)}, bf16[512,128]{1,0:T(8,128)(2,1)S(1)}, u32[]{:S(2)}, u32[]{:S(2)}) collective-permute-start(bf16[512,128]{1,0:T(8,128)(2,1)S(1)} %get-tuple-element.20.q_ref), channel_id=1, source_target_pairs={{0,48},{48,0},{16,32},{32,16},{1,49},{49,1},{17,33},{33,17},{2,50}... | collective-permute-start | bytes 393224 | tf_op jit(solution)/shard_map/ppermute | solution.py:426
  120.0 13.3 %collective-permute-start.11 = (bf16[512,128]{1,0:T(8,128)(2,1)S(1)}, bf16[512,128]{1,0:T(8,128)(2,1)S(1)}, u32[]{:S(2)}, u32[]{:S(2)}) collective-permute-start(bf16[512,128]{1,0:T(8,128)(2,1)S(1)} %get-tuple-element.20.q_ref), channel_id=1, source_target_pairs={{0,32},{32,0},{1,33},{33,1},{2,34},{34,2},{3,35},{35,3},{4,36},{36... | collective-permute-start | bytes 393224 | tf_op jit(solution)/shard_map/ppermute | solution.py:426
  121.9 11.4 %collective-permute-start.10 = (bf16[512,128]{1,0:T(8,128)(2,1)S(1)}, bf16[512,128]{1,0:T(8,128)(2,1)S(1)}, u32[]{:S(2)}, u32[]{:S(2)}) collective-permute-start(bf16[512,128]{1,0:T(8,128)(2,1)S(1)} %get-tuple-element.20.q_ref), channel_id=1, source_target_pairs={{0,16},{16,0},{1,17},{17,1},{2,18},{18,2},{3,19},{19,3},{4,20},{20... | collective-permute-start | bytes 393224 | tf_op jit(solution)/shard_map/ppermute | solution.py:426
  125.7 16.4 %collective-permute-start.16 = (bf16[256,256]{1,0:T(8,128)(2,1)S(1)}, bf16[256,256]{1,0:T(8,128)(2,1)S(1)}, u32[]{:S(2)}, u32[]{:S(2)}) collective-permute-start(bf16[256,256]{1,0:T(8,128)(2,1)S(1)} %slice.109), channel_id=1, source_target_pairs={{0,192},{64,0},{128,64},{192,128},{1,193},{65,1},{129,65},{193,129... | collective-permute-start | bytes 393224 | tf_op jit(solution)/shard_map/ppermute | solution.py:432
  131.2 10.9 %collective-permute-start.15 = (bf16[256,256]{1,0:T(8,128)(2,1)S(1)}, bf16[256,256]{1,0:T(8,128)(2,1)S(1)}, u32[]{:S(2)}, u32[]{:S(2)}) collective-permute-start(bf16[256,256]{1,0:T(8,128)(2,1)S(1)} %slice.108), channel_id=1, source_target_pairs={{0,64},{64,128},{128,192},{192,0},{1,65},{65,129},{129,193},{193,1... | collective-permute-start | bytes 393224 | tf_op jit(solution)/shard_map/ppermute | solution.py:431
  147.9 11.2 %all-to-all-start = ((bf16[4,576,128]{2,1,0:T(8,128)(2,1)}), bf16[4,576,128]{2,1,0:T(8,128)(2,1)S(1)}, u32[]{:S(2)}, u32[]{:S(2)}) async-start(bf16[4,576,128]{2,1,0:T(8,128)(2,1)} %rest.1), calls=%async_computation | async-start | bytes 1179648 | tf_op jit(solution)/shard_map/all_to_all | solution.py:441
  (7 other events, 41.3 us)
Sparse Core Ops, SparseCore 0:
  9.5 72.9 all-gather.1

commit v8 on v7

--- a/solution.py
+++ b/solution.py
@@ -54,17 +54,17 @@
 
 
 def project_kernel(
-    slots, x0, a0, a1, b0, b1, c0, c1, text, w_hbm,
+    slots, x0, x1, a0, a1, b0, b1, c0, c1, text, w_hbm,
     q_out, kv_out, text_out,
-    held, mod, extra, normed, w_ref, kv, in_sems, w_sem, out_sems,
+    held, mod, extra, normed, w_ref, q, kv, in_sems, w_sem, out_sems,
 ):
-    rows = x0.shape[0]
-    half = rows // 2
+    half = x0.shape[0]
+    rows = 2 * half
     width = text.shape[1]
     tile = rows // 4
-    arrived = [(x0, 0)]
-    for slot, (low, high) in enumerate(((a0, a1), (b0, b1), (c0, c1))):
-        arrived += [(low, (slot + 1) * rows), (high, (slot + 1) * rows + half)]
+    arrived = []
+    for slot, (low, high) in enumerate(((x0, x1), (a0, a1), (b0, b1), (c0, c1))):
+        arrived += [(low, slot * rows), (high, slot * rows + half)]
 
     def tail(i):
         piece, at = arrived[i]
@@ -125,12 +125,16 @@
             fetch.wait()
         out = jnp.dot(normed[first:last, :], w_ref[...], preferred_element_type=F32).astype(BF)
         span = pl.ds(first, 2 * rows)
-        q_out[span, :] = out[: 2 * rows, :128]
+        q[span, :] = out[: 2 * rows, :128]
         kv[span, :] = out[: 2 * rows, 128:]
-        sends.append(
-            pltpu.make_async_copy(kv.at[span, :], kv_out.at[span, :], out_sems.at[part])
-        )
-        sends[-1].start()
+        new = [pltpu.make_async_copy(kv.at[span, :], kv_out.at[span, :], out_sems.at[part, 4])]
+        for i in range(4):
+            new.append(
+                pltpu.make_async_copy(q.at[span, :], q_out.at[i, span, :], out_sems.at[part, i])
+            )
+        for send in new:
+            send.start()
+        sends += new
         if part:
             text_out[...] = out[2 * rows :, 128:]
     for send in sends:
@@ -138,27 +142,29 @@
 
 
 def project(slots, pieces, text, weight):
-    rows, lanes = pieces[0].shape
+    half, lanes = pieces[0].shape
+    rows = 2 * half
     width = text.shape[1]
     return pl.pallas_call(
         project_kernel,
         out_shape=[
-            jax.ShapeDtypeStruct((4 * rows, 128), BF),
+            pltpu.MemorySpace.HBM((4, 4 * rows, 128), BF),
             pltpu.MemorySpace.HBM((4 * rows, 256), BF),
             jax.ShapeDtypeStruct((text.shape[0], 256), BF),
         ],
-        in_specs=[pl.BlockSpec(memory_space=pltpu.SMEM)] + [hbm()] * 7 + [vmem(), hbm()],
-        out_specs=[vmem(), hbm(), vmem()],
+        in_specs=[pl.BlockSpec(memory_space=pltpu.SMEM)] + [hbm()] * 8 + [vmem(), hbm()],
+        out_specs=[hbm(), hbm(), vmem()],
         scratch_shapes=[
             pltpu.VMEM((4 * rows, width), BF),
             pltpu.VMEM((2, width), F32),
             pltpu.VMEM((4 * rows, 128), BF),
             pltpu.VMEM((4 * rows + text.shape[0], width), BF),
             pltpu.VMEM(weight.shape, BF),
+            pltpu.VMEM((4 * rows, 128), BF),
             pltpu.VMEM((4 * rows, 256), BF),
-            pltpu.SemaphoreType.DMA((2, 7)),
+            pltpu.SemaphoreType.DMA((2, 8)),
             pltpu.SemaphoreType.DMA,
-            pltpu.SemaphoreType.DMA((2,)),
+            pltpu.SemaphoreType.DMA((2, 5)),
         ],
         compiler_params=params(28),
         cost_estimate=pl.CostEstimate(
@@ -193,7 +199,7 @@
     position = info[0] + lane
     valid = (position >= info[1]) & (position < info[2]) & (lane < TEXT_PART)
     q = q.astype(F32)
-    outs, sums = [], []
+    accs, tops = [], []
     for head in range(2):
         own = jnp.where(lane // HD == head, q, 0.0).astype(BF)
         s = lax.dot_general(
@@ -208,18 +214,19 @@
         if has_text:
             p_text = jnp.where(valid, jnp.exp2(text * SCALE2 - top), 0.0).astype(BF)
             p = jnp.concatenate([p, p_text], axis=1)
-        acc = jnp.dot(p, values[...], preferred_element_type=F32)
-        total = acc[:, 128:]
-        outs.append(acc[:, :128] / total)
-        sums.append(top + jnp.log(total) * LOG2E)
-    return jnp.where(lane < HD, outs[0], outs[1]), jnp.where(lane < HD, sums[0], sums[1])
-
-
-def first_kernel(info, q1, q2, q3, kv0, kv1, kv2, text_kv, o_ref, keys, values, held, sems):
+        accs.append(jnp.dot(p, values[...], preferred_element_type=F32))
+        tops.append(top)
+    total = jnp.where(lane < HD, accs[0][:, 128:], accs[1][:, 128:])
+    weighted = jnp.where(lane < HD, accs[0][:, :128], accs[1][:, :128])
+    return weighted / total, jnp.where(lane < HD, tops[0], tops[1]) + jnp.log(total) * LOG2E
+
+
+def first_kernel(info, q_ref, kv0, kv1, kv2, text_kv, o_ref, keys, values, held, sems):
     load_keys((kv0, kv1, kv2), text_kv, keys, values)
     sends = []
-    for i, q_ref in enumerate((q1, q2, q3)):
-        held[i, 0], held[i, 1] = softmax_block(info, q_ref[...], keys, values, True)
+    for i in range(3):
+        q = q_ref[jnp.bitwise_xor(info[3], i + 1)]
+        held[i, 0], held[i, 1] = softmax_block(info, q, keys, values, True)
         sends.append(pltpu.make_async_copy(held.at[i], o_ref.at[i], sems.at[i]))
         sends[-1].start()
     for send in sends:
@@ -227,19 +234,21 @@
 
 
 def rest_kernel(
-    info, q1, q2, q3, kv3, kv4, before_hbm, o_ref, keys, values, held, before, sems, in_sems
+    info, q_ref, kv3, kv4, before_hbm, o_ref, keys, values, held, before, sems, in_sems
 ):
     fetches = [
         pltpu.make_async_copy(before_hbm.at[i], before.at[i], in_sems.at[i]) for i in range(3)
     ]
     for fetch in fetches:
         fetch.start()
-    count = q1.shape[0]
+    count = q_ref.shape[1]
     load_keys((kv3, kv4), None, keys, values)
-    lane = lax.broadcasted_iota(jnp.int32, (128, 128), 1)
+    term = lax.broadcasted_iota(jnp.int32, (STAT_ROWS, 128), 0)
+    lane = lax.broadcasted_iota(jnp.int32, (STAT_ROWS, 128), 1)
     sends = []
-    for i, q_ref in enumerate((q1, q2, q3)):
-        out, lse = softmax_block(info, q_ref[...], keys, values, False)
+    for i in range(3):
+        member = jnp.bitwise_xor(info[3], i + 1)
+        out, lse = softmax_block(info, q_ref[member], keys, values, False)
         fetches[i].wait()
         earlier = before[i, 1]
         top = jnp.maximum(lse, earlier)
@@ -247,18 +256,17 @@
         total = new + old
         held[i, :count, :] = ((new * out + old * before[i, 0]) / total).astype(BF)
         lse = top + jnp.log(total) * LOG2E
+        across = jnp.zeros((STAT_ROWS, count), F32)
+        for part in range(3):
+            piece = lse.astype(BF)
+            lse = lse - piece.astype(F32)
+            pick = jnp.where((term % 8 == part) & (lane == term // 8 * HD), 1.0, 0.0).astype(BF)
+            across = across + lax.dot_general(
+                pick, piece, (((1,), (1,)), ((), ())), preferred_element_type=F32
+            )
         for tile in range(count // 128):
-            rest = lse[tile * 128 : (tile + 1) * 128]
-            stats = jnp.zeros((128, 128), F32)
-            for part in range(3):
-                piece = rest.astype(BF).astype(F32)
-                stats = jnp.where(lane % HD == part, piece, stats)
-                rest = rest - piece
-            across = jnp.transpose(stats)
-            across = jnp.concatenate([across[:8], across[HD : HD + 8]], axis=0)
             at = count + tile * STAT_ROWS
-            held[i, at : at + STAT_ROWS, :] = across.astype(BF)
-        member = jnp.bitwise_xor(info[3], i + 1)
+            held[i, at : at + STAT_ROWS, :] = across[:, tile * 128 : (tile + 1) * 128].astype(BF)
         sends.append(pltpu.make_async_copy(held.at[i], o_ref.at[member], sems.at[i]))
         sends[-1].start()
     for send in sends:
@@ -267,16 +275,16 @@
 
 def own_kernel(info, q_ref, kv0, kv1, kv2, kv3, kv4, text_kv, o_ref, keys, values, held, sems):
     load_keys((kv0, kv1, kv2, kv3, kv4), text_kv, keys, values)
-    held[0], held[1] = softmax_block(info, q_ref[...], keys, values, True)
+    held[0], held[1] = softmax_block(info, q_ref[info[3]], keys, values, True)
     copy = pltpu.make_async_copy(held, o_ref, sems.at[0])
     copy.start()
     copy.wait()
 
 
-def attend(kernel, name, out_shape, held, info, qs, blocks, text_kv=None, before=None):
+def attend(kernel, name, peers, out_shape, held, info, qs, blocks, text_kv=None, before=None):
     keys = sum(block.shape[0] for block in blocks) + (0 if text_kv is None else 128)
-    count = qs[0].shape[0]
-    operands = [*qs, *blocks] + ([] if text_kv is None else [text_kv])
+    count = qs.shape[1]
+    operands = [qs, *blocks] + ([] if text_kv is None else [text_kv])
     specs = [pl.BlockSpec(memory_space=pltpu.SMEM)] + [vmem()] * len(operands)
     scratch = [
         pltpu.VMEM((keys, 128), BF),
@@ -297,9 +305,9 @@
         scratch_shapes=scratch + sems,
         compiler_params=params(24),
         cost_estimate=pl.CostEstimate(
-            flops=4 * len(qs) * count * keys * 256,
-            bytes_accessed=512 * (len(qs) * count + keys),
-            transcendentals=2 * len(qs) * count * keys,
+            flops=4 * peers * count * keys * 256,
+            bytes_accessed=512 * (peers * count + keys),
+            transcendentals=2 * peers * count * keys,
         ),
         name=name,
     )(info, *operands)
@@ -409,7 +417,7 @@
     a1, b0 = lax.ppermute(high, "x", up), lax.ppermute(low, "x", down)
     a0, b1 = lax.optimization_barrier((a0, b1))
     c0, c1 = lax.ppermute(a0, "x", up), lax.ppermute(b1, "x", down)
-    pieces = (tokens, a0, a1, b0, b1, c0, c1)
+    pieces = (low, high, a0, a1, b0, b1, c0, c1)
     distance = (jnp.arange(4, dtype=jnp.int32) - x_at) % 4
     slots = jnp.where(distance == 0, 0, jnp.where(distance == 3, 1, distance + 1))
 
@@ -418,12 +426,7 @@
     text_rows = lax.dynamic_slice_in_dim(prompt_rows[0], start, TEXT_PART, axis=0)
     queries, kv, text_kv = project(slots, pieces, text_rows, weight)
     group = ("v", "zl")
-    swaps = (
-        ("zl", [(0, 1), (1, 0)]),
-        ("v", [(0, 1), (1, 0)]),
-        (group, [(0, 3), (3, 0), (1, 2), (2, 1)]),
-    )
-    qs = [lax.ppermute(queries, axis, swap) for axis, swap in swaps]
+    qs = lax.all_to_all(queries, group, split_axis=0, concat_axis=0, tiled=True)
     near = [lax.ppermute(kv, "u", up), lax.ppermute(kv, "u", down)]
     near = lax.optimization_barrier(near)
     count = kv.shape[0]
@@ -434,14 +437,14 @@
     info = jnp.stack([start, lower, text_len[0], member])
     shape = (3, 2, count, 128)
     first = jax.ShapeDtypeStruct(shape, F32)
-    first = attend(first_kernel, "first", first, shape, info, qs, [kv, *near], text_kv)
+    first = attend(first_kernel, "first", 3, first, shape, info, qs, [kv, *near], text_kv)
     shape = (4, count + count // 128 * STAT_ROWS, 128)
     parts = jax.ShapeDtypeStruct(shape, BF)
-    parts = attend(rest_kernel, "rest", parts, (3,) + shape[1:], info, qs, far, None, first)
+    parts = attend(rest_kernel, "rest", 3, parts, (3,) + shape[1:], info, qs, far, None, first)
     parts = lax.all_to_all(parts, group, split_axis=0, concat_axis=0, tiled=True)
     shape = (2, count, 128)
     own = jax.ShapeDtypeStruct(shape, F32)
-    own = attend(own_kernel, "own", own, shape, info, [queries], [kv, *near, *far], text_kv)
+    own = attend(own_kernel, "own", 1, own, shape, info, qs, [kv, *near, *far], text_kv)
     shape = (frames, tile_h, 16 * tile_w, head_width)
     return combine(slots, info, parts, own, shape)[None]
 

time: 170 us -> 172 us (1.012)
  waiting for transfers between devices: 28.7 us -> 37.7 us
  starting transfers between devices: 65.1 us -> 60.2 us
    ppermute x3 -> x0, starting transfers between devices: 11.1 us -> none  [on_device(): qs = [lax.ppermute(queries, axis, swap) for axis, swap in swaps]]
    ppermute x2, waiting for transfers between devices: 0.56 us -> 10.7 us  [on_device(): near = [lax.ppermute(kv, 'u', up), lax.ppermute(kv, 'u', down)]]
    all_to_all x0 -> x1, starting transfers between devices: none -> 5.41 us  [on_device(): qs = lax.all_to_all(queries, group, split_axis=0, concat_axis=0, tiled=True)]
    ppermute x1, starting transfers between devices: 5.48 us -> 1.92 us  [on_device(): lax.ppermute(near[1][count // 2:], 'u', down)]
    ppermute x1, starting transfers between devices: 2.1 us -> 5 us  [on_device(): lax.ppermute(near[0][:count // 2], 'u', up)]
  transfers between devices with their start and end apart: 19 -> 17, of which waited for: 9 -> 10; matrix products, arithmetic and copies ran while one was open for 3% -> 3% of each run, Pallas kernels for 7% -> 7%
where the time goes in v8:
time: 172 us; the launch traced here: 171 us
  starting transfers between devices  60.2 us (35%)
  waiting for transfers between devices  37.7 us (22%)
  Pallas kernels  27.8 us (16%)
  blocking collectives  22.5 us (13%)
  between operations  15.1 us (9%)
  local copies, waits for them, and re-layouts  5.23 us (3%)
  other arithmetic  2.82 us (2%)
    all_gather x1, blocking collectives, on_device(): tokens = lax.all_gather(peg, 'zh', axis=0, tiled=True)  22.5 us
    pallas_call x3, Pallas kernels, attend(): pl.pallas_call(kernel, out_shape=pltpu.MemorySpace.HBM(out_shape.shape, o...  18 us
    ppermute x2, waiting for transfers between devices, with_halo(): lax.ppermute(lax.slice_in_dim(block, 0, width, axis=dim), axis, backward)  11.9 us
    ppermute x2, waiting for transfers between devices, on_device(): near = [lax.ppermute(kv, 'u', up), lax.ppermute(kv, 'u', down)]  10.7 us
    ppermute x2, starting transfers between devices, with_halo(): lax.ppermute(lax.slice_in_dim(block, block.shape[dim] - width, None, axis...  10.3 us
    ppermute x2, starting transfers between devices, on_device(): near = [lax.ppermute(kv, 'u', up), lax.ppermute(kv, 'u', down)]  8.81 us
    ppermute x2, starting transfers between devices, on_device(): c0, c1 = (lax.ppermute(a0, 'x', up), lax.ppermute(b1, 'x', down))  7.61 us
    ppermute x2, waiting for transfers between devices, on_device(): c0, c1 = (lax.ppermute(a0, 'x', up), lax.ppermute(b1, 'x', down))  7.55 us
  transfers between devices with their start and end apart: 17, of which 10 were waited for; matrix products, arithmetic and copies ran while one was open for 3% of the time, Pallas kernels for 7%

profile of v8, /device:TPU:6, one launch (start us, length us, event | category | flops | bytes accessed | tf_op | source)
XLA Modules:
  0.0 171.5 jit_solution(6325584256918661830)
XLA Ops:
  9.1 4.3 %collective-permute-start = (bf16[1,2,1,4,3072]{4,3,2,1,0:T(4,128)(2,1)S(1)}, bf16[1,2,1,4,3072]{4,3,2,1,0:T(4,128)(2,1)S(1)}, u32[]{:S(2)}, u32[]{:S(2)}) collective-permute-start(bf16[1,2,1,4,3072]{4,3,2,1,0:T(4,128)(2,1)S(1)} %get-tuple-element.29), channel_id=1, source_target_pairs={{0,16},{16,32},{32,48},{48,64},{64,80},{80,96},{96,112},{112,128},... | collective-permute-start | bytes 147464 | tf_op jit(solution)/shard_map/ppermute | solution.py:41
  15.5 3.9 %collective-permute-done.1 = bf16[1,2,1,4,3072]{4,3,2,1,0:T(4,128)(2,1)S(1)} collective-permute-done((bf16[1,2,1,4,3072]{4,3,2,1,0:T(4,128)(2,1)S(1)}, bf16[1,2,1,4,3072]{4,3,2,1,0:T(4,128)(2,1)S(1)}, u32[]{:S(2)}, u32[]{:S(2)}) %collective-permute-start.1) | collective-permute-done | bytes 49184 | tf_op jit(solution)/shard_map/ppermute | solution.py:44
  20.8 6.0 %collective-permute-start.2 = (bf16[1,2,6,1,3072]{4,3,2,1,0:T(2,128)(2,1)S(1)}, bf16[1,2,6,1,3072]{4,3,2,1,0:T(2,128)(2,1)S(1)}, u32[]{:S(2)}, u32[]{:S(2)}) collective-permute-start(bf16[1,2,6,1,3072]{4,3,2,1,0:T(2,128)(2,1)S(1)} %get-tuple-element.27), channel_id=1, source_target_pairs={{0,1},{1,2},{2,3},{3,4},{4,5},{5,6},{6,7},{7,8},{8,9},{9,10},{10,1... | collective-permute-start | bytes 221192 | tf_op jit(solution)/shard_map/ppermute | solution.py:41
  30.2 8.0 %collective-permute-done.3 = bf16[1,2,6,1,3072]{4,3,2,1,0:T(2,128)(2,1)S(1)} collective-permute-done((bf16[1,2,6,1,3072]{4,3,2,1,0:T(2,128)(2,1)S(1)}, bf16[1,2,6,1,3072]{4,3,2,1,0:T(2,128)(2,1)S(1)}, u32[]{:S(2)}, u32[]{:S(2)}) %collective-permute-start.3) | collective-permute-done | bytes 73760 | tf_op jit(solution)/shard_map/ppermute | solution.py:44
  39.6 22.5 %all_gather.6 = bf16[128,3200]{1,0:T(8,128)(2,1)S(1)} all-gather(bf16[32,3200]{1,0:T(8,128)(2,1)S(1)} %pad_maximum_fusion.1), channel_id=1, replica_groups=mesh['item'=2,'u'=4,'v'=2,'zl'=2,'zh'=4,'x'=4] {'zh'}, dimensions={0}, use_global_device_ids=true | all-gather | bytes 1024000 | tf_op jit(solution)/shard_map/all_gather | solution.py:411
  64.2 5.4 %collective-permute-start.4 = (bf16[64,3200]{1,0:T(8,128)(2,1)S(1)}, bf16[64,3200]{1,0:T(8,128)(2,1)}, u32[]{:S(2)}, u32[]{:S(2)}) collective-permute-start(bf16[64,3200]{1,0:T(8,128)(2,1)S(1)} %get-tuple-element.26.x0), channel_id=1, source_target_pairs={{0,1},{1,2},{2,3},{3,0},{4,5},{5,6},{6,7},{7,4},{8,9},{9,10},{10,1... | collective-permute-start | bytes 1228808 | tf_op jit(solution)/shard_map/ppermute | solution.py:416
  69.6 3.9 %collective-permute-start.6 = (bf16[64,3200]{1,0:T(8,128)(2,1)S(1)}, bf16[64,3200]{1,0:T(8,128)(2,1)S(1)}, u32[]{:S(2)}, u32[]{:S(2)}) collective-permute-start(bf16[64,3200]{1,0:T(8,128)(2,1)S(1)} %get-tuple-element.25.x1), channel_id=1, source_target_pairs={{0,1},{1,2},{2,3},{3,0},{4,5},{5,6},{6,7},{7,4},{8,9},{9,10},{10,1... | collective-permute-start | bytes 1228808 | tf_op jit(solution)/shard_map/ppermute | solution.py:417
  75.5 4.0 %collective-permute-done.4.a0 = bf16[64,3200]{1,0:T(8,128)(2,1)} collective-permute-done((bf16[64,3200]{1,0:T(8,128)(2,1)S(1)}, bf16[64,3200]{1,0:T(8,128)(2,1)}, u32[]{:S(2)}, u32[]{:S(2)}) %collective-permute-start.4) | collective-permute-done | bytes 409632 | tf_op jit(solution)/shard_map/ppermute | solution.py:416
  79.5 5.7 %collective-permute-start.8 = (bf16[64,3200]{1,0:T(8,128)(2,1)}, bf16[64,3200]{1,0:T(8,128)(2,1)S(1)}, u32[]{:S(2)}, u32[]{:S(2)}) collective-permute-start(bf16[64,3200]{1,0:T(8,128)(2,1)} %collective-permute-done.4.a0), channel_id=1, source_target_pairs={{0,1},{1,2},{2,3},{3,0},{4,5},{5,6},{6,7},{7,4},{8,9},{9,10},{10,1... | collective-permute-start | bytes 1228808 | tf_op jit(solution)/shard_map/ppermute | solution.py:419
  85.2 1.9 %collective-permute-start.9 = (bf16[64,3200]{1,0:T(8,128)(2,1)S(1)}, bf16[64,3200]{1,0:T(8,128)(2,1)}, u32[]{:S(2)}, u32[]{:S(2)}) collective-permute-start(bf16[64,3200]{1,0:T(8,128)(2,1)S(1)} %collective-permute-done.5.b1), channel_id=1, source_target_pairs={{0,3},{1,0},{2,1},{3,2},{4,7},{5,4},{6,5},{7,6},{8,11},{9,8},{10,9... | collective-permute-start | bytes 1228808 | tf_op jit(solution)/shard_map/ppermute | solution.py:419
  88.1 2.9 %collective-permute-done.8.c0 = bf16[64,3200]{1,0:T(8,128)(2,1)S(1)} collective-permute-done((bf16[64,3200]{1,0:T(8,128)(2,1)}, bf16[64,3200]{1,0:T(8,128)(2,1)S(1)}, u32[]{:S(2)}, u32[]{:S(2)}) %collective-permute-start.8) | collective-permute-done | bytes 409632 | tf_op jit(solution)/shard_map/ppermute | solution.py:419
  91.7 4.6 %collective-permute-done.9.c1 = bf16[64,3200]{1,0:T(8,128)(2,1)} collective-permute-done((bf16[64,3200]{1,0:T(8,128)(2,1)S(1)}, bf16[64,3200]{1,0:T(8,128)(2,1)}, u32[]{:S(2)}, u32[]{:S(2)}) %collective-permute-start.9) | collective-permute-done | bytes 409632 | tf_op jit(solution)/shard_map/ppermute | solution.py:419
  96.4 7.1 %project.1 = (bf16[4,512,128]{2,1,0:T(8,128)(2,1)}, bf16[512,256]{1,0:T(8,128)(2,1)}, bf16[64,256]{1,0:T(8,128)(2,1)S(1)}) custom-call(s32[4]{0:T(128)S(1)} %compare_select_fusion.3.slots, bf16[64,3200]{1,0:T(8,128)(2,1)} %copy-done.5, bf16[64,3200]{1,0:T(8,128)(2,1)} %copy-done.4, bf16[64,3200]{1,0:T(8,128)(2,1)} %collective-permute-done.4.a0, ...), custom_call_target="tpu_custom_call" | custom-call | flops 1207959552 | bytes 5636096 | tf_op jit(solution)/shard_map/project/pallas_call | solution.py:148
  103.4 5.4 %all-to-all-start = ((bf16[4,512,128]{2,1,0:T(8,128)(2,1)}), bf16[4,512,128]{2,1,0:T(8,128)(2,1)S(1)}, u32[]{:S(2)}, u32[]{:S(2)}) async-start(bf16[4,512,128]{2,1,0:T(8,128)(2,1)} %get-tuple-element.20), calls=%async_computation | async-start | bytes 1048576 | tf_op jit(solution)/shard_map/all_to_all | solution.py:429
  108.8 6.9 %collective-permute-start.11 = (bf16[512,256]{1,0:T(8,128)(2,1)}, bf16[512,256]{1,0:T(8,128)(2,1)S(1)}, u32[]{:S(2)}, u32[]{:S(2)}) collective-permute-start(bf16[512,256]{1,0:T(8,128)(2,1)} %get-tuple-element.21.kv0), channel_id=1, source_target_pairs={{0,192},{64,0},{128,64},{192,128},{1,193},{65,1},{129,65},{193,129... | collective-permute-start | bytes 786440 | tf_op jit(solution)/shard_map/ppermute | solution.py:430
  118.4 2.6 %collective-permute-done.11.kv2 = bf16[512,256]{1,0:T(8,128)(2,1)S(1)} collective-permute-done((bf16[512,256]{1,0:T(8,128)(2,1)}, bf16[512,256]{1,0:T(8,128)(2,1)S(1)}, u32[]{:S(2)}, u32[]{:S(2)}) %collective-permute-start.11) | collective-permute-done | bytes 262176 | tf_op jit(solution)/shard_map/ppermute | solution.py:430
  121.0 8.2 %collective-permute-done.10.kv1 = bf16[512,256]{1,0:T(8,128)(2,1)S(1)} collective-permute-done((bf16[512,256]{1,0:T(8,128)(2,1)}, bf16[512,256]{1,0:T(8,128)(2,1)S(1)}, u32[]{:S(2)}, u32[]{:S(2)}) %collective-permute-start.10) | collective-permute-done | bytes 262176 | tf_op jit(solution)/shard_map/ppermute | solution.py:430
  131.1 5.0 %collective-permute-start.12 = (bf16[256,256]{1,0:T(8,128)(2,1)S(1)}, bf16[256,256]{1,0:T(8,128)(2,1)S(1)}, u32[]{:S(2)}, u32[]{:S(2)}) collective-permute-start(bf16[256,256]{1,0:T(8,128)(2,1)S(1)} %slice.108), channel_id=1, source_target_pairs={{0,64},{64,128},{128,192},{192,0},{1,65},{65,129},{129,193},{193,1... | collective-permute-start | bytes 393224 | tf_op jit(solution)/shard_map/ppermute | solution.py:434
  136.1 7.8 %first.1.before_hbm = f32[3,2,512,128]{3,2,1,0:T(8,128)} custom-call(s32[4]{0:T(128)S(1)} %pad_add_fusion.info, bf16[4,512,128]{2,1,0:T(8,128)(2,1)S(1)} %all-to-all-done.q_ref, bf16[512,256]{1,0:T(8,128)(2,1)S(1)} %copy-done.1, bf16[512,256]{1,0:T(8,128)(2,1)S(1)} %collective-permute-done.10.kv1, bf16[512,256]{1,0:T(8,128)(2,1)S(1)} %collective-permute-done.11.kv2, ...), custom_call_target="tpu_custom_call" | custom-call | flops 2617245696 | bytes 1638400 | tf_op jit(solution)/shard_map/first/pallas_call | solution.py:300
  144.0 5.9 %rest.1 = bf16[4,576,128]{2,1,0:T(8,128)(2,1)} custom-call(s32[4]{0:T(128)S(1)} %pad_add_fusion.info, bf16[4,512,128]{2,1,0:T(8,128)(2,1)S(1)} %all-to-all-done.q_ref, bf16[256,256]{1,0:T(8,128)(2,1)S(1)} %collective-permute-done.12.kv3, bf16[256,256]{1,0:T(8,128)(2,1)S(1)} %collective-permute-done.13.kv4, f32[3,2,512,128]{3,2,1,0:T(8,128)} %first.1.before_hbm), custom_call_target="tpu_custom_call" | custom-call | flops 805306368 | bytes 1048576 | tf_op jit(solution)/shard_map/rest/pallas_call | solution.py:300
  149.9 4.7 %all-to-all-start.1 = ((bf16[4,576,128]{2,1,0:T(8,128)(2,1)}), bf16[4,576,128]{2,1,0:T(8,128)(2,1)S(1)}, u32[]{:S(2)}, u32[]{:S(2)}) async-start(bf16[4,576,128]{2,1,0:T(8,128)(2,1)} %rest.1), calls=%async_computation.1 | async-start | bytes 1179648 | tf_op jit(solution)/shard_map/all_to_all | solution.py:444
  155.5 4.3 %own.1.own_hbm = f32[2,512,128]{2,1,0:T(8,128)} custom-call(s32[4]{0:T(128)S(1)} %pad_add_fusion.info, bf16[4,512,128]{2,1,0:T(8,128)(2,1)S(1)} %all-to-all-done.q_ref, bf16[512,256]{1,0:T(8,128)(2,1)S(1)} %copy-done.1, bf16[512,256]{1,0:T(8,128)(2,1)S(1)} %collective-permute-done.10.kv1, bf16[512,256]{1,0:T(8,128)(2,1)S(1)} %collective-permute-done.11.kv2, ...), custom_call_target="tpu_custom_call" | custom-call | flops 1140850688 | bytes 1376256 | tf_op jit(solution)/shard_map/own/pallas_call | solution.py:300
  159.8 2.1 %all-to-all-done.1.parts_ref = bf16[4,576,128]{2,1,0:T(8,128)(2,1)S(1)} async-done(((bf16[4,576,128]{2,1,0:T(8,128)(2,1)}), bf16[4,576,128]{2,1,0:T(8,128)(2,1)S(1)}, u32[]{:S(2)}, u32[]{:S(2)}) %all-to-all-start.1) | async-done | bytes 589856 | tf_op jit(solution)/shard_map/all_to_all | solution.py:444
  161.9 2.7 %combine.1 = bf16[2,4,64,128]{3,2,1,0:T(8,128)(2,1)} custom-call(s32[4]{0:T(128)S(1)} %compare_select_fusion.3.slots, s32[4]{0:T(128)S(1)} %pad_add_fusion.info, bf16[4,576,128]{2,1,0:T(8,128)(2,1)S(1)} %all-to-all-done.1.parts_ref, f32[2,512,128]{2,1,0:T(8,128)} %own.1.own_hbm), custom_call_target="tpu_custom_call" | custom-call | tf_op jit(solution)/shard_map/combine/pallas_call | solution.py:362
  (64 shorter events, 20.6 us)
Async XLA Ops:
  6.5 80.6 %copy-start = (bf16[1,226,3072]{2,1,0:T(8,128)(2,1)S(1)}, bf16[1,226,3072]{2,1,0:T(8,128)(2,1)}, u32[]{:S(2)}) copy-start(bf16[1,226,3072]{2,1,0:T(8,128)(2,1)} %param.8) | copy-start | bytes 4165636
  6.5 31.6 %copy-start.6 = (bf16[1,2,4,4,3072]{4,3,2,1,0:T(4,128)(2,1)S(1)}, bf16[1,2,4,4,3072]{4,3,2,1,0:T(4,128)(2,1)}, u32[]{:S(2)}) copy-start(bf16[1,2,4,4,3072]{4,3,2,1,0:T(4,128)(2,1)} %param.7) | copy-start | bytes 589828
  6.5 22.2 %copy-start.11 = (bf16[512,384]{1,0:T(8,128)(2,1)S(1)}, bf16[512,384]{1,0:T(8,128)(2,1)}, u32[]{:S(2)}) copy-start(bf16[512,384]{1,0:T(8,128)(2,1)} %param.10) | copy-start | bytes 1179652
  6.5 22.6 %copy-start.12 = (bf16[3,3,3072]{2,1,0:T(4,128)(2,1)S(1)}, bf16[3,3,3072]{2,1,0:T(4,128)(2,1)}, u32[]{:S(2)}) copy-start(bf16[3,3,3072]{2,1,0:T(4,128)(2,1)} %param.9) | copy-start | bytes 165892
  6.5 89.8 %all-gather.2.cloned.1.call-start = ((), (), s32[]{:S(2)}) async-start(), calls=%async_computation.2 | async-start | bytes 2433024 | tf_op jit(solution)/shard_map/all_gather | solution.py:391
  9.1 6.3 %collective-permute-start = (bf16[1,2,1,4,3072]{4,3,2,1,0:T(4,128)(2,1)S(1)}, bf16[1,2,1,4,3072]{4,3,2,1,0:T(4,128)(2,1)S(1)}, u32[]{:S(2)}, u32[]{:S(2)}) collective-permute-start(bf16[1,2,1,4,3072]{4,3,2,1,0:T(4,128)(2,1)S(1)} %get-tuple-element.29), channel_id=1, source_target_pairs={{0,16},{16,32},{32,48},{48,64},{64,80},{80,96},{96,112},{112,128},... | collective-permute-start | bytes 147464 | tf_op jit(solution)/shard_map/ppermute | solution.py:41
  13.4 6.0 %collective-permute-start.1 = (bf16[1,2,1,4,3072]{4,3,2,1,0:T(4,128)(2,1)S(1)}, bf16[1,2,1,4,3072]{4,3,2,1,0:T(4,128)(2,1)S(1)}, u32[]{:S(2)}, u32[]{:S(2)}) collective-permute-start(bf16[1,2,1,4,3072]{4,3,2,1,0:T(4,128)(2,1)S(1)} %get-tuple-element.30), channel_id=1, source_target_pairs={{16,0},{32,16},{48,32},{64,48},{80,64},{96,80},{112,96},{128,112},... | collective-permute-start | bytes 147464 | tf_op jit(solution)/shard_map/ppermute | solution.py:44
  20.8 9.4 %collective-permute-start.2 = (bf16[1,2,6,1,3072]{4,3,2,1,0:T(2,128)(2,1)S(1)}, bf16[1,2,6,1,3072]{4,3,2,1,0:T(2,128)(2,1)S(1)}, u32[]{:S(2)}, u32[]{:S(2)}) collective-permute-start(bf16[1,2,6,1,3072]{4,3,2,1,0:T(2,128)(2,1)S(1)} %get-tuple-element.27), channel_id=1, source_target_pairs={{0,1},{1,2},{2,3},{3,4},{4,5},{5,6},{6,7},{7,8},{8,9},{9,10},{10,1... | collective-permute-start | bytes 221192 | tf_op jit(solution)/shard_map/ppermute | solution.py:41
  26.8 11.4 %collective-permute-start.3 = (bf16[1,2,6,1,3072]{4,3,2,1,0:T(2,128)(2,1)S(1)}, bf16[1,2,6,1,3072]{4,3,2,1,0:T(2,128)(2,1)S(1)}, u32[]{:S(2)}, u32[]{:S(2)}) collective-permute-start(bf16[1,2,6,1,3072]{4,3,2,1,0:T(2,128)(2,1)S(1)} %get-tuple-element.28), channel_id=1, source_target_pairs={{1,0},{2,1},{3,2},{4,3},{5,4},{6,5},{7,6},{8,7},{9,8},{10,9},{11,1... | collective-permute-start | bytes 221192 | tf_op jit(solution)/shard_map/ppermute | solution.py:44
  62.2 34.1 %copy-start.4 = (bf16[64,3200]{1,0:T(8,128)(2,1)}, bf16[64,3200]{1,0:T(8,128)(2,1)S(1)}, u32[]{:S(2)}) copy-start(bf16[64,3200]{1,0:T(8,128)(2,1)S(1)} %get-tuple-element.25.x1) | copy-start | bytes 1228804
  62.2 34.1 %copy-start.5 = (bf16[64,3200]{1,0:T(8,128)(2,1)}, bf16[64,3200]{1,0:T(8,128)(2,1)S(1)}, u32[]{:S(2)}) copy-start(bf16[64,3200]{1,0:T(8,128)(2,1)S(1)} %get-tuple-element.26.x0) | copy-start | bytes 1228804
  62.2 13.2 %collective-permute-start.5 = (bf16[64,3200]{1,0:T(8,128)(2,1)S(1)}, bf16[64,3200]{1,0:T(8,128)(2,1)S(1)}, u32[]{:S(2)}, u32[]{:S(2)}) collective-permute-start(bf16[64,3200]{1,0:T(8,128)(2,1)S(1)} %get-tuple-element.25.x1), channel_id=1, source_target_pairs={{0,3},{1,0},{2,1},{3,2},{4,7},{5,4},{6,5},{7,6},{8,11},{9,8},{10,9... | collective-permute-start | bytes 1228808 | tf_op jit(solution)/shard_map/ppermute | solution.py:416
  64.2 15.3 %collective-permute-start.4 = (bf16[64,3200]{1,0:T(8,128)(2,1)S(1)}, bf16[64,3200]{1,0:T(8,128)(2,1)}, u32[]{:S(2)}, u32[]{:S(2)}) collective-permute-start(bf16[64,3200]{1,0:T(8,128)(2,1)S(1)} %get-tuple-element.26.x0), channel_id=1, source_target_pairs={{0,1},{1,2},{2,3},{3,0},{4,5},{5,6},{6,7},{7,4},{8,9},{9,10},{10,1... | collective-permute-start | bytes 1228808 | tf_op jit(solution)/shard_map/ppermute | solution.py:416
  69.6 17.7 %collective-permute-start.6 = (bf16[64,3200]{1,0:T(8,128)(2,1)S(1)}, bf16[64,3200]{1,0:T(8,128)(2,1)S(1)}, u32[]{:S(2)}, u32[]{:S(2)}) collective-permute-start(bf16[64,3200]{1,0:T(8,128)(2,1)S(1)} %get-tuple-element.25.x1), channel_id=1, source_target_pairs={{0,1},{1,2},{2,3},{3,0},{4,5},{5,6},{6,7},{7,4},{8,9},{9,10},{10,1... | collective-permute-start | bytes 1228808 | tf_op jit(solution)/shard_map/ppermute | solution.py:417
  73.5 14.1 %collective-permute-start.7 = (bf16[64,3200]{1,0:T(8,128)(2,1)S(1)}, bf16[64,3200]{1,0:T(8,128)(2,1)S(1)}, u32[]{:S(2)}, u32[]{:S(2)}) collective-permute-start(bf16[64,3200]{1,0:T(8,128)(2,1)S(1)} %get-tuple-element.26.x0), channel_id=1, source_target_pairs={{0,3},{1,0},{2,1},{3,2},{4,7},{5,4},{6,5},{7,6},{8,11},{9,8},{10,9... | collective-permute-start | bytes 1228808 | tf_op jit(solution)/shard_map/ppermute | solution.py:417
  79.5 11.5 %collective-permute-start.8 = (bf16[64,3200]{1,0:T(8,128)(2,1)}, bf16[64,3200]{1,0:T(8,128)(2,1)S(1)}, u32[]{:S(2)}, u32[]{:S(2)}) collective-permute-start(bf16[64,3200]{1,0:T(8,128)(2,1)} %collective-permute-done.4.a0), channel_id=1, source_target_pairs={{0,1},{1,2},{2,3},{3,0},{4,5},{5,6},{6,7},{7,4},{8,9},{9,10},{10,1... | collective-permute-start | bytes 1228808 | tf_op jit(solution)/shard_map/ppermute | solution.py:419
  85.2 11.2 %collective-permute-start.9 = (bf16[64,3200]{1,0:T(8,128)(2,1)S(1)}, bf16[64,3200]{1,0:T(8,128)(2,1)}, u32[]{:S(2)}, u32[]{:S(2)}) collective-permute-start(bf16[64,3200]{1,0:T(8,128)(2,1)S(1)} %collective-permute-done.5.b1), channel_id=1, source_target_pairs={{0,3},{1,0},{2,1},{3,2},{4,7},{5,4},{6,5},{7,6},{8,11},{9,8},{10,9... | collective-permute-start | bytes 1228808 | tf_op jit(solution)/shard_map/ppermute | solution.py:419
  103.4 32.7 %copy-start.1 = (bf16[512,256]{1,0:T(8,128)(2,1)S(1)}, bf16[512,256]{1,0:T(8,128)(2,1)}, u32[]{:S(2)}) copy-start(bf16[512,256]{1,0:T(8,128)(2,1)} %get-tuple-element.21.kv0) | copy-start | bytes 786436
  103.4 32.7 %all-to-all-start = ((bf16[4,512,128]{2,1,0:T(8,128)(2,1)}), bf16[4,512,128]{2,1,0:T(8,128)(2,1)S(1)}, u32[]{:S(2)}, u32[]{:S(2)}) async-start(bf16[4,512,128]{2,1,0:T(8,128)(2,1)} %get-tuple-element.20), calls=%async_computation | async-start | bytes 1048576 | tf_op jit(solution)/shard_map/all_to_all | solution.py:429
  108.8 12.1 %collective-permute-start.11 = (bf16[512,256]{1,0:T(8,128)(2,1)}, bf16[512,256]{1,0:T(8,128)(2,1)S(1)}, u32[]{:S(2)}, u32[]{:S(2)}) collective-permute-start(bf16[512,256]{1,0:T(8,128)(2,1)} %get-tuple-element.21.kv0), channel_id=1, source_target_pairs={{0,192},{64,0},{128,64},{192,128},{1,193},{65,1},{129,65},{193,129... | collective-permute-start | bytes 786440 | tf_op jit(solution)/shard_map/ppermute | solution.py:430
  115.7 13.4 %collective-permute-start.10 = (bf16[512,256]{1,0:T(8,128)(2,1)}, bf16[512,256]{1,0:T(8,128)(2,1)S(1)}, u32[]{:S(2)}, u32[]{:S(2)}) collective-permute-start(bf16[512,256]{1,0:T(8,128)(2,1)} %get-tuple-element.21.kv0), channel_id=1, source_target_pairs={{0,64},{64,128},{128,192},{192,0},{1,65},{65,129},{129,193},{193,1... | collective-permute-start | bytes 786440 | tf_op jit(solution)/shard_map/ppermute | solution.py:430
  129.2 14.8 %collective-permute-start.13 = (bf16[256,256]{1,0:T(8,128)(2,1)S(1)}, bf16[256,256]{1,0:T(8,128)(2,1)S(1)}, u32[]{:S(2)}, u32[]{:S(2)}) collective-permute-start(bf16[256,256]{1,0:T(8,128)(2,1)S(1)} %slice.109), channel_id=1, source_target_pairs={{0,192},{64,0},{128,64},{192,128},{1,193},{65,1},{129,65},{193,129... | collective-permute-start | bytes 393224 | tf_op jit(solution)/shard_map/ppermute | solution.py:435
  131.1 12.9 %collective-permute-start.12 = (bf16[256,256]{1,0:T(8,128)(2,1)S(1)}, bf16[256,256]{1,0:T(8,128)(2,1)S(1)}, u32[]{:S(2)}, u32[]{:S(2)}) collective-permute-start(bf16[256,256]{1,0:T(8,128)(2,1)S(1)} %slice.108), channel_id=1, source_target_pairs={{0,64},{64,128},{128,192},{192,0},{1,65},{65,129},{129,193},{193,1... | collective-permute-start | bytes 393224 | tf_op jit(solution)/shard_map/ppermute | solution.py:434
  149.9 12.0 %all-to-all-start.1 = ((bf16[4,576,128]{2,1,0:T(8,128)(2,1)}), bf16[4,576,128]{2,1,0:T(8,128)(2,1)S(1)}, u32[]{:S(2)}, u32[]{:S(2)}) async-start(bf16[4,576,128]{2,1,0:T(8,128)(2,1)} %rest.1), calls=%async_computation.1 | async-start | bytes 1179648 | tf_op jit(solution)/shard_map/all_to_all | solution.py:444
  (6 other events, 32.1 us)
Sparse Core Ops, SparseCore 0:
  9.5 72.9 all-gather.1

commit v9 on v8

--- a/solution.py
+++ b/solution.py
@@ -56,7 +56,7 @@
 def project_kernel(
     slots, x0, x1, a0, a1, b0, b1, c0, c1, text, w_hbm,
     q_out, kv_out, text_out,
-    held, mod, extra, normed, w_ref, q, kv, in_sems, w_sem, out_sems,
+    held, mod, extra, normed, w_ref, in_sems, w_sem,
 ):
     half = x0.shape[0]
     rows = 2 * half
@@ -111,7 +111,6 @@
         result = centered * lax.rsqrt(spread + 1e-06) * gain + shift
         normed[at : at + rows_in.shape[0], :] = result.astype(BF)
 
-    sends = []
     norm(text[...], 4 * rows)
     for part in range(2):
         first = 2 * rows * part
@@ -125,20 +124,10 @@
             fetch.wait()
         out = jnp.dot(normed[first:last, :], w_ref[...], preferred_element_type=F32).astype(BF)
         span = pl.ds(first, 2 * rows)
-        q[span, :] = out[: 2 * rows, :128]
-        kv[span, :] = out[: 2 * rows, 128:]
-        new = [pltpu.make_async_copy(kv.at[span, :], kv_out.at[span, :], out_sems.at[part, 4])]
-        for i in range(4):
-            new.append(
-                pltpu.make_async_copy(q.at[span, :], q_out.at[i, span, :], out_sems.at[part, i])
-            )
-        for send in new:
-            send.start()
-        sends += new
+        q_out[span, :] = out[: 2 * rows, :128]
+        kv_out[span, :] = out[: 2 * rows, 128:]
         if part:
             text_out[...] = out[2 * rows :, 128:]
-    for send in sends:
-        send.wait()
 
 
 def project(slots, pieces, text, weight):
@@ -148,23 +137,20 @@
     return pl.pallas_call(
         project_kernel,
         out_shape=[
-            pltpu.MemorySpace.HBM((4, 4 * rows, 128), BF),
-            pltpu.MemorySpace.HBM((4 * rows, 256), BF),
+            jax.ShapeDtypeStruct((4 * rows, 128), BF),
+            jax.ShapeDtypeStruct((4 * rows, 256), BF),
             jax.ShapeDtypeStruct((text.shape[0], 256), BF),
         ],
         in_specs=[pl.BlockSpec(memory_space=pltpu.SMEM)] + [hbm()] * 8 + [vmem(), hbm()],
-        out_specs=[hbm(), hbm(), vmem()],
+        out_specs=[vmem()] * 3,
         scratch_shapes=[
             pltpu.VMEM((4 * rows, width), BF),
             pltpu.VMEM((2, width), F32),
             pltpu.VMEM((4 * rows, 128), BF),
             pltpu.VMEM((4 * rows + text.shape[0], width), BF),
             pltpu.VMEM(weight.shape, BF),
-            pltpu.VMEM((4 * rows, 128), BF),
-            pltpu.VMEM((4 * rows, 256), BF),
             pltpu.SemaphoreType.DMA((2, 8)),
             pltpu.SemaphoreType.DMA,
-            pltpu.SemaphoreType.DMA((2, 5)),
         ],
         compiler_params=params(28),
         cost_estimate=pl.CostEstimate(
@@ -221,11 +207,10 @@
     return weighted / total, jnp.where(lane < HD, tops[0], tops[1]) + jnp.log(total) * LOG2E
 
 
-def first_kernel(info, q_ref, kv0, kv1, kv2, text_kv, o_ref, keys, values, held, sems):
+def first_kernel(info, q1, q23, kv0, kv1, kv2, text_kv, o_ref, keys, values, held, sems):
     load_keys((kv0, kv1, kv2), text_kv, keys, values)
     sends = []
-    for i in range(3):
-        q = q_ref[jnp.bitwise_xor(info[3], i + 1)]
+    for i, q in enumerate((q1[...], q23[0], q23[1])):
         held[i, 0], held[i, 1] = softmax_block(info, q, keys, values, True)
         sends.append(pltpu.make_async_copy(held.at[i], o_ref.at[i], sems.at[i]))
         sends[-1].start()
@@ -234,21 +219,21 @@
 
 
 def rest_kernel(
-    info, q_ref, kv3, kv4, before_hbm, o_ref, keys, values, held, before, sems, in_sems
+    info, q1, q23, kv3, kv4, before_hbm, o_ref, keys, values, held, before, sems, in_sems
 ):
     fetches = [
         pltpu.make_async_copy(before_hbm.at[i], before.at[i], in_sems.at[i]) for i in range(3)
     ]
     for fetch in fetches:
         fetch.start()
-    count = q_ref.shape[1]
+    count = q1.shape[0]
     load_keys((kv3, kv4), None, keys, values)
     term = lax.broadcasted_iota(jnp.int32, (STAT_ROWS, 128), 0)
     lane = lax.broadcasted_iota(jnp.int32, (STAT_ROWS, 128), 1)
     sends = []
-    for i in range(3):
+    for i, q in enumerate((q1[...], q23[0], q23[1])):
         member = jnp.bitwise_xor(info[3], i + 1)
-        out, lse = softmax_block(info, q_ref[member], keys, values, False)
+        out, lse = softmax_block(info, q, keys, values, False)
         fetches[i].wait()
         earlier = before[i, 1]
         top = jnp.maximum(lse, earlier)
@@ -275,7 +260,7 @@
 
 def own_kernel(info, q_ref, kv0, kv1, kv2, kv3, kv4, text_kv, o_ref, keys, values, held, sems):
     load_keys((kv0, kv1, kv2, kv3, kv4), text_kv, keys, values)
-    held[0], held[1] = softmax_block(info, q_ref[info[3]], keys, values, True)
+    held[0], held[1] = softmax_block(info, q_ref[...], keys, values, True)
     copy = pltpu.make_async_copy(held, o_ref, sems.at[0])
     copy.start()
     copy.wait()
@@ -283,8 +268,8 @@
 
 def attend(kernel, name, peers, out_shape, held, info, qs, blocks, text_kv=None, before=None):
     keys = sum(block.shape[0] for block in blocks) + (0 if text_kv is None else 128)
-    count = qs.shape[1]
-    operands = [qs, *blocks] + ([] if text_kv is None else [text_kv])
+    count = qs[0].shape[0]
+    operands = [*qs, *blocks] + ([] if text_kv is None else [text_kv])
     specs = [pl.BlockSpec(memory_space=pltpu.SMEM)] + [vmem()] * len(operands)
     scratch = [
         pltpu.VMEM((keys, 128), BF),
@@ -426,7 +411,10 @@
     text_rows = lax.dynamic_slice_in_dim(prompt_rows[0], start, TEXT_PART, axis=0)
     queries, kv, text_kv = project(slots, pieces, text_rows, weight)
     group = ("v", "zl")
-    qs = lax.all_to_all(queries, group, split_axis=0, concat_axis=0, tiled=True)
+    swap = [(0, 1), (1, 0)]
+    beside = lax.ppermute(queries, "zl", swap)
+    across = lax.ppermute(jnp.stack([queries, beside]), "v", swap)
+    qs = [beside, across]
     near = [lax.ppermute(kv, "u", up), lax.ppermute(kv, "u", down)]
     near = lax.optimization_barrier(near)
     count = kv.shape[0]
@@ -444,7 +432,7 @@
     parts = lax.all_to_all(parts, group, split_axis=0, concat_axis=0, tiled=True)
     shape = (2, count, 128)
     own = jax.ShapeDtypeStruct(shape, F32)
-    own = attend(own_kernel, "own", 1, own, shape, info, qs, [kv, *near, *far], text_kv)
+    own = attend(own_kernel, "own", 1, own, shape, info, [queries], [kv, *near, *far], text_kv)
     shape = (frames, tile_h, 16 * tile_w, head_width)
     return combine(slots, info, parts, own, shape)[None]
 

time: 172 us -> 171 us (level)
  waiting for transfers between devices: 37.7 us -> 35 us
  starting transfers between devices: 60.2 us -> 62.2 us
    ppermute x0 -> x2, starting transfers between devices: none -> 10.5 us  [the longest x1 5.9 us: on_device(): beside = lax.ppermute(queries, 'zl', swap)]
    all_to_all x1 -> x0, starting transfers between devices: 5.41 us -> none  [on_device(): qs = lax.all_to_all(queries, group, split_axis=0, concat_axis=0, tiled=True)]
    ppermute x2, waiting for transfers between devices: 10.7 us -> 7.56 us  [on_device(): near = [lax.ppermute(kv, 'u', up), lax.ppermute(kv, 'u', down)]]
    ppermute x2, starting transfers between devices: 8.81 us -> 6.74 us  [on_device(): near = [lax.ppermute(kv, 'u', up), lax.ppermute(kv, 'u', down)]]
  transfers between devices with their start and end apart: 17 -> 18, of which waited for: 10 -> 9; matrix products, arithmetic and copies ran while one was open for 3% -> 3% of each run, Pallas kernels for 7% -> 7%
where the time goes in v9:
time: 171 us; the launch traced here: 169 us
  starting transfers between devices  62.2 us (36%)
  waiting for transfers between devices  35 us (20%)
  Pallas kernels  26.9 us (16%)
  blocking collectives  22.5 us (13%)
  between operations  15.1 us (9%)
  local copies, waits for them, and re-layouts  4.31 us (3%)
  other arithmetic  2.85 us (2%)
    all_gather x1, blocking collectives, on_device(): tokens = lax.all_gather(peg, 'zh', axis=0, tiled=True)  22.5 us
    pallas_call x3, Pallas kernels, attend(): pl.pallas_call(kernel, out_shape=pltpu.MemorySpace.HBM(out_shape.shape, o...  18 us
    ppermute x2, waiting for transfers between devices, with_halo(): lax.ppermute(lax.slice_in_dim(block, 0, width, axis=dim), axis, backward)  11.9 us
    ppermute x2, starting transfers between devices, with_halo(): lax.ppermute(lax.slice_in_dim(block, block.shape[dim] - width, None, axis...  10.3 us
    ppermute x2, starting transfers between devices, on_device(): c0, c1 = (lax.ppermute(a0, 'x', up), lax.ppermute(b1, 'x', down))  7.61 us
    ppermute x2, waiting for transfers between devices, on_device(): near = [lax.ppermute(kv, 'u', up), lax.ppermute(kv, 'u', down)]  7.56 us
    ppermute x2, waiting for transfers between devices, on_device(): c0, c1 = (lax.ppermute(a0, 'x', up), lax.ppermute(b1, 'x', down))  7.56 us
    ppermute x2, starting transfers between devices, on_device(): a0, b1 = (lax.ppermute(low, 'x', up), lax.ppermute(high, 'x', down))  7.34 us
  transfers between devices with their start and end apart: 18, of which 9 were waited for; matrix products, arithmetic and copies ran while one was open for 3% of the time, Pallas kernels for 7%

profile of v9, /device:TPU:6, one launch (start us, length us, event | category | flops | bytes accessed | tf_op | source)
XLA Modules:
  0.0 169.1 jit_solution(5265604700695482158)
XLA Ops:
  9.1 4.3 %collective-permute-start = (bf16[1,2,1,4,3072]{4,3,2,1,0:T(4,128)(2,1)S(1)}, bf16[1,2,1,4,3072]{4,3,2,1,0:T(4,128)(2,1)S(1)}, u32[]{:S(2)}, u32[]{:S(2)}) collective-permute-start(bf16[1,2,1,4,3072]{4,3,2,1,0:T(4,128)(2,1)S(1)} %get-tuple-element.29), channel_id=1, source_target_pairs={{0,16},{16,32},{32,48},{48,64},{64,80},{80,96},{96,112},{112,128},... | collective-permute-start | bytes 147464 | tf_op jit(solution)/shard_map/ppermute | solution.py:41
  15.5 3.9 %collective-permute-done.1 = bf16[1,2,1,4,3072]{4,3,2,1,0:T(4,128)(2,1)S(1)} collective-permute-done((bf16[1,2,1,4,3072]{4,3,2,1,0:T(4,128)(2,1)S(1)}, bf16[1,2,1,4,3072]{4,3,2,1,0:T(4,128)(2,1)S(1)}, u32[]{:S(2)}, u32[]{:S(2)}) %collective-permute-start.1) | collective-permute-done | bytes 49184 | tf_op jit(solution)/shard_map/ppermute | solution.py:44
  20.8 6.0 %collective-permute-start.2 = (bf16[1,2,6,1,3072]{4,3,2,1,0:T(2,128)(2,1)S(1)}, bf16[1,2,6,1,3072]{4,3,2,1,0:T(2,128)(2,1)S(1)}, u32[]{:S(2)}, u32[]{:S(2)}) collective-permute-start(bf16[1,2,6,1,3072]{4,3,2,1,0:T(2,128)(2,1)S(1)} %get-tuple-element.27), channel_id=1, source_target_pairs={{0,1},{1,2},{2,3},{3,4},{4,5},{5,6},{6,7},{7,8},{8,9},{9,10},{10,1... | collective-permute-start | bytes 221192 | tf_op jit(solution)/shard_map/ppermute | solution.py:41
  30.2 8.0 %collective-permute-done.3 = bf16[1,2,6,1,3072]{4,3,2,1,0:T(2,128)(2,1)S(1)} collective-permute-done((bf16[1,2,6,1,3072]{4,3,2,1,0:T(2,128)(2,1)S(1)}, bf16[1,2,6,1,3072]{4,3,2,1,0:T(2,128)(2,1)S(1)}, u32[]{:S(2)}, u32[]{:S(2)}) %collective-permute-start.3) | collective-permute-done | bytes 73760 | tf_op jit(solution)/shard_map/ppermute | solution.py:44
  39.6 22.5 %all_gather.6 = bf16[128,3200]{1,0:T(8,128)(2,1)S(1)} all-gather(bf16[32,3200]{1,0:T(8,128)(2,1)S(1)} %pad_maximum_fusion.2), channel_id=1, replica_groups=mesh['item'=2,'u'=4,'v'=2,'zl'=2,'zh'=4,'x'=4] {'zh'}, dimensions={0}, use_global_device_ids=true | all-gather | bytes 1024000 | tf_op jit(solution)/shard_map/all_gather | solution.py:396
  64.2 5.4 %collective-permute-start.4 = (bf16[64,3200]{1,0:T(8,128)(2,1)S(1)}, bf16[64,3200]{1,0:T(8,128)(2,1)}, u32[]{:S(2)}, u32[]{:S(2)}) collective-permute-start(bf16[64,3200]{1,0:T(8,128)(2,1)S(1)} %get-tuple-element.26.x0), channel_id=1, source_target_pairs={{0,1},{1,2},{2,3},{3,0},{4,5},{5,6},{6,7},{7,4},{8,9},{9,10},{10,1... | collective-permute-start | bytes 1228808 | tf_op jit(solution)/shard_map/ppermute | solution.py:401
  69.6 3.9 %collective-permute-start.6 = (bf16[64,3200]{1,0:T(8,128)(2,1)S(1)}, bf16[64,3200]{1,0:T(8,128)(2,1)S(1)}, u32[]{:S(2)}, u32[]{:S(2)}) collective-permute-start(bf16[64,3200]{1,0:T(8,128)(2,1)S(1)} %get-tuple-element.25.x1), channel_id=1, source_target_pairs={{0,1},{1,2},{2,3},{3,0},{4,5},{5,6},{6,7},{7,4},{8,9},{9,10},{10,1... | collective-permute-start | bytes 1228808 | tf_op jit(solution)/shard_map/ppermute | solution.py:402
  75.5 4.0 %collective-permute-done.4.a0 = bf16[64,3200]{1,0:T(8,128)(2,1)} collective-permute-done((bf16[64,3200]{1,0:T(8,128)(2,1)S(1)}, bf16[64,3200]{1,0:T(8,128)(2,1)}, u32[]{:S(2)}, u32[]{:S(2)}) %collective-permute-start.4) | collective-permute-done | bytes 409632 | tf_op jit(solution)/shard_map/ppermute | solution.py:401
  79.5 5.7 %collective-permute-start.8 = (bf16[64,3200]{1,0:T(8,128)(2,1)}, bf16[64,3200]{1,0:T(8,128)(2,1)S(1)}, u32[]{:S(2)}, u32[]{:S(2)}) collective-permute-start(bf16[64,3200]{1,0:T(8,128)(2,1)} %collective-permute-done.4.a0), channel_id=1, source_target_pairs={{0,1},{1,2},{2,3},{3,0},{4,5},{5,6},{6,7},{7,4},{8,9},{9,10},{10,1... | collective-permute-start | bytes 1228808 | tf_op jit(solution)/shard_map/ppermute | solution.py:404
  88.0 2.9 %collective-permute-done.8.c0 = bf16[64,3200]{1,0:T(8,128)(2,1)S(1)} collective-permute-done((bf16[64,3200]{1,0:T(8,128)(2,1)}, bf16[64,3200]{1,0:T(8,128)(2,1)S(1)}, u32[]{:S(2)}, u32[]{:S(2)}) %collective-permute-start.8) | collective-permute-done | bytes 409632 | tf_op jit(solution)/shard_map/ppermute | solution.py:404
  91.7 4.6 %collective-permute-done.9.c1 = bf16[64,3200]{1,0:T(8,128)(2,1)} collective-permute-done((bf16[64,3200]{1,0:T(8,128)(2,1)S(1)}, bf16[64,3200]{1,0:T(8,128)(2,1)}, u32[]{:S(2)}, u32[]{:S(2)}) %collective-permute-start.9) | collective-permute-done | bytes 409632 | tf_op jit(solution)/shard_map/ppermute | solution.py:404
  96.4 6.2 %project.1 = (bf16[512,128]{1,0:T(8,128)(2,1)S(1)}, bf16[512,256]{1,0:T(8,128)(2,1)S(1)}, bf16[64,256]{1,0:T(8,128)(2,1)S(1)}) custom-call(s32[4]{0:T(128)S(1)} %compare_select_fusion.3.slots, bf16[64,3200]{1,0:T(8,128)(2,1)} %copy-done.2, bf16[64,3200]{1,0:T(8,128)(2,1)} %copy-done.1, bf16[64,3200]{1,0:T(8,128)(2,1)} %collective-permute-done.4.a0, ...), custom_call_target="tpu_custom_call" | custom-call | flops 1207959552 | bytes 5636096 | tf_op jit(solution)/shard_map/project/pallas_call | solution.py:137
  102.6 5.9 %collective-permute-start.10 = (bf16[512,128]{1,0:T(8,128)(2,1)S(1)}, bf16[512,128]{1,0:T(8,128)(2,1)S(1)}, u32[]{:S(2)}, u32[]{:S(2)}) collective-permute-start(bf16[512,128]{1,0:T(8,128)(2,1)S(1)} %get-tuple-element.20.q_ref), channel_id=1, source_target_pairs={{0,16},{16,0},{1,17},{17,1},{2,18},{18,2},{3,19},{19,3},{4,20},{20... | collective-permute-start | bytes 393224 | tf_op jit(solution)/shard_map/ppermute | solution.py:415
  108.5 2.2 %collective-permute-start.13 = (bf16[512,256]{1,0:T(8,128)(2,1)S(1)}, bf16[512,256]{1,0:T(8,128)(2,1)S(1)}, u32[]{:S(2)}, u32[]{:S(2)}) collective-permute-start(bf16[512,256]{1,0:T(8,128)(2,1)S(1)} %get-tuple-element.21.kv0), channel_id=1, source_target_pairs={{0,192},{64,0},{128,64},{192,128},{1,193},{65,1},{129,65},{193,129... | collective-permute-start | bytes 786440 | tf_op jit(solution)/shard_map/ppermute | solution.py:418
  110.7 4.6 %collective-permute-start.12 = (bf16[512,256]{1,0:T(8,128)(2,1)S(1)}, bf16[512,256]{1,0:T(8,128)(2,1)S(1)}, u32[]{:S(2)}, u32[]{:S(2)}) collective-permute-start(bf16[512,256]{1,0:T(8,128)(2,1)S(1)} %get-tuple-element.21.kv0), channel_id=1, source_target_pairs={{0,64},{64,128},{128,192},{192,0},{1,65},{65,129},{129,193},{193,1... | collective-permute-start | bytes 786440 | tf_op jit(solution)/shard_map/ppermute | solution.py:418
  115.3 4.6 %collective-permute-start.11 = (bf16[2,512,128]{2,1,0:T(8,128)(2,1)S(1)}, bf16[2,512,128]{2,1,0:T(8,128)(2,1)S(1)}, u32[]{:S(2)}, u32[]{:S(2)}) collective-permute-start(bf16[2,512,128]{2,1,0:T(8,128)(2,1)S(1)} %pad_maximum_fusion.1), channel_id=1, source_target_pairs={{0,32},{32,0},{1,33},{33,1},{2,34},{34,2},{3,35},{35,3},{4,36},{36... | collective-permute-start | bytes 786440 | tf_op jit(solution)/shard_map/ppermute | solution.py:416
  120.6 7.6 %collective-permute-done.12.kv1 = bf16[512,256]{1,0:T(8,128)(2,1)S(1)} collective-permute-done((bf16[512,256]{1,0:T(8,128)(2,1)S(1)}, bf16[512,256]{1,0:T(8,128)(2,1)S(1)}, u32[]{:S(2)}, u32[]{:S(2)}) %collective-permute-start.12) | collective-permute-done | bytes 262176 | tf_op jit(solution)/shard_map/ppermute | solution.py:418
  130.1 5.0 %collective-permute-start.14 = (bf16[256,256]{1,0:T(8,128)(2,1)S(1)}, bf16[256,256]{1,0:T(8,128)(2,1)S(1)}, u32[]{:S(2)}, u32[]{:S(2)}) collective-permute-start(bf16[256,256]{1,0:T(8,128)(2,1)S(1)} %slice.108), channel_id=1, source_target_pairs={{0,64},{64,128},{128,192},{192,0},{1,65},{65,129},{129,193},{193,1... | collective-permute-start | bytes 393224 | tf_op jit(solution)/shard_map/ppermute | solution.py:422
  135.2 7.8 %first.1.before_hbm = f32[3,2,512,128]{3,2,1,0:T(8,128)} custom-call(s32[4]{0:T(128)S(1)} %pad_add_fusion.info, bf16[512,128]{1,0:T(8,128)(2,1)S(1)} %collective-permute-done.10.q1, bf16[2,512,128]{2,1,0:T(8,128)(2,1)S(1)} %collective-permute-done.11.q23, bf16[512,256]{1,0:T(8,128)(2,1)S(1)} %get-tuple-element.21.kv0, ...), custom_call_target="tpu_custom_call" | custom-call | flops 2617245696 | bytes 1638400 | tf_op jit(solution)/shard_map/first/pallas_call | solution.py:285
  143.0 5.8 %rest.1 = bf16[4,576,128]{2,1,0:T(8,128)(2,1)} custom-call(s32[4]{0:T(128)S(1)} %pad_add_fusion.info, bf16[512,128]{1,0:T(8,128)(2,1)S(1)} %collective-permute-done.10.q1, bf16[2,512,128]{2,1,0:T(8,128)(2,1)S(1)} %collective-permute-done.11.q23, bf16[256,256]{1,0:T(8,128)(2,1)S(1)} %collective-permute-done.14.kv3, ...), custom_call_target="tpu_custom_call" | custom-call | flops 805306368 | bytes 1048576 | tf_op jit(solution)/shard_map/rest/pallas_call | solution.py:285
  148.8 3.7 %all-to-all-start = ((bf16[4,576,128]{2,1,0:T(8,128)(2,1)}), bf16[4,576,128]{2,1,0:T(8,128)(2,1)S(1)}, u32[]{:S(2)}, u32[]{:S(2)}) async-start(bf16[4,576,128]{2,1,0:T(8,128)(2,1)} %rest.1), calls=%async_computation | async-start | bytes 1179648 | tf_op jit(solution)/shard_map/all_to_all | solution.py:432
  152.6 4.3 %own.1.own_hbm = f32[2,512,128]{2,1,0:T(8,128)} custom-call(s32[4]{0:T(128)S(1)} %pad_add_fusion.info, bf16[512,128]{1,0:T(8,128)(2,1)S(1)} %get-tuple-element.20.q_ref, bf16[512,256]{1,0:T(8,128)(2,1)S(1)} %get-tuple-element.21.kv0, bf16[512,256]{1,0:T(8,128)(2,1)S(1)} %collective-permute-done.12.kv1, bf16[512,256]{1,0:T(8,128)(2,1)S(1)} %collective-permute-done.13.kv2, ...), custom_call_target="tpu_custom_call" | custom-call | flops 1140850688 | bytes 1376256 | tf_op jit(solution)/shard_map/own/pallas_call | solution.py:285
  156.9 2.6 %all-to-all-done.parts_ref = bf16[4,576,128]{2,1,0:T(8,128)(2,1)S(1)} async-done(((bf16[4,576,128]{2,1,0:T(8,128)(2,1)}), bf16[4,576,128]{2,1,0:T(8,128)(2,1)S(1)}, u32[]{:S(2)}, u32[]{:S(2)}) %all-to-all-start) | async-done | bytes 589856 | tf_op jit(solution)/shard_map/all_to_all | solution.py:432
  159.5 2.7 %combine.1 = bf16[2,4,64,128]{3,2,1,0:T(8,128)(2,1)} custom-call(s32[4]{0:T(128)S(1)} %compare_select_fusion.3.slots, s32[4]{0:T(128)S(1)} %pad_add_fusion.info, bf16[4,576,128]{2,1,0:T(8,128)(2,1)S(1)} %all-to-all-done.parts_ref, f32[2,512,128]{2,1,0:T(8,128)} %own.1.own_hbm), custom_call_target="tpu_custom_call" | custom-call | tf_op jit(solution)/shard_map/combine/pallas_call | solution.py:347
  (61 shorter events, 19.7 us)
Async XLA Ops:
  6.5 80.6 %copy-start = (bf16[1,226,3072]{2,1,0:T(8,128)(2,1)S(1)}, bf16[1,226,3072]{2,1,0:T(8,128)(2,1)}, u32[]{:S(2)}) copy-start(bf16[1,226,3072]{2,1,0:T(8,128)(2,1)} %param.8) | copy-start | bytes 4165636
  6.5 31.6 %copy-start.3 = (bf16[1,2,4,4,3072]{4,3,2,1,0:T(4,128)(2,1)S(1)}, bf16[1,2,4,4,3072]{4,3,2,1,0:T(4,128)(2,1)}, u32[]{:S(2)}) copy-start(bf16[1,2,4,4,3072]{4,3,2,1,0:T(4,128)(2,1)} %param.7) | copy-start | bytes 589828
  6.5 22.2 %copy-start.8 = (bf16[512,384]{1,0:T(8,128)(2,1)S(1)}, bf16[512,384]{1,0:T(8,128)(2,1)}, u32[]{:S(2)}) copy-start(bf16[512,384]{1,0:T(8,128)(2,1)} %param.10) | copy-start | bytes 1179652
  6.5 22.6 %copy-start.9 = (bf16[3,3,3072]{2,1,0:T(4,128)(2,1)S(1)}, bf16[3,3,3072]{2,1,0:T(4,128)(2,1)}, u32[]{:S(2)}) copy-start(bf16[3,3,3072]{2,1,0:T(4,128)(2,1)} %param.9) | copy-start | bytes 165892
  6.5 89.8 %all-gather.2.cloned.1.call-start = ((), (), s32[]{:S(2)}) async-start(), calls=%async_computation.1 | async-start | bytes 2433024 | tf_op jit(solution)/shard_map/all_gather | solution.py:376
  9.1 6.3 %collective-permute-start = (bf16[1,2,1,4,3072]{4,3,2,1,0:T(4,128)(2,1)S(1)}, bf16[1,2,1,4,3072]{4,3,2,1,0:T(4,128)(2,1)S(1)}, u32[]{:S(2)}, u32[]{:S(2)}) collective-permute-start(bf16[1,2,1,4,3072]{4,3,2,1,0:T(4,128)(2,1)S(1)} %get-tuple-element.29), channel_id=1, source_target_pairs={{0,16},{16,32},{32,48},{48,64},{64,80},{80,96},{96,112},{112,128},... | collective-permute-start | bytes 147464 | tf_op jit(solution)/shard_map/ppermute | solution.py:41
  13.4 6.0 %collective-permute-start.1 = (bf16[1,2,1,4,3072]{4,3,2,1,0:T(4,128)(2,1)S(1)}, bf16[1,2,1,4,3072]{4,3,2,1,0:T(4,128)(2,1)S(1)}, u32[]{:S(2)}, u32[]{:S(2)}) collective-permute-start(bf16[1,2,1,4,3072]{4,3,2,1,0:T(4,128)(2,1)S(1)} %get-tuple-element.30), channel_id=1, source_target_pairs={{16,0},{32,16},{48,32},{64,48},{80,64},{96,80},{112,96},{128,112},... | collective-permute-start | bytes 147464 | tf_op jit(solution)/shard_map/ppermute | solution.py:44
  20.8 9.4 %collective-permute-start.2 = (bf16[1,2,6,1,3072]{4,3,2,1,0:T(2,128)(2,1)S(1)}, bf16[1,2,6,1,3072]{4,3,2,1,0:T(2,128)(2,1)S(1)}, u32[]{:S(2)}, u32[]{:S(2)}) collective-permute-start(bf16[1,2,6,1,3072]{4,3,2,1,0:T(2,128)(2,1)S(1)} %get-tuple-element.27), channel_id=1, source_target_pairs={{0,1},{1,2},{2,3},{3,4},{4,5},{5,6},{6,7},{7,8},{8,9},{9,10},{10,1... | collective-permute-start | bytes 221192 | tf_op jit(solution)/shard_map/ppermute | solution.py:41
  26.8 11.4 %collective-permute-start.3 = (bf16[1,2,6,1,3072]{4,3,2,1,0:T(2,128)(2,1)S(1)}, bf16[1,2,6,1,3072]{4,3,2,1,0:T(2,128)(2,1)S(1)}, u32[]{:S(2)}, u32[]{:S(2)}) collective-permute-start(bf16[1,2,6,1,3072]{4,3,2,1,0:T(2,128)(2,1)S(1)} %get-tuple-element.28), channel_id=1, source_target_pairs={{1,0},{2,1},{3,2},{4,3},{5,4},{6,5},{7,6},{8,7},{9,8},{10,9},{11,1... | collective-permute-start | bytes 221192 | tf_op jit(solution)/shard_map/ppermute | solution.py:44
  62.2 34.1 %copy-start.2 = (bf16[64,3200]{1,0:T(8,128)(2,1)}, bf16[64,3200]{1,0:T(8,128)(2,1)S(1)}, u32[]{:S(2)}) copy-start(bf16[64,3200]{1,0:T(8,128)(2,1)S(1)} %get-tuple-element.26.x0) | copy-start | bytes 1228804
  62.2 34.1 %copy-start.1 = (bf16[64,3200]{1,0:T(8,128)(2,1)}, bf16[64,3200]{1,0:T(8,128)(2,1)S(1)}, u32[]{:S(2)}) copy-start(bf16[64,3200]{1,0:T(8,128)(2,1)S(1)} %get-tuple-element.25.x1) | copy-start | bytes 1228804
  62.2 13.2 %collective-permute-start.5 = (bf16[64,3200]{1,0:T(8,128)(2,1)S(1)}, bf16[64,3200]{1,0:T(8,128)(2,1)S(1)}, u32[]{:S(2)}, u32[]{:S(2)}) collective-permute-start(bf16[64,3200]{1,0:T(8,128)(2,1)S(1)} %get-tuple-element.25.x1), channel_id=1, source_target_pairs={{0,3},{1,0},{2,1},{3,2},{4,7},{5,4},{6,5},{7,6},{8,11},{9,8},{10,9... | collective-permute-start | bytes 1228808 | tf_op jit(solution)/shard_map/ppermute | solution.py:401
  64.2 15.3 %collective-permute-start.4 = (bf16[64,3200]{1,0:T(8,128)(2,1)S(1)}, bf16[64,3200]{1,0:T(8,128)(2,1)}, u32[]{:S(2)}, u32[]{:S(2)}) collective-permute-start(bf16[64,3200]{1,0:T(8,128)(2,1)S(1)} %get-tuple-element.26.x0), channel_id=1, source_target_pairs={{0,1},{1,2},{2,3},{3,0},{4,5},{5,6},{6,7},{7,4},{8,9},{9,10},{10,1... | collective-permute-start | bytes 1228808 | tf_op jit(solution)/shard_map/ppermute | solution.py:401
  69.6 17.7 %collective-permute-start.6 = (bf16[64,3200]{1,0:T(8,128)(2,1)S(1)}, bf16[64,3200]{1,0:T(8,128)(2,1)S(1)}, u32[]{:S(2)}, u32[]{:S(2)}) collective-permute-start(bf16[64,3200]{1,0:T(8,128)(2,1)S(1)} %get-tuple-element.25.x1), channel_id=1, source_target_pairs={{0,1},{1,2},{2,3},{3,0},{4,5},{5,6},{6,7},{7,4},{8,9},{9,10},{10,1... | collective-permute-start | bytes 1228808 | tf_op jit(solution)/shard_map/ppermute | solution.py:402
  73.5 14.1 %collective-permute-start.7 = (bf16[64,3200]{1,0:T(8,128)(2,1)S(1)}, bf16[64,3200]{1,0:T(8,128)(2,1)S(1)}, u32[]{:S(2)}, u32[]{:S(2)}) collective-permute-start(bf16[64,3200]{1,0:T(8,128)(2,1)S(1)} %get-tuple-element.26.x0), channel_id=1, source_target_pairs={{0,3},{1,0},{2,1},{3,2},{4,7},{5,4},{6,5},{7,6},{8,11},{9,8},{10,9... | collective-permute-start | bytes 1228808 | tf_op jit(solution)/shard_map/ppermute | solution.py:402
  79.5 11.5 %collective-permute-start.8 = (bf16[64,3200]{1,0:T(8,128)(2,1)}, bf16[64,3200]{1,0:T(8,128)(2,1)S(1)}, u32[]{:S(2)}, u32[]{:S(2)}) collective-permute-start(bf16[64,3200]{1,0:T(8,128)(2,1)} %collective-permute-done.4.a0), channel_id=1, source_target_pairs={{0,1},{1,2},{2,3},{3,0},{4,5},{5,6},{6,7},{7,4},{8,9},{9,10},{10,1... | collective-permute-start | bytes 1228808 | tf_op jit(solution)/shard_map/ppermute | solution.py:404
  85.2 11.2 %collective-permute-start.9 = (bf16[64,3200]{1,0:T(8,128)(2,1)S(1)}, bf16[64,3200]{1,0:T(8,128)(2,1)}, u32[]{:S(2)}, u32[]{:S(2)}) collective-permute-start(bf16[64,3200]{1,0:T(8,128)(2,1)S(1)} %collective-permute-done.5.b1), channel_id=1, source_target_pairs={{0,3},{1,0},{2,1},{3,2},{4,7},{5,4},{6,5},{7,6},{8,11},{9,8},{10,9... | collective-permute-start | bytes 1228808 | tf_op jit(solution)/shard_map/ppermute | solution.py:404
  102.6 12.7 %collective-permute-start.10 = (bf16[512,128]{1,0:T(8,128)(2,1)S(1)}, bf16[512,128]{1,0:T(8,128)(2,1)S(1)}, u32[]{:S(2)}, u32[]{:S(2)}) collective-permute-start(bf16[512,128]{1,0:T(8,128)(2,1)S(1)} %get-tuple-element.20.q_ref), channel_id=1, source_target_pairs={{0,16},{16,0},{1,17},{17,1},{2,18},{18,2},{3,19},{19,3},{4,20},{20... | collective-permute-start | bytes 393224 | tf_op jit(solution)/shard_map/ppermute | solution.py:415
  108.5 12.1 %collective-permute-start.13 = (bf16[512,256]{1,0:T(8,128)(2,1)S(1)}, bf16[512,256]{1,0:T(8,128)(2,1)S(1)}, u32[]{:S(2)}, u32[]{:S(2)}) collective-permute-start(bf16[512,256]{1,0:T(8,128)(2,1)S(1)} %get-tuple-element.21.kv0), channel_id=1, source_target_pairs={{0,192},{64,0},{128,64},{192,128},{1,193},{65,1},{129,65},{193,129... | collective-permute-start | bytes 786440 | tf_op jit(solution)/shard_map/ppermute | solution.py:418
  110.7 17.5 %collective-permute-start.12 = (bf16[512,256]{1,0:T(8,128)(2,1)S(1)}, bf16[512,256]{1,0:T(8,128)(2,1)S(1)}, u32[]{:S(2)}, u32[]{:S(2)}) collective-permute-start(bf16[512,256]{1,0:T(8,128)(2,1)S(1)} %get-tuple-element.21.kv0), channel_id=1, source_target_pairs={{0,64},{64,128},{128,192},{192,0},{1,65},{65,129},{129,193},{193,1... | collective-permute-start | bytes 786440 | tf_op jit(solution)/shard_map/ppermute | solution.py:418
  115.3 19.8 %collective-permute-start.11 = (bf16[2,512,128]{2,1,0:T(8,128)(2,1)S(1)}, bf16[2,512,128]{2,1,0:T(8,128)(2,1)S(1)}, u32[]{:S(2)}, u32[]{:S(2)}) collective-permute-start(bf16[2,512,128]{2,1,0:T(8,128)(2,1)S(1)} %pad_maximum_fusion.1), channel_id=1, source_target_pairs={{0,32},{32,0},{1,33},{33,1},{2,34},{34,2},{3,35},{35,3},{4,36},{36... | collective-permute-start | bytes 786440 | tf_op jit(solution)/shard_map/ppermute | solution.py:416
  128.2 14.8 %collective-permute-start.15 = (bf16[256,256]{1,0:T(8,128)(2,1)S(1)}, bf16[256,256]{1,0:T(8,128)(2,1)S(1)}, u32[]{:S(2)}, u32[]{:S(2)}) collective-permute-start(bf16[256,256]{1,0:T(8,128)(2,1)S(1)} %slice.109), channel_id=1, source_target_pairs={{0,192},{64,0},{128,64},{192,128},{1,193},{65,1},{129,65},{193,129... | collective-permute-start | bytes 393224 | tf_op jit(solution)/shard_map/ppermute | solution.py:423
  130.1 12.8 %collective-permute-start.14 = (bf16[256,256]{1,0:T(8,128)(2,1)S(1)}, bf16[256,256]{1,0:T(8,128)(2,1)S(1)}, u32[]{:S(2)}, u32[]{:S(2)}) collective-permute-start(bf16[256,256]{1,0:T(8,128)(2,1)S(1)} %slice.108), channel_id=1, source_target_pairs={{0,64},{64,128},{128,192},{192,0},{1,65},{65,129},{129,193},{193,1... | collective-permute-start | bytes 393224 | tf_op jit(solution)/shard_map/ppermute | solution.py:422
  148.8 10.6 %all-to-all-start = ((bf16[4,576,128]{2,1,0:T(8,128)(2,1)}), bf16[4,576,128]{2,1,0:T(8,128)(2,1)S(1)}, u32[]{:S(2)}, u32[]{:S(2)}) async-start(bf16[4,576,128]{2,1,0:T(8,128)(2,1)} %rest.1), calls=%async_computation | async-start | bytes 1179648 | tf_op jit(solution)/shard_map/all_to_all | solution.py:432
  (4 other events, 25.4 us)
Sparse Core Ops, SparseCore 0:
  9.5 72.9 all-gather.1

commit v10 on v9

--- a/solution.py
+++ b/solution.py
@@ -207,34 +207,23 @@
     return weighted / total, jnp.where(lane < HD, tops[0], tops[1]) + jnp.log(total) * LOG2E
 
 
-def first_kernel(info, q1, q23, kv0, kv1, kv2, text_kv, o_ref, keys, values, held, sems):
+def first_kernel(info, q1, q2, q3, kv0, kv1, kv2, text_kv, o_ref, keys, values):
     load_keys((kv0, kv1, kv2), text_kv, keys, values)
-    sends = []
-    for i, q in enumerate((q1[...], q23[0], q23[1])):
-        held[i, 0], held[i, 1] = softmax_block(info, q, keys, values, True)
-        sends.append(pltpu.make_async_copy(held.at[i], o_ref.at[i], sems.at[i]))
-        sends[-1].start()
-    for send in sends:
-        send.wait()
+    for i, q_ref in enumerate((q1, q2, q3)):
+        o_ref[i, 0], o_ref[i, 1] = softmax_block(info, q_ref[...], keys, values, True)
 
 
 def rest_kernel(
-    info, q1, q23, kv3, kv4, before_hbm, o_ref, keys, values, held, before, sems, in_sems
+    info, q1, q2, q3, kv3, kv4, before, o_ref, keys, values, held, sems
 ):
-    fetches = [
-        pltpu.make_async_copy(before_hbm.at[i], before.at[i], in_sems.at[i]) for i in range(3)
-    ]
-    for fetch in fetches:
-        fetch.start()
     count = q1.shape[0]
     load_keys((kv3, kv4), None, keys, values)
     term = lax.broadcasted_iota(jnp.int32, (STAT_ROWS, 128), 0)
     lane = lax.broadcasted_iota(jnp.int32, (STAT_ROWS, 128), 1)
     sends = []
-    for i, q in enumerate((q1[...], q23[0], q23[1])):
+    for i, q_ref in enumerate((q1, q2, q3)):
         member = jnp.bitwise_xor(info[3], i + 1)
-        out, lse = softmax_block(info, q, keys, values, False)
-        fetches[i].wait()
+        out, lse = softmax_block(info, q_ref[...], keys, values, False)
         earlier = before[i, 1]
         top = jnp.maximum(lse, earlier)
         new, old = jnp.exp2(lse - top), jnp.exp2(earlier - top)
@@ -269,25 +258,18 @@
 def attend(kernel, name, peers, out_shape, held, info, qs, blocks, text_kv=None, before=None):
     keys = sum(block.shape[0] for block in blocks) + (0 if text_kv is None else 128)
     count = qs[0].shape[0]
-    operands = [*qs, *blocks] + ([] if text_kv is None else [text_kv])
-    specs = [pl.BlockSpec(memory_space=pltpu.SMEM)] + [vmem()] * len(operands)
-    scratch = [
-        pltpu.VMEM((keys, 128), BF),
-        pltpu.VMEM((keys, 256), BF),
-        pltpu.VMEM(held, out_shape.dtype),
-    ]
-    sems = [pltpu.SemaphoreType.DMA((3,))]
-    if before is not None:
-        operands.append(keep(before))
-        specs.append(hbm())
-        scratch.append(pltpu.VMEM(before.shape, before.dtype))
-        sems = sems * 2
+    operands = [*qs, *blocks] + [x for x in (text_kv, before) if x is not None]
+    scratch = [pltpu.VMEM((keys, 128), BF), pltpu.VMEM((keys, 256), BF)]
+    out_spec = vmem()
+    if held is not None:
+        scratch += [pltpu.VMEM(held, out_shape.dtype), pltpu.SemaphoreType.DMA((3,))]
+        out_shape, out_spec = pltpu.MemorySpace.HBM(out_shape.shape, out_shape.dtype), hbm()
     return pl.pallas_call(
         kernel,
-        out_shape=pltpu.MemorySpace.HBM(out_shape.shape, out_shape.dtype),
-        in_specs=specs,
-        out_specs=hbm(),
-        scratch_shapes=scratch + sems,
+        out_shape=out_shape,
+        in_specs=[pl.BlockSpec(memory_space=pltpu.SMEM)] + [vmem()] * len(operands),
+        out_specs=out_spec,
+        scratch_shapes=scratch,
         compiler_params=params(24),
         cost_estimate=pl.CostEstimate(
             flops=4 * peers * count * keys * 256,
@@ -411,10 +393,12 @@
     text_rows = lax.dynamic_slice_in_dim(prompt_rows[0], start, TEXT_PART, axis=0)
     queries, kv, text_kv = project(slots, pieces, text_rows, weight)
     group = ("v", "zl")
-    swap = [(0, 1), (1, 0)]
-    beside = lax.ppermute(queries, "zl", swap)
-    across = lax.ppermute(jnp.stack([queries, beside]), "v", swap)
-    qs = [beside, across]
+    swaps = (
+        ("zl", [(0, 1), (1, 0)]),
+        ("v", [(0, 1), (1, 0)]),
+        (group, [(0, 3), (3, 0), (1, 2), (2, 1)]),
+    )
+    qs = [lax.ppermute(queries, axis, swap) for axis, swap in swaps]
     near = [lax.ppermute(kv, "u", up), lax.ppermute(kv, "u", down)]
     near = lax.optimization_barrier(near)
     count = kv.shape[0]
@@ -425,7 +409,7 @@
     info = jnp.stack([start, lower, text_len[0], member])
     shape = (3, 2, count, 128)
     first = jax.ShapeDtypeStruct(shape, F32)
-    first = attend(first_kernel, "first", 3, first, shape, info, qs, [kv, *near], text_kv)
+    first = attend(first_kernel, "first", 3, first, None, info, qs, [kv, *near], text_kv)
     shape = (4, count + count // 128 * STAT_ROWS, 128)
     parts = jax.ShapeDtypeStruct(shape, BF)
     parts = attend(rest_kernel, "rest", 3, parts, (3,) + shape[1:], info, qs, far, None, first)

time: 171 us -> 166 us (0.971)
  waiting for transfers between devices: 35 us -> 28.9 us
  starting transfers between devices: 62.2 us -> 65.5 us
    ppermute x2, waiting for transfers between devices: 7.56 us -> 0.45 us  [on_device(): near = [lax.ppermute(kv, 'u', up), lax.ppermute(kv, 'u', down)]]
    ppermute x1, starting transfers between devices: 1.92 us -> 5.59 us  [on_device(): lax.ppermute(near[1][count // 2:], 'u', down)]
    ppermute x1, starting transfers between devices: 5 us -> 2.1 us  [on_device(): lax.ppermute(near[0][:count // 2], 'u', up)]
    ppermute x2 -> x3, starting transfers between devices: 10.5 us -> 11 us  [on_device(): qs = [lax.ppermute(queries, axis, swap) for axis, swap in swaps]]
  transfers between devices with their start and end apart: 18 -> 19, of which waited for: 9 -> 10; matrix products, arithmetic and copies ran while one was open for 3% -> 3% of each run, Pallas kernels for 7% -> 7%
where the time goes in v10:
time: 166 us; the launch traced here: 165 us
  starting transfers between devices  65.5 us (39%)
  waiting for transfers between devices  28.9 us (17%)
  Pallas kernels  25.4 us (15%)
  blocking collectives  22.5 us (14%)
  between operations  15.1 us (9%)
  local copies, waits for them, and re-layouts  4.3 us (3%)
  other arithmetic  2.82 us (2%)
    all_gather x1, blocking collectives, on_device(): tokens = lax.all_gather(peg, 'zh', axis=0, tiled=True)  22.5 us
    pallas_call x3, Pallas kernels, attend(): pl.pallas_call(kernel, out_shape=out_shape, in_specs=[pl.BlockSpec(memory...  16.5 us
    ppermute x2, waiting for transfers between devices, with_halo(): lax.ppermute(lax.slice_in_dim(block, 0, width, axis=dim), axis, backward)  11.9 us
    ppermute x3, starting transfers between devices, on_device(): qs = [lax.ppermute(queries, axis, swap) for axis, swap in swaps]  11 us
    ppermute x2, starting transfers between devices, with_halo(): lax.ppermute(lax.slice_in_dim(block, block.shape[dim] - width, None, axis...  10.3 us
    ppermute x2, starting transfers between devices, on_device(): near = [lax.ppermute(kv, 'u', up), lax.ppermute(kv, 'u', down)]  8.08 us
    ppermute x2, starting transfers between devices, on_device(): c0, c1 = (lax.ppermute(a0, 'x', up), lax.ppermute(b1, 'x', down))  7.61 us
    ppermute x2, waiting for transfers between devices, on_device(): c0, c1 = (lax.ppermute(a0, 'x', up), lax.ppermute(b1, 'x', down))  7.56 us
  transfers between devices with their start and end apart: 19, of which 10 were waited for; matrix products, arithmetic and copies ran while one was open for 3% of the time, Pallas kernels for 7%

profile of v10, /device:TPU:6, one launch (start us, length us, event | category | flops | bytes accessed | tf_op | source)
XLA Modules:
  0.0 164.8 jit_solution(702094410220610386)
XLA Ops:
  9.1 4.3 %collective-permute-start = (bf16[1,2,1,4,3072]{4,3,2,1,0:T(4,128)(2,1)S(1)}, bf16[1,2,1,4,3072]{4,3,2,1,0:T(4,128)(2,1)S(1)}, u32[]{:S(2)}, u32[]{:S(2)}) collective-permute-start(bf16[1,2,1,4,3072]{4,3,2,1,0:T(4,128)(2,1)S(1)} %get-tuple-element.29), channel_id=1, source_target_pairs={{0,16},{16,32},{32,48},{48,64},{64,80},{80,96},{96,112},{112,128},... | collective-permute-start | bytes 147464 | tf_op jit(solution)/shard_map/ppermute | solution.py:41
  15.5 3.9 %collective-permute-done.1 = bf16[1,2,1,4,3072]{4,3,2,1,0:T(4,128)(2,1)S(1)} collective-permute-done((bf16[1,2,1,4,3072]{4,3,2,1,0:T(4,128)(2,1)S(1)}, bf16[1,2,1,4,3072]{4,3,2,1,0:T(4,128)(2,1)S(1)}, u32[]{:S(2)}, u32[]{:S(2)}) %collective-permute-start.1) | collective-permute-done | bytes 49184 | tf_op jit(solution)/shard_map/ppermute | solution.py:44
  20.8 6.0 %collective-permute-start.2 = (bf16[1,2,6,1,3072]{4,3,2,1,0:T(2,128)(2,1)S(1)}, bf16[1,2,6,1,3072]{4,3,2,1,0:T(2,128)(2,1)S(1)}, u32[]{:S(2)}, u32[]{:S(2)}) collective-permute-start(bf16[1,2,6,1,3072]{4,3,2,1,0:T(2,128)(2,1)S(1)} %get-tuple-element.27), channel_id=1, source_target_pairs={{0,1},{1,2},{2,3},{3,4},{4,5},{5,6},{6,7},{7,8},{8,9},{9,10},{10,1... | collective-permute-start | bytes 221192 | tf_op jit(solution)/shard_map/ppermute | solution.py:41
  30.2 8.0 %collective-permute-done.3 = bf16[1,2,6,1,3072]{4,3,2,1,0:T(2,128)(2,1)S(1)} collective-permute-done((bf16[1,2,6,1,3072]{4,3,2,1,0:T(2,128)(2,1)S(1)}, bf16[1,2,6,1,3072]{4,3,2,1,0:T(2,128)(2,1)S(1)}, u32[]{:S(2)}, u32[]{:S(2)}) %collective-permute-start.3) | collective-permute-done | bytes 73760 | tf_op jit(solution)/shard_map/ppermute | solution.py:44
  39.6 22.5 %all_gather.6 = bf16[128,3200]{1,0:T(8,128)(2,1)S(1)} all-gather(bf16[32,3200]{1,0:T(8,128)(2,1)S(1)} %pad_maximum_fusion.1), channel_id=1, replica_groups=mesh['item'=2,'u'=4,'v'=2,'zl'=2,'zh'=4,'x'=4] {'zh'}, dimensions={0}, use_global_device_ids=true | all-gather | bytes 1024000 | tf_op jit(solution)/shard_map/all_gather | solution.py:378
  64.2 5.4 %collective-permute-start.4 = (bf16[64,3200]{1,0:T(8,128)(2,1)S(1)}, bf16[64,3200]{1,0:T(8,128)(2,1)}, u32[]{:S(2)}, u32[]{:S(2)}) collective-permute-start(bf16[64,3200]{1,0:T(8,128)(2,1)S(1)} %get-tuple-element.26.x0), channel_id=1, source_target_pairs={{0,1},{1,2},{2,3},{3,0},{4,5},{5,6},{6,7},{7,4},{8,9},{9,10},{10,1... | collective-permute-start | bytes 1228808 | tf_op jit(solution)/shard_map/ppermute | solution.py:383
  69.6 3.9 %collective-permute-start.6 = (bf16[64,3200]{1,0:T(8,128)(2,1)S(1)}, bf16[64,3200]{1,0:T(8,128)(2,1)S(1)}, u32[]{:S(2)}, u32[]{:S(2)}) collective-permute-start(bf16[64,3200]{1,0:T(8,128)(2,1)S(1)} %get-tuple-element.25.x1), channel_id=1, source_target_pairs={{0,1},{1,2},{2,3},{3,0},{4,5},{5,6},{6,7},{7,4},{8,9},{9,10},{10,1... | collective-permute-start | bytes 1228808 | tf_op jit(solution)/shard_map/ppermute | solution.py:384
  75.5 4.0 %collective-permute-done.4.a0 = bf16[64,3200]{1,0:T(8,128)(2,1)} collective-permute-done((bf16[64,3200]{1,0:T(8,128)(2,1)S(1)}, bf16[64,3200]{1,0:T(8,128)(2,1)}, u32[]{:S(2)}, u32[]{:S(2)}) %collective-permute-start.4) | collective-permute-done | bytes 409632 | tf_op jit(solution)/shard_map/ppermute | solution.py:383
  79.5 5.7 %collective-permute-start.8 = (bf16[64,3200]{1,0:T(8,128)(2,1)}, bf16[64,3200]{1,0:T(8,128)(2,1)S(1)}, u32[]{:S(2)}, u32[]{:S(2)}) collective-permute-start(bf16[64,3200]{1,0:T(8,128)(2,1)} %collective-permute-done.4.a0), channel_id=1, source_target_pairs={{0,1},{1,2},{2,3},{3,0},{4,5},{5,6},{6,7},{7,4},{8,9},{9,10},{10,1... | collective-permute-start | bytes 1228808 | tf_op jit(solution)/shard_map/ppermute | solution.py:386
  85.2 1.9 %collective-permute-start.9 = (bf16[64,3200]{1,0:T(8,128)(2,1)S(1)}, bf16[64,3200]{1,0:T(8,128)(2,1)}, u32[]{:S(2)}, u32[]{:S(2)}) collective-permute-start(bf16[64,3200]{1,0:T(8,128)(2,1)S(1)} %collective-permute-done.5.b1), channel_id=1, source_target_pairs={{0,3},{1,0},{2,1},{3,2},{4,7},{5,4},{6,5},{7,6},{8,11},{9,8},{10,9... | collective-permute-start | bytes 1228808 | tf_op jit(solution)/shard_map/ppermute | solution.py:386
  88.0 2.9 %collective-permute-done.8.c0 = bf16[64,3200]{1,0:T(8,128)(2,1)S(1)} collective-permute-done((bf16[64,3200]{1,0:T(8,128)(2,1)}, bf16[64,3200]{1,0:T(8,128)(2,1)S(1)}, u32[]{:S(2)}, u32[]{:S(2)}) %collective-permute-start.8) | collective-permute-done | bytes 409632 | tf_op jit(solution)/shard_map/ppermute | solution.py:386
  91.7 4.6 %collective-permute-done.9.c1 = bf16[64,3200]{1,0:T(8,128)(2,1)} collective-permute-done((bf16[64,3200]{1,0:T(8,128)(2,1)S(1)}, bf16[64,3200]{1,0:T(8,128)(2,1)}, u32[]{:S(2)}, u32[]{:S(2)}) %collective-permute-start.9) | collective-permute-done | bytes 409632 | tf_op jit(solution)/shard_map/ppermute | solution.py:386
  96.4 6.2 %project.1 = (bf16[512,128]{1,0:T(8,128)(2,1)S(1)}, bf16[512,256]{1,0:T(8,128)(2,1)S(1)}, bf16[64,256]{1,0:T(8,128)(2,1)S(1)}) custom-call(s32[4]{0:T(128)S(1)} %compare_select_fusion.3.slots, bf16[64,3200]{1,0:T(8,128)(2,1)} %copy-done.2, bf16[64,3200]{1,0:T(8,128)(2,1)} %copy-done.1, bf16[64,3200]{1,0:T(8,128)(2,1)} %collective-permute-done.4.a0, ...), custom_call_target="tpu_custom_call" | custom-call | flops 1207959552 | bytes 5636096 | tf_op jit(solution)/shard_map/project/pallas_call | solution.py:137
  102.6 6.2 %collective-permute-start.14 = (bf16[512,256]{1,0:T(8,128)(2,1)S(1)}, bf16[512,256]{1,0:T(8,128)(2,1)S(1)}, u32[]{:S(2)}, u32[]{:S(2)}) collective-permute-start(bf16[512,256]{1,0:T(8,128)(2,1)S(1)} %get-tuple-element.21.kv0), channel_id=1, source_target_pairs={{0,192},{64,0},{128,64},{192,128},{1,193},{65,1},{129,65},{193,129... | collective-permute-start | bytes 786440 | tf_op jit(solution)/shard_map/ppermute | solution.py:402
  110.7 6.6 %collective-permute-start.12 = (bf16[512,128]{1,0:T(8,128)(2,1)S(1)}, bf16[512,128]{1,0:T(8,128)(2,1)S(1)}, u32[]{:S(2)}, u32[]{:S(2)}) collective-permute-start(bf16[512,128]{1,0:T(8,128)(2,1)S(1)} %get-tuple-element.20.q_ref), channel_id=1, source_target_pairs={{0,48},{48,0},{16,32},{32,16},{1,49},{49,1},{17,33},{33,17},{2,50}... | collective-permute-start | bytes 393224 | tf_op jit(solution)/shard_map/ppermute | solution.py:401
  119.3 2.5 %collective-permute-start.10 = (bf16[512,128]{1,0:T(8,128)(2,1)S(1)}, bf16[512,128]{1,0:T(8,128)(2,1)S(1)}, u32[]{:S(2)}, u32[]{:S(2)}) collective-permute-start(bf16[512,128]{1,0:T(8,128)(2,1)S(1)} %get-tuple-element.20.q_ref), channel_id=1, source_target_pairs={{0,16},{16,0},{1,17},{17,1},{2,18},{18,2},{3,19},{19,3},{4,20},{20... | collective-permute-start | bytes 393224 | tf_op jit(solution)/shard_map/ppermute | solution.py:401
  123.0 5.6 %collective-permute-start.16 = (bf16[256,256]{1,0:T(8,128)(2,1)S(1)}, bf16[256,256]{1,0:T(8,128)(2,1)S(1)}, u32[]{:S(2)}, u32[]{:S(2)}) collective-permute-start(bf16[256,256]{1,0:T(8,128)(2,1)S(1)} %slice.109), channel_id=1, source_target_pairs={{0,192},{64,0},{128,64},{192,128},{1,193},{65,1},{129,65},{193,129... | collective-permute-start | bytes 393224 | tf_op jit(solution)/shard_map/ppermute | solution.py:407
  128.6 2.1 %collective-permute-start.15 = (bf16[256,256]{1,0:T(8,128)(2,1)S(1)}, bf16[256,256]{1,0:T(8,128)(2,1)S(1)}, u32[]{:S(2)}, u32[]{:S(2)}) collective-permute-start(bf16[256,256]{1,0:T(8,128)(2,1)S(1)} %slice.108), channel_id=1, source_target_pairs={{0,64},{64,128},{128,192},{192,0},{1,65},{65,129},{129,193},{193,1... | collective-permute-start | bytes 393224 | tf_op jit(solution)/shard_map/ppermute | solution.py:406
  130.7 7.0 %first.1.before = f32[3,2,512,128]{3,2,1,0:T(8,128)S(1)} custom-call(s32[4]{0:T(128)S(1)} %pad_add_fusion.info, bf16[512,128]{1,0:T(8,128)(2,1)S(1)} %collective-permute-done.10.q1, bf16[512,128]{1,0:T(8,128)(2,1)S(1)} %collective-permute-done.11.q2, bf16[512,128]{1,0:T(8,128)(2,1)S(1)} %collective-permute-done.12.q3, ...), custom_call_target="tpu_custom_call" | custom-call | flops 2617245696 | bytes 1638400 | tf_op jit(solution)/shard_map/first/pallas_call | solution.py:267
  138.7 5.1 %rest.1 = bf16[4,576,128]{2,1,0:T(8,128)(2,1)} custom-call(s32[4]{0:T(128)S(1)} %pad_add_fusion.info, bf16[512,128]{1,0:T(8,128)(2,1)S(1)} %collective-permute-done.10.q1, bf16[512,128]{1,0:T(8,128)(2,1)S(1)} %collective-permute-done.11.q2, bf16[512,128]{1,0:T(8,128)(2,1)S(1)} %collective-permute-done.12.q3, ...), custom_call_target="tpu_custom_call" | custom-call | flops 805306368 | bytes 1048576 | tf_op jit(solution)/shard_map/rest/pallas_call | solution.py:267
  143.8 4.4 %all-to-all-start = ((bf16[4,576,128]{2,1,0:T(8,128)(2,1)}), bf16[4,576,128]{2,1,0:T(8,128)(2,1)S(1)}, u32[]{:S(2)}, u32[]{:S(2)}) async-start(bf16[4,576,128]{2,1,0:T(8,128)(2,1)} %rest.1), calls=%async_computation | async-start | bytes 1179648 | tf_op jit(solution)/shard_map/all_to_all | solution.py:416
  148.2 4.3 %own.1.own_hbm = f32[2,512,128]{2,1,0:T(8,128)} custom-call(s32[4]{0:T(128)S(1)} %pad_add_fusion.info, bf16[512,128]{1,0:T(8,128)(2,1)S(1)} %get-tuple-element.20.q_ref, bf16[512,256]{1,0:T(8,128)(2,1)S(1)} %get-tuple-element.21.kv0, bf16[512,256]{1,0:T(8,128)(2,1)S(1)} %collective-permute-done.13.kv1, bf16[512,256]{1,0:T(8,128)(2,1)S(1)} %collective-permute-done.14.kv2, ...), custom_call_target="tpu_custom_call" | custom-call | flops 1140850688 | bytes 1376256 | tf_op jit(solution)/shard_map/own/pallas_call | solution.py:267
  152.6 2.6 %all-to-all-done.parts_ref = bf16[4,576,128]{2,1,0:T(8,128)(2,1)S(1)} async-done(((bf16[4,576,128]{2,1,0:T(8,128)(2,1)}), bf16[4,576,128]{2,1,0:T(8,128)(2,1)S(1)}, u32[]{:S(2)}, u32[]{:S(2)}) %all-to-all-start) | async-done | bytes 589856 | tf_op jit(solution)/shard_map/all_to_all | solution.py:416
  155.2 2.7 %combine.1 = bf16[2,4,64,128]{3,2,1,0:T(8,128)(2,1)} custom-call(s32[4]{0:T(128)S(1)} %compare_select_fusion.3.slots, s32[4]{0:T(128)S(1)} %pad_add_fusion.info, bf16[4,576,128]{2,1,0:T(8,128)(2,1)S(1)} %all-to-all-done.parts_ref, f32[2,512,128]{2,1,0:T(8,128)} %own.1.own_hbm), custom_call_target="tpu_custom_call" | custom-call | tf_op jit(solution)/shard_map/combine/pallas_call | solution.py:329
  (62 shorter events, 21.0 us)
Async XLA Ops:
  6.5 80.6 %copy-start = (bf16[1,226,3072]{2,1,0:T(8,128)(2,1)S(1)}, bf16[1,226,3072]{2,1,0:T(8,128)(2,1)}, u32[]{:S(2)}) copy-start(bf16[1,226,3072]{2,1,0:T(8,128)(2,1)} %param.8) | copy-start | bytes 4165636
  6.5 31.6 %copy-start.3 = (bf16[1,2,4,4,3072]{4,3,2,1,0:T(4,128)(2,1)S(1)}, bf16[1,2,4,4,3072]{4,3,2,1,0:T(4,128)(2,1)}, u32[]{:S(2)}) copy-start(bf16[1,2,4,4,3072]{4,3,2,1,0:T(4,128)(2,1)} %param.7) | copy-start | bytes 589828
  6.5 22.6 %copy-start.9 = (bf16[3,3,3072]{2,1,0:T(4,128)(2,1)S(1)}, bf16[3,3,3072]{2,1,0:T(4,128)(2,1)}, u32[]{:S(2)}) copy-start(bf16[3,3,3072]{2,1,0:T(4,128)(2,1)} %param.9) | copy-start | bytes 165892
  6.5 89.8 %all-gather.2.cloned.1.call-start = ((), (), s32[]{:S(2)}) async-start(), calls=%async_computation.1 | async-start | bytes 2433024 | tf_op jit(solution)/shard_map/all_gather | solution.py:358
  9.1 6.3 %collective-permute-start = (bf16[1,2,1,4,3072]{4,3,2,1,0:T(4,128)(2,1)S(1)}, bf16[1,2,1,4,3072]{4,3,2,1,0:T(4,128)(2,1)S(1)}, u32[]{:S(2)}, u32[]{:S(2)}) collective-permute-start(bf16[1,2,1,4,3072]{4,3,2,1,0:T(4,128)(2,1)S(1)} %get-tuple-element.29), channel_id=1, source_target_pairs={{0,16},{16,32},{32,48},{48,64},{64,80},{80,96},{96,112},{112,128},... | collective-permute-start | bytes 147464 | tf_op jit(solution)/shard_map/ppermute | solution.py:41
  13.4 6.0 %collective-permute-start.1 = (bf16[1,2,1,4,3072]{4,3,2,1,0:T(4,128)(2,1)S(1)}, bf16[1,2,1,4,3072]{4,3,2,1,0:T(4,128)(2,1)S(1)}, u32[]{:S(2)}, u32[]{:S(2)}) collective-permute-start(bf16[1,2,1,4,3072]{4,3,2,1,0:T(4,128)(2,1)S(1)} %get-tuple-element.30), channel_id=1, source_target_pairs={{16,0},{32,16},{48,32},{64,48},{80,64},{96,80},{112,96},{128,112},... | collective-permute-start | bytes 147464 | tf_op jit(solution)/shard_map/ppermute | solution.py:44
  20.8 9.4 %collective-permute-start.2 = (bf16[1,2,6,1,3072]{4,3,2,1,0:T(2,128)(2,1)S(1)}, bf16[1,2,6,1,3072]{4,3,2,1,0:T(2,128)(2,1)S(1)}, u32[]{:S(2)}, u32[]{:S(2)}) collective-permute-start(bf16[1,2,6,1,3072]{4,3,2,1,0:T(2,128)(2,1)S(1)} %get-tuple-element.27), channel_id=1, source_target_pairs={{0,1},{1,2},{2,3},{3,4},{4,5},{5,6},{6,7},{7,8},{8,9},{9,10},{10,1... | collective-permute-start | bytes 221192 | tf_op jit(solution)/shard_map/ppermute | solution.py:41
  26.8 11.4 %collective-permute-start.3 = (bf16[1,2,6,1,3072]{4,3,2,1,0:T(2,128)(2,1)S(1)}, bf16[1,2,6,1,3072]{4,3,2,1,0:T(2,128)(2,1)S(1)}, u32[]{:S(2)}, u32[]{:S(2)}) collective-permute-start(bf16[1,2,6,1,3072]{4,3,2,1,0:T(2,128)(2,1)S(1)} %get-tuple-element.28), channel_id=1, source_target_pairs={{1,0},{2,1},{3,2},{4,3},{5,4},{6,5},{7,6},{8,7},{9,8},{10,9},{11,1... | collective-permute-start | bytes 221192 | tf_op jit(solution)/shard_map/ppermute | solution.py:44
  62.2 34.1 %copy-start.2 = (bf16[64,3200]{1,0:T(8,128)(2,1)}, bf16[64,3200]{1,0:T(8,128)(2,1)S(1)}, u32[]{:S(2)}) copy-start(bf16[64,3200]{1,0:T(8,128)(2,1)S(1)} %get-tuple-element.26.x0) | copy-start | bytes 1228804
  62.2 34.1 %copy-start.1 = (bf16[64,3200]{1,0:T(8,128)(2,1)}, bf16[64,3200]{1,0:T(8,128)(2,1)S(1)}, u32[]{:S(2)}) copy-start(bf16[64,3200]{1,0:T(8,128)(2,1)S(1)} %get-tuple-element.25.x1) | copy-start | bytes 1228804
  62.2 13.2 %collective-permute-start.5 = (bf16[64,3200]{1,0:T(8,128)(2,1)S(1)}, bf16[64,3200]{1,0:T(8,128)(2,1)S(1)}, u32[]{:S(2)}, u32[]{:S(2)}) collective-permute-start(bf16[64,3200]{1,0:T(8,128)(2,1)S(1)} %get-tuple-element.25.x1), channel_id=1, source_target_pairs={{0,3},{1,0},{2,1},{3,2},{4,7},{5,4},{6,5},{7,6},{8,11},{9,8},{10,9... | collective-permute-start | bytes 1228808 | tf_op jit(solution)/shard_map/ppermute | solution.py:383
  64.2 15.3 %collective-permute-start.4 = (bf16[64,3200]{1,0:T(8,128)(2,1)S(1)}, bf16[64,3200]{1,0:T(8,128)(2,1)}, u32[]{:S(2)}, u32[]{:S(2)}) collective-permute-start(bf16[64,3200]{1,0:T(8,128)(2,1)S(1)} %get-tuple-element.26.x0), channel_id=1, source_target_pairs={{0,1},{1,2},{2,3},{3,0},{4,5},{5,6},{6,7},{7,4},{8,9},{9,10},{10,1... | collective-permute-start | bytes 1228808 | tf_op jit(solution)/shard_map/ppermute | solution.py:383
  69.6 17.7 %collective-permute-start.6 = (bf16[64,3200]{1,0:T(8,128)(2,1)S(1)}, bf16[64,3200]{1,0:T(8,128)(2,1)S(1)}, u32[]{:S(2)}, u32[]{:S(2)}) collective-permute-start(bf16[64,3200]{1,0:T(8,128)(2,1)S(1)} %get-tuple-element.25.x1), channel_id=1, source_target_pairs={{0,1},{1,2},{2,3},{3,0},{4,5},{5,6},{6,7},{7,4},{8,9},{9,10},{10,1... | collective-permute-start | bytes 1228808 | tf_op jit(solution)/shard_map/ppermute | solution.py:384
  73.5 14.1 %collective-permute-start.7 = (bf16[64,3200]{1,0:T(8,128)(2,1)S(1)}, bf16[64,3200]{1,0:T(8,128)(2,1)S(1)}, u32[]{:S(2)}, u32[]{:S(2)}) collective-permute-start(bf16[64,3200]{1,0:T(8,128)(2,1)S(1)} %get-tuple-element.26.x0), channel_id=1, source_target_pairs={{0,3},{1,0},{2,1},{3,2},{4,7},{5,4},{6,5},{7,6},{8,11},{9,8},{10,9... | collective-permute-start | bytes 1228808 | tf_op jit(solution)/shard_map/ppermute | solution.py:384
  79.5 11.5 %collective-permute-start.8 = (bf16[64,3200]{1,0:T(8,128)(2,1)}, bf16[64,3200]{1,0:T(8,128)(2,1)S(1)}, u32[]{:S(2)}, u32[]{:S(2)}) collective-permute-start(bf16[64,3200]{1,0:T(8,128)(2,1)} %collective-permute-done.4.a0), channel_id=1, source_target_pairs={{0,1},{1,2},{2,3},{3,0},{4,5},{5,6},{6,7},{7,4},{8,9},{9,10},{10,1... | collective-permute-start | bytes 1228808 | tf_op jit(solution)/shard_map/ppermute | solution.py:386
  85.2 11.2 %collective-permute-start.9 = (bf16[64,3200]{1,0:T(8,128)(2,1)S(1)}, bf16[64,3200]{1,0:T(8,128)(2,1)}, u32[]{:S(2)}, u32[]{:S(2)}) collective-permute-start(bf16[64,3200]{1,0:T(8,128)(2,1)S(1)} %collective-permute-done.5.b1), channel_id=1, source_target_pairs={{0,3},{1,0},{2,1},{3,2},{4,7},{5,4},{6,5},{7,6},{8,11},{9,8},{10,9... | collective-permute-start | bytes 1228808 | tf_op jit(solution)/shard_map/ppermute | solution.py:386
  102.6 19.9 %collective-permute-start.14 = (bf16[512,256]{1,0:T(8,128)(2,1)S(1)}, bf16[512,256]{1,0:T(8,128)(2,1)S(1)}, u32[]{:S(2)}, u32[]{:S(2)}) collective-permute-start(bf16[512,256]{1,0:T(8,128)(2,1)S(1)} %get-tuple-element.21.kv0), channel_id=1, source_target_pairs={{0,192},{64,0},{128,64},{192,128},{1,193},{65,1},{129,65},{193,129... | collective-permute-start | bytes 786440 | tf_op jit(solution)/shard_map/ppermute | solution.py:402
  108.8 14.2 %collective-permute-start.13 = (bf16[512,256]{1,0:T(8,128)(2,1)S(1)}, bf16[512,256]{1,0:T(8,128)(2,1)S(1)}, u32[]{:S(2)}, u32[]{:S(2)}) collective-permute-start(bf16[512,256]{1,0:T(8,128)(2,1)S(1)} %get-tuple-element.21.kv0), channel_id=1, source_target_pairs={{0,64},{64,128},{128,192},{192,0},{1,65},{65,129},{129,193},{193,1... | collective-permute-start | bytes 786440 | tf_op jit(solution)/shard_map/ppermute | solution.py:402
  110.7 20.0 %collective-permute-start.12 = (bf16[512,128]{1,0:T(8,128)(2,1)S(1)}, bf16[512,128]{1,0:T(8,128)(2,1)S(1)}, u32[]{:S(2)}, u32[]{:S(2)}) collective-permute-start(bf16[512,128]{1,0:T(8,128)(2,1)S(1)} %get-tuple-element.20.q_ref), channel_id=1, source_target_pairs={{0,48},{48,0},{16,32},{32,16},{1,49},{49,1},{17,33},{33,17},{2,50}... | collective-permute-start | bytes 393224 | tf_op jit(solution)/shard_map/ppermute | solution.py:401
  117.4 13.3 %collective-permute-start.11 = (bf16[512,128]{1,0:T(8,128)(2,1)S(1)}, bf16[512,128]{1,0:T(8,128)(2,1)S(1)}, u32[]{:S(2)}, u32[]{:S(2)}) collective-permute-start(bf16[512,128]{1,0:T(8,128)(2,1)S(1)} %get-tuple-element.20.q_ref), channel_id=1, source_target_pairs={{0,32},{32,0},{1,33},{33,1},{2,34},{34,2},{3,35},{35,3},{4,36},{36... | collective-permute-start | bytes 393224 | tf_op jit(solution)/shard_map/ppermute | solution.py:401
  119.3 11.4 %collective-permute-start.10 = (bf16[512,128]{1,0:T(8,128)(2,1)S(1)}, bf16[512,128]{1,0:T(8,128)(2,1)S(1)}, u32[]{:S(2)}, u32[]{:S(2)}) collective-permute-start(bf16[512,128]{1,0:T(8,128)(2,1)S(1)} %get-tuple-element.20.q_ref), channel_id=1, source_target_pairs={{0,16},{16,0},{1,17},{17,1},{2,18},{18,2},{3,19},{19,3},{4,20},{20... | collective-permute-start | bytes 393224 | tf_op jit(solution)/shard_map/ppermute | solution.py:401
  123.0 14.7 %collective-permute-start.16 = (bf16[256,256]{1,0:T(8,128)(2,1)S(1)}, bf16[256,256]{1,0:T(8,128)(2,1)S(1)}, u32[]{:S(2)}, u32[]{:S(2)}) collective-permute-start(bf16[256,256]{1,0:T(8,128)(2,1)S(1)} %slice.109), channel_id=1, source_target_pairs={{0,192},{64,0},{128,64},{192,128},{1,193},{65,1},{129,65},{193,129... | collective-permute-start | bytes 393224 | tf_op jit(solution)/shard_map/ppermute | solution.py:407
  128.6 10.1 %collective-permute-start.15 = (bf16[256,256]{1,0:T(8,128)(2,1)S(1)}, bf16[256,256]{1,0:T(8,128)(2,1)S(1)}, u32[]{:S(2)}, u32[]{:S(2)}) collective-permute-start(bf16[256,256]{1,0:T(8,128)(2,1)S(1)} %slice.108), channel_id=1, source_target_pairs={{0,64},{64,128},{128,192},{192,0},{1,65},{65,129},{129,193},{193,1... | collective-permute-start | bytes 393224 | tf_op jit(solution)/shard_map/ppermute | solution.py:406
  143.8 11.4 %all-to-all-start = ((bf16[4,576,128]{2,1,0:T(8,128)(2,1)}), bf16[4,576,128]{2,1,0:T(8,128)(2,1)S(1)}, u32[]{:S(2)}, u32[]{:S(2)}) async-start(bf16[4,576,128]{2,1,0:T(8,128)(2,1)} %rest.1), calls=%async_computation | async-start | bytes 1179648 | tf_op jit(solution)/shard_map/all_to_all | solution.py:416
  (5 other events, 47.5 us)
Sparse Core Ops, SparseCore 0:
  9.5 72.9 all-gather.1

commit v11 on v10

--- a/solution.py
+++ b/solution.py
@@ -214,10 +214,10 @@
 
 
 def rest_kernel(
-    info, q1, q2, q3, kv3, kv4, before, o_ref, keys, values, held, sems
+    info, q1, q2, q3, kv3, before, o_ref, keys, values, held, sems
 ):
     count = q1.shape[0]
-    load_keys((kv3, kv4), None, keys, values)
+    load_keys((kv3,), None, keys, values)
     term = lax.broadcasted_iota(jnp.int32, (STAT_ROWS, 128), 0)
     lane = lax.broadcasted_iota(jnp.int32, (STAT_ROWS, 128), 1)
     sends = []
@@ -247,8 +247,8 @@
         send.wait()
 
 
-def own_kernel(info, q_ref, kv0, kv1, kv2, kv3, kv4, text_kv, o_ref, keys, values, held, sems):
-    load_keys((kv0, kv1, kv2, kv3, kv4), text_kv, keys, values)
+def own_kernel(info, q_ref, kv0, kv1, kv2, kv3, text_kv, o_ref, keys, values, held, sems):
+    load_keys((kv0, kv1, kv2, kv3), text_kv, keys, values)
     held[0], held[1] = softmax_block(info, q_ref[...], keys, values, True)
     copy = pltpu.make_async_copy(held, o_ref, sems.at[0])
     copy.start()
@@ -400,23 +400,19 @@
     )
     qs = [lax.ppermute(queries, axis, swap) for axis, swap in swaps]
     near = [lax.ppermute(kv, "u", up), lax.ppermute(kv, "u", down)]
-    near = lax.optimization_barrier(near)
+    far = lax.ppermute(kv, "u", [(i, (i + 2) % 4) for i in range(4)])
     count = kv.shape[0]
-    far = [
-        lax.ppermute(near[0][: count // 2], "u", up),
-        lax.ppermute(near[1][count // 2 :], "u", down),
-    ]
     info = jnp.stack([start, lower, text_len[0], member])
     shape = (3, 2, count, 128)
     first = jax.ShapeDtypeStruct(shape, F32)
     first = attend(first_kernel, "first", 3, first, None, info, qs, [kv, *near], text_kv)
     shape = (4, count + count // 128 * STAT_ROWS, 128)
     parts = jax.ShapeDtypeStruct(shape, BF)
-    parts = attend(rest_kernel, "rest", 3, parts, (3,) + shape[1:], info, qs, far, None, first)
+    parts = attend(rest_kernel, "rest", 3, parts, (3,) + shape[1:], info, qs, [far], None, first)
     parts = lax.all_to_all(parts, group, split_axis=0, concat_axis=0, tiled=True)
     shape = (2, count, 128)
     own = jax.ShapeDtypeStruct(shape, F32)
-    own = attend(own_kernel, "own", 1, own, shape, info, [queries], [kv, *near, *far], text_kv)
+    own = attend(own_kernel, "own", 1, own, shape, info, [queries], [kv, *near, far], text_kv)
     shape = (frames, tile_h, 16 * tile_w, head_width)
     return combine(slots, info, parts, own, shape)[None]
 

time: 166 us -> 166 us (level)
    ppermute x2 -> x1, starting transfers between devices: 7.7 us -> 5.16 us  [on_device(): far = lax.ppermute(kv, 'u', [(i, (i + 2) % 4) for i in range(4)])]
    all_to_all x1, starting transfers between devices: 4.4 us -> 6.18 us  [on_device(): lax.all_to_all(parts, group, split_axis=0, concat_axis=0, tiled=True)]
  transfers between devices with their start and end apart: 19 -> 18, of which waited for: 10 -> 9; matrix products, arithmetic and copies ran while one was open for 3% -> 3% of each run, Pallas kernels for 7% -> 7%
where the time goes in v11:
time: 166 us; the launch traced here: 165 us
  starting transfers between devices  64.8 us (39%)
  waiting for transfers between devices  29.8 us (18%)
  Pallas kernels  25.5 us (15%)
  blocking collectives  22.5 us (14%)
  between operations  15.1 us (9%)
  local copies, waits for them, and re-layouts  3.95 us (2%)
  other arithmetic  2.82 us (2%)
    all_gather x1, blocking collectives, on_device(): tokens = lax.all_gather(peg, 'zh', axis=0, tiled=True)  22.5 us
    pallas_call x3, Pallas kernels, attend(): pl.pallas_call(kernel, out_shape=out_shape, in_specs=[pl.BlockSpec(memory...  16.5 us
    ppermute x2, waiting for transfers between devices, with_halo(): lax.ppermute(lax.slice_in_dim(block, 0, width, axis=dim), axis, backward)  11.9 us
    ppermute x3, starting transfers between devices, on_device(): qs = [lax.ppermute(queries, axis, swap) for axis, swap in swaps]  11.1 us
    ppermute x2, starting transfers between devices, with_halo(): lax.ppermute(lax.slice_in_dim(block, block.shape[dim] - width, None, axis...  10.3 us
    ppermute x2, starting transfers between devices, on_device(): near = [lax.ppermute(kv, 'u', up), lax.ppermute(kv, 'u', down)]  8.08 us
    ppermute x2, waiting for transfers between devices, on_device(): c0, c1 = (lax.ppermute(a0, 'x', up), lax.ppermute(b1, 'x', down))  7.86 us
    ppermute x2, starting transfers between devices, on_device(): c0, c1 = (lax.ppermute(a0, 'x', up), lax.ppermute(b1, 'x', down))  7.51 us
  transfers between devices with their start and end apart: 18, of which 9 were waited for; matrix products, arithmetic and copies ran while one was open for 3% of the time, Pallas kernels for 7%

profile of v11, /device:TPU:6, one launch (start us, length us, event | category | flops | bytes accessed | tf_op | source)
XLA Modules:
  0.0 164.6 jit_solution(812998187856528162)
XLA Ops:
  9.1 4.3 %collective-permute-start = (bf16[1,2,1,4,3072]{4,3,2,1,0:T(4,128)(2,1)S(1)}, bf16[1,2,1,4,3072]{4,3,2,1,0:T(4,128)(2,1)S(1)}, u32[]{:S(2)}, u32[]{:S(2)}) collective-permute-start(bf16[1,2,1,4,3072]{4,3,2,1,0:T(4,128)(2,1)S(1)} %get-tuple-element.25), channel_id=1, source_target_pairs={{0,16},{16,32},{32,48},{48,64},{64,80},{80,96},{96,112},{112,128},... | collective-permute-start | bytes 147464 | tf_op jit(solution)/shard_map/ppermute | solution.py:41
  15.5 3.9 %collective-permute-done.1 = bf16[1,2,1,4,3072]{4,3,2,1,0:T(4,128)(2,1)S(1)} collective-permute-done((bf16[1,2,1,4,3072]{4,3,2,1,0:T(4,128)(2,1)S(1)}, bf16[1,2,1,4,3072]{4,3,2,1,0:T(4,128)(2,1)S(1)}, u32[]{:S(2)}, u32[]{:S(2)}) %collective-permute-start.1) | collective-permute-done | bytes 49184 | tf_op jit(solution)/shard_map/ppermute | solution.py:44
  20.8 6.0 %collective-permute-start.2 = (bf16[1,2,6,1,3072]{4,3,2,1,0:T(2,128)(2,1)S(1)}, bf16[1,2,6,1,3072]{4,3,2,1,0:T(2,128)(2,1)S(1)}, u32[]{:S(2)}, u32[]{:S(2)}) collective-permute-start(bf16[1,2,6,1,3072]{4,3,2,1,0:T(2,128)(2,1)S(1)} %get-tuple-element.23), channel_id=1, source_target_pairs={{0,1},{1,2},{2,3},{3,4},{4,5},{5,6},{6,7},{7,8},{8,9},{9,10},{10,1... | collective-permute-start | bytes 221192 | tf_op jit(solution)/shard_map/ppermute | solution.py:41
  26.8 1.9 %collective-permute-start.3 = (bf16[1,2,6,1,3072]{4,3,2,1,0:T(2,128)(2,1)S(1)}, bf16[1,2,6,1,3072]{4,3,2,1,0:T(2,128)(2,1)S(1)}, u32[]{:S(2)}, u32[]{:S(2)}) collective-permute-start(bf16[1,2,6,1,3072]{4,3,2,1,0:T(2,128)(2,1)S(1)} %get-tuple-element.24), channel_id=1, source_target_pairs={{1,0},{2,1},{3,2},{4,3},{5,4},{6,5},{7,6},{8,7},{9,8},{10,9},{11,1... | collective-permute-start | bytes 221192 | tf_op jit(solution)/shard_map/ppermute | solution.py:44
  30.2 8.0 %collective-permute-done.3 = bf16[1,2,6,1,3072]{4,3,2,1,0:T(2,128)(2,1)S(1)} collective-permute-done((bf16[1,2,6,1,3072]{4,3,2,1,0:T(2,128)(2,1)S(1)}, bf16[1,2,6,1,3072]{4,3,2,1,0:T(2,128)(2,1)S(1)}, u32[]{:S(2)}, u32[]{:S(2)}) %collective-permute-start.3) | collective-permute-done | bytes 73760 | tf_op jit(solution)/shard_map/ppermute | solution.py:44
  39.6 22.5 %all_gather.6 = bf16[128,3200]{1,0:T(8,128)(2,1)S(1)} all-gather(bf16[32,3200]{1,0:T(8,128)(2,1)S(1)} %pad_maximum_fusion.1), channel_id=1, replica_groups=mesh['item'=2,'u'=4,'v'=2,'zl'=2,'zh'=4,'x'=4] {'zh'}, dimensions={0}, use_global_device_ids=true | all-gather | bytes 1024000 | tf_op jit(solution)/shard_map/all_gather | solution.py:378
  64.2 5.4 %collective-permute-start.4 = (bf16[64,3200]{1,0:T(8,128)(2,1)S(1)}, bf16[64,3200]{1,0:T(8,128)(2,1)S(1)}, u32[]{:S(2)}, u32[]{:S(2)}) collective-permute-start(bf16[64,3200]{1,0:T(8,128)(2,1)S(1)} %get-tuple-element.22.x0), channel_id=1, source_target_pairs={{0,1},{1,2},{2,3},{3,0},{4,5},{5,6},{6,7},{7,4},{8,9},{9,10},{10,1... | collective-permute-start | bytes 1228808 | tf_op jit(solution)/shard_map/ppermute | solution.py:383
  69.6 3.9 %collective-permute-start.6 = (bf16[64,3200]{1,0:T(8,128)(2,1)S(1)}, bf16[64,3200]{1,0:T(8,128)(2,1)S(1)}, u32[]{:S(2)}, u32[]{:S(2)}) collective-permute-start(bf16[64,3200]{1,0:T(8,128)(2,1)S(1)} %get-tuple-element.21.x1), channel_id=1, source_target_pairs={{0,1},{1,2},{2,3},{3,0},{4,5},{5,6},{6,7},{7,4},{8,9},{9,10},{10,1... | collective-permute-start | bytes 1228808 | tf_op jit(solution)/shard_map/ppermute | solution.py:384
  75.5 4.0 %collective-permute-done.4.a0 = bf16[64,3200]{1,0:T(8,128)(2,1)S(1)} collective-permute-done((bf16[64,3200]{1,0:T(8,128)(2,1)S(1)}, bf16[64,3200]{1,0:T(8,128)(2,1)S(1)}, u32[]{:S(2)}, u32[]{:S(2)}) %collective-permute-start.4) | collective-permute-done | bytes 409632 | tf_op jit(solution)/shard_map/ppermute | solution.py:383
  79.5 5.6 %collective-permute-start.8 = (bf16[64,3200]{1,0:T(8,128)(2,1)S(1)}, bf16[64,3200]{1,0:T(8,128)(2,1)S(1)}, u32[]{:S(2)}, u32[]{:S(2)}) collective-permute-start(bf16[64,3200]{1,0:T(8,128)(2,1)S(1)} %collective-permute-done.4.a0), channel_id=1, source_target_pairs={{0,1},{1,2},{2,3},{3,0},{4,5},{5,6},{6,7},{7,4},{8,9},{9,10},{10,1... | collective-permute-start | bytes 1228808 | tf_op jit(solution)/shard_map/ppermute | solution.py:386
  85.1 1.9 %collective-permute-start.9 = (bf16[64,3200]{1,0:T(8,128)(2,1)S(1)}, bf16[64,3200]{1,0:T(8,128)(2,1)}, u32[]{:S(2)}, u32[]{:S(2)}) collective-permute-start(bf16[64,3200]{1,0:T(8,128)(2,1)S(1)} %collective-permute-done.5.b1), channel_id=1, source_target_pairs={{0,3},{1,0},{2,1},{3,2},{4,7},{5,4},{6,5},{7,6},{8,11},{9,8},{10,9... | collective-permute-start | bytes 1228808 | tf_op jit(solution)/shard_map/ppermute | solution.py:386
  87.6 2.9 %collective-permute-done.8.c0 = bf16[64,3200]{1,0:T(8,128)(2,1)S(1)} collective-permute-done((bf16[64,3200]{1,0:T(8,128)(2,1)S(1)}, bf16[64,3200]{1,0:T(8,128)(2,1)S(1)}, u32[]{:S(2)}, u32[]{:S(2)}) %collective-permute-start.8) | collective-permute-done | bytes 409632 | tf_op jit(solution)/shard_map/ppermute | solution.py:386
  91.3 4.9 %collective-permute-done.9.c1 = bf16[64,3200]{1,0:T(8,128)(2,1)} collective-permute-done((bf16[64,3200]{1,0:T(8,128)(2,1)S(1)}, bf16[64,3200]{1,0:T(8,128)(2,1)}, u32[]{:S(2)}, u32[]{:S(2)}) %collective-permute-start.9) | collective-permute-done | bytes 409632 | tf_op jit(solution)/shard_map/ppermute | solution.py:386
  96.3 6.2 %project.1 = (bf16[512,128]{1,0:T(8,128)(2,1)S(1)}, bf16[512,256]{1,0:T(8,128)(2,1)S(1)}, bf16[64,256]{1,0:T(8,128)(2,1)S(1)}) custom-call(s32[4]{0:T(128)S(1)} %compare_select_fusion.3.slots, bf16[64,3200]{1,0:T(8,128)(2,1)} %copy-done.2, bf16[64,3200]{1,0:T(8,128)(2,1)} %copy-done.1, bf16[64,3200]{1,0:T(8,128)(2,1)} %copy-done.5, ...), custom_call_target="tpu_custom_call" | custom-call | flops 1207959552 | bytes 5636096 | tf_op jit(solution)/shard_map/project/pallas_call | solution.py:137
  102.5 6.2 %collective-permute-start.15 = (bf16[512,256]{1,0:T(8,128)(2,1)S(1)}, bf16[512,256]{1,0:T(8,128)(2,1)S(1)}, u32[]{:S(2)}, u32[]{:S(2)}) collective-permute-start(bf16[512,256]{1,0:T(8,128)(2,1)S(1)} %get-tuple-element.19.kv0), channel_id=1, source_target_pairs={{0,192},{64,0},{128,64},{192,128},{1,193},{65,1},{129,65},{193,129... | collective-permute-start | bytes 786440 | tf_op jit(solution)/shard_map/ppermute | solution.py:402
  110.6 6.7 %collective-permute-start.12 = (bf16[512,128]{1,0:T(8,128)(2,1)S(1)}, bf16[512,128]{1,0:T(8,128)(2,1)S(1)}, u32[]{:S(2)}, u32[]{:S(2)}) collective-permute-start(bf16[512,128]{1,0:T(8,128)(2,1)S(1)} %get-tuple-element.18.q_ref), channel_id=1, source_target_pairs={{0,48},{48,0},{16,32},{32,16},{1,49},{49,1},{17,33},{33,17},{2,50}... | collective-permute-start | bytes 393224 | tf_op jit(solution)/shard_map/ppermute | solution.py:401
  119.3 2.5 %collective-permute-start.10 = (bf16[512,128]{1,0:T(8,128)(2,1)S(1)}, bf16[512,128]{1,0:T(8,128)(2,1)S(1)}, u32[]{:S(2)}, u32[]{:S(2)}) collective-permute-start(bf16[512,128]{1,0:T(8,128)(2,1)S(1)} %get-tuple-element.18.q_ref), channel_id=1, source_target_pairs={{0,16},{16,0},{1,17},{17,1},{2,18},{18,2},{3,19},{19,3},{4,20},{20... | collective-permute-start | bytes 393224 | tf_op jit(solution)/shard_map/ppermute | solution.py:401
  122.4 5.2 %collective-permute-start.13 = (bf16[512,256]{1,0:T(8,128)(2,1)S(1)}, bf16[512,256]{1,0:T(8,128)(2,1)S(1)}, u32[]{:S(2)}, u32[]{:S(2)}) collective-permute-start(bf16[512,256]{1,0:T(8,128)(2,1)S(1)} %get-tuple-element.19.kv0), channel_id=1, source_target_pairs={{0,128},{64,192},{128,0},{192,64},{1,129},{65,193},{129,1},{193,65... | collective-permute-start | bytes 786440 | tf_op jit(solution)/shard_map/ppermute | solution.py:403
  127.7 7.0 %first.1.before = f32[3,2,512,128]{3,2,1,0:T(8,128)S(1)} custom-call(s32[4]{0:T(128)S(1)} %pad_add_fusion.info, bf16[512,128]{1,0:T(8,128)(2,1)S(1)} %collective-permute-done.10.q1, bf16[512,128]{1,0:T(8,128)(2,1)S(1)} %collective-permute-done.11.q2, bf16[512,128]{1,0:T(8,128)(2,1)S(1)} %collective-permute-done.12.q3, ...), custom_call_target="tpu_custom_call" | custom-call | flops 2617245696 | bytes 1638400 | tf_op jit(solution)/shard_map/first/pallas_call | solution.py:267
  136.4 5.1 %rest.1 = bf16[4,576,128]{2,1,0:T(8,128)(2,1)} custom-call(s32[4]{0:T(128)S(1)} %pad_add_fusion.info, bf16[512,128]{1,0:T(8,128)(2,1)S(1)} %collective-permute-done.10.q1, bf16[512,128]{1,0:T(8,128)(2,1)S(1)} %collective-permute-done.11.q2, bf16[512,128]{1,0:T(8,128)(2,1)S(1)} %collective-permute-done.12.q3, ...), custom_call_target="tpu_custom_call" | custom-call | flops 805306368 | bytes 1048576 | tf_op jit(solution)/shard_map/rest/pallas_call | solution.py:267
  141.5 6.2 %all-to-all-start = ((bf16[4,576,128]{2,1,0:T(8,128)(2,1)}), bf16[4,576,128]{2,1,0:T(8,128)(2,1)S(1)}, u32[]{:S(2)}, u32[]{:S(2)}) async-start(bf16[4,576,128]{2,1,0:T(8,128)(2,1)} %rest.1), calls=%async_computation | async-start | bytes 1179648 | tf_op jit(solution)/shard_map/all_to_all | solution.py:412
  147.7 4.4 %own.1.own_hbm = f32[2,512,128]{2,1,0:T(8,128)} custom-call(s32[4]{0:T(128)S(1)} %pad_add_fusion.info, bf16[512,128]{1,0:T(8,128)(2,1)S(1)} %get-tuple-element.18.q_ref, bf16[512,256]{1,0:T(8,128)(2,1)S(1)} %get-tuple-element.19.kv0, bf16[512,256]{1,0:T(8,128)(2,1)S(1)} %collective-permute-done.14.kv1, bf16[512,256]{1,0:T(8,128)(2,1)S(1)} %collective-permute-done.15.kv2, ...), custom_call_target="tpu_custom_call" | custom-call | flops 1140850688 | bytes 1376256 | tf_op jit(solution)/shard_map/own/pallas_call | solution.py:267
  152.1 3.0 %all-to-all-done.parts_ref = bf16[4,576,128]{2,1,0:T(8,128)(2,1)S(1)} async-done(((bf16[4,576,128]{2,1,0:T(8,128)(2,1)}), bf16[4,576,128]{2,1,0:T(8,128)(2,1)S(1)}, u32[]{:S(2)}, u32[]{:S(2)}) %all-to-all-start) | async-done | bytes 589856 | tf_op jit(solution)/shard_map/all_to_all | solution.py:412
  155.0 2.7 %combine.1 = bf16[2,4,64,128]{3,2,1,0:T(8,128)(2,1)} custom-call(s32[4]{0:T(128)S(1)} %compare_select_fusion.3.slots, s32[4]{0:T(128)S(1)} %pad_add_fusion.info, bf16[4,576,128]{2,1,0:T(8,128)(2,1)S(1)} %all-to-all-done.parts_ref, f32[2,512,128]{2,1,0:T(8,128)} %own.1.own_hbm), custom_call_target="tpu_custom_call" | custom-call | tf_op jit(solution)/shard_map/combine/pallas_call | solution.py:329
  (60 shorter events, 19.1 us)
Async XLA Ops:
  6.5 80.5 %copy-start = (bf16[1,226,3072]{2,1,0:T(8,128)(2,1)S(1)}, bf16[1,226,3072]{2,1,0:T(8,128)(2,1)}, u32[]{:S(2)}) copy-start(bf16[1,226,3072]{2,1,0:T(8,128)(2,1)} %param.8) | copy-start | bytes 4165636
  6.5 31.6 %copy-start.3 = (bf16[1,2,4,4,3072]{4,3,2,1,0:T(4,128)(2,1)S(1)}, bf16[1,2,4,4,3072]{4,3,2,1,0:T(4,128)(2,1)}, u32[]{:S(2)}) copy-start(bf16[1,2,4,4,3072]{4,3,2,1,0:T(4,128)(2,1)} %param.7) | copy-start | bytes 589828
  6.5 22.2 %copy-start.9 = (bf16[512,384]{1,0:T(8,128)(2,1)S(1)}, bf16[512,384]{1,0:T(8,128)(2,1)}, u32[]{:S(2)}) copy-start(bf16[512,384]{1,0:T(8,128)(2,1)} %param.10) | copy-start | bytes 1179652
  6.5 22.6 %copy-start.10 = (bf16[3,3,3072]{2,1,0:T(4,128)(2,1)S(1)}, bf16[3,3,3072]{2,1,0:T(4,128)(2,1)}, u32[]{:S(2)}) copy-start(bf16[3,3,3072]{2,1,0:T(4,128)(2,1)} %param.9) | copy-start | bytes 165892
  6.5 89.7 %all-gather.2.cloned.1.call-start = ((), (), s32[]{:S(2)}) async-start(), calls=%async_computation.1 | async-start | bytes 2433024 | tf_op jit(solution)/shard_map/all_gather | solution.py:358
  9.1 6.3 %collective-permute-start = (bf16[1,2,1,4,3072]{4,3,2,1,0:T(4,128)(2,1)S(1)}, bf16[1,2,1,4,3072]{4,3,2,1,0:T(4,128)(2,1)S(1)}, u32[]{:S(2)}, u32[]{:S(2)}) collective-permute-start(bf16[1,2,1,4,3072]{4,3,2,1,0:T(4,128)(2,1)S(1)} %get-tuple-element.25), channel_id=1, source_target_pairs={{0,16},{16,32},{32,48},{48,64},{64,80},{80,96},{96,112},{112,128},... | collective-permute-start | bytes 147464 | tf_op jit(solution)/shard_map/ppermute | solution.py:41
  13.4 6.0 %collective-permute-start.1 = (bf16[1,2,1,4,3072]{4,3,2,1,0:T(4,128)(2,1)S(1)}, bf16[1,2,1,4,3072]{4,3,2,1,0:T(4,128)(2,1)S(1)}, u32[]{:S(2)}, u32[]{:S(2)}) collective-permute-start(bf16[1,2,1,4,3072]{4,3,2,1,0:T(4,128)(2,1)S(1)} %get-tuple-element.26), channel_id=1, source_target_pairs={{16,0},{32,16},{48,32},{64,48},{80,64},{96,80},{112,96},{128,112},... | collective-permute-start | bytes 147464 | tf_op jit(solution)/shard_map/ppermute | solution.py:44
  20.8 9.4 %collective-permute-start.2 = (bf16[1,2,6,1,3072]{4,3,2,1,0:T(2,128)(2,1)S(1)}, bf16[1,2,6,1,3072]{4,3,2,1,0:T(2,128)(2,1)S(1)}, u32[]{:S(2)}, u32[]{:S(2)}) collective-permute-start(bf16[1,2,6,1,3072]{4,3,2,1,0:T(2,128)(2,1)S(1)} %get-tuple-element.23), channel_id=1, source_target_pairs={{0,1},{1,2},{2,3},{3,4},{4,5},{5,6},{6,7},{7,8},{8,9},{9,10},{10,1... | collective-permute-start | bytes 221192 | tf_op jit(solution)/shard_map/ppermute | solution.py:41
  26.8 11.4 %collective-permute-start.3 = (bf16[1,2,6,1,3072]{4,3,2,1,0:T(2,128)(2,1)S(1)}, bf16[1,2,6,1,3072]{4,3,2,1,0:T(2,128)(2,1)S(1)}, u32[]{:S(2)}, u32[]{:S(2)}) collective-permute-start(bf16[1,2,6,1,3072]{4,3,2,1,0:T(2,128)(2,1)S(1)} %get-tuple-element.24), channel_id=1, source_target_pairs={{1,0},{2,1},{3,2},{4,3},{5,4},{6,5},{7,6},{8,7},{9,8},{10,9},{11,1... | collective-permute-start | bytes 221192 | tf_op jit(solution)/shard_map/ppermute | solution.py:44
  62.2 34.0 %copy-start.2 = (bf16[64,3200]{1,0:T(8,128)(2,1)}, bf16[64,3200]{1,0:T(8,128)(2,1)S(1)}, u32[]{:S(2)}) copy-start(bf16[64,3200]{1,0:T(8,128)(2,1)S(1)} %get-tuple-element.22.x0) | copy-start | bytes 1228804
  62.2 34.0 %copy-start.1 = (bf16[64,3200]{1,0:T(8,128)(2,1)}, bf16[64,3200]{1,0:T(8,128)(2,1)S(1)}, u32[]{:S(2)}) copy-start(bf16[64,3200]{1,0:T(8,128)(2,1)S(1)} %get-tuple-element.21.x1) | copy-start | bytes 1228804
  62.2 13.2 %collective-permute-start.5 = (bf16[64,3200]{1,0:T(8,128)(2,1)S(1)}, bf16[64,3200]{1,0:T(8,128)(2,1)S(1)}, u32[]{:S(2)}, u32[]{:S(2)}) collective-permute-start(bf16[64,3200]{1,0:T(8,128)(2,1)S(1)} %get-tuple-element.21.x1), channel_id=1, source_target_pairs={{0,3},{1,0},{2,1},{3,2},{4,7},{5,4},{6,5},{7,6},{8,11},{9,8},{10,9... | collective-permute-start | bytes 1228808 | tf_op jit(solution)/shard_map/ppermute | solution.py:383
  64.2 15.3 %collective-permute-start.4 = (bf16[64,3200]{1,0:T(8,128)(2,1)S(1)}, bf16[64,3200]{1,0:T(8,128)(2,1)S(1)}, u32[]{:S(2)}, u32[]{:S(2)}) collective-permute-start(bf16[64,3200]{1,0:T(8,128)(2,1)S(1)} %get-tuple-element.22.x0), channel_id=1, source_target_pairs={{0,1},{1,2},{2,3},{3,0},{4,5},{5,6},{6,7},{7,4},{8,9},{9,10},{10,1... | collective-permute-start | bytes 1228808 | tf_op jit(solution)/shard_map/ppermute | solution.py:383
  69.6 17.6 %collective-permute-start.6 = (bf16[64,3200]{1,0:T(8,128)(2,1)S(1)}, bf16[64,3200]{1,0:T(8,128)(2,1)S(1)}, u32[]{:S(2)}, u32[]{:S(2)}) collective-permute-start(bf16[64,3200]{1,0:T(8,128)(2,1)S(1)} %get-tuple-element.21.x1), channel_id=1, source_target_pairs={{0,1},{1,2},{2,3},{3,0},{4,5},{5,6},{6,7},{7,4},{8,9},{9,10},{10,1... | collective-permute-start | bytes 1228808 | tf_op jit(solution)/shard_map/ppermute | solution.py:384
  73.5 14.1 %collective-permute-start.7 = (bf16[64,3200]{1,0:T(8,128)(2,1)S(1)}, bf16[64,3200]{1,0:T(8,128)(2,1)S(1)}, u32[]{:S(2)}, u32[]{:S(2)}) collective-permute-start(bf16[64,3200]{1,0:T(8,128)(2,1)S(1)} %get-tuple-element.22.x0), channel_id=1, source_target_pairs={{0,3},{1,0},{2,1},{3,2},{4,7},{5,4},{6,5},{7,6},{8,11},{9,8},{10,9... | collective-permute-start | bytes 1228808 | tf_op jit(solution)/shard_map/ppermute | solution.py:384
  79.5 11.0 %collective-permute-start.8 = (bf16[64,3200]{1,0:T(8,128)(2,1)S(1)}, bf16[64,3200]{1,0:T(8,128)(2,1)S(1)}, u32[]{:S(2)}, u32[]{:S(2)}) collective-permute-start(bf16[64,3200]{1,0:T(8,128)(2,1)S(1)} %collective-permute-done.4.a0), channel_id=1, source_target_pairs={{0,1},{1,2},{2,3},{3,0},{4,5},{5,6},{6,7},{7,4},{8,9},{9,10},{10,1... | collective-permute-start | bytes 1228808 | tf_op jit(solution)/shard_map/ppermute | solution.py:386
  85.1 11.2 %collective-permute-start.9 = (bf16[64,3200]{1,0:T(8,128)(2,1)S(1)}, bf16[64,3200]{1,0:T(8,128)(2,1)}, u32[]{:S(2)}, u32[]{:S(2)}) collective-permute-start(bf16[64,3200]{1,0:T(8,128)(2,1)S(1)} %collective-permute-done.5.b1), channel_id=1, source_target_pairs={{0,3},{1,0},{2,1},{3,2},{4,7},{5,4},{6,5},{7,6},{8,11},{9,8},{10,9... | collective-permute-start | bytes 1228808 | tf_op jit(solution)/shard_map/ppermute | solution.py:386
  102.5 25.2 %collective-permute-start.15 = (bf16[512,256]{1,0:T(8,128)(2,1)S(1)}, bf16[512,256]{1,0:T(8,128)(2,1)S(1)}, u32[]{:S(2)}, u32[]{:S(2)}) collective-permute-start(bf16[512,256]{1,0:T(8,128)(2,1)S(1)} %get-tuple-element.19.kv0), channel_id=1, source_target_pairs={{0,192},{64,0},{128,64},{192,128},{1,193},{65,1},{129,65},{193,129... | collective-permute-start | bytes 786440 | tf_op jit(solution)/shard_map/ppermute | solution.py:402
  108.7 19.0 %collective-permute-start.14 = (bf16[512,256]{1,0:T(8,128)(2,1)S(1)}, bf16[512,256]{1,0:T(8,128)(2,1)S(1)}, u32[]{:S(2)}, u32[]{:S(2)}) collective-permute-start(bf16[512,256]{1,0:T(8,128)(2,1)S(1)} %get-tuple-element.19.kv0), channel_id=1, source_target_pairs={{0,64},{64,128},{128,192},{192,0},{1,65},{65,129},{129,193},{193,1... | collective-permute-start | bytes 786440 | tf_op jit(solution)/shard_map/ppermute | solution.py:402
  110.6 11.8 %collective-permute-start.12 = (bf16[512,128]{1,0:T(8,128)(2,1)S(1)}, bf16[512,128]{1,0:T(8,128)(2,1)S(1)}, u32[]{:S(2)}, u32[]{:S(2)}) collective-permute-start(bf16[512,128]{1,0:T(8,128)(2,1)S(1)} %get-tuple-element.18.q_ref), channel_id=1, source_target_pairs={{0,48},{48,0},{16,32},{32,16},{1,49},{49,1},{17,33},{33,17},{2,50}... | collective-permute-start | bytes 393224 | tf_op jit(solution)/shard_map/ppermute | solution.py:401
  117.4 10.3 %collective-permute-start.11 = (bf16[512,128]{1,0:T(8,128)(2,1)S(1)}, bf16[512,128]{1,0:T(8,128)(2,1)S(1)}, u32[]{:S(2)}, u32[]{:S(2)}) collective-permute-start(bf16[512,128]{1,0:T(8,128)(2,1)S(1)} %get-tuple-element.18.q_ref), channel_id=1, source_target_pairs={{0,32},{32,0},{1,33},{33,1},{2,34},{34,2},{3,35},{35,3},{4,36},{36... | collective-permute-start | bytes 393224 | tf_op jit(solution)/shard_map/ppermute | solution.py:401
  119.3 8.4 %collective-permute-start.10 = (bf16[512,128]{1,0:T(8,128)(2,1)S(1)}, bf16[512,128]{1,0:T(8,128)(2,1)S(1)}, u32[]{:S(2)}, u32[]{:S(2)}) collective-permute-start(bf16[512,128]{1,0:T(8,128)(2,1)S(1)} %get-tuple-element.18.q_ref), channel_id=1, source_target_pairs={{0,16},{16,0},{1,17},{17,1},{2,18},{18,2},{3,19},{19,3},{4,20},{20... | collective-permute-start | bytes 393224 | tf_op jit(solution)/shard_map/ppermute | solution.py:401
  122.4 14.0 %collective-permute-start.13 = (bf16[512,256]{1,0:T(8,128)(2,1)S(1)}, bf16[512,256]{1,0:T(8,128)(2,1)S(1)}, u32[]{:S(2)}, u32[]{:S(2)}) collective-permute-start(bf16[512,256]{1,0:T(8,128)(2,1)S(1)} %get-tuple-element.19.kv0), channel_id=1, source_target_pairs={{0,128},{64,192},{128,0},{192,64},{1,129},{65,193},{129,1},{193,65... | collective-permute-start | bytes 786440 | tf_op jit(solution)/shard_map/ppermute | solution.py:403
  141.5 13.5 %all-to-all-start = ((bf16[4,576,128]{2,1,0:T(8,128)(2,1)}), bf16[4,576,128]{2,1,0:T(8,128)(2,1)S(1)}, u32[]{:S(2)}, u32[]{:S(2)}) async-start(bf16[4,576,128]{2,1,0:T(8,128)(2,1)} %rest.1), calls=%async_computation | async-start | bytes 1179648 | tf_op jit(solution)/shard_map/all_to_all | solution.py:412
  (5 other events, 44.6 us)
Sparse Core Ops, SparseCore 0:
  9.5 72.9 all-gather.1
